TPU v7x, 32 devices: a whole 2x2x4 slice. The times are simulated.
32 devices in a mesh: dp: 8 (over y, x, core), tensor: 4 (over z).
Axes of the slice: x: 2, y: 2, z: 4, core: 2. Of those that a mesh axis runs over, the one named last changes fastest.
Arguments:
- residual: bfloat16 [8192, 2048], P(('dp', 'tensor')), may hold values from -6 to 6
- attn_gain: float32 [2048], replicated, may hold values from 0.5 to 1.5
- w_query: bfloat16 [2048, 2048], P('dp', 'tensor'), may hold values from -0.125 to 0.125
- w_key: bfloat16 [2048, 2048], P('dp', 'tensor'), may hold values from -0.125 to 0.125
- w_value: bfloat16 [2048, 2048], P('dp', 'tensor'), may hold values from -0.125 to 0.125
- query_gain: float32 [2048], replicated, may hold values from 0.5 to 1.5
- key_gain: float32 [2048], replicated, may hold values from 0.5 to 1.5
- w_out: bfloat16 [2048, 2048], P('tensor', 'dp'), may hold values from -2 to 2
- moe_gain: float32 [2048], replicated, may hold values from 0.5 to 1.5
- router: bfloat16 [2048, 64], replicated, may hold values from -0.15625 to 0.15625
- w_gate: bfloat16 [64, 2048, 1024], P('dp', None, 'tensor'), may hold values from -0.125 to 0.125
- w_up: bfloat16 [64, 2048, 1024], P('dp', None, 'tensor'), may hold values from -0.125 to 0.125
- w_down: bfloat16 [64, 1024, 2048], P('dp', 'tensor'), may hold values from -6 to 6
- segment_path: int32 [3, 8192], P(None, 'dp'), may hold values from 0 to 63, as said below
- token_valid: int32 [8192], P('dp'), may hold values from 0 to 1, as said below
- routes: int32 [8192, 8], P(('dp', 'tensor')), may hold values from 0 to 63, all different within a row
- route_order: int32 [8192, 8], P(('dp', 'tensor')), may hold values from 0 to 2047, as said below
- cotangent: bfloat16 [8192, 2048], P(('dp', 'tensor')), may hold values from -6 to 6
Outputs:
- block_out: bfloat16 [8192, 2048], P(('dp', 'tensor'))
- grad_input: float32 [8192, 2048], P(('dp', 'tensor'))
- grad_attn_gain: float32 [2048], replicated
- grad_w_query: float32 [2048, 2048], P('dp', 'tensor')
- grad_w_key: float32 [2048, 2048], P('dp', 'tensor')
- grad_w_value: float32 [2048, 2048], P('dp', 'tensor')
- grad_query_gain: float32 [2048], replicated
- grad_key_gain: float32 [2048], replicated
- grad_w_out: float32 [2048, 2048], P('tensor', 'dp')
- grad_moe_gain: float32 [2048], replicated
- grad_router: float32 [2048, 64], replicated
- grad_w_gate: float32 [64, 2048, 1024], P('dp', None, 'tensor')
- grad_w_up: float32 [64, 2048, 1024], P('dp', None, 'tensor')
- grad_w_down: float32 [64, 1024, 2048], P('dp', 'tensor')
Inputs may be any that keep to these rules, and one draw needn't show every extreme that they name: `segment_path`: each group of 1024 consecutive tokens holds one tree in depth-first order: a trunk, then four branches, each followed by its two leaves, then padding tokens at the end. Row 0 is a token's segment id, row 1 its segment's parent's id (the trunk's own id on the trunk), row 2 the trunk's id. The 13 segment ids of a group are distinct. Padding tokens carry the path of the group's last leaf. `token_valid`: 1 on the tree's tokens, 0 on the padding tokens at the end of each group; every group has padding. `route_order`: within each aligned block of 256 tokens, the 2048 entries are a permutation of 0 to 2047.
All inputs are finite; a program needn't handle non-finite values.
Results may differ from a plain program's by a relative error of at most 0.02.
Values may be sent and summed in bfloat16 or wider, within the bound.
A program may use at most 448 MiB of HBM per device.

v0:
```python
import jax
import jax.numpy as jnp
from jax import lax
from jax.sharding import PartitionSpec as P

H = 16
HD = 128


norm_eps = 1e-05
rope_base = 10000.0
masked_score = -1e30


def slot_ranks(expert_ids, route_rank, live_pairs, experts, capacity):
    pairs = expert_ids.shape[0]
    by_order = jnp.zeros((pairs,), jnp.int32).at[route_rank].set(lax.iota(jnp.int32, pairs))
    sorted_ids = expert_ids[by_order]
    sorted_live = live_pairs[by_order]
    hits = (
        (sorted_ids[:, None] == lax.iota(jnp.int32, experts)[None, :]) & (sorted_live[:, None] == 1)
    ).astype(jnp.int32)
    earlier = jnp.cumsum(hits, axis=0) - hits
    rank_sorted = jnp.sum(earlier * hits, axis=1)
    keep_sorted = ((sorted_live == 1) & (rank_sorted < capacity)).astype(jnp.int32)
    ranks = jnp.zeros((pairs,), jnp.int32).at[by_order].set(rank_sorted)
    kept = jnp.zeros((pairs,), jnp.int32).at[by_order].set(keep_sorted)
    return (ranks, kept)


def visible_block(row_paths, key_paths, key_valid, row_first):
    row_count = row_paths.shape[1]
    key_count = key_paths.shape[1]
    key_segment = key_paths[0][None, :]
    on_path = (
        (key_segment == row_paths[0][:, None])
        | (key_segment == row_paths[1][:, None])
        | (key_segment == row_paths[2][:, None])
    )
    row_place = row_first + lax.iota(jnp.int32, row_count)
    key_place = lax.iota(jnp.int32, key_count)
    earlier = key_place[None, :] <= row_place[:, None]
    return on_path & earlier & (key_valid[None, :] == 1) | (
        key_place[None, :] == row_place[:, None]
    )


def rotation(positions, head_dim):
    half = head_dim // 2
    freqs = jnp.exp(-jnp.log(rope_base) * 2.0 * lax.iota(jnp.float32, half) / head_dim)
    angles = positions.astype(jnp.float32)[:, None] * freqs[None, :]
    return (jnp.cos(angles), jnp.sin(angles))


def rotate(values, cosine, sine):
    half = values.shape[-1] // 2
    first = values[..., :half]
    second = values[..., half:]
    cosine = cosine[:, None, :]
    sine = sine[:, None, :]
    return jnp.concatenate(
        (first * cosine - second * sine, second * cosine + first * sine), axis=-1
    )


def unrotate(grads, cosine, sine):
    half = grads.shape[-1] // 2
    first = grads[..., :half]
    second = grads[..., half:]
    cosine = cosine[:, None, :]
    sine = sine[:, None, :]
    return jnp.concatenate(
        (first * cosine + second * sine, second * cosine - first * sine), axis=-1
    )


def rms_apply(values, gain):
    scale = lax.rsqrt(jnp.mean(values * values, axis=-1, keepdims=True) + norm_eps)
    return (values * scale * gain, scale)


def rms_grad(values, scale, gain, grads, inner, width):
    grad_values = scale * gain * grads - values * scale**3 * inner / width
    grad_gain = jnp.sum(grads * values * scale, axis=0)
    return (grad_values, grad_gain)


def tensor_sums(pair):
    return lax.psum((pair[0], pair[1]), "tensor")


def heads_to_rows(term, rows):
    return lax.psum_scatter(
        term(jnp.int32(0), rows * lax.axis_size("tensor")),
        "tensor",
        scatter_dimension=0,
        tiled=True,
    )


def own_exchange(slots):
    return lax.all_to_all(slots, "dp", split_axis=1, concat_axis=1, tiled=True)


def to_experts(slots):
    return own_exchange(slots)


def from_experts(slots):
    return lax.all_to_all(slots, "dp", split_axis=1, concat_axis=1, tiled=True)


def body(
    residual,
    attn_gain,
    w_query,
    w_key,
    w_value,
    query_gain,
    key_gain,
    w_out,
    moe_gain,
    router,
    w_gate,
    w_up,
    w_down,
    segment_path,
    token_valid,
    routes,
    route_order,
    cotangent,
):
    tensor_rank = lax.axis_index("tensor")
    tok_dev, width = residual.shape
    seq_len = segment_path.shape[1]
    top_count = routes.shape[1]
    experts = router.shape[1]
    local_experts = w_gate.shape[0]
    dp_groups = experts // local_experts
    capacity = 9 * tok_dev * top_count // (8 * experts)
    full_width = H * HD
    block_rows = min(512, seq_len)
    block_count = seq_len // block_rows
    score_scale = HD ** (-0.5)
    gathered_query, gathered_key, gathered_value, gathered_out = (
        lax.all_gather(w_query, "dp", axis=0, tiled=True),
        lax.all_gather(w_key, "dp", axis=0, tiled=True),
        lax.all_gather(w_value, "dp", axis=0, tiled=True),
        lax.all_gather(w_out, "dp", axis=1, tiled=True),
    )
    head_cols = gathered_query.shape[1]
    local_heads = head_cols // HD
    joined_weight = jnp.concatenate((gathered_query, gathered_key, gathered_value), axis=1)
    residual_float = residual.astype(jnp.float32)
    normed_one, scale_one = rms_apply(residual_float, attn_gain)
    hidden = normed_one.astype(jnp.bfloat16)
    hidden_all = lax.all_gather(hidden, "tensor", axis=0, tiled=True)
    projected = jnp.dot(hidden_all, joined_weight, preferred_element_type=jnp.float32)
    q_raw = projected[:, :head_cols]
    k_raw = projected[:, head_cols : 2 * head_cols]
    value_low = projected[:, 2 * head_cols :].astype(jnp.bfloat16).reshape(seq_len, local_heads, HD)
    query_sq, key_sq = tensor_sums((jnp.sum(q_raw * q_raw, axis=1), jnp.sum(k_raw * k_raw, axis=1)))
    query_scale = lax.rsqrt(query_sq / full_width + norm_eps)[:, None]
    key_scale = lax.rsqrt(key_sq / full_width + norm_eps)[:, None]
    query_gain_dev = lax.dynamic_slice_in_dim(query_gain, tensor_rank * head_cols, head_cols)
    key_gain_dev = lax.dynamic_slice_in_dim(key_gain, tensor_rank * head_cols, head_cols)
    block_starts = lax.iota(jnp.int32, block_count) * block_rows

    def block_mask(row_first):
        row_paths = lax.dynamic_slice_in_dim(segment_path, row_first, block_rows, 1)
        return visible_block(row_paths, segment_path, token_valid, row_first)

    def count_seen(row_first):
        return jnp.sum(block_mask(row_first).astype(jnp.int32), axis=1)

    positions = lax.map(count_seen, block_starts).reshape(seq_len) - 1
    cosine, sine = rotation(positions, HD)
    query_low = rotate(
        (q_raw * query_scale * query_gain_dev).reshape(seq_len, local_heads, HD), cosine, sine
    ).astype(jnp.bfloat16)
    key_low = rotate(
        (k_raw * key_scale * key_gain_dev).reshape(seq_len, local_heads, HD), cosine, sine
    ).astype(jnp.bfloat16)

    def attend(row_first):
        visible = block_mask(row_first)
        query_block = lax.dynamic_slice_in_dim(query_low, row_first, block_rows, 0)
        scores = (
            jnp.einsum("qhd,khd->hqk", query_block, key_low, preferred_element_type=jnp.float32)
            * score_scale
        )
        scores = jnp.where(visible[None], scores, masked_score)
        top_score = jnp.max(scores, axis=-1, keepdims=True)
        exp_scores = jnp.exp(scores - top_score)
        total = jnp.sum(exp_scores, axis=-1, keepdims=True)
        weights_low = (exp_scores / total).astype(jnp.bfloat16)
        mixed_block = jnp.einsum(
            "hqk,khd->qhd", weights_low, value_low, preferred_element_type=jnp.float32
        )
        return (mixed_block.astype(jnp.bfloat16), (top_score + jnp.log(total))[..., 0])

    mixed_blocks, log_totals = lax.map(attend, block_starts)
    attn_mixed = mixed_blocks.reshape(seq_len, head_cols)

    def attn_term(first_row, row_count):
        return jnp.dot(attn_mixed, gathered_out, preferred_element_type=jnp.float32)

    x_one = residual_float + heads_to_rows(attn_term, tok_dev)
    normed_two, scale_two = rms_apply(x_one, moe_gain)
    hidden_two = normed_two.astype(jnp.bfloat16)
    logits = jnp.dot(hidden_two, router, preferred_element_type=jnp.float32)
    probs = jax.nn.softmax(logits, axis=-1)
    gates = jnp.take_along_axis(probs, routes, axis=1)
    valid_dev = lax.dynamic_slice_in_dim(token_valid, tensor_rank * tok_dev, tok_dev)
    pair_count = tok_dev * top_count
    expert_ids = routes.reshape(pair_count)
    ranks, kept = slot_ranks(
        expert_ids,
        route_order.reshape(pair_count),
        jnp.repeat(valid_dev, top_count),
        experts,
        capacity,
    )
    slot_total = capacity * experts
    pair_slot = jnp.where(kept == 1, ranks * experts + expert_ids, slot_total)
    pair_token = lax.iota(jnp.int32, pair_count) // top_count
    slot_token = (
        jnp.full((slot_total + 1,), tok_dev, jnp.int32).at[pair_slot].set(pair_token)[:slot_total]
    )
    gate_kept = gates.reshape(pair_count) * kept.astype(jnp.float32)
    gate_slot = jnp.zeros((slot_total + 1,), jnp.float32).at[pair_slot].set(gate_kept)[:slot_total]
    zero_row = jnp.zeros((1, width), jnp.bfloat16)
    rows_pad = jnp.concatenate((hidden_two, zero_row), axis=0)
    send_rows = rows_pad[slot_token].reshape(capacity, dp_groups, local_experts, width)
    expert_in = to_experts(send_rows)
    gate_weight, up_weight, down_weight = (
        lax.all_gather(w_gate, "tensor", axis=2, tiled=True),
        lax.all_gather(w_up, "tensor", axis=2, tiled=True),
        lax.all_gather(w_down, "tensor", axis=1, tiled=True),
    )
    gate_pre = jnp.einsum(
        "rged,edf->rgef", expert_in, gate_weight, preferred_element_type=jnp.float32
    )
    up_pre = jnp.einsum("rged,edf->rgef", expert_in, up_weight, preferred_element_type=jnp.float32)
    sigmoid_gate = jax.nn.sigmoid(gate_pre)
    silu_gate = gate_pre * sigmoid_gate
    act = (silu_gate * up_pre).astype(jnp.bfloat16)
    expert_out = jnp.einsum(
        "rgef,efd->rged", act, down_weight, preferred_element_type=jnp.float32
    ).astype(jnp.bfloat16)
    returned = from_experts(expert_out)
    out_pad = jnp.concatenate((returned.reshape(slot_total, width), zero_row), axis=0)
    pair_out = out_pad[pair_slot].reshape(tok_dev, top_count, width)
    moe_out = jnp.sum(
        pair_out.astype(jnp.float32) * gate_kept.reshape(tok_dev, top_count, 1), axis=1
    )
    block_out = (x_one + moe_out).astype(jnp.bfloat16)
    grad_out = cotangent.astype(jnp.float32)
    grad_gates = jnp.sum(
        pair_out.astype(jnp.float32) * grad_out[:, None, :], axis=-1
    ) * kept.reshape(tok_dev, top_count).astype(jnp.float32)
    cot_pad = jnp.concatenate((cotangent, zero_row), axis=0)
    grad_rows_send = (
        (cot_pad[slot_token].astype(jnp.float32) * gate_slot[:, None])
        .astype(jnp.bfloat16)
        .reshape(capacity, dp_groups, local_experts, width)
    )
    grad_expert_out = to_experts(grad_rows_send)
    grad_act = jnp.einsum(
        "rged,efd->rgef", grad_expert_out, down_weight, preferred_element_type=jnp.float32
    )
    grad_down_part = jnp.einsum(
        "rgef,rged->efd", act, grad_expert_out, preferred_element_type=jnp.float32
    )
    grad_gate_pre = (
        grad_act * up_pre * sigmoid_gate * (1.0 + gate_pre * (1.0 - sigmoid_gate))
    ).astype(jnp.bfloat16)
    grad_up_pre = (grad_act * silu_gate).astype(jnp.bfloat16)
    grad_gate_part = jnp.einsum(
        "rged,rgef->edf", expert_in, grad_gate_pre, preferred_element_type=jnp.float32
    )
    grad_up_part = jnp.einsum(
        "rged,rgef->edf", expert_in, grad_up_pre, preferred_element_type=jnp.float32
    )
    from_gate = jnp.einsum(
        "rgef,edf->rged", grad_gate_pre, gate_weight, preferred_element_type=jnp.float32
    )
    grad_expert_in = (
        from_gate
        + jnp.einsum("rgef,edf->rged", grad_up_pre, up_weight, preferred_element_type=jnp.float32)
    ).astype(jnp.bfloat16)
    grad_w_gate, grad_w_up, grad_w_down = (
        lax.psum_scatter(
            grad_gate_part.astype(jnp.bfloat16), "tensor", scatter_dimension=2, tiled=True
        ).astype(jnp.float32),
        lax.psum_scatter(
            grad_up_part.astype(jnp.bfloat16), "tensor", scatter_dimension=2, tiled=True
        ).astype(jnp.float32),
        lax.psum_scatter(
            grad_down_part.astype(jnp.bfloat16), "tensor", scatter_dimension=1, tiled=True
        ).astype(jnp.float32),
    )
    grad_returned = from_experts(grad_expert_in)
    grad_pad = jnp.concatenate((grad_returned.reshape(slot_total, width), zero_row), axis=0)
    grad_hidden_two = jnp.sum(
        grad_pad[pair_slot].reshape(tok_dev, top_count, width).astype(jnp.float32), axis=1
    )
    route_hits = (routes[:, :, None] == lax.iota(jnp.int32, experts)[None, None, :]).astype(
        jnp.float32
    )
    grad_probs = jnp.sum(route_hits * grad_gates[:, :, None], axis=1)
    grad_logits = probs * (grad_probs - jnp.sum(probs * grad_probs, axis=-1, keepdims=True))
    router_float = router.astype(jnp.float32)
    grad_hidden_two = grad_hidden_two + lax.dot_general(
        grad_logits, router_float, (((1,), (1,)), ((), ())), precision=lax.Precision.HIGHEST
    )
    grad_router_part = lax.dot_general(
        hidden_two.astype(jnp.float32),
        grad_logits,
        (((0,), (0,)), ((), ())),
        precision=lax.Precision.HIGHEST,
    )
    inner_two = jnp.sum(grad_hidden_two * moe_gain * x_one, axis=-1, keepdims=True)
    grad_norm_two, grad_moe_gain_part = rms_grad(
        x_one, scale_two, moe_gain, grad_hidden_two, inner_two, width
    )
    grad_x_one = grad_out + grad_norm_two
    grad_attn_all = lax.all_gather(grad_x_one.astype(jnp.bfloat16), "tensor", axis=0, tiled=True)
    grad_out_weight = lax.dot_general(
        attn_mixed, grad_attn_all, (((0,), (0,)), ((), ())), preferred_element_type=jnp.float32
    )
    grad_mixed = (
        lax.dot_general(
            grad_attn_all,
            gathered_out,
            (((1,), (1,)), ((), ())),
            preferred_element_type=jnp.float32,
        )
        .astype(jnp.bfloat16)
        .reshape(seq_len, local_heads, HD)
    )

    def attend_back(carry, pieces):
        grad_key_sum, grad_value_sum = carry
        row_first, log_total = pieces
        visible = block_mask(row_first)
        query_block = lax.dynamic_slice_in_dim(query_low, row_first, block_rows, 0)
        grad_block = lax.dynamic_slice_in_dim(grad_mixed, row_first, block_rows, 0)
        scores = (
            jnp.einsum("qhd,khd->hqk", query_block, key_low, preferred_element_type=jnp.float32)
            * score_scale
        )
        scores = jnp.where(visible[None], scores, masked_score)
        weights = jnp.exp(scores - log_total[..., None])
        grad_weights = jnp.einsum(
            "qhd,khd->hqk", grad_block, value_low, preferred_element_type=jnp.float32
        )
        inner = jnp.sum(weights * grad_weights, axis=-1, keepdims=True)
        grad_scores = (weights * (grad_weights - inner)).astype(jnp.bfloat16)
        grad_query_block = (
            jnp.einsum("hqk,khd->qhd", grad_scores, key_low, preferred_element_type=jnp.float32)
            * score_scale
        )
        grad_key_sum = (
            grad_key_sum
            + jnp.einsum(
                "hqk,qhd->khd", grad_scores, query_block, preferred_element_type=jnp.float32
            )
            * score_scale
        )
        grad_value_sum = grad_value_sum + jnp.einsum(
            "hqk,qhd->khd",
            weights.astype(jnp.bfloat16),
            grad_block,
            preferred_element_type=jnp.float32,
        )
        return ((grad_key_sum, grad_value_sum), grad_query_block)

    zero_heads = jnp.zeros((seq_len, local_heads, HD), jnp.float32)
    (grad_key_all, grad_value_all), grad_query_blocks = lax.scan(
        attend_back, (zero_heads, zero_heads), (block_starts, log_totals)
    )
    grad_q_norm = unrotate(
        grad_query_blocks.reshape(seq_len, local_heads, HD), cosine, sine
    ).reshape(seq_len, head_cols)
    grad_k_norm = unrotate(grad_key_all, cosine, sine).reshape(seq_len, head_cols)
    query_inner, key_inner = tensor_sums(
        (
            jnp.sum(grad_q_norm * query_gain_dev * q_raw, axis=1),
            jnp.sum(grad_k_norm * key_gain_dev * k_raw, axis=1),
        )
    )
    grad_q_raw, grad_query_gain_dev = rms_grad(
        q_raw, query_scale, query_gain_dev, grad_q_norm, query_inner[:, None], full_width
    )
    grad_k_raw, grad_key_gain_dev = rms_grad(
        k_raw, key_scale, key_gain_dev, grad_k_norm, key_inner[:, None], full_width
    )
    grad_joined = jnp.concatenate(
        (grad_q_raw, grad_k_raw, grad_value_all.reshape(seq_len, head_cols)), axis=1
    ).astype(jnp.bfloat16)
    grad_joined_weight = lax.dot_general(
        hidden_all, grad_joined, (((0,), (0,)), ((), ())), preferred_element_type=jnp.float32
    )

    def back_term(first_row, row_count):
        return lax.dot_general(
            grad_joined, joined_weight, (((1,), (1,)), ((), ())), preferred_element_type=jnp.float32
        )

    grad_hidden = heads_to_rows(back_term, tok_dev)
    inner_one = jnp.sum(grad_hidden * attn_gain * residual_float, axis=-1, keepdims=True)
    grad_norm_one, grad_attn_gain_part = rms_grad(
        residual_float, scale_one, attn_gain, grad_hidden, inner_one, width
    )
    grad_input = grad_x_one + grad_norm_one
    grad_w_query, grad_w_key, grad_w_value, grad_w_out = (
        lax.psum_scatter(
            grad_joined_weight[:, :head_cols].astype(jnp.bfloat16),
            "dp",
            scatter_dimension=0,
            tiled=True,
        ).astype(jnp.float32),
        lax.psum_scatter(
            grad_joined_weight[:, head_cols : 2 * head_cols].astype(jnp.bfloat16),
            "dp",
            scatter_dimension=0,
            tiled=True,
        ).astype(jnp.float32),
        lax.psum_scatter(
            grad_joined_weight[:, 2 * head_cols :].astype(jnp.bfloat16),
            "dp",
            scatter_dimension=0,
            tiled=True,
        ).astype(jnp.float32),
        lax.psum_scatter(
            grad_out_weight.astype(jnp.bfloat16), "dp", scatter_dimension=1, tiled=True
        ).astype(jnp.float32),
    )
    zero_width = jnp.zeros((full_width,), jnp.float32)
    grad_query_full = lax.dynamic_update_slice_in_dim(
        zero_width, grad_query_gain_dev, tensor_rank * head_cols, 0
    )
    grad_key_full = lax.dynamic_update_slice_in_dim(
        zero_width, grad_key_gain_dev, tensor_rank * head_cols, 0
    )
    summed = lax.psum(
        (grad_attn_gain_part, grad_moe_gain_part, grad_query_full, grad_key_full, grad_router_part),
        ("dp", "tensor"),
    )
    return (
        block_out,
        grad_input,
        summed[0],
        grad_w_query,
        grad_w_key,
        grad_w_value,
        summed[2],
        summed[3],
        grad_w_out,
        summed[1],
        summed[4],
        grad_w_gate,
        grad_w_up,
        grad_w_down,
    )


def solution(mesh):
    in_specs = (
        P(("dp", "tensor"), None),
        P(),
        P("dp", "tensor"),
        P("dp", "tensor"),
        P("dp", "tensor"),
        P(),
        P(),
        P("tensor", "dp"),
        P(),
        P(),
        P("dp", None, "tensor"),
        P("dp", None, "tensor"),
        P("dp", "tensor", None),
        P(None, "dp"),
        P("dp"),
        P(("dp", "tensor"), None),
        P(("dp", "tensor"), None),
        P(("dp", "tensor"), None),
    )
    out_specs = (
        P(("dp", "tensor"), None),
        P(("dp", "tensor"), None),
        P(),
        P("dp", "tensor"),
        P("dp", "tensor"),
        P("dp", "tensor"),
        P(),
        P(),
        P("tensor", "dp"),
        P(),
        P(),
        P("dp", None, "tensor"),
        P("dp", None, "tensor"),
        P("dp", "tensor", None),
    )
    return jax.shard_map(body, mesh=mesh, in_specs=in_specs, out_specs=out_specs, check_vma=False)
```

profile of v0, /device:TPU:0, one launch (start us, length us, event | category | flops | bytes accessed | tf_op | source)
XLA Modules:
  0.0 4818.6 jit_solution(612761811683468921)
XLA Ops:
  15.8 9.3 while.37
  28.2 12.4 all-gather.12.cloned.1.call-done
  43.8 26.6 all-gather.14.cloned.1.call-done
  73.5 26.7 all-gather.16.cloned.1.call-done
  103.3 79.7 %all-gather.10.cloned.1.call-done = bf16[1024,2048]{1,0:T(8,128)(2,1)} async-done(((bf16[256,2048]{1,0:T(8,128)(2,1)}), bf16[1024,2048]{1,0:T(8,128)(2,1)}) %all-gather.10.cloned.1.call-update) | async-done | bytes 4194320 | tf_op jit(solution)/shard_map/all_gather | solution.py:157
  183.0 10.0 fusion.135
  195.9 9.3 all-reduce.6
  222.3 26.9 while.38
  249.3 8.7 fusion.102
  261.2 8.0 scatter_custom_fusion
  269.3 11.8 gather_fusion.1
  281.1 11.8 gather_fusion
  293.0 18.1 reduce-window.6
  312.4 8.0 scatter_custom_fusion.2
  320.4 8.0 scatter_custom_fusion.1
  329.1 8.1 scatter_custom_fusion.3
  337.2 64.6 %reduce-scatter.10.cloned.1.call-done = f32[256,2048]{1,0:T(8,128)} async-done(((f32[1024,2048]{1,0:T(8,128)}), f32[256,2048]{1,0:T(8,128)}) %reduce-scatter.10.cloned.1.call-update) | async-done | bytes 2097168 | tf_op jit(solution)/shard_map/reduce_scatter | solution.py:93
  405.5 9.8 gather_fusion.2
  415.3 11.3 copy.220
  432.4 9.8 gather_fusion.4
  443.5 16.8 gather_fusion.6
  460.8 8.1 scatter_custom_fusion.4
  469.0 9.0 fusion.54
  478.0 9.4 copy.228
  487.4 50.2 %all-to-all-done = bf16[36,8,8,2048]{3,2,0,1:T(8,128)(2,1)} async-done(((bf16[36,8,8,2048]{3,2,0,1:T(8,128)(2,1)}), bf16[36,8,8,2048]{3,2,0,1:T(8,128)(2,1)}, u32[]{:S(2)}, u32[]{:S(2)}) %all-to-all-start) | async-done | bytes 9437216 | tf_op jit(solution)/shard_map/all_to_all | solution.py:102
  542.8 422.3 %all-gather.22.cloned.1.call-done = bf16[8,2048,1024]{2,1,0:T(8,128)(2,1)} async-done(((bf16[8,2048,256]{2,1,0:T(8,128)(2,1)}), bf16[8,2048,1024]{2,1,0:T(8,128)(2,1)}) %all-gather.22.cloned.1.call-update) | async-done | bytes 33554448 | tf_op jit(solution)/shard_map/all_gather | solution.py:238
  965.1 37.2 fusion.44
  1002.2 523.5 %all-gather.20.cloned.1.call-done = bf16[8,2048,1024]{2,1,0:T(8,128)(2,1)} async-done(((bf16[8,2048,256]{2,1,0:T(8,128)(2,1)}), bf16[8,2048,1024]{2,1,0:T(8,128)(2,1)}) %all-gather.20.cloned.1.call-update) | async-done | bytes 33554448 | tf_op jit(solution)/shard_map/all_gather | solution.py:237
  1525.8 37.4 fusion.48
  1563.2 523.8 %all-gather.24.cloned.1.call-done = bf16[8,1024,2048]{2,1,0:T(8,128)(2,1)} async-done(((bf16[8,256,2048]{2,1,0:T(8,128)(2,1)}), bf16[8,1024,2048]{2,1,0:T(8,128)(2,1)}) %all-gather.24.cloned.1.call-update) | async-done | bytes 33554448 | tf_op jit(solution)/shard_map/all_gather | solution.py:239
  2087.0 68.5 %fusion.60 = (bf16[36,8,8,1024]{3,1,0,2:T(8,128)(2,1)}, bf16[36,8,8,1024]{3,1,0,2:T(8,128)(2,1)}, bf16[36,8,8,1024]{3,1,0,2:T(8,128)(2,1)}) fusion(f32[8,36,8,1024]{3,2,1,0:T(8,128)} %fusion.44, f32[8,36,8,1024]{3,2,1,0:T(8,128)} %fusion.48, bf16[8,1024,2048]{2,1,0:T(8,128)(2,1)} %all-gather.24.cloned.1.call-done, bf16[36,8,8,2048]{3,2,0,1:T(8,128)(2,1)} %all-to-all-done.2), kind=kOutput, calls=%fused_computation.107 | convolution fusion | flops 9699065856 | bytes 76021760 | tf_op jit(solution)/shard_map/rged,efd->rgef/dot_general | solution.py:269
  2155.4 21.7 fusion.42
  2177.1 23.7 fusion.57
  2200.9 12.6 copy.230
  2218.8 29.1 convert_bitcast_fusion
  2247.8 12.6 copy.223
  2260.5 63.6 %all-to-all-done.3 = bf16[36,8,8,2048]{3,2,0,1:T(8,128)(2,1)} async-done(((bf16[36,8,8,2048]{3,2,0,1:T(8,128)(2,1)}), bf16[36,8,8,2048]{3,2,0,1:T(8,128)(2,1)}, u32[]{:S(2)}, u32[]{:S(2)}) %all-to-all-start.3) | async-done | bytes 9437216 | tf_op jit(solution)/shard_map/all_to_all | solution.py:110
  2332.3 9.4 copy.231
  2341.7 9.4 concatenate.39
  2351.1 21.4 gather_fusion.5
  2372.5 11.3 convert_reduce_fusion.1
  2383.8 50.6 %all-to-all-done.1 = bf16[36,8,8,2048]{3,2,0,1:T(8,128)(2,1)} async-done(((bf16[36,8,8,2048]{3,2,0,1:T(8,128)(2,1)}), bf16[36,8,8,2048]{3,2,0,1:T(8,128)(2,1)}, u32[]{:S(2)}, u32[]{:S(2)}) %all-to-all-start.1) | async-done | bytes 9437216 | tf_op jit(solution)/shard_map/all_to_all | solution.py:110
  2434.5 9.4 copy.224
  2443.8 9.4 concatenate.37
  2453.2 21.6 gather_fusion.3
  2474.9 10.0 fusion.56
  2495.7 77.2 %all-gather.26.cloned.1.call-done = bf16[1024,2048]{1,0:T(8,128)(2,1)} async-done(((bf16[256,2048]{1,0:T(8,128)(2,1)}), bf16[1024,2048]{1,0:T(8,128)(2,1)}) %all-gather.26.cloned.1.call-update) | async-done | bytes 4194320 | tf_op jit(solution)/shard_map/all_gather | solution.py:328
  2579.2 67.1 %while.39 = (s32[]{:T(128)}, f32[1024,4,128]{0,2,1:T(8,128)S(1)}, f32[1024,4,128]{0,2,1:T(8,128)}, f32[2,512,4,128]{3,1,0,2:T(8,128)}, s32[2]{0:T(128)S(1)}, /*i...) while((s32[]{:T(128)}, f32[1024,4,128]{0,2,1:T(8,128)S(1)}, ...), condition=%wide.region_32.33_spmd.clone, body=%wide.region_30.32_spmd.clone.sunk | while | flops 2723937792 | bytes 163676752 | solution.py:380
  2659.7 9.1 all-reduce.5
  2694.6 11.0 fusion.99
  2705.6 32.9 bitcast_convert_fusion.2
  2738.6 32.8 bitcast_convert_fusion.1
  2771.5 29.1 bitcast_convert_fusion
  2807.6 8.9 reduce-scatter.18.cloned.1.call-done
  2818.4 42.8 reduce-scatter.20.cloned.1.call-done
  2863.0 145.5 %reduce-scatter.12.cloned.1.call-done = f32[256,2048]{1,0:T(8,128)} async-done(((f32[1024,2048]{1,0:T(8,128)}), f32[256,2048]{1,0:T(8,128)}) %reduce-scatter.12.cloned.1.call-update) | async-done | bytes 2097168 | tf_op jit(solution)/shard_map/reduce_scatter | solution.py:93
  3012.8 46.0 all-reduce.4
  3058.7 505.8 %reduce-scatter.22.cloned.1.call-done = bf16[8,2048,256]{2,1,0:T(8,128)(2,1)} async-done(((bf16[8,2048,1024]{2,1,0:T(8,128)(2,1)}), bf16[8,2048,256]{2,1,0:T(8,128)(2,1)}) %reduce-scatter.22.cloned.1.call-update) | async-done | bytes 8388624 | tf_op jit(solution)/shard_map/reduce_scatter | solution.py:293
  3564.5 11.2 convert_element_type.196
  3575.7 543.9 %reduce-scatter.24.cloned.1.call-done = bf16[8,2048,256]{2,1,0:T(8,128)(2,1)} async-done(((bf16[8,2048,1024]{2,1,0:T(8,128)(2,1)}), bf16[8,2048,256]{2,1,0:T(8,128)(2,1)}) %reduce-scatter.24.cloned.1.call-update) | async-done | bytes 8388624 | tf_op jit(solution)/shard_map/reduce_scatter | solution.py:296
  4119.7 11.2 convert_element_type.198
  4130.9 543.8 %reduce-scatter.26.cloned.1.call-done = bf16[8,256,2048]{2,1,0:T(8,128)(2,1)} async-done(((bf16[8,1024,2048]{2,1,0:T(8,128)(2,1)}), bf16[8,256,2048]{2,1,0:T(8,128)(2,1)}) %reduce-scatter.26.cloned.1.call-update) | async-done | bytes 8388624 | tf_op jit(solution)/shard_map/reduce_scatter | solution.py:299
  4674.7 11.7 convert_element_type.200
  4686.4 123.6 %all-reduce.9.cloned.1.call-done = f32[2048,64]{0,1:T(8,128)} async-done(((f32[2048,64]{0,1:T(8,128)}), f32[2048,64]{0,1:T(8,128)}) %all-reduce.9.cloned.1.call-update) | async-done | bytes 524304 | tf_op jit(solution)/shard_map/psum | solution.py:447
  (434 shorter events, 239.3 us)
Async XLA Ops:
  7.2 435.2 %copy-start = (bf16[2048,64]{0,1:T(8,128)(2,1)S(1)}, bf16[2048,64]{0,1:T(8,128)(2,1)}, u32[]{:S(2)}) copy-start(bf16[2048,64]{0,1:T(8,128)(2,1)} %param.33) | copy-start | bytes 786436
  7.2 33.4 all-gather.12.cloned.1.call-start
  7.9 62.5 %all-gather.14.cloned.1.call-start = ((), (), s32[]{:S(2)}) async-start(), calls=%async_computation.15 | async-start | bytes 2359296 | tf_op jit(solution)/shard_map/all_gather | solution.py:147
  8.7 91.5 %all-gather.16.cloned.1.call-start = ((), (), s32[]{:S(2)}) async-start(), calls=%async_computation.16 | async-start | bytes 2359296 | tf_op jit(solution)/shard_map/all_gather | solution.py:148
  9.4 173.6 %all-gather.10.cloned.1.call-start = ((), (), s32[]{:S(2)}) async-start(), calls=%async_computation.13 | async-start | bytes 5242880 | tf_op jit(solution)/shard_map/all_gather | solution.py:157
  11.6 16.7 copy-start.75
  13.6 235.8 %all-gather.18.cloned.1.call-start = ((), (), s32[]{:S(2)}) async-start(), calls=%async_computation.17 | async-start | bytes 2359296 | tf_op jit(solution)/shard_map/all_gather | solution.py:149
  14.2 387.7 %reduce-scatter.10.cloned.1.call-start = ((), (), s32[]{:S(2)}) async-start(), calls=%async_computation.18 | async-start | bytes 10485760 | tf_op jit(solution)/shard_map/reduce_scatter | solution.py:93
  15.0 190.8 %copy-start.70 = (f32[512]{0:T(512)}, f32[512]{0:T(512)S(1)}, u32[]{:S(2)}) copy-start(f32[512]{0:T(512)S(1)} %dynamic_slice.42) | copy-start | bytes 6148
  15.8 190.0 %copy-start.72 = (f32[512]{0:T(512)}, f32[512]{0:T(512)S(1)}, u32[]{:S(2)}) copy-start(f32[512]{0:T(512)S(1)} %dynamic_slice.41) | copy-start | bytes 6148
  249.2 8.8 copy-start.6
  249.2 8.8 copy-start.10
  249.2 8.8 copy-start.12
  249.3 8.8 copy-start.40
  249.3 8.8 copy-start.56
  249.3 8.8 copy-start.93
  249.3 11.6 copy-start.51
  258.1 707.0 %all-gather.22.cloned.1.call-start = ((), (), s32[]{:S(2)}) async-start(), calls=%async_computation.20 | async-start | bytes 41943040 | tf_op jit(solution)/shard_map/all_gather | solution.py:238
  258.9 1266.9 %all-gather.20.cloned.1.call-start = ((), (), s32[]{:S(2)}) async-start(), calls=%async_computation.19 | async-start | bytes 41943040 | tf_op jit(solution)/shard_map/all_gather | solution.py:237
  259.6 1827.3 %all-gather.24.cloned.1.call-start = ((), (), s32[]{:S(2)}) async-start(), calls=%async_computation.21 | async-start | bytes 41943040 | tf_op jit(solution)/shard_map/all_gather | solution.py:239
  292.9 108.9 %copy-start.16 = (bf16[256,2048]{1,0:T(8,128)(2,1)S(1)}, bf16[256,2048]{1,0:T(8,128)(2,1)}, u32[]{:S(2)}) copy-start(bf16[256,2048]{1,0:T(8,128)(2,1)} %param.24) | copy-start | bytes 3145732
  337.2 68.0 %copy-start.60 = (f32[2048]{0:T(1024)S(1)}, f32[2048]{0:T(1024)}, u32[]{:S(2)}) copy-start(f32[2048]{0:T(1024)} %param.32) | copy-start | bytes 24580
  405.4 37.0 copy-start.21
  426.6 111.0 %all-to-all-start = ((bf16[36,8,8,2048]{3,2,0,1:T(8,128)(2,1)}), bf16[36,8,8,2048]{3,2,0,1:T(8,128)(2,1)}, u32[]{:S(2)}, u32[]{:S(2)}) async-start(bf16[36,8,8,2048]{3,2,0,1:T(8,128)(2,1)} %copy.220), calls=%async_computation.1 | async-start | bytes 18874368 | tf_op jit(solution)/shard_map/all_to_all | solution.py:102
  442.9 17.5 copy-start.74
  443.5 16.8 copy-start.81
  443.5 16.8 copy-start.2
  460.8 8.1 copy-start.68
  537.6 1025.6 %all-to-all-start.2 = ((bf16[36,8,8,2048]{3,2,0,1:T(8,128)(2,1)}), bf16[36,8,8,2048]{3,2,0,1:T(8,128)(2,1)}, u32[]{:S(2)}, u32[]{:S(2)}) async-start(bf16[36,8,8,2048]{3,2,0,1:T(8,128)(2,1)} %copy.228), calls=%async_computation.3 | async-start | bytes 18874368 | tf_op jit(solution)/shard_map/all_to_all | solution.py:102
  2213.5 110.5 %all-to-all-start.3 = ((bf16[36,8,8,2048]{3,2,0,1:T(8,128)(2,1)}), bf16[36,8,8,2048]{3,2,0,1:T(8,128)(2,1)}, u32[]{:S(2)}, u32[]{:S(2)}) async-start(bf16[36,8,8,2048]{3,2,0,1:T(8,128)(2,1)} %copy.230), calls=%async_computation.4 | async-start | bytes 18874368 | tf_op jit(solution)/shard_map/all_to_all | solution.py:110
  2260.5 68.8 %copy-start.24 = (bf16[256,2048]{1,0:T(8,128)(2,1)S(1)}, bf16[256,2048]{1,0:T(8,128)(2,1)}, u32[]{:S(2)}) copy-start(bf16[256,2048]{1,0:T(8,128)(2,1)} %param.41) | copy-start | bytes 3145732
  2324.1 110.4 %all-to-all-start.1 = ((bf16[36,8,8,2048]{3,2,0,1:T(8,128)(2,1)}), bf16[36,8,8,2048]{3,2,0,1:T(8,128)(2,1)}, u32[]{:S(2)}, u32[]{:S(2)}) async-start(bf16[36,8,8,2048]{3,2,0,1:T(8,128)(2,1)} %copy.223), calls=%async_computation.2 | async-start | bytes 18874368 | tf_op jit(solution)/shard_map/all_to_all | solution.py:110
  2329.2 243.7 %all-gather.26.cloned.1.call-start = ((), (), s32[]{:S(2)}) async-start(), calls=%async_computation.22 | async-start | bytes 5242880 | tf_op jit(solution)/shard_map/all_gather | solution.py:328
  2341.7 9.4 copy-start.59
  2474.8 10.0 copy-start.53
  2474.8 12.3 copy-start.55
  2474.8 13.0 copy-start.47
  2474.8 13.8 copy-start.3
  2474.8 13.8 copy-start.14
  2474.8 13.8 copy-start.61
  2495.5 308.5 %reduce-scatter.14.cloned.1.call-start = ((), (), s32[]{:S(2)}) async-start(), calls=%async_computation.24 | async-start | bytes 2359296 | tf_op jit(solution)/shard_map/reduce_scatter | solution.py:418
  2495.6 83.5 %copy-start.7 = (bf16[1024,4,128]{2,0,1:T(8,128)(2,1)S(1)}, bf16[1024,4,128]{2,0,1:T(8,128)(2,1)}, u32[]{:S(2)}) copy-start(bf16[1024,4,128]{2,0,1:T(8,128)(2,1)} %copy-done.6) | copy-start | bytes 3145732
  2495.6 83.5 %copy-start.41 = (s32[3,1024]{1,0:T(4,128)S(1)}, s32[3,1024]{1,0:T(4,128)}, u32[]{:S(2)}) copy-start(s32[3,1024]{1,0:T(4,128)} %copy-done.40) | copy-start | bytes 36868
  2495.6 83.5 %copy-start.52 = (s32[1024]{0:T(1024)S(1)}, s32[1024]{0:T(1024)}, u32[]{:S(2)}) copy-start(s32[1024]{0:T(1024)} %copy-done.51) | copy-start | bytes 12292
  2495.6 83.5 %copy-start.57 = (f32[2,4,512]{2,1,0:T(4,128)S(1)}, f32[2,4,512]{2,1,0:T(4,128)}, u32[]{:S(2)}) copy-start(f32[2,4,512]{2,1,0:T(4,128)} %copy-done.56) | copy-start | bytes 49156
  2495.6 83.5 %copy-start.94 = (s32[2]{0:T(128)S(1)}, s32[2]{0:T(128)}, u32[]{:S(2)}) copy-start(s32[2]{0:T(128)} %copy-done.93) | copy-start | bytes 28
  2589.6 7.6 copy-start.8
  2589.6 7.6 slice-start
  2656.7 12.1 copy-start.77
  2656.7 12.1 copy-start.78
  2685.6 120.2 %reduce-scatter.16.cloned.1.call-start = ((), (), s32[]{:S(2)}) async-start(), calls=%async_computation.25 | async-start | bytes 2359296 | tf_op jit(solution)/shard_map/reduce_scatter | solution.py:424
  2686.2 130.3 %reduce-scatter.18.cloned.1.call-start = ((), (), s32[]{:S(2)}) async-start(), calls=%async_computation.26 | async-start | bytes 2359296 | tf_op jit(solution)/shard_map/reduce_scatter | solution.py:430
  2687.0 174.3 %reduce-scatter.20.cloned.1.call-start = ((), (), s32[]{:S(2)}) async-start(), calls=%async_computation.27 | async-start | bytes 2359296 | tf_op jit(solution)/shard_map/reduce_scatter | solution.py:436
  2693.0 315.5 %reduce-scatter.12.cloned.1.call-start = ((), (), s32[]{:S(2)}) async-start(), calls=%async_computation.23 | async-start | bytes 10485760 | tf_op jit(solution)/shard_map/reduce_scatter | solution.py:93
  2705.6 858.9 %reduce-scatter.22.cloned.1.call-start = ((), (), s32[]{:S(2)}) async-start(), calls=%async_computation.29 | async-start | bytes 41943040 | tf_op jit(solution)/shard_map/reduce_scatter | solution.py:293
  2738.6 1381.1 %reduce-scatter.24.cloned.1.call-start = ((), (), s32[]{:S(2)}) async-start(), calls=%async_computation.30 | async-start | bytes 41943040 | tf_op jit(solution)/shard_map/reduce_scatter | solution.py:296
  2771.5 1903.2 %reduce-scatter.26.cloned.1.call-start = ((), (), s32[]{:S(2)}) async-start(), calls=%async_computation.31 | async-start | bytes 41943040 | tf_op jit(solution)/shard_map/reduce_scatter | solution.py:299
  2800.7 2009.3 %all-reduce.9.cloned.1.call-start = ((), (), s32[]{:S(2)}) async-start(), calls=%async_computation.28 | async-start | bytes 1048576 | tf_op jit(solution)/shard_map/psum | solution.py:447
  2803.4 205.1 %copy-start.17 = (bf16[256,2048]{1,0:T(8,128)(2,1)S(1)}, bf16[256,2048]{1,0:T(8,128)(2,1)}, u32[]{:S(2)}) copy-start(bf16[256,2048]{1,0:T(8,128)(2,1)} %param.24) | copy-start | bytes 3145732
  2803.4 205.1 %copy-start.58 = (f32[2048]{0:T(1024)S(1)}, f32[2048]{0:T(1024)}, u32[]{:S(2)}) copy-start(f32[2048]{0:T(1024)} %param.25) | copy-start | bytes 24580
  2803.4 205.1 %copy-start.76 = (f32[256]{0:T(256)S(1)}, f32[256]{0:T(256)}, u32[]{:S(2)}) copy-start(f32[256]{0:T(256)} %copy-done.75) | copy-start | bytes 3076
  2816.5 194.3 %copy-start.28 = (f32[256,2048]{1,0:T(8,128)S(1)}, f32[256,2048]{1,0:T(8,128)}, u32[]{:S(2)}) copy-start(f32[256,2048]{1,0:T(8,128)} %get-tuple-element.399) | copy-start | bytes 6291460
  2818.4 192.3 %copy-start.87 = (f32[256]{0:T(256)S(1)}, f32[256]{0:T(256)}, u32[]{:S(2)}) copy-start(f32[256]{0:T(256)} %get-tuple-element.453) | copy-start | bytes 3076
  4674.7 137.2 %copy-start.1 = (bf16[2048,64]{0,1:T(8,128)(2,1)S(1)}, bf16[2048,64]{0,1:T(8,128)(2,1)}, u32[]{:S(2)}) copy-start(bf16[2048,64]{0,1:T(8,128)(2,1)} %param.33) | copy-start | bytes 786436
  (70 other events, 239.7 us)
Sparse Core Ops, SparseCore 0:
  9.9 30.6 all-gather.11
  42.5 27.8 all-gather.13
  72.3 27.8 all-gather.15
  102.2 80.7 all-gather.9
  184.7 26.7 all-gather.17
  258.2 143.5 reduce-scatter.9
  403.4 561.6 all-gather.21
  966.6 559.0 all-gather.19
  1527.4 559.5 all-gather.23
  2495.6 77.1 all-gather.25
  2685.7 40.2 reduce-scatter.13
  2730.1 41.2 reduce-scatter.15
  2775.2 41.1 reduce-scatter.17
  2820.0 41.2 reduce-scatter.19
  2864.0 144.4 reduce-scatter.11
  3010.7 553.7 reduce-scatter.21
  3566.8 552.7 reduce-scatter.23
  4121.9 552.7 reduce-scatter.25
  4681.4 128.5 all-reduce.8
where the time goes:
time: 4830 us; the launch traced here: 4820 us
  waiting for transfers between devices  3840 us (80%)
  matrix products  425 us (9%)
  local copies, waits for them, and re-layouts  279 us (6%)
  other arithmetic  158 us (3%)
  blocking collectives  64.4 us (1%)
    reduce_scatter x1, waiting for transfers between devices, body(): lax.psum_scatter(grad_up_part.astype(jnp.bfloat16), 'tensor', scatter_dim...  544 us
    reduce_scatter x1, waiting for transfers between devices, body(): lax.psum_scatter(grad_down_part.astype(jnp.bfloat16), 'tensor', scatter_d...  544 us
    all_gather x1, waiting for transfers between devices, body(): lax.all_gather(w_down, 'tensor', axis=1, tiled=True)  524 us
    all_gather x1, waiting for transfers between devices, body(): lax.all_gather(w_gate, 'tensor', axis=2, tiled=True)  524 us
    reduce_scatter x1, waiting for transfers between devices, body(): lax.psum_scatter(grad_gate_part.astype(jnp.bfloat16), 'tensor', scatter_d...  506 us
    all_gather x1, waiting for transfers between devices, body(): lax.all_gather(w_up, 'tensor', axis=2, tiled=True)  422 us
    reduce_scatter x2, waiting for transfers between devices, heads_to_rows(): lax.psum_scatter(term(jnp.int32(0), rows * lax.axis_size('tensor')), 'ten...  210 us
    psum x1, waiting for transfers between devices, body(): lax.psum((grad_attn_gain_part, grad_moe_gain_part, grad_query_full, grad_...  124 us
  transfers between devices with their start and end apart: 23, of which 19 were waited for; matrix products, arithmetic and copies ran while one was open for 12% of the time, Pallas kernels for 0%

commit v1 on v0

--- a/solution.py
+++ b/solution.py
@@ -1,6 +1,10 @@
+import functools
+
 import jax
 import jax.numpy as jnp
 from jax import lax
+from jax.experimental import pallas as pl
+from jax.experimental.pallas import tpu as pltpu
 from jax.sharding import PartitionSpec as P
 
 H = 16
@@ -12,20 +16,222 @@
 masked_score = -1e30
 
 
-def slot_ranks(expert_ids, route_rank, live_pairs, experts, capacity):
-    pairs = expert_ids.shape[0]
-    by_order = jnp.zeros((pairs,), jnp.int32).at[route_rank].set(lax.iota(jnp.int32, pairs))
-    sorted_ids = expert_ids[by_order]
-    sorted_live = live_pairs[by_order]
-    hits = (
-        (sorted_ids[:, None] == lax.iota(jnp.int32, experts)[None, :]) & (sorted_live[:, None] == 1)
-    ).astype(jnp.int32)
-    earlier = jnp.cumsum(hits, axis=0) - hits
-    rank_sorted = jnp.sum(earlier * hits, axis=1)
-    keep_sorted = ((sorted_live == 1) & (rank_sorted < capacity)).astype(jnp.int32)
-    ranks = jnp.zeros((pairs,), jnp.int32).at[by_order].set(rank_sorted)
-    kept = jnp.zeros((pairs,), jnp.int32).at[by_order].set(keep_sorted)
-    return (ranks, kept)
+def padded(count, step):
+    return -(-count // step) * step
+
+
+def slot_table(routes, route_order, valid, experts, capacity):
+    far = jnp.int32(1 << 30)
+    expert = lax.iota(jnp.int32, experts)[:, None, None]
+    hits = (routes[None] == expert) & (valid[None, :, None] == 1)
+    order = jnp.min(jnp.where(hits, route_order[None], far), axis=-1)
+    ranks = jnp.sum((order[:, None, :] < order[:, :, None]).astype(jnp.int32), axis=-1)
+    return jnp.where((order < far) & (ranks < capacity), ranks, -1)
+
+
+def slot_hits(slots, expert, rows):
+    tokens = slots.shape[-1]
+    return lax.broadcasted_iota(jnp.int32, (rows, tokens), 0) == slots[expert : expert + 1, :]
+
+
+def dispatch_kernel(slots_ref, gates_ref, rows_ref, cots_ref, x_ref, c_ref, gate_ref):
+    pair, experts, tokens = slots_ref.shape
+    rows = x_ref.shape[1] // pair
+    width = rows_ref.shape[1]
+    picks = []
+    for b in range(pair):
+        slots = slots_ref[b]
+        pieces = []
+        for e in range(experts):
+            hit = slot_hits(slots, e, rows)
+            pieces.append(hit.astype(jnp.float32))
+            gate = jnp.sum(jnp.where(hit, gates_ref[b, e : e + 1, :], 0.0), axis=1, keepdims=True)
+            gate_ref[e, b * rows : (b + 1) * rows, :] = jnp.broadcast_to(gate, (rows, 128))
+        picks.append(jnp.concatenate(pieces, axis=0).astype(jnp.bfloat16))
+    step = min(512, width)
+    for source, target in ((rows_ref, x_ref), (cots_ref, c_ref)):
+        for first in range(0, width, step):
+            parts = [
+                jnp.dot(
+                    picks[b],
+                    source[b * tokens : (b + 1) * tokens, first : first + step],
+                    preferred_element_type=jnp.float32,
+                )
+                for b in range(pair)
+            ]
+            for e in range(experts):
+                target[e, :, first : first + step] = jnp.concatenate(
+                    [part[e * rows : (e + 1) * rows] for part in parts], axis=0
+                ).astype(jnp.bfloat16)
+
+
+def dispatch(slots, gates, rows_all, cots_all, rows):
+    blocks, experts, tokens = slots.shape
+    width = rows_all.shape[1]
+    pair = 2
+    out = jax.ShapeDtypeStruct((experts, blocks * rows, width), jnp.bfloat16)
+    table = pl.BlockSpec((pair, experts, tokens), lambda i: (i, 0, 0))
+    source = pl.BlockSpec((pair * tokens, width), lambda i: (i, 0))
+    target = pl.BlockSpec((experts, pair * rows, width), lambda i: (0, i, 0))
+    return pl.pallas_call(
+        dispatch_kernel,
+        grid=(blocks // pair,),
+        out_shape=(out, out, jax.ShapeDtypeStruct((experts, blocks * rows, 128), jnp.float32)),
+        in_specs=[table, table, source, source],
+        out_specs=[target, target, pl.BlockSpec((experts, pair * rows, 128), lambda i: (0, i, 0))],
+        compiler_params=pltpu.CompilerParams(vmem_limit_bytes=50 << 20),
+        cost_estimate=pl.CostEstimate(
+            flops=4 * blocks * experts * rows * tokens * width,
+            bytes_accessed=4 * blocks * (tokens + experts * rows) * width,
+            transcendentals=0,
+        ),
+        name="dispatch",
+    )(slots, gates, rows_all, cots_all)
+
+
+def turned(left, right):
+    return lax.dot_general(left, right, (((0,), (0,)), ((), ())), preferred_element_type=jnp.float32)
+
+
+def across(left, right):
+    return lax.dot_general(left, right, (((1,), (1,)), ((), ())), preferred_element_type=jnp.float32)
+
+
+def expert_kernel(rows, first_ref, x_ref, c_ref, gate_ref, wg_ref, wu_ref, wd_ref,
+                  o_ref, dx_ref, dwg_ref, dwu_ref, dwd_ref):
+    expert = pl.program_id(0)
+    tile, width = x_ref.shape[1:]
+    units = wg_ref.shape[2]
+    room = o_ref.shape[2]
+    blocks = tile // rows
+    gate = gate_ref[0, :, 0:1]
+    x = x_ref[0]
+    c = c_ref[0]
+    gate_pre = jnp.dot(x, wg_ref[0], preferred_element_type=jnp.float32)
+    up_pre = jnp.dot(x, wu_ref[0], preferred_element_type=jnp.float32)
+    back = across(c, wd_ref[0])
+    sig = jax.nn.sigmoid(gate_pre)
+    silu = gate_pre * sig
+    act = (silu * up_pre).astype(jnp.bfloat16)
+    act_float = act.astype(jnp.float32)
+    grad_gate = jnp.sum(act_float * back, axis=1, keepdims=True)
+    grad_act = back * gate
+    grad_gate_pre = (grad_act * up_pre * sig * (1.0 + gate_pre * (1.0 - sig))).astype(jnp.bfloat16)
+    grad_up_pre = (grad_act * silu).astype(jnp.bfloat16)
+    gated = (act_float * gate).astype(jnp.bfloat16)
+
+    def spread(values):
+        values = values.reshape(blocks, rows, values.shape[1])
+        if room > rows:
+            empty = jnp.zeros((blocks, room - rows, values.shape[2]), jnp.float32)
+            values = jnp.concatenate((values, empty), axis=1)
+        return values.astype(jnp.bfloat16)
+
+    step = min(512, width)
+    for first in range(0, width, step):
+        part = slice(first, first + step)
+        out = jnp.dot(act, wd_ref[0, :, part], preferred_element_type=jnp.float32) * gate
+        o_ref[:, 0, :, part] = spread(out)
+        grad = across(grad_gate_pre, wg_ref[0, part, :]) + across(grad_up_pre, wu_ref[0, part, :])
+        dx_ref[:, 0, :, part] = spread(grad)
+    lanes = lax.broadcasted_iota(jnp.int32, (tile, 128), 1)
+    dx_ref[:, 0, :, width:] = spread(jnp.where(lanes == first_ref[0] + expert, grad_gate, 0.0))
+
+    @pl.when(pl.program_id(1) == 0)
+    def _():
+        for ref in (dwg_ref, dwu_ref, dwd_ref):
+            ref[...] = jnp.zeros_like(ref)
+
+    for first in range(0, width, step):
+        part = slice(first, first + step)
+        dwg_ref[0, part, :] += turned(x_ref[0, :, part], grad_gate_pre)
+        dwu_ref[0, part, :] += turned(x_ref[0, :, part], grad_up_pre)
+        dwd_ref[0, :, part] += turned(gated, c_ref[0, :, part])
+
+
+def expert_pass(first_expert, x_slots, c_slots, gate_slots, w_gate, w_up, w_down, blocks, room):
+    experts, total, width = x_slots.shape
+    units = w_gate.shape[2]
+    rows = total // blocks
+    group = next(n for n in (16, 8, 4, 2, 1) if blocks % n == 0 and (n * rows <= 768 or n == 1))
+    tile = group * rows
+    extra = 128
+    tall = pl.BlockSpec((1, width, units), lambda e, r, _: (e, 0, 0))
+    wide = pl.BlockSpec((1, units, width), lambda e, r, _: (e, 0, 0))
+    slot = pl.BlockSpec((1, tile, width), lambda e, r, _: (e, r, 0))
+    kernel = functools.partial(expert_kernel, rows)
+    return pl.pallas_call(
+        kernel,
+        grid_spec=pltpu.PrefetchScalarGridSpec(
+            num_scalar_prefetch=1,
+            grid=(experts, total // tile),
+            in_specs=[slot, slot, pl.BlockSpec((1, tile, 128), lambda e, r, _: (e, r, 0)), tall, tall, wide],
+            out_specs=[
+                pl.BlockSpec((group, 1, room, width), lambda e, r, _: (r, e, 0, 0)),
+                pl.BlockSpec((group, 1, room, width + extra), lambda e, r, _: (r, e, 0, 0)),
+                tall, tall, wide,
+            ],
+        ),
+        out_shape=(
+            jax.ShapeDtypeStruct((blocks, experts, room, width), jnp.bfloat16),
+            jax.ShapeDtypeStruct((blocks, experts, room, width + extra), jnp.bfloat16),
+            jax.ShapeDtypeStruct(w_gate.shape, jnp.float32),
+            jax.ShapeDtypeStruct(w_up.shape, jnp.float32),
+            jax.ShapeDtypeStruct(w_down.shape, jnp.float32),
+        ),
+        compiler_params=pltpu.CompilerParams(vmem_limit_bytes=60 << 20),
+        cost_estimate=pl.CostEstimate(
+            flops=18 * experts * total * width * units,
+            bytes_accessed=8 * experts * total * width + 18 * experts * width * units,
+            transcendentals=experts * total * units,
+        ),
+        name="experts",
+    )(first_expert, x_slots, c_slots, gate_slots, w_gate, w_up, w_down)
+
+
+def combine_kernel(slots_ref, o_ref, dx_ref, out_ref, grad_ref):
+    _, experts, tokens = slots_ref.shape
+    room, width = o_ref.shape[2:]
+    slots = slots_ref[0]
+    picks = jnp.concatenate(
+        [slot_hits(slots, e, room).astype(jnp.float32) for e in range(experts)], axis=0
+    ).astype(jnp.bfloat16)
+    for source, target in ((o_ref, out_ref), (dx_ref, grad_ref)):
+        columns = target.shape[1]
+        for first in range(0, columns, 512):
+            part = slice(first, min(first + 512, columns))
+            values = source[0, :, :, part].reshape(experts * room, part.stop - first)
+            target[:, part] = turned(picks, values).astype(jnp.bfloat16)
+
+
+def combine(slots, outs, grads):
+    blocks, experts, tokens = slots.shape
+    room, width = outs.shape[2:]
+    wider = grads.shape[3]
+    return pl.pallas_call(
+        combine_kernel,
+        grid=(blocks,),
+        out_shape=(
+            jax.ShapeDtypeStruct((blocks * tokens, width), jnp.bfloat16),
+            jax.ShapeDtypeStruct((blocks * tokens, wider), jnp.bfloat16),
+        ),
+        in_specs=[
+            pl.BlockSpec((1, experts, tokens), lambda i: (i, 0, 0)),
+            pl.BlockSpec((1, experts, room, width), lambda i: (i, 0, 0, 0)),
+            pl.BlockSpec((1, experts, room, wider), lambda i: (i, 0, 0, 0)),
+        ],
+        out_specs=[
+            pl.BlockSpec((tokens, width), lambda i: (i, 0)),
+            pl.BlockSpec((tokens, wider), lambda i: (i, 0)),
+        ],
+        compiler_params=pltpu.CompilerParams(vmem_limit_bytes=50 << 20),
+        cost_estimate=pl.CostEstimate(
+            flops=2 * blocks * experts * room * tokens * (width + wider),
+            bytes_accessed=2 * blocks * (tokens + experts * room) * (width + wider),
+            transcendentals=0,
+        ),
+        name="combine",
+    )(slots, outs, grads)
 
 
 def visible_block(row_paths, key_paths, key_valid, row_first):
@@ -98,16 +304,11 @@
     )
 
 
-def own_exchange(slots):
-    return lax.all_to_all(slots, "dp", split_axis=1, concat_axis=1, tiled=True)
-
-
-def to_experts(slots):
-    return own_exchange(slots)
-
-
-def from_experts(slots):
-    return lax.all_to_all(slots, "dp", split_axis=1, concat_axis=1, tiled=True)
+def sum_to_blocks(rows, tokens):
+    dp = lax.axis_size("dp")
+    pieces = rows.reshape(dp, rows.shape[0] // dp, rows.shape[1])
+    part = lax.psum_scatter(pieces, "dp", scatter_dimension=0, tiled=False)
+    return lax.psum_scatter(part, "tensor", scatter_dimension=0, tiled=True)
 
 
 def body(
@@ -210,105 +411,37 @@
     hidden_two = normed_two.astype(jnp.bfloat16)
     logits = jnp.dot(hidden_two, router, preferred_element_type=jnp.float32)
     probs = jax.nn.softmax(logits, axis=-1)
-    gates = jnp.take_along_axis(probs, routes, axis=1)
+    everyone = ("dp", "tensor")
+    cots_all = lax.all_gather(cotangent, everyone, axis=0, tiled=True)
     valid_dev = lax.dynamic_slice_in_dim(token_valid, tensor_rank * tok_dev, tok_dev)
-    pair_count = tok_dev * top_count
-    expert_ids = routes.reshape(pair_count)
-    ranks, kept = slot_ranks(
-        expert_ids,
-        route_order.reshape(pair_count),
-        jnp.repeat(valid_dev, top_count),
-        experts,
-        capacity,
-    )
-    slot_total = capacity * experts
-    pair_slot = jnp.where(kept == 1, ranks * experts + expert_ids, slot_total)
-    pair_token = lax.iota(jnp.int32, pair_count) // top_count
-    slot_token = (
-        jnp.full((slot_total + 1,), tok_dev, jnp.int32).at[pair_slot].set(pair_token)[:slot_total]
-    )
-    gate_kept = gates.reshape(pair_count) * kept.astype(jnp.float32)
-    gate_slot = jnp.zeros((slot_total + 1,), jnp.float32).at[pair_slot].set(gate_kept)[:slot_total]
-    zero_row = jnp.zeros((1, width), jnp.bfloat16)
-    rows_pad = jnp.concatenate((hidden_two, zero_row), axis=0)
-    send_rows = rows_pad[slot_token].reshape(capacity, dp_groups, local_experts, width)
-    expert_in = to_experts(send_rows)
-    gate_weight, up_weight, down_weight = (
-        lax.all_gather(w_gate, "tensor", axis=2, tiled=True),
-        lax.all_gather(w_up, "tensor", axis=2, tiled=True),
-        lax.all_gather(w_down, "tensor", axis=1, tiled=True),
-    )
-    gate_pre = jnp.einsum(
-        "rged,edf->rgef", expert_in, gate_weight, preferred_element_type=jnp.float32
-    )
-    up_pre = jnp.einsum("rged,edf->rgef", expert_in, up_weight, preferred_element_type=jnp.float32)
-    sigmoid_gate = jax.nn.sigmoid(gate_pre)
-    silu_gate = gate_pre * sigmoid_gate
-    act = (silu_gate * up_pre).astype(jnp.bfloat16)
-    expert_out = jnp.einsum(
-        "rgef,efd->rged", act, down_weight, preferred_element_type=jnp.float32
-    ).astype(jnp.bfloat16)
-    returned = from_experts(expert_out)
-    out_pad = jnp.concatenate((returned.reshape(slot_total, width), zero_row), axis=0)
-    pair_out = out_pad[pair_slot].reshape(tok_dev, top_count, width)
-    moe_out = jnp.sum(
-        pair_out.astype(jnp.float32) * gate_kept.reshape(tok_dev, top_count, 1), axis=1
-    )
+    slots_own = slot_table(routes, route_order, valid_dev, experts, capacity)
+    slots_all = lax.all_gather(slots_own.astype(jnp.bfloat16), everyone, axis=0)
+    first_expert = lax.axis_index("dp") * local_experts
+    slots = lax.dynamic_slice_in_dim(slots_all, first_expert, local_experts, 1).astype(jnp.int32)
+    gates_all = lax.all_gather(probs.T, everyone, axis=0)
+    gates = lax.dynamic_slice_in_dim(gates_all, first_expert, local_experts, 1)
+    rows_all = lax.all_gather(hidden_two, everyone, axis=0, tiled=True)
+    blocks = slots.shape[0]
+    slot_rows = padded(capacity, 8)
+    x_slots, c_slots, gate_slots = dispatch(slots, gates, rows_all, cots_all, slot_rows)
+    outs, grads, grad_w_gate, grad_w_up, grad_w_down = expert_pass(
+        first_expert.reshape(1),
+        x_slots,
+        c_slots,
+        gate_slots,
+        w_gate,
+        w_up,
+        w_down,
+        blocks,
+        padded(slot_rows, 16),
+    )
+    out_part, grad_part = combine(slots, outs, grads)
+    grad_rows = sum_to_blocks(grad_part, tok_dev).astype(jnp.float32)
+    moe_out = sum_to_blocks(out_part, tok_dev).astype(jnp.float32)
     block_out = (x_one + moe_out).astype(jnp.bfloat16)
     grad_out = cotangent.astype(jnp.float32)
-    grad_gates = jnp.sum(
-        pair_out.astype(jnp.float32) * grad_out[:, None, :], axis=-1
-    ) * kept.reshape(tok_dev, top_count).astype(jnp.float32)
-    cot_pad = jnp.concatenate((cotangent, zero_row), axis=0)
-    grad_rows_send = (
-        (cot_pad[slot_token].astype(jnp.float32) * gate_slot[:, None])
-        .astype(jnp.bfloat16)
-        .reshape(capacity, dp_groups, local_experts, width)
-    )
-    grad_expert_out = to_experts(grad_rows_send)
-    grad_act = jnp.einsum(
-        "rged,efd->rgef", grad_expert_out, down_weight, preferred_element_type=jnp.float32
-    )
-    grad_down_part = jnp.einsum(
-        "rgef,rged->efd", act, grad_expert_out, preferred_element_type=jnp.float32
-    )
-    grad_gate_pre = (
-        grad_act * up_pre * sigmoid_gate * (1.0 + gate_pre * (1.0 - sigmoid_gate))
-    ).astype(jnp.bfloat16)
-    grad_up_pre = (grad_act * silu_gate).astype(jnp.bfloat16)
-    grad_gate_part = jnp.einsum(
-        "rged,rgef->edf", expert_in, grad_gate_pre, preferred_element_type=jnp.float32
-    )
-    grad_up_part = jnp.einsum(
-        "rged,rgef->edf", expert_in, grad_up_pre, preferred_element_type=jnp.float32
-    )
-    from_gate = jnp.einsum(
-        "rgef,edf->rged", grad_gate_pre, gate_weight, preferred_element_type=jnp.float32
-    )
-    grad_expert_in = (
-        from_gate
-        + jnp.einsum("rgef,edf->rged", grad_up_pre, up_weight, preferred_element_type=jnp.float32)
-    ).astype(jnp.bfloat16)
-    grad_w_gate, grad_w_up, grad_w_down = (
-        lax.psum_scatter(
-            grad_gate_part.astype(jnp.bfloat16), "tensor", scatter_dimension=2, tiled=True
-        ).astype(jnp.float32),
-        lax.psum_scatter(
-            grad_up_part.astype(jnp.bfloat16), "tensor", scatter_dimension=2, tiled=True
-        ).astype(jnp.float32),
-        lax.psum_scatter(
-            grad_down_part.astype(jnp.bfloat16), "tensor", scatter_dimension=1, tiled=True
-        ).astype(jnp.float32),
-    )
-    grad_returned = from_experts(grad_expert_in)
-    grad_pad = jnp.concatenate((grad_returned.reshape(slot_total, width), zero_row), axis=0)
-    grad_hidden_two = jnp.sum(
-        grad_pad[pair_slot].reshape(tok_dev, top_count, width).astype(jnp.float32), axis=1
-    )
-    route_hits = (routes[:, :, None] == lax.iota(jnp.int32, experts)[None, None, :]).astype(
-        jnp.float32
-    )
-    grad_probs = jnp.sum(route_hits * grad_gates[:, :, None], axis=1)
+    grad_hidden_two = grad_rows[:, :width]
+    grad_probs = grad_rows[:, width : width + experts]
     grad_logits = probs * (grad_probs - jnp.sum(probs * grad_probs, axis=-1, keepdims=True))
     router_float = router.astype(jnp.float32)
     grad_hidden_two = grad_hidden_two + lax.dot_general(

time: 4830 us -> 2270 us (0.47)
  waiting for transfers between devices: 3840 us -> 1660 us
  matrix products: 425 us -> 100 us
  Pallas kernels: 0 us -> 273 us
  local copies, waits for them, and re-layouts: 279 us -> 47.5 us
  other arithmetic: 158 us -> 86.3 us
    reduce_scatter x3 -> x4, waiting for transfers between devices: 1590 us -> 577 us  [the longest x2 422 us: sum_to_blocks(): part = lax.psum_scatter(pieces, 'dp', scatter_dimension=0, tiled=False)]
    all_gather x3 -> x4, waiting for transfers between devices: 1470 us -> 461 us  [the longest x1 196 us: body(): rows_all = lax.all_gather(hidden_two, everyone, axis=0, tiled=True)]
    dot_general x9 -> x0, matrix products: 312 us -> none  [the longest x1 68.5 us: body(): jnp.einsum('rged,efd->rgef', grad_expert_out, down_weight, preferred_elem...]
    pallas_call x0 -> x3, Pallas kernels: none -> 273 us  [the longest x1 141 us: expert_pass(): pl.pallas_call(kernel, grid_spec=pltpu.PrefetchScalarGridSpec(num_scalar_...]
    all_to_all x4 -> x0, waiting for transfers between devices: 164 us -> none  [the longest x2 114 us: from_experts(): return lax.all_to_all(slots, 'dp', split_axis=1, concat_axis=1, tiled=True)]
    psum x1, waiting for transfers between devices: 124 us -> 0.01 us  [body(): lax.psum((grad_attn_gain_part, grad_moe_gain_part, grad_query_full, grad_...]
    gather x11 -> x0, local copies, waits for them, and re-layouts: 103 us -> none  [the longest x1 21.6 us: body(): pair_out = out_pad[pair_slot].reshape(tok_dev, top_count, width)]
    reduce_scatter x2, waiting for transfers between devices: 210 us -> 285 us  [heads_to_rows(): lax.psum_scatter(term(jnp.int32(0), rows * lax.axis_size('tensor')), 'ten...]
  transfers between devices with their start and end apart: 23 -> 21, of which waited for: 19 -> 18; matrix products, arithmetic and copies ran while one was open for 12% -> 9% of each run, Pallas kernels for 0% -> 0%
where the time goes in v1:
time: 2270 us; the launch traced here: 2260 us
  waiting for transfers between devices  1660 us (73%)
  Pallas kernels  273 us (12%)
  matrix products  100 us (4%)
  other arithmetic  86.3 us (4%)
  blocking collectives  60.3 us (3%)
  local copies, waits for them, and re-layouts  47.5 us (2%)
    reduce_scatter x2, waiting for transfers between devices, sum_to_blocks(): part = lax.psum_scatter(pieces, 'dp', scatter_dimension=0, tiled=False)  422 us
    reduce_scatter x2, waiting for transfers between devices, heads_to_rows(): lax.psum_scatter(term(jnp.int32(0), rows * lax.axis_size('tensor')), 'ten...  285 us
    all_gather x1, waiting for transfers between devices, body(): rows_all = lax.all_gather(hidden_two, everyone, axis=0, tiled=True)  196 us
    all_gather x1, waiting for transfers between devices, body(): cots_all = lax.all_gather(cotangent, everyone, axis=0, tiled=True)  195 us
    reduce_scatter x2, waiting for transfers between devices, sum_to_blocks(): return lax.psum_scatter(part, 'tensor', scatter_dimension=0, tiled=True)  155 us
    pallas_call x1, Pallas kernels, expert_pass(): pl.pallas_call(kernel, grid_spec=pltpu.PrefetchScalarGridSpec(num_scalar_...  141 us
    all_gather x1, waiting for transfers between devices, body(): lax.all_gather(grad_x_one.astype(jnp.bfloat16), 'tensor', axis=0, tiled=T...  81.3 us
    all_gather x1, waiting for transfers between devices, body(): hidden_all = lax.all_gather(hidden, 'tensor', axis=0, tiled=True)  79.7 us
  transfers between devices with their start and end apart: 21, of which 18 were waited for; matrix products, arithmetic and copies ran while one was open for 9% of the time, Pallas kernels for 0%

profile of v1, /device:TPU:0, one launch (start us, length us, event | category | flops | bytes accessed | tf_op | source)
XLA Modules:
  0.0 2260.4 jit_solution(11564785205677522582)
XLA Ops:
  16.6 9.4 while.37
  26.0 3.1 multiply_cosine_fusion
  29.1 12.3 all-gather.14.cloned.1.call-done
  41.4 3.1 constant_dynamic-update-slice_fusion.2
  44.5 26.7 %all-gather.16.cloned.1.call-done = bf16[2048,512]{1,0:T(8,128)(2,1)} async-done(((bf16[256,512]{1,0:T(8,128)(2,1)}), bf16[2048,512]{1,0:T(8,128)(2,1)}) %all-gather.16.cloned.1.call-update) | async-done | bytes 2097168 | tf_op jit(solution)/shard_map/all_gather | solution.py:348
  71.2 3.2 constant_dynamic-update-slice_fusion.1
  74.4 26.7 %all-gather.18.cloned.1.call-done = bf16[2048,512]{1,0:T(8,128)(2,1)} async-done(((bf16[256,512]{1,0:T(8,128)(2,1)}), bf16[2048,512]{1,0:T(8,128)(2,1)}) %all-gather.18.cloned.1.call-update) | async-done | bytes 2097168 | tf_op jit(solution)/shard_map/all_gather | solution.py:349
  101.1 3.1 constant_dynamic-update-slice_fusion
  104.1 79.7 %all-gather.12.cloned.1.call-done = bf16[1024,2048]{1,0:T(8,128)(2,1)} async-done(((bf16[256,2048]{1,0:T(8,128)(2,1)}), bf16[1024,2048]{1,0:T(8,128)(2,1)}) %all-gather.12.cloned.1.call-update) | async-done | bytes 4194320 | tf_op jit(solution)/shard_map/all_gather | solution.py:358
  183.8 10.0 fusion.87
  194.2 2.3 copy-done.9
  196.6 9.3 all-reduce.2
  206.6 4.7 multiply_multiply_fusion
  213.2 3.2 fusion.84
  223.0 26.7 %while.38 = (s32[]{:T(128)}, bf16[2,512,4,128]{3,2,1,0:T(4,128)(2,1)}, f32[2,4,512]{2,1,0:T(4,128)S(1)}, s32[3,1024]{1,0:T(4,128)S(1)}, s32[2]{0:T(128)S(1)}, /*...) while((s32[]{:T(128)}, ...), condition=%wide.region_11.12_spmd, body=%wide.region_8.11_spmd.sunk | while | flops 1104412160 | bytes 31564516 | solution.py:403
  229.4 2.4 fusion.130
  231.8 3.1 fusion.131
  242.5 2.4 fusion.130
  244.9 3.1 fusion.131
  249.8 8.7 fusion.67
  259.6 5.2 convert_reduce_fusion.1
  265.5 138.6 %reduce-scatter.11.cloned.1.call-done = f32[256,2048]{1,0:T(8,128)} async-done(((f32[1024,2048]{1,0:T(8,128)}), f32[256,2048]{1,0:T(8,128)}) %reduce-scatter.11.cloned.1.call-update) | async-done | bytes 2097168 | tf_op jit(solution)/shard_map/reduce_scatter | solution.py:299
  410.6 12.8 all-gather.22.cloned.1.call-done
  424.4 58.0 %all-gather.30.cloned.1.call-done = f32[2048,256]{1,0:T(8,128)} async-done(((f32[64,256]{1,0:T(8,128)}), f32[2048,256]{1,0:T(8,128)}) %all-gather.30.cloned.1.call-update) | async-done | bytes 2097168 | tf_op jit(solution)/shard_map/all_gather | solution.py:421
  483.4 195.1 %all-gather.26.cloned.1.call-done.cots_ref = bf16[8192,2048]{1,0:T(8,128)(2,1)} async-done(((bf16[256,2048]{1,0:T(8,128)(2,1)}), bf16[8192,2048]{1,0:T(8,128)(2,1)}) %all-gather.26.cloned.1.call-update) | async-done | bytes 33554448 | tf_op jit(solution)/shard_map/all_gather | solution.py:415
  678.5 195.5 %all-gather.24.cloned.1.call-done.rows_ref = bf16[8192,2048]{1,0:T(8,128)(2,1)} async-done(((bf16[256,2048]{1,0:T(8,128)(2,1)}), bf16[8192,2048]{1,0:T(8,128)(2,1)}) %all-gather.24.cloned.1.call-update) | async-done | bytes 33554448 | tf_op jit(solution)/shard_map/all_gather | solution.py:423
  874.0 56.7 %dispatch.1 = (bf16[8,1280,2048]{2,1,0:T(8,128)(2,1)}, bf16[8,1280,2048]{2,1,0:T(8,128)(2,1)}, f32[8,1280,128]{2,1,0:T(8,128)}) custom-call(s32[32,8,256]{2,1,0:T(8,128)S(1)} %dynamic-slice_convert_fusion.slots_ref, f32[32,8,256]{2,1,0:T(8,128)S(1)} %constant_dynamic-slice_fusion.3.gates_ref, bf16[8192,2048]{1,0:T(8,128)(2,1)} %all-gather.24.cloned.1.call-done.rows_ref, ...), custom_call_target="tpu_custom_call" | custom-call | flops 21474836480 | bytes 150994944 | tf_op jit(solution)/shard_map/dispatch/pallas_call | solution.py:76
  930.8 140.7 %experts.1 = (bf16[32,8,48,2048]{3,2,1,0:T(8,128)(2,1)}, bf16[32,8,48,2176]{3,2,1,0:T(8,128)(2,1)}, f32[8,2048,256]{2,1,0:T(8,128)}, f32[8,2048,256]{2,1,0:T(8,128)}, f32[8,256,2048]{2,1,0:T(8,128)}) custom-call(s32[1]{0:T(128)} %bitcast.16.first_ref, bf16[8,1280,2048]{2,1,0:T(8,128)(2,1)} %get-tuple-element.165.x_ref, ...), custom_call_target="tpu_custom_call" | custom-call | flops 96636764160 | bytes 243269632 | tf_op jit(solution)/shard_map/experts/pallas_call | solution.py:163
  1071.5 75.1 %combine.1 = (bf16[8192,2048]{1,0:T(8,128)(2,1)}, bf16[8192,2176]{1,0:T(8,128)(2,1)}) custom-call(s32[32,8,256]{2,1,0:T(8,128)S(1)} %dynamic-slice_convert_fusion.slots_ref, bf16[32,8,48,2048]{3,2,1,0:T(8,128)(2,1)} %get-tuple-element.168.o_ref, bf16[32,8,48,2176]{3,2,1,0:T(8,128)(2,1)} %get-tuple-element.169.dx_ref), custom_call_target="tpu_custom_call" | custom-call | flops 26575110144 | bytes 173015040 | tf_op jit(solution)/shard_map/combine/pallas_call | solution.py:211
  1147.4 212.6 %reduce-scatter.17.cloned.1.call-done = bf16[1,1024,2176]{2,1,0:T(8,128)(2,1)} async-done(((bf16[8,1024,2176]{2,1,0:T(8,128)(2,1)}), bf16[1,1024,2176]{2,1,0:T(8,128)(2,1)}) %reduce-scatter.17.cloned.1.call-update) | async-done | bytes 4456464 | tf_op jit(solution)/shard_map/reduce_scatter | solution.py:310
  1360.1 209.2 %reduce-scatter.13.cloned.1.call-done = bf16[1,1024,2048]{2,1,0:T(8,128)(2,1)} async-done(((bf16[8,1024,2048]{2,1,0:T(8,128)(2,1)}), bf16[1,1024,2048]{2,1,0:T(8,128)(2,1)}) %reduce-scatter.13.cloned.1.call-update) | async-done | bytes 4194320 | tf_op jit(solution)/shard_map/reduce_scatter | solution.py:310
  1569.5 83.0 %reduce-scatter.19.cloned.1.call-done = bf16[256,2176]{1,0:T(8,128)(2,1)} async-done(((bf16[1024,2176]{1,0:T(8,128)(2,1)}), bf16[256,2176]{1,0:T(8,128)(2,1)}) %reduce-scatter.19.cloned.1.call-update) | async-done | bytes 1114128 | tf_op jit(solution)/shard_map/reduce_scatter | solution.py:311
  1655.9 4.2 multiply_reduce_fusion.1
  1660.1 72.0 %reduce-scatter.15.cloned.1.call-done = bf16[256,2048]{1,0:T(8,128)(2,1)} async-done(((bf16[1024,2048]{1,0:T(8,128)(2,1)}), bf16[256,2048]{1,0:T(8,128)(2,1)}) %reduce-scatter.15.cloned.1.call-update) | async-done | bytes 1048592 | tf_op jit(solution)/shard_map/reduce_scatter | solution.py:311
  1732.1 4.7 fusion.82
  1736.9 81.3 %all-gather.28.cloned.1.call-done = bf16[1024,2048]{1,0:T(8,128)(2,1)} async-done(((bf16[256,2048]{1,0:T(8,128)(2,1)}), bf16[1024,2048]{1,0:T(8,128)(2,1)}) %all-gather.28.cloned.1.call-update) | async-done | bytes 4194320 | tf_op jit(solution)/shard_map/all_gather | solution.py:461
  1818.2 6.3 convolution_convert_fusion.1
  1824.7 6.3 convolution_convert_fusion.2
  1831.0 52.6 %while.39 = (s32[]{:T(128)}, f32[1024,4,128]{0,2,1:T(8,128)S(1)}, f32[1024,4,128]{0,2,1:T(8,128)}, f32[2,512,4,128]{3,1,0,2:T(8,128)}, s32[2]{0:T(128)S(1)}, /*i...) while((s32[]{:T(128)}, f32[1024,4,128]{0,2,1:T(8,128)S(1)}, ...), condition=%wide.region_26.27_spmd.clone, body=%wide.region_24.26_spmd.clone.sunk | while | flops 2723937792 | bytes 180454416 | solution.py:513
  1835.7 2.5 fusion.141
  1838.3 3.6 multiply_reduce_fusion.8
  1841.9 3.7 multiply_convert_fusion.3
  1845.6 3.8 bitcast_add_fusion.4
  1852.8 4.0 bitcast_add_fusion.5
  1861.4 2.5 fusion.141
  1863.9 3.6 multiply_reduce_fusion.8
  1867.6 3.7 multiply_convert_fusion.3
  1871.3 3.8 bitcast_add_fusion.4
  1875.1 2.2 fusion.143
  1878.3 5.2 bitcast_add_fusion.5
  1885.4 7.3 multiply_add_fusion.1
  1896.1 5.1 fusion.57
  1901.2 9.3 all-reduce.1
  1910.6 5.4 fusion.59
  1917.0 7.5 convolution_convert_fusion
  1924.5 2.7 fusion.83
  1928.9 10.8 fusion.64
  1940.9 2.5 fusion.76
  1945.9 21.9 reduce-scatter.23.cloned.1.call-done
  1969.6 43.0 %reduce-scatter.25.cloned.1.call-done = bf16[256,512]{1,0:T(8,128)(2,1)} async-done(((bf16[2048,512]{1,0:T(8,128)(2,1)}), bf16[256,512]{1,0:T(8,128)(2,1)}) %reduce-scatter.25.cloned.1.call-update) | async-done | bytes 262160 | tf_op jit(solution)/shard_map/reduce_scatter | solution.py:557
  2014.5 42.5 %reduce-scatter.27.cloned.1.call-done = bf16[256,512]{1,0:T(8,128)(2,1)} async-done(((bf16[2048,512]{1,0:T(8,128)(2,1)}), bf16[256,512]{1,0:T(8,128)(2,1)}) %reduce-scatter.27.cloned.1.call-update) | async-done | bytes 262160 | tf_op jit(solution)/shard_map/reduce_scatter | solution.py:563
  2058.8 146.0 %reduce-scatter.21.cloned.1.call-done = f32[256,2048]{1,0:T(8,128)} async-done(((f32[1024,2048]{1,0:T(8,128)}), f32[256,2048]{1,0:T(8,128)}) %reduce-scatter.21.cloned.1.call-update) | async-done | bytes 2097168 | tf_op jit(solution)/shard_map/reduce_scatter | solution.py:299
  2204.9 2.3 fusion.51
  2209.2 41.6 %all-reduce = (f32[2048]{0:T(1024)}, f32[2048]{0:T(1024)}, f32[2048]{0:T(1024)}, f32[2048]{0:T(1024)}) all-reduce(f32[2048]{0:T(1024)S(1)} %get-tuple-element.312, f32[2048]{0:T(1024)S(1)} %dynamic_update_slice.22, f32[2048]{0:T(1024)S(1)} %dynamic_update_slice.23, ...), channel_id=1, replica_groups=mesh['dp'=8,'tensor'=4] {'dp','tensor'}, use_global_device_ids=true, to_apply=%region_34.35 | all-reduce | flops 8192 | bytes 65536 | tf_op jit(solution)/shard_map/psum | solution.py:580
  (313 shorter events, 79.5 us)
Async XLA Ops:
  8.0 399.6 %copy-start = (bf16[2048,64]{0,1:T(8,128)(2,1)S(1)}, bf16[2048,64]{0,1:T(8,128)(2,1)}, u32[]{:S(2)}) copy-start(bf16[2048,64]{0,1:T(8,128)(2,1)} %param.33) | copy-start | bytes 786436
  8.0 33.4 %all-gather.14.cloned.1.call-start = ((), (), s32[]{:S(2)}) async-start(), calls=%async_computation.11 | async-start | bytes 2359296 | tf_op jit(solution)/shard_map/all_gather | solution.py:347
  8.8 62.5 %all-gather.16.cloned.1.call-start = ((), (), s32[]{:S(2)}) async-start(), calls=%async_computation.12 | async-start | bytes 2359296 | tf_op jit(solution)/shard_map/all_gather | solution.py:348
  9.5 91.5 %all-gather.18.cloned.1.call-start = ((), (), s32[]{:S(2)}) async-start(), calls=%async_computation.13 | async-start | bytes 2359296 | tf_op jit(solution)/shard_map/all_gather | solution.py:349
  10.3 6.4 copy-start.34
  10.3 6.4 copy-start.41
  10.3 173.6 %all-gather.12.cloned.1.call-start = ((), (), s32[]{:S(2)}) async-start(), calls=%async_computation.10 | async-start | bytes 5242880 | tf_op jit(solution)/shard_map/all_gather | solution.py:358
  12.4 16.7 copy-start.63
  14.4 235.4 %all-gather.20.cloned.1.call-start = ((), (), s32[]{:S(2)}) async-start(), calls=%async_computation.14 | async-start | bytes 2359296 | tf_op jit(solution)/shard_map/all_gather | solution.py:350
  15.0 389.1 %reduce-scatter.11.cloned.1.call-start = ((), (), s32[]{:S(2)}) async-start(), calls=%async_computation.15 | async-start | bytes 10485760 | tf_op jit(solution)/shard_map/reduce_scatter | solution.py:299
  15.9 190.7 %copy-start.53 = (f32[512]{0:T(512)}, f32[512]{0:T(512)S(1)}, u32[]{:S(2)}) copy-start(f32[512]{0:T(512)S(1)} %dynamic_slice.47) | copy-start | bytes 6148
  16.6 189.9 %copy-start.55 = (f32[512]{0:T(512)}, f32[512]{0:T(512)S(1)}, u32[]{:S(2)}) copy-start(f32[512]{0:T(512)S(1)} %dynamic_slice.48) | copy-start | bytes 6148
  206.6 4.7 copy-start.47
  206.6 4.7 copy-start.49
  249.7 8.8 copy-start.4
  249.7 8.8 copy-start.8
  249.7 8.8 copy-start.10
  249.8 8.8 copy-start.35
  249.8 8.8 copy-start.44
  249.8 8.8 copy-start.75
  249.8 8.9 copy-start.42
  258.6 145.4 %copy-start.13 = (bf16[256,2048]{1,0:T(8,128)(2,1)S(1)}, bf16[256,2048]{1,0:T(8,128)(2,1)}, u32[]{:S(2)}) copy-start(bf16[256,2048]{1,0:T(8,128)(2,1)} %param.24) | copy-start | bytes 3145732
  258.6 164.8 %all-gather.22.cloned.1.call-start = ((), (), s32[]{:S(2)}) async-start(), calls=%async_computation.16 | async-start | bytes 1081344 | tf_op jit(solution)/shard_map/all_gather | solution.py:418
  265.4 141.9 %copy-start.51 = (f32[2048]{0:T(1024)S(1)}, f32[2048]{0:T(1024)}, u32[]{:S(2)}) copy-start(f32[2048]{0:T(1024)} %param.32) | copy-start | bytes 24580
  265.4 217.0 %all-gather.30.cloned.1.call-start = ((), (), s32[]{:S(2)}) async-start(), calls=%async_computation.30 | async-start | bytes 2162688 | tf_op jit(solution)/shard_map/all_gather | solution.py:421
  408.1 74.4 %copy-start.57 = (f32[256]{0:T(256)}, f32[256]{0:T(256)S(1)}, u32[]{:S(2)}) copy-start(f32[256]{0:T(256)S(1)} %get-tuple-element.425) | copy-start | bytes 3076
  408.4 74.1 %copy-start.60 = (f32[256]{0:T(256)}, f32[256]{0:T(256)S(1)}, u32[]{:S(2)}) copy-start(f32[256]{0:T(256)S(1)} %fusion.73) | copy-start | bytes 3076
  409.3 269.2 %all-gather.26.cloned.1.call-start = ((), (), s32[]{:S(2)}) async-start(), calls=%async_computation.18 | async-start | bytes 34603008 | tf_op jit(solution)/shard_map/all_gather | solution.py:415
  409.8 464.2 %all-gather.24.cloned.1.call-start = ((), (), s32[]{:S(2)}) async-start(), calls=%async_computation.17 | async-start | bytes 34603008 | tf_op jit(solution)/shard_map/all_gather | solution.py:423
  410.6 949.4 %reduce-scatter.17.cloned.1.call-start = ((), (), s32[]{:S(2)}) async-start(), calls=%async_computation.21 | async-start | bytes 40108032 | tf_op jit(solution)/shard_map/reduce_scatter | solution.py:310
  1146.6 422.7 %reduce-scatter.13.cloned.1.call-start = ((), (), s32[]{:S(2)}) async-start(), calls=%async_computation.19 | async-start | bytes 37748736 | tf_op jit(solution)/shard_map/reduce_scatter | solution.py:310
  1147.3 505.3 %reduce-scatter.19.cloned.1.call-start = ((), (), s32[]{:S(2)}) async-start(), calls=%async_computation.22 | async-start | bytes 5570560 | tf_op jit(solution)/shard_map/reduce_scatter | solution.py:311
  1360.0 372.1 %reduce-scatter.15.cloned.1.call-start = ((), (), s32[]{:S(2)}) async-start(), calls=%async_computation.20 | async-start | bytes 5242880 | tf_op jit(solution)/shard_map/reduce_scatter | solution.py:311
  1569.3 84.7 %copy-start.31 = (f32[256,64]{1,0:T(8,128)S(1)}, f32[256,64]{1,0:T(8,128)}, u32[]{:S(2)}) copy-start(f32[256,64]{1,0:T(8,128)} %copy-done.30) | copy-start | bytes 196612
  1569.3 84.7 %copy-start.58 = (f32[256]{0:T(256)S(1)}, f32[256]{0:T(256)}, u32[]{:S(2)}) copy-start(f32[256]{0:T(256)} %copy-done.57) | copy-start | bytes 3076
  1569.3 84.7 %copy-start.61 = (f32[256]{0:T(256)S(1)}, f32[256]{0:T(256)}, u32[]{:S(2)}) copy-start(f32[256]{0:T(256)} %copy-done.60) | copy-start | bytes 3076
  1569.3 86.6 %copy-start.16 = (f32[256,2048]{1,0:T(8,128)S(1)}, f32[256,2048]{1,0:T(8,128)}, u32[]{:S(2)}) copy-start(f32[256,2048]{1,0:T(8,128)} %copy-done.15) | copy-start | bytes 6291460
  1569.3 86.6 %copy-start.52 = (f32[2048]{0:T(1024)S(1)}, f32[2048]{0:T(1024)}, u32[]{:S(2)}) copy-start(f32[2048]{0:T(1024)} %param.32) | copy-start | bytes 24580
  1569.3 248.9 %all-gather.28.cloned.1.call-start = ((), (), s32[]{:S(2)}) async-start(), calls=%async_computation.23 | async-start | bytes 5242880 | tf_op jit(solution)/shard_map/all_gather | solution.py:461
  1655.9 76.1 %copy-start.29 = (bf16[256,2048]{1,0:T(8,128)(2,1)S(1)}, bf16[256,2048]{1,0:T(8,128)(2,1)}, u32[]{:S(2)}) copy-start(bf16[256,2048]{1,0:T(8,128)(2,1)} %param.41) | copy-start | bytes 3145732
  1736.8 207.3 %reduce-scatter.29.cloned.1.call-start = ((), (), s32[]{:S(2)}) async-start(), calls=%async_computation.28 | async-start | bytes 2359296 | tf_op jit(solution)/shard_map/reduce_scatter | solution.py:569
  1824.6 6.4 copy-start.5
  1824.6 6.4 copy-start.36
  1824.6 6.3 copy-start.43
  1824.6 6.3 copy-start.45
  1824.6 6.3 copy-start.76
  1824.6 143.2 %reduce-scatter.23.cloned.1.call-start = ((), (), s32[]{:S(2)}) async-start(), calls=%async_computation.25 | async-start | bytes 2359296 | tf_op jit(solution)/shard_map/reduce_scatter | solution.py:551
  1835.7 6.2 copy-start.6
  1845.6 6.3 copy-start.2
  1861.3 6.2 copy-start.6
  1871.3 6.1 copy-start.2
  1896.1 14.5 copy-start.65
  1896.1 14.5 copy-start.66
  1910.6 6.4 copy-start.39
  1910.6 6.4 copy-start.74
  1927.3 85.2 %reduce-scatter.25.cloned.1.call-start = ((), (), s32[]{:S(2)}) async-start(), calls=%async_computation.26 | async-start | bytes 2359296 | tf_op jit(solution)/shard_map/reduce_scatter | solution.py:557
  1927.9 129.1 %reduce-scatter.27.cloned.1.call-start = ((), (), s32[]{:S(2)}) async-start(), calls=%async_computation.27 | async-start | bytes 2359296 | tf_op jit(solution)/shard_map/reduce_scatter | solution.py:563
  1928.5 276.4 %reduce-scatter.21.cloned.1.call-start = ((), (), s32[]{:S(2)}) async-start(), calls=%async_computation.24 | async-start | bytes 10485760 | tf_op jit(solution)/shard_map/reduce_scatter | solution.py:299
  1939.8 311.0 %all-reduce.5.cloned.1.call-start = ((), (), s32[]{:S(2)}) async-start(), calls=%async_computation.29 | async-start | bytes 1048576 | tf_op jit(solution)/shard_map/psum | solution.py:580
  1943.5 261.4 %copy-start.14 = (bf16[256,2048]{1,0:T(8,128)(2,1)S(1)}, bf16[256,2048]{1,0:T(8,128)(2,1)}, u32[]{:S(2)}) copy-start(bf16[256,2048]{1,0:T(8,128)(2,1)} %param.24) | copy-start | bytes 3145732
  1943.5 261.4 %copy-start.46 = (f32[2048]{0:T(1024)S(1)}, f32[2048]{0:T(1024)}, u32[]{:S(2)}) copy-start(f32[2048]{0:T(1024)} %param.25) | copy-start | bytes 24580
  1943.5 261.4 %copy-start.64 = (f32[256]{0:T(256)S(1)}, f32[256]{0:T(256)}, u32[]{:S(2)}) copy-start(f32[256]{0:T(256)} %copy-done.63) | copy-start | bytes 3076
  2012.6 194.6 %copy-start.20 = (f32[256,2048]{1,0:T(8,128)S(1)}, f32[256,2048]{1,0:T(8,128)}, u32[]{:S(2)}) copy-start(f32[256,2048]{1,0:T(8,128)} %get-tuple-element.375) | copy-start | bytes 6291460
  2014.5 192.6 %copy-start.73 = (f32[256]{0:T(256)S(1)}, f32[256]{0:T(256)}, u32[]{:S(2)}) copy-start(f32[256]{0:T(256)} %get-tuple-element.421) | copy-start | bytes 3076
  (42 other events, 94.4 us)
Sparse Core Ops, SparseCore 0:
  10.8 30.6 all-gather.13
  43.3 27.8 all-gather.15
  73.1 27.8 all-gather.17
  103.0 80.7 all-gather.11
  185.6 26.7 all-gather.19
  258.8 145.2 reduce-scatter.10
  1146.7 213.2 reduce-scatter.16
  1364.0 205.2 reduce-scatter.12
  1571.6 80.9 reduce-scatter.18
  1654.7 77.2 reduce-scatter.14
  1736.9 81.2 all-gather.27
  1824.7 39.7 reduce-scatter.28
  1927.4 40.2 reduce-scatter.22
  1971.3 41.2 reduce-scatter.24
  2015.7 41.3 reduce-scatter.26
  2059.4 145.4 reduce-scatter.20
Sparse Core Ops, SparseCore 1:
  265.5 157.9 all-gather.21
  426.8 55.5 all-gather.29
  485.2 193.2 all-gather.25
  681.4 192.5 all-gather.23
  1947.3 189.9 all-reduce.4

commit v2 on v1

--- a/solution.py
+++ b/solution.py
@@ -34,7 +34,7 @@
     return lax.broadcasted_iota(jnp.int32, (rows, tokens), 0) == slots[expert : expert + 1, :]
 
 
-def dispatch_kernel(slots_ref, gates_ref, rows_ref, cots_ref, x_ref, c_ref, gate_ref):
+def dispatch_kernel(slots_ref, gates_ref, rows_ref, x_ref, gate_ref):
     pair, experts, tokens = slots_ref.shape
     rows = x_ref.shape[1] // pair
     width = rows_ref.shape[1]
@@ -45,27 +45,31 @@
         for e in range(experts):
             hit = slot_hits(slots, e, rows)
             pieces.append(hit.astype(jnp.float32))
-            gate = jnp.sum(jnp.where(hit, gates_ref[b, e : e + 1, :], 0.0), axis=1, keepdims=True)
-            gate_ref[e, b * rows : (b + 1) * rows, :] = jnp.broadcast_to(gate, (rows, 128))
+            if gate_ref is not None:
+                gate = jnp.sum(jnp.where(hit, gates_ref[b, e : e + 1, :], 0.0), axis=1, keepdims=True)
+                gate_ref[e, b * rows : (b + 1) * rows, :] = jnp.broadcast_to(gate, (rows, 128))
         picks.append(jnp.concatenate(pieces, axis=0).astype(jnp.bfloat16))
     step = min(512, width)
-    for source, target in ((rows_ref, x_ref), (cots_ref, c_ref)):
-        for first in range(0, width, step):
-            parts = [
-                jnp.dot(
-                    picks[b],
-                    source[b * tokens : (b + 1) * tokens, first : first + step],
-                    preferred_element_type=jnp.float32,
-                )
-                for b in range(pair)
-            ]
-            for e in range(experts):
-                target[e, :, first : first + step] = jnp.concatenate(
-                    [part[e * rows : (e + 1) * rows] for part in parts], axis=0
-                ).astype(jnp.bfloat16)
-
-
-def dispatch(slots, gates, rows_all, cots_all, rows):
+    for first in range(0, width, step):
+        parts = [
+            jnp.dot(
+                picks[b],
+                rows_ref[b * tokens : (b + 1) * tokens, first : first + step],
+                preferred_element_type=jnp.float32,
+            )
+            for b in range(pair)
+        ]
+        for e in range(experts):
+            x_ref[e, :, first : first + step] = jnp.concatenate(
+                [part[e * rows : (e + 1) * rows] for part in parts], axis=0
+            ).astype(jnp.bfloat16)
+
+
+def plain_dispatch_kernel(slots_ref, rows_ref, x_ref):
+    dispatch_kernel(slots_ref, None, rows_ref, x_ref, None)
+
+
+def dispatch(slots, gates, rows_all, rows):
     blocks, experts, tokens = slots.shape
     width = rows_all.shape[1]
     pair = 2
@@ -73,20 +77,27 @@
     table = pl.BlockSpec((pair, experts, tokens), lambda i: (i, 0, 0))
     source = pl.BlockSpec((pair * tokens, width), lambda i: (i, 0))
     target = pl.BlockSpec((experts, pair * rows, width), lambda i: (0, i, 0))
+    settings = dict(
+        grid=(blocks // pair,),
+        compiler_params=pltpu.CompilerParams(vmem_limit_bytes=50 << 20),
+        cost_estimate=pl.CostEstimate(
+            flops=2 * blocks * experts * rows * tokens * width,
+            bytes_accessed=2 * blocks * (tokens + experts * rows) * width,
+            transcendentals=0,
+        ),
+    )
+    if gates is None:
+        return pl.pallas_call(
+            plain_dispatch_kernel, out_shape=out, in_specs=[table, source], out_specs=target, name="pick", **settings
+        )(slots, rows_all)
     return pl.pallas_call(
         dispatch_kernel,
-        grid=(blocks // pair,),
-        out_shape=(out, out, jax.ShapeDtypeStruct((experts, blocks * rows, 128), jnp.float32)),
-        in_specs=[table, table, source, source],
-        out_specs=[target, target, pl.BlockSpec((experts, pair * rows, 128), lambda i: (0, i, 0))],
-        compiler_params=pltpu.CompilerParams(vmem_limit_bytes=50 << 20),
-        cost_estimate=pl.CostEstimate(
-            flops=4 * blocks * experts * rows * tokens * width,
-            bytes_accessed=4 * blocks * (tokens + experts * rows) * width,
-            transcendentals=0,
-        ),
+        out_shape=(out, jax.ShapeDtypeStruct((experts, blocks * rows, 128), jnp.float32)),
+        in_specs=[table, table, source],
+        out_specs=[target, pl.BlockSpec((experts, pair * rows, 128), lambda i: (0, i, 0))],
         name="dispatch",
-    )(slots, gates, rows_all, cots_all)
+        **settings,
+    )(slots, gates, rows_all)
 
 
 def turned(left, right):
@@ -234,6 +245,442 @@
     )(slots, outs, grads)
 
 
+MESH = pl.DeviceIdType.MESH
+
+
+def place():
+    dp, z = lax.axis_index("dp"), lax.axis_index("tensor")
+    return dp // 4, dp // 2 % 2, dp % 2, z
+
+
+def peer(y, x, core, z):
+    return (y * 4 + x * 2 + core, z)
+
+
+def block_of(y, x, core, z):
+    return (y * 4 + x * 2 + core) * 4 + z
+
+
+def greet(line):
+    y, x, core, z = place()
+    barrier = pltpu.get_barrier_semaphore()
+    for near in ((y, x, 1 - core, z), (y, 1 - x, core, z), (1 - y, x, core, z)):
+        pl.semaphore_signal(barrier, inc=1, device_id=peer(*near), device_id_type=MESH)
+
+    @pl.when(z > 0)
+    def _():
+        pl.semaphore_signal(barrier, inc=1, device_id=peer(y, x, core, z - 1), device_id_type=MESH)
+
+    @pl.when(z < line - 1)
+    def _():
+        pl.semaphore_signal(barrier, inc=1, device_id=peer(y, x, core, z + 1), device_id_type=MESH)
+
+    pl.semaphore_wait(barrier, 3 + (z + line - 1) // line + (2 * line - 2 - z) // line)
+
+
+def gather_kernel(line, count, *refs):
+    owns, outs = refs[:count], refs[count : 2 * count]
+    local_sem, send_sem, recv_sem = refs[2 * count :]
+    y, x, core, z = place()
+    greet(line)
+    waits = []
+    sent = [0]
+
+    def send(cond, n, block, source_own, target):
+        rows = owns[n].shape[0]
+        part = pl.ds(block * rows, rows)
+        copy = pltpu.make_async_remote_copy(
+            src_ref=owns[n] if source_own else outs[n].at[part],
+            dst_ref=outs[n].at[part],
+            send_sem=send_sem.at[sent[0]],
+            recv_sem=recv_sem.at[n, block],
+            device_id=peer(*target),
+            device_id_type=MESH,
+        )
+        sent[0] += 1
+        waits.append((cond, copy))
+        if cond is None:
+            copy.start()
+        else:
+            pl.when(cond)(copy.start)
+
+    def arrive(n, block):
+        rows = owns[n].shape[0]
+        part = pl.ds(block * rows, rows)
+        pltpu.make_async_copy(outs[n].at[part], outs[n].at[part], recv_sem.at[n, block]).wait()
+
+    def both(a, b):
+        return b if a is None else a & b
+
+    sibling, near_x, near_y = (y, x, 1 - core, z), (y, 1 - x, core, z), (1 - y, x, core, z)
+    mine = block_of(y, x, core, z)
+    locals_ = []
+    for n in range(count):
+        rows = owns[n].shape[0]
+        own_copy = pltpu.make_async_copy(owns[n], outs[n].at[pl.ds(mine * rows, rows)], local_sem.at[n])
+        own_copy.start()
+        locals_.append(own_copy)
+
+    def own_column(n, step, sign):
+        zz = z + sign * step
+        valid = None if step == 0 else (zz >= 0) & (zz < line)
+        block = block_of(y, x, core, zz)
+
+        def fetch():
+            if step:
+                arrive(n, block)
+
+        if step:
+            pl.when(valid)(fetch)
+        if step == 0:
+            send(z > 0, n, block, True, (y, x, core, z - 1))
+            send(z < line - 1, n, block, True, (y, x, core, z + 1))
+        elif sign < 0:
+            send(both(valid, z < line - 1), n, block, False, (y, x, core, z + 1))
+        else:
+            send(both(valid, z > 0), n, block, False, (y, x, core, z - 1))
+        send(valid, n, block, step == 0, near_x)
+        send(valid, n, block, step == 0, near_y)
+        send(valid, n, block, step == 0, sibling)
+
+    def next_column(n, step, sign, along_x):
+        zz = z + sign * step
+        valid = None if step == 0 else (zz >= 0) & (zz < line)
+        yy, xx = (y, 1 - x) if along_x else (1 - y, x)
+        block = block_of(yy, xx, core, zz)
+        if step:
+            pl.when(valid)(lambda: arrive(n, block))
+        else:
+            arrive(n, block)
+        if step % 2 == (0 if along_x else 1):
+            send(valid, n, block, False, near_y if along_x else near_x)
+        send(valid, n, block, False, sibling)
+
+    def far_column(n, step, sign):
+        zz = z + sign * step
+        valid = None if step == 0 else (zz >= 0) & (zz < line)
+        block = block_of(1 - y, 1 - x, core, zz)
+        if step:
+            pl.when(valid)(lambda: arrive(n, block))
+        else:
+            arrive(n, block)
+        send(valid, n, block, False, sibling)
+
+    def signs(step):
+        return (1,) if step == 0 else (-1, 1)
+
+    for n in range(count):
+        own_column(n, 0, 1)
+    for step in range(line + 1):
+        for n in range(count):
+            if step + 1 < line:
+                for sign in signs(step + 1):
+                    own_column(n, step + 1, sign)
+            if step < line:
+                for sign in signs(step):
+                    next_column(n, step, sign, True)
+                    next_column(n, step, sign, False)
+            if step:
+                for sign in signs(step - 1):
+                    far_column(n, step - 1, sign)
+    for yy in range(2):
+        for xx in range(2):
+            for zz in range(line):
+                for n in range(count):
+                    arrive(n, block_of(yy, xx, 1 - core, zz))
+    for cond, copy in waits:
+        if cond is None:
+            copy.wait_send()
+        else:
+            pl.when(cond)(copy.wait_send)
+    for copy in locals_:
+        copy.wait()
+
+
+def gather_all(arrays, collective_id):
+    count = len(arrays)
+    any_ref = pl.BlockSpec(memory_space=pl.ANY)
+    line = lax.axis_size("tensor")
+    devices = 8 * line
+    return pl.pallas_call(
+        functools.partial(gather_kernel, line, count),
+        out_shape=[jax.ShapeDtypeStruct((devices * a.shape[0],) + a.shape[1:], a.dtype) for a in arrays],
+        in_specs=[any_ref] * count,
+        out_specs=[any_ref] * count,
+        scratch_shapes=[
+            pltpu.SemaphoreType.DMA((count,)),
+            pltpu.SemaphoreType.DMA((count * 80,)),
+            pltpu.SemaphoreType.DMA((count, devices)),
+        ],
+        compiler_params=pltpu.CompilerParams(collective_id=collective_id, has_side_effects=True),
+        name="gather_all",
+    )(*arrays)
+
+
+def reduce_kernel(line, slots_ref, grads_ref, outs_ref, sum_ref, part_ref,
+                  grad_in, out_in, out_stage, stage, near, far_x, far_y, from_x, from_y, up, down,
+                  in_sem, part_sem, stage_sem, near_sem, send_sem, far_sem, x_sem, y_sem, line_sem):
+    y, x, core, z = place()
+    tokens, width = sum_ref.shape
+    half = tokens // 2
+    experts, room = grads_ref.shape[1:3]
+    rounds = line
+    greet(line)
+
+    def goal(r):
+        early = 1 - r // 2
+        return (line - 1) * (r % 2) * early + (r - 1) * (1 - early)
+
+    def block_at(q):
+        r, j = q // 8, q % 8
+        column = j % 4
+        dy, dx = (column + 1) % 2, 1 - column // 2
+        own = j // 4
+        target_core = core * own + (1 - core) * (1 - own)
+        return block_of((y + dy) % 2, (x + dx) % 2, target_core, goal(r))
+
+    def load(q):
+        b = block_at(q)
+        return (
+            pltpu.make_async_copy(grads_ref.at[b], grad_in.at[q % 2], in_sem.at[0, q % 2]),
+            pltpu.make_async_copy(outs_ref.at[b], out_in.at[q % 2], in_sem.at[1, q % 2]),
+        )
+
+    def to_part(q):
+        b = block_at(q)
+        return pltpu.make_async_copy(out_stage.at[q % 2], part_ref.at[pl.ds(b * tokens, tokens)], part_sem.at[q % 2])
+
+    def to_sibling(r, j):
+        return pltpu.make_async_remote_copy(
+            src_ref=stage.at[j], dst_ref=near.at[r * 4 + j], send_sem=stage_sem.at[j], recv_sem=near_sem.at[r * 4 + j],
+            device_id=peer(y, x, 1 - core, z), device_id_type=MESH,
+        )
+
+    near_x, near_y = peer(y, 1 - x, core, z), peer(1 - y, x, core, z)
+
+    def rows(h):
+        return pl.ds(h * half, half)
+
+    def cross(kind, r):
+        column, h, target, sem, index, lane = {
+            "far_x": (0, 0, far_x.at[r], far_sem.at[0, r], near_x, 0),
+            "far_y": (0, 1, far_y.at[r], far_sem.at[1, r], near_y, 1),
+            "x0": (1, 0, from_x.at[r, rows(0)], x_sem.at[r, 0], near_x, 2),
+            "x1": (1, 1, from_x.at[r, rows(1)], x_sem.at[r, 1], near_x, 3),
+            "y0": (2, 0, from_y.at[r, rows(0)], y_sem.at[r, 0], near_y, 4),
+            "y1": (2, 1, from_y.at[r, rows(1)], y_sem.at[r, 1], near_y, 5),
+        }[kind]
+        return pltpu.make_async_remote_copy(
+            src_ref=near.at[r * 4 + column, rows(h)], dst_ref=target, send_sem=send_sem.at[lane, r], recv_sem=sem,
+            device_id=index, device_id_type=MESH,
+        )
+
+    def along(sign, r):
+        target = up if sign > 0 else down
+        lane = 0 if sign > 0 else 1
+        return pltpu.make_async_remote_copy(
+            src_ref=near.at[r * 4 + 3], dst_ref=target.at[r], send_sem=send_sem.at[6 + lane, r], recv_sem=line_sem.at[lane, r],
+            device_id=peer(y, x, core, z + sign), device_id_type=MESH,
+        )
+
+    def term(q, source, target_width, store):
+        picks = jnp.concatenate(
+            [slot_hits(slots_ref[block_at(q)], e, room).astype(jnp.float32) for e in range(experts)], axis=0
+        ).astype(jnp.bfloat16)
+        for first in range(0, target_width, 512):
+            part = slice(first, min(first + 512, target_width))
+            values = source[q % 2, :, :, part].reshape(experts * room, part.stop - first)
+            store(part, turned(picks, values))
+
+    for copy in load(0):
+        copy.start()
+
+    def one(r, j, own):
+        q = r * 8 + own * 4 + j
+        for copy in load(q):
+            copy.wait()
+
+        @pl.when(q + 1 < rounds * 8)
+        def _():
+            for copy in load(q + 1):
+                copy.start()
+
+        if own:
+            near_slot = r * 4 + j
+            to_sibling(r, j).wait_recv()
+
+            def keep(part, value):
+                near[near_slot, :, part] = (value + near[near_slot, :, part].astype(jnp.float32)).astype(jnp.bfloat16)
+
+            term(q, grad_in, width, keep)
+        else:
+
+            @pl.when(r > 0)
+            def _():
+                to_sibling(r - 1, j).wait_send()
+
+            def keep(part, value):
+                stage[j, :, part] = value.astype(jnp.bfloat16)
+
+            term(q, grad_in, width, keep)
+            to_sibling(r, j).start()
+
+        @pl.when(q >= 2)
+        def _():
+            to_part(q - 2).wait()
+
+        def put(part, value):
+            out_stage[q % 2, :, part] = value.astype(jnp.bfloat16)
+
+        term(q, out_in, out_stage.shape[2], put)
+        to_part(q).start()
+
+    def add(target, h, *sources):
+        for first in range(0, width, 512):
+            part = slice(first, min(first + 512, width))
+            total = near[target, h, part].astype(jnp.float32)
+            for source in sources:
+                total = total + source(part).astype(jnp.float32)
+            near[target, h, part] = total.astype(jnp.bfloat16)
+
+    def work(s, carry):
+        @pl.when(s < rounds)
+        def _():
+            r = s
+            lax.fori_loop(0, 4, lambda j, c: (one(r, j, 0), c)[1], 0)
+            lax.fori_loop(0, 4, lambda j, c: (one(r, j, 1), c)[1], 0)
+            for kind in ("far_x", "far_y", "x0", "y1"):
+                cross(kind, r).start()
+            cross("far_y", r).wait_recv()
+            add(r * 4 + 1, rows(1), lambda part: far_y[r, :, part])
+            cross("x1", r).start()
+            cross("far_x", r).wait_recv()
+            add(r * 4 + 2, rows(0), lambda part: far_x[r, :, part])
+            cross("y0", r).start()
+
+        @pl.when((s >= 1) & (s < rounds + 1))
+        def _():
+            r = s - 1
+            for kind in ("x0", "x1", "y0", "y1"):
+                cross(kind, r).wait_recv()
+            for h in range(2):
+                add(
+                    r * 4 + 3,
+                    rows(h),
+                    lambda part: from_x[r, rows(h), part],
+                    lambda part: from_y[r, rows(h), part],
+                )
+
+        for hop in range(line - 1):
+            r = s - 1 - hop
+            live = (r >= 0) & (r < rounds)
+            held = r * live.astype(jnp.int32)
+
+            @pl.when(live & (goal(held) > z) & (z == hop))
+            def _():
+                if hop:
+                    along(1, held).wait_recv()
+                    for h in range(2):
+                        add(held * 4 + 3, rows(h), lambda part: up[held, rows(h), part])
+                along(1, held).start()
+
+            @pl.when(live & (goal(held) < z) & (line - 1 - z == hop))
+            def _():
+                if hop:
+                    along(-1, held).wait_recv()
+                    for h in range(2):
+                        add(held * 4 + 3, rows(h), lambda part: down[held, rows(h), part])
+                along(-1, held).start()
+
+        return carry
+
+    lax.fori_loop(0, rounds + line - 1, work, 0)
+
+    mine = (z + (z + 2) // 3) % 4 + z // 3
+    sum_ref[...] = near[mine * 4 + 3].astype(jnp.float32)
+
+    @pl.when(z > 0)
+    def _():
+        along(1, mine).wait_recv()
+        sum_ref[...] += up[mine].astype(jnp.float32)
+
+    @pl.when(z < line - 1)
+    def _():
+        along(-1, mine).wait_recv()
+        sum_ref[...] += down[mine].astype(jnp.float32)
+
+    def finish(r, carry):
+        for kind in ("far_x", "far_y", "x0", "x1", "y0", "y1"):
+            cross(kind, r).wait_send()
+
+        @pl.when(goal(r) > z)
+        def _():
+            along(1, r).wait_send()
+
+        @pl.when(goal(r) < z)
+        def _():
+            along(-1, r).wait_send()
+
+        return carry
+
+    lax.fori_loop(0, rounds, finish, 0)
+    for j in range(4):
+        to_sibling(rounds - 1, j).wait_send()
+    for q in (rounds * 8 - 2, rounds * 8 - 1):
+        to_part(q).wait()
+
+
+def reduce_all(slots, outs, grads, collective_id):
+    blocks, experts, tokens = slots.shape
+    room, width = outs.shape[2:]
+    wider = grads.shape[3]
+    line = 4
+    low = jnp.bfloat16
+    any_ref = pl.BlockSpec(memory_space=pl.ANY)
+    vmem = pl.BlockSpec(memory_space=pltpu.VMEM)
+    dma = pltpu.SemaphoreType.DMA
+    return pl.pallas_call(
+        functools.partial(reduce_kernel, line),
+        out_shape=(
+            jax.ShapeDtypeStruct((tokens, wider), jnp.float32),
+            jax.ShapeDtypeStruct((blocks * tokens, width), low),
+        ),
+        in_specs=[vmem, any_ref, any_ref],
+        out_specs=[vmem, any_ref],
+        scratch_shapes=[
+            pltpu.VMEM((2, experts, room, wider), low),
+            pltpu.VMEM((2, experts, room, width), low),
+            pltpu.VMEM((2, tokens, width), low),
+            pltpu.VMEM((4, tokens, wider), low),
+            pltpu.VMEM((line * 4, tokens, wider), low),
+            pltpu.VMEM((line, tokens // 2, wider), low),
+            pltpu.VMEM((line, tokens // 2, wider), low),
+            pltpu.VMEM((line, tokens, wider), low),
+            pltpu.VMEM((line, tokens, wider), low),
+            pltpu.VMEM((line, tokens, wider), low),
+            pltpu.VMEM((line, tokens, wider), low),
+            dma((2, 2)),
+            dma((2,)),
+            dma((4,)),
+            dma((line * 4,)),
+            dma((8, line)),
+            dma((2, line)),
+            dma((line, 2)),
+            dma((line, 2)),
+            dma((2, line)),
+        ],
+        compiler_params=pltpu.CompilerParams(
+            collective_id=collective_id, has_side_effects=True, vmem_limit_bytes=62 << 20
+        ),
+        cost_estimate=pl.CostEstimate(
+            flops=2 * blocks * experts * room * tokens * (width + wider),
+            bytes_accessed=2 * blocks * experts * room * (width + wider),
+            transcendentals=0,
+        ),
+        name="reduce_all",
+    )(slots, grads, outs)
+
+
 def visible_block(row_paths, key_paths, key_valid, row_first):
     row_count = row_paths.shape[1]
     key_count = key_paths.shape[1]
@@ -297,17 +744,20 @@
 
 def heads_to_rows(term, rows):
     return lax.psum_scatter(
-        term(jnp.int32(0), rows * lax.axis_size("tensor")),
+        term(jnp.int32(0), rows * lax.axis_size("tensor")).astype(jnp.bfloat16),
         "tensor",
         scatter_dimension=0,
         tiled=True,
-    )
-
-
-def sum_to_blocks(rows, tokens):
+    ).astype(jnp.float32)
+
+
+def sum_over_dp(rows):
     dp = lax.axis_size("dp")
     pieces = rows.reshape(dp, rows.shape[0] // dp, rows.shape[1])
-    part = lax.psum_scatter(pieces, "dp", scatter_dimension=0, tiled=False)
+    return lax.psum_scatter(pieces, "dp", scatter_dimension=0, tiled=False)
+
+
+def sum_over_tensor(part):
     return lax.psum_scatter(part, "tensor", scatter_dimension=0, tiled=True)
 
 
@@ -343,6 +793,17 @@
     block_rows = min(512, seq_len)
     block_count = seq_len // block_rows
     score_scale = HD ** (-0.5)
+    everyone = ("dp", "tensor")
+    direct = dp_groups == 8 and lax.axis_size("tensor") == 4
+    first_expert = lax.axis_index("dp") * local_experts
+    slot_rows = padded(capacity, 8)
+    valid_dev = lax.dynamic_slice_in_dim(token_valid, tensor_rank * tok_dev, tok_dev)
+    slots_own = slot_table(routes, route_order, valid_dev, experts, capacity)
+    slots_all = lax.all_gather(slots_own.astype(jnp.bfloat16), everyone, axis=0)
+    slots = lax.dynamic_slice_in_dim(slots_all, first_expert, local_experts, 1).astype(jnp.int32)
+    blocks = slots.shape[0]
+    cots_all = lax.all_gather(cotangent, everyone, axis=0, tiled=True)
+    c_slots = dispatch(slots, None, cots_all, slot_rows)
     gathered_query, gathered_key, gathered_value, gathered_out = (
         lax.all_gather(w_query, "dp", axis=0, tiled=True),
         lax.all_gather(w_key, "dp", axis=0, tiled=True),
@@ -407,23 +868,20 @@
         return jnp.dot(attn_mixed, gathered_out, preferred_element_type=jnp.float32)
 
     x_one = residual_float + heads_to_rows(attn_term, tok_dev)
+    x_one, c_slots = lax.optimization_barrier((x_one, c_slots))
     normed_two, scale_two = rms_apply(x_one, moe_gain)
     hidden_two = normed_two.astype(jnp.bfloat16)
     logits = jnp.dot(hidden_two, router, preferred_element_type=jnp.float32)
     probs = jax.nn.softmax(logits, axis=-1)
-    everyone = ("dp", "tensor")
-    cots_all = lax.all_gather(cotangent, everyone, axis=0, tiled=True)
-    valid_dev = lax.dynamic_slice_in_dim(token_valid, tensor_rank * tok_dev, tok_dev)
-    slots_own = slot_table(routes, route_order, valid_dev, experts, capacity)
-    slots_all = lax.all_gather(slots_own.astype(jnp.bfloat16), everyone, axis=0)
-    first_expert = lax.axis_index("dp") * local_experts
-    slots = lax.dynamic_slice_in_dim(slots_all, first_expert, local_experts, 1).astype(jnp.int32)
-    gates_all = lax.all_gather(probs.T, everyone, axis=0)
+    gates_own = probs.T
+    if direct:
+        rows_all, gates_all = gather_all([hidden_two, gates_own], 1)
+        gates_all = gates_all.reshape(-1, experts, tok_dev)
+    else:
+        gates_all = lax.all_gather(gates_own, everyone, axis=0)
+        rows_all = lax.all_gather(hidden_two, everyone, axis=0, tiled=True)
     gates = lax.dynamic_slice_in_dim(gates_all, first_expert, local_experts, 1)
-    rows_all = lax.all_gather(hidden_two, everyone, axis=0, tiled=True)
-    blocks = slots.shape[0]
-    slot_rows = padded(capacity, 8)
-    x_slots, c_slots, gate_slots = dispatch(slots, gates, rows_all, cots_all, slot_rows)
+    x_slots, gate_slots = dispatch(slots, gates, rows_all, slot_rows)
     outs, grads, grad_w_gate, grad_w_up, grad_w_down = expert_pass(
         first_expert.reshape(1),
         x_slots,
@@ -435,10 +893,12 @@
         blocks,
         padded(slot_rows, 16),
     )
-    out_part, grad_part = combine(slots, outs, grads)
-    grad_rows = sum_to_blocks(grad_part, tok_dev).astype(jnp.float32)
-    moe_out = sum_to_blocks(out_part, tok_dev).astype(jnp.float32)
-    block_out = (x_one + moe_out).astype(jnp.bfloat16)
+    if direct:
+        grad_rows, out_part = reduce_all(slots, outs, grads, 2)
+    else:
+        out_part, grad_part = combine(slots, outs, grads)
+        grad_rows = sum_over_tensor(sum_over_dp(grad_part)).astype(jnp.float32)
+    out_part = sum_over_dp(out_part)
     grad_out = cotangent.astype(jnp.float32)
     grad_hidden_two = grad_rows[:, :width]
     grad_probs = grad_rows[:, width : width + experts]
@@ -532,6 +992,8 @@
     grad_joined = jnp.concatenate(
         (grad_q_raw, grad_k_raw, grad_value_all.reshape(seq_len, head_cols)), axis=1
     ).astype(jnp.bfloat16)
+    out_part, grad_joined = lax.optimization_barrier((out_part, grad_joined))
+    block_out = (x_one + sum_over_tensor(out_part).astype(jnp.float32)).astype(jnp.bfloat16)
     grad_joined_weight = lax.dot_general(
         hidden_all, grad_joined, (((0,), (0,)), ((), ())), preferred_element_type=jnp.float32
     )

time: 2270 us -> 1910 us (0.84)
  waiting for transfers between devices: 1660 us -> 1020 us
  Pallas kernels: 273 us -> 552 us
    reduce_scatter x6 -> x4, waiting for transfers between devices: 861 us -> 333 us  [the longest x2 155 us: heads_to_rows(): lax.psum_scatter(term(jnp.int32(0), rows * lax.axis_size('tensor')).astyp...]
    pallas_call x2 -> x4, Pallas kernels: 132 us -> 411 us  [the longest x1 191 us: reduce_all(): pl.pallas_call(functools.partial(reduce_kernel, line), out_shape=(jax.Sha...]
    all_gather x2 -> x0, waiting for transfers between devices: 254 us -> none  [the longest x1 196 us: body(): rows_all = lax.all_gather(hidden_two, everyone, axis=0, tiled=True)]
    psum x1, waiting for transfers between devices: 0.01 us -> 89.9 us  [body(): lax.psum((grad_attn_gain_part, grad_moe_gain_part, grad_query_full, grad_...]
    all_gather x1, waiting for transfers between devices: 81.3 us -> 106 us  [body(): lax.all_gather(grad_x_one.astype(jnp.bfloat16), 'tensor', axis=0, tiled=T...]
  transfers between devices with their start and end apart: 21 -> 17, of which waited for: 18 -> 16; matrix products, arithmetic and copies ran while one was open for 9% -> 11% of each run, Pallas kernels for 0% -> 0%
where the time goes in v2:
time: 1910 us; the launch traced here: 1900 us
  waiting for transfers between devices  1020 us (53%)
  Pallas kernels  552 us (29%)
  matrix products  104 us (5%)
  other arithmetic  84.5 us (4%)
  blocking collectives  60.9 us (3%)
  local copies, waits for them, and re-layouts  51.1 us (3%)
    all_gather x1, waiting for transfers between devices, body(): cots_all = lax.all_gather(cotangent, everyone, axis=0, tiled=True)  197 us
    pallas_call x1, Pallas kernels, reduce_all(): pl.pallas_call(functools.partial(reduce_kernel, line), out_shape=(jax.Sha...  191 us
    reduce_scatter x2, waiting for transfers between devices, heads_to_rows(): lax.psum_scatter(term(jnp.int32(0), rows * lax.axis_size('tensor')).astyp...  155 us
    pallas_call x1, Pallas kernels, gather_all(): pl.pallas_call(functools.partial(gather_kernel, line, count), out_shape=[...  153 us
    pallas_call x1, Pallas kernels, expert_pass(): pl.pallas_call(kernel, grid_spec=pltpu.PrefetchScalarGridSpec(num_scalar_...  141 us
    all_gather x1, waiting for transfers between devices, body(): lax.all_gather(grad_x_one.astype(jnp.bfloat16), 'tensor', axis=0, tiled=T...  106 us
    reduce_scatter x1, waiting for transfers between devices, sum_over_dp(): return lax.psum_scatter(pieces, 'dp', scatter_dimension=0, tiled=False)  104 us
    psum x1, waiting for transfers between devices, body(): lax.psum((grad_attn_gain_part, grad_moe_gain_part, grad_query_full, grad_...  89.9 us
  transfers between devices with their start and end apart: 17, of which 16 were waited for; matrix products, arithmetic and copies ran while one was open for 11% of the time, Pallas kernels for 0%

profile of v2, /device:TPU:0, one launch (start us, length us, event | category | flops | bytes accessed | tf_op | source)
XLA Modules:
  0.0 1904.7 jit_solution(13362578762154178958)
XLA Ops:
  14.6 5.2 convert_reduce_fusion.1
  22.1 9.4 while.37
  31.5 3.1 multiply_cosine_fusion
  34.5 6.0 all-gather.11.cloned.1.call-done
  40.6 3.2 constant_dynamic-update-slice_fusion.2
  43.7 26.7 %all-gather.13.cloned.1.call-done = bf16[2048,512]{1,0:T(8,128)(2,1)} async-done(((bf16[256,512]{1,0:T(8,128)(2,1)}), bf16[2048,512]{1,0:T(8,128)(2,1)}) %all-gather.13.cloned.1.call-update) | async-done | bytes 2097168 | tf_op jit(solution)/shard_map/all_gather | solution.py:809
  70.4 3.1 constant_dynamic-update-slice_fusion.1
  73.5 26.7 %all-gather.15.cloned.1.call-done = bf16[2048,512]{1,0:T(8,128)(2,1)} async-done(((bf16[256,512]{1,0:T(8,128)(2,1)}), bf16[2048,512]{1,0:T(8,128)(2,1)}) %all-gather.15.cloned.1.call-update) | async-done | bytes 2097168 | tf_op jit(solution)/shard_map/all_gather | solution.py:810
  100.2 3.1 constant_dynamic-update-slice_fusion
  103.3 79.7 %all-gather.9.cloned.1.call-done = bf16[1024,2048]{1,0:T(8,128)(2,1)} async-done(((bf16[256,2048]{1,0:T(8,128)(2,1)}), bf16[1024,2048]{1,0:T(8,128)(2,1)}) %all-gather.9.cloned.1.call-update) | async-done | bytes 4194320 | tf_op jit(solution)/shard_map/all_gather | solution.py:819
  183.0 10.0 fusion.83
  195.8 9.6 all-reduce.2
  206.0 4.7 multiply_multiply_fusion
  212.7 3.2 fusion.80
  222.5 26.4 %while.38 = (s32[]{:T(128)}, bf16[2,512,4,128]{3,2,1,0:T(4,128)(2,1)}, f32[2,4,512]{2,1,0:T(4,128)S(1)}, s32[3,1024]{1,0:T(4,128)S(1)}, s32[2]{0:T(128)S(1)}, /*...) while((s32[]{:T(128)}, ...), condition=%wide.region_11.12_spmd, body=%wide.region_8.0_spmd.sunk | while | flops 1104412160 | bytes 31564516 | solution.py:864
  228.9 2.4 fusion.128
  231.3 3.1 fusion.129
  242.0 2.4 fusion.128
  244.4 3.1 fusion.129
  249.0 7.3 convolution_convert_fusion.2
  257.2 11.4 all-gather.19.cloned.1.call-done
  269.6 77.7 %reduce-scatter.9.cloned.1.call-done = bf16[256,2048]{1,0:T(8,128)(2,1)} async-done(((bf16[1024,2048]{1,0:T(8,128)(2,1)}), bf16[256,2048]{1,0:T(8,128)(2,1)}) %reduce-scatter.9.cloned.1.call-update) | async-done | bytes 1048592 | tf_op jit(solution)/shard_map/reduce_scatter | solution.py:746
  349.2 196.8 %all-gather.21.cloned.1.call-done.rows_ref = bf16[8192,2048]{1,0:T(8,128)(2,1)} async-done(((bf16[256,2048]{1,0:T(8,128)(2,1)}), bf16[8192,2048]{1,0:T(8,128)(2,1)}) %all-gather.21.cloned.1.call-update) | async-done | bytes 33554448 | tf_op jit(solution)/shard_map/all_gather | solution.py:805
  546.0 33.1 %pick.1.c_ref = bf16[8,1280,2048]{2,1,0:T(8,128)(2,1)} custom-call(s32[32,8,256]{2,1,0:T(8,128)S(1)} %dynamic-slice_convert_fusion.slots_ref, bf16[8192,2048]{1,0:T(8,128)(2,1)} %all-gather.21.cloned.1.call-done.rows_ref), custom_call_target="tpu_custom_call" | custom-call | flops 10737418240 | bytes 75497472 | tf_op jit(solution)/shard_map/pick/pallas_call | solution.py:90
  582.7 153.1 %gather_all.1 = (bf16[8192,2048]{1,0:T(8,128)(2,1)}, f32[2048,256]{1,0:T(8,128)}) custom-call(bf16[256,2048]{1,0:T(8,128)(2,1)} %copy-done.23, f32[64,256]{1,0:T(8,128)} %copy.101.refs_1_), custom_call_target="tpu_custom_call" | custom-call | tf_op jit(solution)/shard_map/gather_all/pallas_call | solution.py:405
  736.8 34.2 %dispatch.1 = (bf16[8,1280,2048]{2,1,0:T(8,128)(2,1)}, f32[8,1280,128]{2,1,0:T(8,128)}) custom-call(s32[32,8,256]{2,1,0:T(8,128)S(1)} %dynamic-slice_convert_fusion.slots_ref, f32[32,8,256]{2,1,0:T(8,128)S(1)} %constant_dynamic-slice_fusion.3.gates_ref, bf16[8192,2048]{1,0:T(8,128)(2,1)} %get-tuple-element.172.rows_ref), custom_call_target="tpu_custom_call" | custom-call | flops 10737418240 | bytes 75497472 | tf_op jit(solution)/shard_map/dispatch/pallas_call | solution.py:93
  770.9 140.7 %experts.1 = (bf16[32,8,48,2048]{3,2,1,0:T(8,128)(2,1)}, bf16[32,8,48,2176]{3,2,1,0:T(8,128)(2,1)}, f32[8,2048,256]{2,1,0:T(8,128)}, f32[8,2048,256]{2,1,0:T(8,128)}, f32[8,256,2048]{2,1,0:T(8,128)}) custom-call(s32[1]{0:T(128)} %bitcast.16.first_ref, bf16[8,1280,2048]{2,1,0:T(8,128)(2,1)} %get-tuple-element.173.x_ref, bf16[8,1280,2048]{2,1,0:T(8,128)(2,1)} %pick.1.c_ref, ...), custom_call_target="tpu_custom_call" | custom-call | flops 96636764160 | bytes 243269632 | tf_op jit(solution)/shard_map/experts/pallas_call | solution.py:174
  911.7 191.0 %reduce_all.1 = (f32[256,2176]{1,0:T(8,128)}, bf16[8192,2048]{1,0:T(8,128)(2,1)}) custom-call(s32[32,8,256]{2,1,0:T(8,128)} %copy-done.1, bf16[32,8,48,2176]{3,2,1,0:T(8,128)(2,1)} %get-tuple-element.176.grads_ref, bf16[32,8,48,2048]{3,2,1,0:T(8,128)(2,1)} %get-tuple-element.177.outs_ref), custom_call_target="tpu_custom_call" | custom-call | flops 26575110144 | bytes 103809024 | tf_op jit(solution)/shard_map/reduce_all/pallas_call | solution.py:642
  1103.8 4.5 multiply_reduce_fusion.1
  1108.4 2.4 fusion.78
  1111.5 105.7 %all-gather.23.cloned.1.call-done = bf16[1024,2048]{1,0:T(8,128)(2,1)} async-done(((bf16[256,2048]{1,0:T(8,128)(2,1)}), bf16[1024,2048]{1,0:T(8,128)(2,1)}) %all-gather.23.cloned.1.call-update) | async-done | bytes 4194320 | tf_op jit(solution)/shard_map/all_gather | solution.py:921
  1217.2 6.2 convolution_convert_fusion.4
  1223.4 58.1 %while.39 = (s32[]{:T(128)}, f32[1024,4,128]{0,2,1:T(8,128)S(1)}, f32[1024,4,128]{0,2,1:T(8,128)}, f32[2,512,4,128]{3,1,0,2:T(8,128)}, s32[2]{0:T(128)S(1)}, /*i...) while((s32[]{:T(128)}, f32[1024,4,128]{0,2,1:T(8,128)S(1)}, ...), condition=%wide.region_23.24_spmd.clone, body=%wide.region_21.23_spmd.clone.sunk | while | flops 2723937792 | bytes 180454416 | solution.py:973
  1228.5 2.6 fusion.139
  1231.2 3.6 multiply_reduce_fusion.8
  1235.7 3.7 multiply_convert_fusion.3
  1239.4 4.8 bitcast_add_fusion.4
  1249.7 4.0 bitcast_add_fusion.5
  1258.3 2.7 fusion.139
  1261.1 3.6 multiply_reduce_fusion.8
  1265.5 3.7 multiply_convert_fusion.3
  1269.2 3.8 bitcast_add_fusion.4
  1276.3 5.3 bitcast_add_fusion.5
  1283.6 6.5 convolution_convert_fusion.3
  1291.7 4.0 multiply_add_fusion.1
  1295.8 2.3 fusion.57
  1299.1 9.5 all-reduce.1
  1308.6 6.3 fusion.59
  1318.0 2.8 pad_maximum_fusion
  1320.9 104.0 %reduce-scatter.11.cloned.1.call-done = bf16[1,1024,2048]{2,1,0:T(8,128)(2,1)} async-done(((bf16[8,1024,2048]{2,1,0:T(8,128)(2,1)}), bf16[1,1024,2048]{2,1,0:T(8,128)(2,1)}) %reduce-scatter.11.cloned.1.call-update) | async-done | bytes 4194320 | tf_op jit(solution)/shard_map/reduce_scatter | solution.py:757
  1424.9 9.8 convolution_convert_fusion
  1434.7 2.8 fusion.79
  1439.6 11.4 convolution_convert_fusion.1
  1452.2 2.5 fusion.74
  1455.4 14.1 reduce-scatter.23.cloned.1.call-done
  1471.2 43.0 %reduce-scatter.17.cloned.1.call-done = bf16[256,512]{1,0:T(8,128)(2,1)} async-done(((bf16[2048,512]{1,0:T(8,128)(2,1)}), bf16[256,512]{1,0:T(8,128)(2,1)}) %reduce-scatter.17.cloned.1.call-update) | async-done | bytes 262160 | tf_op jit(solution)/shard_map/reduce_scatter | solution.py:1013
  1516.0 42.7 %reduce-scatter.19.cloned.1.call-done = bf16[256,512]{1,0:T(8,128)(2,1)} async-done(((bf16[2048,512]{1,0:T(8,128)(2,1)}), bf16[256,512]{1,0:T(8,128)(2,1)}) %reduce-scatter.19.cloned.1.call-update) | async-done | bytes 262160 | tf_op jit(solution)/shard_map/reduce_scatter | solution.py:1019
  1560.5 43.0 %reduce-scatter.21.cloned.1.call-done = bf16[256,512]{1,0:T(8,128)(2,1)} async-done(((bf16[2048,512]{1,0:T(8,128)(2,1)}), bf16[256,512]{1,0:T(8,128)(2,1)}) %reduce-scatter.21.cloned.1.call-update) | async-done | bytes 262160 | tf_op jit(solution)/shard_map/reduce_scatter | solution.py:1025
  1605.3 77.1 %reduce-scatter.15.cloned.1.call-done = bf16[256,2048]{1,0:T(8,128)(2,1)} async-done(((bf16[1024,2048]{1,0:T(8,128)(2,1)}), bf16[256,2048]{1,0:T(8,128)(2,1)}) %reduce-scatter.15.cloned.1.call-update) | async-done | bytes 1048592 | tf_op jit(solution)/shard_map/reduce_scatter | solution.py:746
  1684.4 3.8 fusion.43
  1688.2 73.8 %reduce-scatter.13.cloned.1.call-done = bf16[256,2048]{1,0:T(8,128)(2,1)} async-done(((bf16[1024,2048]{1,0:T(8,128)(2,1)}), bf16[256,2048]{1,0:T(8,128)(2,1)}) %reduce-scatter.13.cloned.1.call-update) | async-done | bytes 1048592 | tf_op jit(solution)/shard_map/reduce_scatter | solution.py:761
  1762.0 2.5 add_convert_fusion
  1764.5 41.8 %all-reduce = (f32[2048]{0:T(1024)}, f32[2048]{0:T(1024)}, f32[2048]{0:T(1024)}, f32[2048]{0:T(1024)}) all-reduce(f32[2048]{0:T(1024)S(1)} %get-tuple-element.322, f32[2048]{0:T(1024)S(1)} %dynamic_update_slice.22, f32[2048]{0:T(1024)S(1)} %dynamic_update_slice.23, ...), channel_id=1, replica_groups=mesh['dp'=8,'tensor'=4] {'dp','tensor'}, use_global_device_ids=true, to_apply=%region_32.33 | all-reduce | flops 8192 | bytes 65536 | tf_op jit(solution)/shard_map/psum | solution.py:1042
  1806.2 89.9 %all-reduce.5.cloned.1.call-done = f32[2048,64]{0,1:T(8,128)} async-done(((f32[2048,64]{0,1:T(8,128)}), f32[2048,64]{0,1:T(8,128)}) %all-reduce.5.cloned.1.call-update) | async-done | bytes 524304 | tf_op jit(solution)/shard_map/psum | solution.py:1042
  (300 shorter events, 86.2 us)
Async XLA Ops:
  7.2 573.9 %copy-start = (bf16[2048,64]{0,1:T(8,128)(2,1)S(1)}, bf16[2048,64]{0,1:T(8,128)(2,1)}, u32[]{:S(2)}) copy-start(bf16[2048,64]{0,1:T(8,128)(2,1)} %param.33) | copy-start | bytes 786436
  7.2 33.4 %all-gather.11.cloned.1.call-start = ((), (), s32[]{:S(2)}) async-start(), calls=%async_computation.9 | async-start | bytes 2359296 | tf_op jit(solution)/shard_map/all_gather | solution.py:808
  7.9 62.4 %all-gather.13.cloned.1.call-start = ((), (), s32[]{:S(2)}) async-start(), calls=%async_computation.10 | async-start | bytes 2359296 | tf_op jit(solution)/shard_map/all_gather | solution.py:809
  8.7 91.5 %all-gather.15.cloned.1.call-start = ((), (), s32[]{:S(2)}) async-start(), calls=%async_computation.11 | async-start | bytes 2359296 | tf_op jit(solution)/shard_map/all_gather | solution.py:810
  9.4 4.8 copy-start.41
  9.4 4.9 copy-start.64
  9.4 4.9 copy-start.65
  9.5 173.5 %all-gather.9.cloned.1.call-start = ((), (), s32[]{:S(2)}) async-start(), calls=%async_computation.8 | async-start | bytes 5242880 | tf_op jit(solution)/shard_map/all_gather | solution.py:819
  11.0 11.1 copy-start.38
  11.6 10.5 copy-start.58
  13.6 235.4 %all-gather.17.cloned.1.call-start = ((), (), s32[]{:S(2)}) async-start(), calls=%async_computation.12 | async-start | bytes 2359296 | tf_op jit(solution)/shard_map/all_gather | solution.py:811
  14.2 254.5 %all-gather.19.cloned.1.call-start = ((), (), s32[]{:S(2)}) async-start(), calls=%async_computation.14 | async-start | bytes 1081344 | tf_op jit(solution)/shard_map/all_gather | solution.py:802
  20.4 326.9 %reduce-scatter.9.cloned.1.call-start = ((), (), s32[]{:S(2)}) async-start(), calls=%async_computation.13 | async-start | bytes 5242880 | tf_op jit(solution)/shard_map/reduce_scatter | solution.py:746
  21.3 184.7 %copy-start.52 = (f32[512]{0:T(512)}, f32[512]{0:T(512)S(1)}, u32[]{:S(2)}) copy-start(f32[512]{0:T(512)S(1)} %dynamic_slice.47) | copy-start | bytes 6148
  22.1 184.0 %copy-start.54 = (f32[512]{0:T(512)}, f32[512]{0:T(512)S(1)}, u32[]{:S(2)}) copy-start(f32[512]{0:T(512)S(1)} %dynamic_slice.48) | copy-start | bytes 6148
  206.0 4.7 copy-start.47
  206.0 4.7 copy-start.49
  248.9 7.4 copy-start.5
  248.9 7.4 copy-start.9
  249.0 7.4 copy-start.14
  249.0 7.4 copy-start.39
  249.0 7.4 copy-start.42
  249.0 7.4 copy-start.44
  249.0 7.4 copy-start.70
  256.4 289.6 %all-gather.21.cloned.1.call-start = ((), (), s32[]{:S(2)}) async-start(), calls=%async_computation.15 | async-start | bytes 34603008 | tf_op jit(solution)/shard_map/all_gather | solution.py:805
  257.2 960.0 %all-gather.23.cloned.1.call-start = ((), (), s32[]{:S(2)}) async-start(), calls=%async_computation.17 | async-start | bytes 5242880 | tf_op jit(solution)/shard_map/all_gather | solution.py:921
  269.6 467.1 %copy-start.1 = (s32[32,8,256]{2,1,0:T(8,128)}, s32[32,8,256]{2,1,0:T(8,128)S(1)}, u32[]{:S(2)}) copy-start(s32[32,8,256]{2,1,0:T(8,128)S(1)} %dynamic-slice_convert_fusion.slots_ref) | copy-start | bytes 786436
  349.2 230.1 %copy-start.10 = (f32[256,2048]{1,0:T(8,128)}, f32[256,2048]{1,0:T(8,128)S(1)}, u32[]{:S(2)}) copy-start(f32[256,2048]{1,0:T(8,128)S(1)} %convert_add_fusion) | copy-start | bytes 6291460
  581.5 522.3 %copy-start.56 = (f32[256]{0:T(256)}, f32[256]{0:T(256)S(1)}, u32[]{:S(2)}) copy-start(f32[256]{0:T(256)S(1)} %get-tuple-element.432) | copy-start | bytes 3076
  581.6 522.2 %copy-start.35 = (f32[256,64]{1,0:T(8,128)}, f32[256,64]{1,0:T(8,128)S(1)}, u32[]{:S(2)}) copy-start(f32[256,64]{1,0:T(8,128)S(1)} %copy.100) | copy-start | bytes 196612
  581.8 522.0 %copy-start.60 = (f32[256]{0:T(256)}, f32[256]{0:T(256)S(1)}, u32[]{:S(2)}) copy-start(f32[256]{0:T(256)S(1)} %fusion.71) | copy-start | bytes 3076
  1103.8 4.6 copy-start.67
  1103.8 4.6 copy-start.11
  1110.8 314.1 %reduce-scatter.11.cloned.1.call-start = ((), (), s32[]{:S(2)}) async-start(), calls=%async_computation.16 | async-start | bytes 37748736 | tf_op jit(solution)/shard_map/reduce_scatter | solution.py:757
  1111.4 358.1 %reduce-scatter.23.cloned.1.call-start = ((), (), s32[]{:S(2)}) async-start(), calls=%async_computation.23 | async-start | bytes 2359296 | tf_op jit(solution)/shard_map/reduce_scatter | solution.py:1031
  1111.5 111.9 %copy-start.6 = (bf16[1024,4,128]{2,0,1:T(8,128)(2,1)S(1)}, bf16[1024,4,128]{2,0,1:T(8,128)(2,1)}, u32[]{:S(2)}) copy-start(bf16[1024,4,128]{2,0,1:T(8,128)(2,1)} %copy-done.5) | copy-start | bytes 3145732
  1111.5 111.9 %copy-start.40 = (s32[3,1024]{1,0:T(4,128)S(1)}, s32[3,1024]{1,0:T(4,128)}, u32[]{:S(2)}) copy-start(s32[3,1024]{1,0:T(4,128)} %copy-done.39) | copy-start | bytes 36868
  1111.5 111.9 %copy-start.43 = (s32[1024]{0:T(1024)S(1)}, s32[1024]{0:T(1024)}, u32[]{:S(2)}) copy-start(s32[1024]{0:T(1024)} %copy-done.42) | copy-start | bytes 12292
  1111.5 111.9 %copy-start.45 = (f32[2,4,512]{2,1,0:T(4,128)S(1)}, f32[2,4,512]{2,1,0:T(4,128)}, u32[]{:S(2)}) copy-start(f32[2,4,512]{2,1,0:T(4,128)} %copy-done.44) | copy-start | bytes 49156
  1111.5 111.9 %copy-start.71 = (s32[2]{0:T(128)S(1)}, s32[2]{0:T(128)}, u32[]{:S(2)}) copy-start(s32[2]{0:T(128)} %copy-done.70) | copy-start | bytes 28
  1228.4 6.3 copy-start.7
  1231.1 4.6 copy-start.2
  1239.3 5.3 copy-start.4
  1239.4 9.7 copy-start.3
  1244.6 5.1 copy-start.28
  1258.3 6.4 copy-start.7
  1269.2 6.2 copy-start.3
  1283.5 6.6 copy-start.30
  1283.5 6.6 copy-start.32
  1290.1 224.1 %reduce-scatter.17.cloned.1.call-start = ((), (), s32[]{:S(2)}) async-start(), calls=%async_computation.20 | async-start | bytes 2359296 | tf_op jit(solution)/shard_map/reduce_scatter | solution.py:1013
  1290.1 5.6 slice-start
  1295.8 12.7 copy-start.62
  1295.8 12.7 copy-start.63
  1437.5 121.2 %reduce-scatter.19.cloned.1.call-start = ((), (), s32[]{:S(2)}) async-start(), calls=%async_computation.21 | async-start | bytes 2359296 | tf_op jit(solution)/shard_map/reduce_scatter | solution.py:1019
  1438.2 165.3 %reduce-scatter.21.cloned.1.call-start = ((), (), s32[]{:S(2)}) async-start(), calls=%async_computation.22 | async-start | bytes 2359296 | tf_op jit(solution)/shard_map/reduce_scatter | solution.py:1025
  1438.8 243.6 %reduce-scatter.15.cloned.1.call-start = ((), (), s32[]{:S(2)}) async-start(), calls=%async_computation.19 | async-start | bytes 5242880 | tf_op jit(solution)/shard_map/reduce_scatter | solution.py:746
  1451.0 311.0 %reduce-scatter.13.cloned.1.call-start = ((), (), s32[]{:S(2)}) async-start(), calls=%async_computation.18 | async-start | bytes 5242880 | tf_op jit(solution)/shard_map/reduce_scatter | solution.py:761
  1451.6 444.5 %all-reduce.5.cloned.1.call-start = ((), (), s32[]{:S(2)}) async-start(), calls=%async_computation.24 | async-start | bytes 1048576 | tf_op jit(solution)/shard_map/psum | solution.py:1042
  1454.8 227.7 %copy-start.17 = (bf16[256,2048]{1,0:T(8,128)(2,1)S(1)}, bf16[256,2048]{1,0:T(8,128)(2,1)}, u32[]{:S(2)}) copy-start(bf16[256,2048]{1,0:T(8,128)(2,1)} %param.24) | copy-start | bytes 3145732
  1454.8 227.7 %copy-start.46 = (f32[2048]{0:T(1024)S(1)}, f32[2048]{0:T(1024)}, u32[]{:S(2)}) copy-start(f32[2048]{0:T(1024)} %param.25) | copy-start | bytes 24580
  1454.8 227.7 %copy-start.59 = (f32[256]{0:T(256)S(1)}, f32[256]{0:T(256)}, u32[]{:S(2)}) copy-start(f32[256]{0:T(256)} %copy-done.58) | copy-start | bytes 3076
  1471.2 213.2 %copy-start.69 = (f32[256]{0:T(256)S(1)}, f32[256]{0:T(256)}, u32[]{:S(2)}) copy-start(f32[256]{0:T(256)} %get-tuple-element.428) | copy-start | bytes 3076
  1684.4 77.6 %copy-start.12 = (f32[256,2048]{1,0:T(8,128)S(1)}, f32[256,2048]{1,0:T(8,128)}, u32[]{:S(2)}) copy-start(f32[256,2048]{1,0:T(8,128)} %copy-done.10) | copy-start | bytes 6291460
  1688.2 76.3 %copy-start.66 = (f32[2048]{0:T(1024)S(1)}, f32[2048]{0:T(1024)}, u32[]{:S(2)}) copy-start(f32[2048]{0:T(1024)} %get-tuple-element.320) | copy-start | bytes 24580
  (35 other events, 94.8 us)
Sparse Core Ops, SparseCore 0:
  9.9 30.5 all-gather.10
  42.4 27.8 all-gather.12
  72.3 27.8 all-gather.14
  102.2 80.7 all-gather.8
  184.7 26.7 all-gather.16
  214.9 53.7 all-gather.18
  271.5 75.7 reduce-scatter.8
  350.7 195.2 all-gather.20
  1110.9 106.2 all-gather.22
  1221.0 203.8 reduce-scatter.10
  1428.2 41.2 reduce-scatter.22
  1472.9 41.2 reduce-scatter.16
  1517.5 41.1 reduce-scatter.18
  1562.2 41.2 reduce-scatter.20
  1605.7 76.7 reduce-scatter.14
  1684.7 77.2 reduce-scatter.12
  1767.7 128.3 all-reduce.4

commit v3 on v2

--- a/solution.py
+++ b/solution.py
@@ -681,6 +681,310 @@
     )(slots, grads, outs)
 
 
+def either(first, second, take):
+    return first * (1 - take) + second * take
+
+
+def remote(source, target, send_sem, recv_sem, where):
+    return pltpu.make_async_remote_copy(
+        src_ref=source, dst_ref=target, send_sem=send_sem, recv_sem=recv_sem,
+        device_id=peer(*where), device_id_type=MESH,
+    )
+
+
+def landed(target, sem):
+    pltpu.make_async_copy(target, target, sem).wait()
+
+
+class LineGather:
+    def __init__(self, own, out, send_sem, recv_sem, line):
+        self.own, self.out, self.send_sem, self.recv_sem, self.line = own, out, send_sem, recv_sem, line
+        self.spot = place()
+        self.rows = own.shape[0]
+
+    def view(self, block):
+        return self.out.at[pl.ds(block * self.rows, self.rows)]
+
+    def inside(self, block):
+        return (block >= 0) & (block < self.line)
+
+    def copy(self, sign, step):
+        y, x, core, z = self.spot
+        block = z - sign * step
+        lane = (1 - sign) // 2
+        source = self.own if step == 0 else self.view(block)
+        return remote(
+            source, self.view(block), self.send_sem.at[lane, step], self.recv_sem.at[lane, step], (y, x, core, z + sign)
+        )
+
+    def sends(self, sign, step):
+        z = self.spot[3]
+        return self.inside(z - sign * step) & self.inside(z + sign)
+
+    def begin(self):
+        for sign in (1, -1):
+            pl.when(self.sends(sign, 0))(self.copy(sign, 0).start)
+
+    def advance(self, step):
+        z = self.spot[3]
+        for sign in (1, -1):
+            block = z - sign * (step + 1)
+            lane = (1 - sign) // 2
+
+            @pl.when(self.inside(block))
+            def _():
+                landed(self.view(block), self.recv_sem.at[lane, step])
+
+            if step + 1 < self.line - 1:
+                pl.when(self.sends(sign, step + 1))(self.copy(sign, step + 1).start)
+
+    def finish(self):
+        for sign in (1, -1):
+            for step in range(self.line - 1):
+                pl.when(self.sends(sign, step))(self.copy(sign, step).wait_send)
+
+
+def start_kernel(line, hidden_ref, wq_ref, wk_ref, wv_ref, wo_ref, hidden_out, joined_out, wo_out,
+                 local_sem, line_send, line_recv, plane_send, plane_recv):
+    y, x, core, z = place()
+    owns = (wq_ref, wk_ref, wv_ref, wo_ref)
+    near_x, near_y, sibling = (y, 1 - x, core, z), (1 - y, x, core, z), (y, x, 1 - core, z)
+
+    def view(n, yy, xx, half=None):
+        group = yy * 4 + xx * 2 + core
+        rows, columns = owns[n].shape
+        first, count = (0, rows) if half is None else (half * (rows // 2), rows // 2)
+        if n < 3:
+            return joined_out.at[pl.ds(group * rows + first, count), pl.ds(n * columns, columns)]
+        return wo_out.at[pl.ds(first, count), pl.ds(pl.multiple_of(group * columns, columns), columns)]
+
+    kinds = ("x", "y", "s", "fy", "fx", "sx", "sy", "sf")
+
+    def copy(kind, n):
+        source, target, where = {
+            "x": (owns[n], view(n, y, x), near_x),
+            "y": (owns[n], view(n, y, x), near_y),
+            "s": (owns[n], view(n, y, x), sibling),
+            "fy": (view(n, y, 1 - x, 0), view(n, y, 1 - x, 0), near_y),
+            "fx": (view(n, 1 - y, x, 1), view(n, 1 - y, x, 1), near_x),
+            "sx": (view(n, y, 1 - x), view(n, y, 1 - x), sibling),
+            "sy": (view(n, 1 - y, x), view(n, 1 - y, x), sibling),
+            "sf": (view(n, 1 - y, 1 - x), view(n, 1 - y, 1 - x), sibling),
+        }[kind]
+        lane = kinds.index(kind)
+        return remote(source, target, plane_send.at[lane, n], plane_recv.at[lane, n], where)
+
+    def other(n, yy, xx):
+        group = yy * 4 + xx * 2 + 1 - core
+        rows, columns = owns[n].shape
+        if n < 3:
+            return joined_out.at[pl.ds(group * rows, rows), pl.ds(n * columns, columns)]
+        return wo_out.at[pl.ds(0, rows), pl.ds(pl.multiple_of(group * columns, columns), columns)]
+
+    greet(line)
+    hidden = LineGather(hidden_ref, hidden_out, line_send, line_recv, line)
+    locals_ = [pltpu.make_async_copy(hidden_ref, hidden.view(z), local_sem.at[4])]
+    locals_ += [pltpu.make_async_copy(owns[n], view(n, y, x), local_sem.at[n]) for n in range(4)]
+    hidden.begin()
+    for n in range(4):
+        for kind in ("x", "y", "s"):
+            copy(kind, n).start()
+    for local in locals_:
+        local.start()
+    for n in range(4):
+        landed(view(n, y, 1 - x), plane_recv.at[0, n])
+        copy("fy", n).start()
+        copy("sx", n).start()
+        landed(view(n, 1 - y, x), plane_recv.at[1, n])
+        copy("fx", n).start()
+        copy("sy", n).start()
+    hidden.advance(0)
+    for n in range(4):
+        landed(view(n, 1 - y, 1 - x, 0), plane_recv.at[3, n])
+        landed(view(n, 1 - y, 1 - x, 1), plane_recv.at[4, n])
+        copy("sf", n).start()
+    for step in range(1, line - 1):
+        hidden.advance(step)
+    for n in range(4):
+        landed(other(n, y, x), plane_recv.at[2, n])
+        landed(other(n, y, 1 - x), plane_recv.at[5, n])
+        landed(other(n, 1 - y, x), plane_recv.at[6, n])
+        landed(other(n, 1 - y, 1 - x), plane_recv.at[7, n])
+    hidden.finish()
+    for n in range(4):
+        for kind in kinds:
+            copy(kind, n).wait_send()
+    for local in locals_:
+        local.wait()
+
+
+def start_exchange(hidden, w_query, w_key, w_value, w_out, collective_id):
+    line = 4
+    any_ref = pl.BlockSpec(memory_space=pl.ANY)
+    dma = pltpu.SemaphoreType.DMA
+    rows, width = hidden.shape
+    part, columns = w_query.shape
+    low = jnp.bfloat16
+    return pl.pallas_call(
+        functools.partial(start_kernel, line),
+        out_shape=(
+            jax.ShapeDtypeStruct((line * rows, width), low),
+            jax.ShapeDtypeStruct((8 * part, 3 * columns), low),
+            jax.ShapeDtypeStruct((w_out.shape[0], 8 * w_out.shape[1]), low),
+        ),
+        in_specs=[any_ref] * 5,
+        out_specs=[any_ref] * 3,
+        scratch_shapes=[dma((5,)), dma((2, line)), dma((2, line)), dma((8, 4)), dma((8, 4))],
+        compiler_params=pltpu.CompilerParams(collective_id=collective_id, has_side_effects=True),
+        cost_estimate=pl.CostEstimate(flops=0, bytes_accessed=150 << 20, transcendentals=0),
+        name="start_exchange",
+    )(hidden, w_query, w_key, w_value, w_out)
+
+
+def line_gather_kernel(line, own_ref, out_ref, local_sem, send_sem, recv_sem):
+    greet(line)
+    gather = LineGather(own_ref, out_ref, send_sem, recv_sem, line)
+    local = pltpu.make_async_copy(own_ref, gather.view(gather.spot[3]), local_sem)
+    gather.begin()
+    local.start()
+    for step in range(line - 1):
+        gather.advance(step)
+    gather.finish()
+    local.wait()
+
+
+def line_gather(own, collective_id):
+    line = 4
+    any_ref = pl.BlockSpec(memory_space=pl.ANY)
+    dma = pltpu.SemaphoreType.DMA
+    return pl.pallas_call(
+        functools.partial(line_gather_kernel, line),
+        out_shape=jax.ShapeDtypeStruct((line * own.shape[0], own.shape[1]), own.dtype),
+        in_specs=[any_ref],
+        out_specs=any_ref,
+        scratch_shapes=[dma(()), dma((2, line)), dma((2, line))],
+        compiler_params=pltpu.CompilerParams(collective_id=collective_id, has_side_effects=True),
+        cost_estimate=pl.CostEstimate(flops=0, bytes_accessed=150 << 20, transcendentals=0),
+        name="line_gather",
+    )(own)
+
+
+class LineReduce:
+    def __init__(self, part, up, down, send_sem, recv_sem, line):
+        self.part, self.up, self.down = part, up, down
+        self.send_sem, self.recv_sem, self.line = send_sem, recv_sem, line
+        self.spot = place()
+
+    def copy(self, sign, goal):
+        y, x, core, z = self.spot
+        lane = (1 - sign) // 2
+        target = self.up if sign > 0 else self.down
+        return remote(
+            self.part.at[goal], target.at[goal], self.send_sem.at[lane, goal], self.recv_sem.at[lane, goal],
+            (y, x, core, z + sign),
+        )
+
+    def order(self, i):
+        z = self.spot[3]
+        return either(self.line - 1 - i, i, z * 2 // self.line)
+
+    def lead(self, goal):
+        z = self.spot[3]
+        pl.when((z == 0) & (goal > 0))(self.copy(1, goal).start)
+        pl.when((z == self.line - 1) & (goal < z))(self.copy(-1, goal).start)
+
+    def advance(self, unit, total_ref):
+        z, line = self.spot[3], self.line
+        for sign in (1, -1):
+            goal = line - 1 - unit + z if sign > 0 else unit - line + 1 + z
+            live = ((z > 0) & (goal < line)) if sign > 0 else ((z < line - 1) & (goal >= 0))
+            inbox = self.up if sign > 0 else self.down
+
+            @pl.when(live)
+            def _():
+                self.copy(sign, goal).wait_recv()
+                if unit < line - 1:
+                    self.part[goal] = (
+                        self.part[goal].astype(jnp.float32) + inbox[goal].astype(jnp.float32)
+                    ).astype(jnp.bfloat16)
+                    self.copy(sign, goal).start()
+                else:
+                    total_ref[...] += inbox[goal].astype(jnp.float32)
+
+    def finish(self):
+        z = self.spot[3]
+
+        def step(goal, carry):
+            pl.when(goal > z)(self.copy(1, goal).wait_send)
+            pl.when(goal < z)(self.copy(-1, goal).wait_send)
+            return carry
+
+        lax.fori_loop(0, self.line, step, 0)
+
+
+def mixed_out_kernel(line, mixed_ref, w_ref, residual_ref, gain_ref, router_ref,
+                     x_ref, hidden_ref, probs_ref, part, up, down, send_sem, recv_sem):
+    rows, width = x_ref.shape
+    greet(line)
+    reduce = LineReduce(part, up, down, send_sem, recv_sem, line)
+    z = reduce.spot[3]
+
+    def term(i, carry):
+        goal = reduce.order(i)
+        first = pl.multiple_of(goal * rows, rows)
+        for column in range(0, width, 512):
+            piece = slice(column, column + 512)
+            value = jnp.dot(mixed_ref[pl.ds(first, rows), :], w_ref[:, piece], preferred_element_type=jnp.float32)
+
+            @pl.when(goal == z)
+            def _():
+                x_ref[:, piece] = value
+
+            part[goal, :, piece] = value.astype(jnp.bfloat16)
+        reduce.lead(goal)
+        return carry
+
+    lax.fori_loop(0, line, term, 0)
+    for unit in range(1, line):
+        reduce.advance(unit, x_ref)
+    x_one = x_ref[...] + residual_ref[...].astype(jnp.float32)
+    x_ref[...] = x_one
+    scale = lax.rsqrt(jnp.mean(x_one * x_one, axis=-1, keepdims=True) + norm_eps)
+    hidden = (x_one * scale * gain_ref[...]).astype(jnp.bfloat16)
+    hidden_ref[...] = hidden
+    logits = lax.dot_general(
+        router_ref[...], hidden, (((1,), (1,)), ((), ())), preferred_element_type=jnp.float32
+    )
+    shifted = jnp.exp(logits - jnp.max(logits, axis=0, keepdims=True))
+    probs_ref[...] = shifted / jnp.sum(shifted, axis=0, keepdims=True)
+    reduce.finish()
+
+
+def mixed_out(mixed, w_out, residual, gain, router_turned, collective_id):
+    line = 4
+    rows, width = residual.shape
+    experts = router_turned.shape[0]
+    vmem = pl.BlockSpec(memory_space=pltpu.VMEM)
+    dma = pltpu.SemaphoreType.DMA
+    block = pltpu.VMEM((line, rows, width), jnp.bfloat16)
+    return pl.pallas_call(
+        functools.partial(mixed_out_kernel, line),
+        out_shape=(
+            jax.ShapeDtypeStruct((rows, width), jnp.float32),
+            jax.ShapeDtypeStruct((rows, width), jnp.bfloat16),
+            jax.ShapeDtypeStruct((experts, rows), jnp.float32),
+        ),
+        in_specs=[vmem] * 5,
+        out_specs=[vmem] * 3,
+        scratch_shapes=[block, block, block, dma((2, line)), dma((2, line))],
+        compiler_params=pltpu.CompilerParams(
+            collective_id=collective_id, has_side_effects=True, vmem_limit_bytes=56 << 20
+        ),
+        cost_estimate=pl.CostEstimate(flops=0, bytes_accessed=150 << 20, transcendentals=0),
+        name="mixed_out",
+    )(mixed, w_out, residual, gain.reshape(1, width), router_turned)
+
+
 def visible_block(row_paths, key_paths, key_valid, row_first):
     row_count = row_paths.shape[1]
     key_count = key_paths.shape[1]
@@ -804,19 +1108,19 @@
     blocks = slots.shape[0]
     cots_all = lax.all_gather(cotangent, everyone, axis=0, tiled=True)
     c_slots = dispatch(slots, None, cots_all, slot_rows)
-    gathered_query, gathered_key, gathered_value, gathered_out = (
-        lax.all_gather(w_query, "dp", axis=0, tiled=True),
-        lax.all_gather(w_key, "dp", axis=0, tiled=True),
-        lax.all_gather(w_value, "dp", axis=0, tiled=True),
-        lax.all_gather(w_out, "dp", axis=1, tiled=True),
-    )
-    head_cols = gathered_query.shape[1]
+    head_cols = w_query.shape[1]
     local_heads = head_cols // HD
-    joined_weight = jnp.concatenate((gathered_query, gathered_key, gathered_value), axis=1)
     residual_float = residual.astype(jnp.float32)
     normed_one, scale_one = rms_apply(residual_float, attn_gain)
     hidden = normed_one.astype(jnp.bfloat16)
-    hidden_all = lax.all_gather(hidden, "tensor", axis=0, tiled=True)
+    if direct:
+        hidden_all, joined_weight, gathered_out = start_exchange(hidden, w_query, w_key, w_value, w_out, 3)
+    else:
+        hidden_all = lax.all_gather(hidden, "tensor", axis=0, tiled=True)
+        joined_weight = jnp.concatenate(
+            [lax.all_gather(w, "dp", axis=0, tiled=True) for w in (w_query, w_key, w_value)], axis=1
+        )
+        gathered_out = lax.all_gather(w_out, "dp", axis=1, tiled=True)
     projected = jnp.dot(hidden_all, joined_weight, preferred_element_type=jnp.float32)
     q_raw = projected[:, :head_cols]
     k_raw = projected[:, head_cols : 2 * head_cols]
@@ -864,16 +1168,21 @@
     mixed_blocks, log_totals = lax.map(attend, block_starts)
     attn_mixed = mixed_blocks.reshape(seq_len, head_cols)
 
-    def attn_term(first_row, row_count):
-        return jnp.dot(attn_mixed, gathered_out, preferred_element_type=jnp.float32)
-
-    x_one = residual_float + heads_to_rows(attn_term, tok_dev)
-    x_one, c_slots = lax.optimization_barrier((x_one, c_slots))
-    normed_two, scale_two = rms_apply(x_one, moe_gain)
-    hidden_two = normed_two.astype(jnp.bfloat16)
-    logits = jnp.dot(hidden_two, router, preferred_element_type=jnp.float32)
-    probs = jax.nn.softmax(logits, axis=-1)
-    gates_own = probs.T
+    if direct:
+        x_one, hidden_two, gates_own = mixed_out(attn_mixed, gathered_out, residual, moe_gain, router.T, 4)
+        probs = gates_own.T
+    else:
+
+        def attn_term(first_row, row_count):
+            return jnp.dot(attn_mixed, gathered_out, preferred_element_type=jnp.float32)
+
+        x_one = residual_float + heads_to_rows(attn_term, tok_dev)
+        hidden_two = rms_apply(x_one, moe_gain)[0].astype(jnp.bfloat16)
+        logits = jnp.dot(hidden_two, router, preferred_element_type=jnp.float32)
+        probs = jax.nn.softmax(logits, axis=-1)
+        gates_own = probs.T
+    hidden_two, c_slots = lax.optimization_barrier((hidden_two, c_slots))
+    scale_two = lax.rsqrt(jnp.mean(x_one * x_one, axis=-1, keepdims=True) + norm_eps)
     if direct:
         rows_all, gates_all = gather_all([hidden_two, gates_own], 1)
         gates_all = gates_all.reshape(-1, experts, tok_dev)
@@ -918,7 +1227,11 @@
         x_one, scale_two, moe_gain, grad_hidden_two, inner_two, width
     )
     grad_x_one = grad_out + grad_norm_two
-    grad_attn_all = lax.all_gather(grad_x_one.astype(jnp.bfloat16), "tensor", axis=0, tiled=True)
+    grad_attn_low = grad_x_one.astype(jnp.bfloat16)
+    if direct:
+        grad_attn_all = line_gather(grad_attn_low, 5)
+    else:
+        grad_attn_all = lax.all_gather(grad_attn_low, "tensor", axis=0, tiled=True)
     grad_out_weight = lax.dot_general(
         attn_mixed, grad_attn_all, (((0,), (0,)), ((), ())), preferred_element_type=jnp.float32
     )

time: 1910 us -> 1620 us (0.85)
  waiting for transfers between devices: 1020 us -> 397 us
  Pallas kernels: 552 us -> 892 us
    pallas_call x0 -> x3, Pallas kernels: none -> 337 us  [the longest x1 134 us: mixed_out(): pl.pallas_call(functools.partial(mixed_out_kernel, line), out_shape=(jax....]
    all_gather x6 -> x0, waiting for transfers between devices: 245 us -> none  [the longest x1 106 us: body(): lax.all_gather(grad_x_one.astype(jnp.bfloat16), 'tensor', axis=0, tiled=T...]
    all_gather x1, waiting for transfers between devices: 197 us -> 0.02 us  [body(): cots_all = lax.all_gather(cotangent, everyone, axis=0, tiled=True)]
    reduce_scatter x1, waiting for transfers between devices: 104 us -> 9.08 us  [sum_over_dp(): return lax.psum_scatter(pieces, 'dp', scatter_dimension=0, tiled=False)]
    reduce_scatter x2 -> x1, waiting for transfers between devices: 155 us -> 77.4 us  [heads_to_rows(): lax.psum_scatter(term(jnp.int32(0), rows * lax.axis_size('tensor')).astyp...]
  transfers between devices with their start and end apart: 17 -> 10, of which waited for: 16 -> 8; matrix products, arithmetic and copies ran while one was open for 11% -> 13% of each run, Pallas kernels for 0% -> 21%
where the time goes in v3:
time: 1620 us; the launch traced here: 1610 us
  Pallas kernels  892 us (55%)
  waiting for transfers between devices  397 us (25%)
  matrix products  108 us (7%)
  other arithmetic  82 us (5%)
  blocking collectives  61.9 us (4%)
  local copies, waits for them, and re-layouts  39.6 us (2%)
    pallas_call x1, Pallas kernels, reduce_all(): pl.pallas_call(functools.partial(reduce_kernel, line), out_shape=(jax.Sha...  191 us
    pallas_call x1, Pallas kernels, gather_all(): pl.pallas_call(functools.partial(gather_kernel, line, count), out_shape=[...  157 us
    pallas_call x1, Pallas kernels, expert_pass(): pl.pallas_call(kernel, grid_spec=pltpu.PrefetchScalarGridSpec(num_scalar_...  141 us
    pallas_call x1, Pallas kernels, mixed_out(): pl.pallas_call(functools.partial(mixed_out_kernel, line), out_shape=(jax....  134 us
    pallas_call x1, Pallas kernels, start_exchange(): pl.pallas_call(functools.partial(start_kernel, line), out_shape=(jax.Shap...  103 us
    pallas_call x1, Pallas kernels, line_gather(): pl.pallas_call(functools.partial(line_gather_kernel, line), out_shape=jax...  100 us
    psum x1, waiting for transfers between devices, body(): lax.psum((grad_attn_gain_part, grad_moe_gain_part, grad_query_full, grad_...  90.7 us
    reduce_scatter x1, waiting for transfers between devices, heads_to_rows(): lax.psum_scatter(term(jnp.int32(0), rows * lax.axis_size('tensor')).astyp...  77.4 us
  transfers between devices with their start and end apart: 10, of which 8 were waited for; matrix products, arithmetic and copies ran while one was open for 13% of the time, Pallas kernels for 21%

profile of v3, /device:TPU:0, one launch (start us, length us, event | category | flops | bytes accessed | tf_op | source)
XLA Modules:
  0.0 1609.0 jit_solution(13070576048592693825)
XLA Ops:
  9.1 5.2 convert_reduce_fusion.1
  19.4 102.7 %start_exchange.1 = (bf16[1024,2048]{1,0:T(8,128)(2,1)}, bf16[2048,1536]{1,0:T(8,128)(2,1)}, bf16[512,2048]{1,0:T(8,128)(2,1)}) custom-call(bf16[256,2048]{1,0:T(8,128)(2,1)} %fusion.46.hidden_ref, bf16[256,512]{1,0:T(8,128)(2,1)} %wq_ref.1, bf16[256,512]{1,0:T(8,128)(2,1)} %wk_ref.1, bf16[256,512]{1,0:T(8,128)(2,1)} %wv_ref.1, bf16[512,256]{1,0:T(8,128)(2,1)} %wo_ref.1), custom_call_target="tpu_custom_call" | custom-call | bytes 157286400 | tf_op jit(solution)/shard_map/start_exchange/pallas_call | solution.py:828
  122.2 10.0 fusion.74
  132.2 2.6 copy-done.7
  135.2 11.6 all-reduce.2
  147.4 4.7 multiply_multiply_fusion
  152.1 1.9 reshape.554
  154.1 9.3 while.37
  163.4 2.9 reshape.553
  166.3 1.9 multiply_cosine_fusion
  175.4 26.9 %while.38 = (s32[]{:T(128)}, bf16[2,512,4,128]{3,2,1,0:T(4,128)(2,1)}, f32[2,4,512]{2,1,0:T(4,128)S(1)}, s32[3,1024]{1,0:T(4,128)S(1)}, s32[2]{0:T(128)S(1)}, /*...) while((s32[]{:T(128)}, ...), condition=%wide.region_11.12_spmd, body=%wide.region_8.0_spmd.sunk | while | flops 1104412160 | bytes 39952676 | solution.py:1168
  180.1 1.9 fusion.115
  182.0 2.4 fusion.116
  184.4 3.1 fusion.117
  193.5 1.8 fusion.115
  195.3 2.4 fusion.116
  197.7 3.1 fusion.117
  202.3 3.2 copy.155
  205.5 133.7 %mixed_out.1 = (f32[256,2048]{1,0:T(8,128)}, bf16[256,2048]{1,0:T(8,128)(2,1)}, f32[64,256]{1,0:T(8,128)}) custom-call(bf16[1024,512]{1,0:T(8,128)(2,1)} %bitcast.202, bf16[512,2048]{1,0:T(8,128)(2,1)} %get-tuple-element.178.w_ref, bf16[256,2048]{1,0:T(8,128)(2,1)} %residual_ref.1, f32[1,2048]{1,0:T(1,128)} %bitcast.217, bf16[64,2048]{1,0:T(8,128)(2,1)} %bitcast.205), custom_call_target="tpu_custom_call" | custom-call | bytes 157286400 | tf_op jit(solution)/shard_map/mixed_out/pallas_call | solution.py:970
  340.3 33.2 %pick.1.c_ref = bf16[8,1280,2048]{2,1,0:T(8,128)(2,1)} custom-call(s32[32,8,256]{2,1,0:T(8,128)S(1)} %dynamic-slice_convert_fusion.slots_ref, bf16[8192,2048]{1,0:T(8,128)(2,1)} %all-gather.5.cloned.1.call-done.rows_ref), custom_call_target="tpu_custom_call" | custom-call | flops 10737418240 | bytes 75497472 | tf_op jit(solution)/shard_map/pick/pallas_call | solution.py:90
  373.5 156.6 %gather_all.1 = (bf16[8192,2048]{1,0:T(8,128)(2,1)}, f32[2048,256]{1,0:T(8,128)}) custom-call(bf16[256,2048]{1,0:T(8,128)(2,1)} %get-tuple-element.181.refs_0_, f32[64,256]{1,0:T(8,128)} %get-tuple-element.182.refs_1_), custom_call_target="tpu_custom_call" | custom-call | tf_op jit(solution)/shard_map/gather_all/pallas_call | solution.py:405
  531.1 34.2 %dispatch.1 = (bf16[8,1280,2048]{2,1,0:T(8,128)(2,1)}, f32[8,1280,128]{2,1,0:T(8,128)}) custom-call(s32[32,8,256]{2,1,0:T(8,128)S(1)} %dynamic-slice_convert_fusion.slots_ref, f32[32,8,256]{2,1,0:T(8,128)S(1)} %constant_dynamic-slice_fusion.3.gates_ref, bf16[8192,2048]{1,0:T(8,128)(2,1)} %get-tuple-element.184.rows_ref), custom_call_target="tpu_custom_call" | custom-call | flops 10737418240 | bytes 75497472 | tf_op jit(solution)/shard_map/dispatch/pallas_call | solution.py:93
  565.3 140.7 %experts.1 = (bf16[32,8,48,2048]{3,2,1,0:T(8,128)(2,1)}, bf16[32,8,48,2176]{3,2,1,0:T(8,128)(2,1)}, f32[8,2048,256]{2,1,0:T(8,128)}, f32[8,2048,256]{2,1,0:T(8,128)}, f32[8,256,2048]{2,1,0:T(8,128)}) custom-call(s32[1]{0:T(128)} %bitcast.18.first_ref, bf16[8,1280,2048]{2,1,0:T(8,128)(2,1)} %get-tuple-element.185.x_ref, bf16[8,1280,2048]{2,1,0:T(8,128)(2,1)} %pick.1.c_ref, ...), custom_call_target="tpu_custom_call" | custom-call | flops 96636764160 | bytes 243269632 | tf_op jit(solution)/shard_map/experts/pallas_call | solution.py:174
  706.0 190.9 %reduce_all.1 = (f32[256,2176]{1,0:T(8,128)}, bf16[8192,2048]{1,0:T(8,128)(2,1)}) custom-call(s32[32,8,256]{2,1,0:T(8,128)} %copy-done, bf16[32,8,48,2176]{3,2,1,0:T(8,128)(2,1)} %get-tuple-element.188.grads_ref, bf16[32,8,48,2048]{3,2,1,0:T(8,128)(2,1)} %get-tuple-element.189.outs_ref), custom_call_target="tpu_custom_call" | custom-call | flops 26575110144 | bytes 103809024 | tf_op jit(solution)/shard_map/reduce_all/pallas_call | solution.py:642
  897.9 2.0 multiply_reduce_fusion.3
  900.9 3.9 multiply_reduce_fusion.1
  904.8 2.4 fusion.70
  907.1 100.2 %line_gather.1 = bf16[1024,2048]{1,0:T(8,128)(2,1)} custom-call(bf16[256,2048]{1,0:T(8,128)(2,1)} %get-tuple-element.396.own_ref), custom_call_target="tpu_custom_call" | custom-call | bytes 157286400 | tf_op jit(solution)/shard_map/line_gather/pallas_call | solution.py:860
  1007.4 6.5 convolution_convert_fusion.3
  1014.0 68.1 %while.39 = (s32[]{:T(128)}, f32[1024,4,128]{0,2,1:T(8,128)S(1)}, f32[1024,4,128]{0,2,1:T(8,128)}, f32[2,512,4,128]{3,1,0,2:T(8,128)}, s32[2]{0:T(128)S(1)}, /*i...) while((s32[]{:T(128)}, f32[1024,4,128]{0,2,1:T(8,128)S(1)}, ...), condition=%wide.region_20.21_spmd.clone, body=%wide.region_18.20_spmd.clone.sunk | while | flops 2723937792 | bytes 163676752 | solution.py:1286
  1016.7 5.6 fusion.127
  1024.3 7.8 multiply_reduce_fusion.7
  1032.2 3.7 multiply_convert_fusion.2
  1035.9 4.1 bitcast_add_fusion.4
  1040.0 5.5 bitcast_add_fusion.5
  1050.8 5.7 fusion.127
  1058.5 7.8 multiply_reduce_fusion.7
  1066.3 3.7 multiply_convert_fusion.2
  1070.1 3.9 bitcast_add_fusion.4
  1074.0 5.4 bitcast_add_fusion.5
  1082.1 1.9 copy.103
  1084.0 5.1 multiply_add_fusion.1
  1089.9 2.5 fusion.57
  1092.5 8.5 all-reduce.1
  1101.0 6.2 convolution_convert_fusion.2
  1107.9 6.5 fusion.59
  1115.8 2.9 pad_maximum_fusion
  1118.7 9.1 reduce-scatter.8.cloned.1.call-done
  1127.8 9.8 convolution_convert_fusion
  1137.6 2.9 fusion.71
  1142.6 11.2 convolution_convert_fusion.1
  1155.4 2.5 fusion.69
  1157.9 14.6 reduce-scatter.20.cloned.1.call-done
  1174.3 42.6 %reduce-scatter.14.cloned.1.call-done = bf16[256,512]{1,0:T(8,128)(2,1)} async-done(((bf16[2048,512]{1,0:T(8,128)(2,1)}), bf16[256,512]{1,0:T(8,128)(2,1)}) %reduce-scatter.14.cloned.1.call-update) | async-done | bytes 262160 | tf_op jit(solution)/shard_map/reduce_scatter | solution.py:1326
  1218.7 43.0 %reduce-scatter.16.cloned.1.call-done = bf16[256,512]{1,0:T(8,128)(2,1)} async-done(((bf16[2048,512]{1,0:T(8,128)(2,1)}), bf16[256,512]{1,0:T(8,128)(2,1)}) %reduce-scatter.16.cloned.1.call-update) | async-done | bytes 262160 | tf_op jit(solution)/shard_map/reduce_scatter | solution.py:1332
  1263.5 42.7 %reduce-scatter.18.cloned.1.call-done = bf16[256,512]{1,0:T(8,128)(2,1)} async-done(((bf16[2048,512]{1,0:T(8,128)(2,1)}), bf16[256,512]{1,0:T(8,128)(2,1)}) %reduce-scatter.18.cloned.1.call-update) | async-done | bytes 262160 | tf_op jit(solution)/shard_map/reduce_scatter | solution.py:1338
  1308.0 77.4 %reduce-scatter.12.cloned.1.call-done = bf16[256,2048]{1,0:T(8,128)(2,1)} async-done(((bf16[1024,2048]{1,0:T(8,128)(2,1)}), bf16[256,2048]{1,0:T(8,128)(2,1)}) %reduce-scatter.12.cloned.1.call-update) | async-done | bytes 1048592 | tf_op jit(solution)/shard_map/reduce_scatter | solution.py:1050
  1385.4 2.0 fusion.51
  1387.4 3.8 fusion.43
  1391.2 73.9 %reduce-scatter.10.cloned.1.call-done = bf16[256,2048]{1,0:T(8,128)(2,1)} async-done(((bf16[1024,2048]{1,0:T(8,128)(2,1)}), bf16[256,2048]{1,0:T(8,128)(2,1)}) %reduce-scatter.10.cloned.1.call-update) | async-done | bytes 1048592 | tf_op jit(solution)/shard_map/reduce_scatter | solution.py:1065
  1465.0 2.5 add_convert_fusion
  1467.5 41.8 %all-reduce = (f32[2048]{0:T(1024)}, f32[2048]{0:T(1024)}, f32[2048]{0:T(1024)}, f32[2048]{0:T(1024)}) all-reduce(f32[2048]{0:T(1024)S(1)} %get-tuple-element.334, f32[2048]{0:T(1024)S(1)} %dynamic_update_slice.22, f32[2048]{0:T(1024)S(1)} %dynamic_update_slice.23, ...), channel_id=1, replica_groups=mesh['dp'=8,'tensor'=4] {'dp','tensor'}, use_global_device_ids=true, to_apply=%region_29.30 | all-reduce | flops 8192 | bytes 65536 | tf_op jit(solution)/shard_map/psum | solution.py:1355
  1509.3 90.7 %all-reduce.5.cloned.1.call-done = f32[2048,64]{0,1:T(8,128)} async-done(((f32[2048,64]{0,1:T(8,128)}), f32[2048,64]{0,1:T(8,128)}) %all-reduce.5.cloned.1.call-update) | async-done | bytes 524304 | tf_op jit(solution)/shard_map/psum | solution.py:1355
  1600.1 1.9 copy.192
  (279 shorter events, 56.6 us)
Async XLA Ops:
  7.2 10.1 copy-start.11
  7.2 11.0 copy-start.47
  7.2 332.1 %all-gather.3.cloned.1.call-start = ((), (), s32[]{:S(2)}) async-start(), calls=%async_computation.7 | async-start | bytes 1081344 | tf_op jit(solution)/shard_map/all_gather | solution.py:1106
  14.9 325.4 %all-gather.5.cloned.1.call-start = ((), (), s32[]{:S(2)}) async-start(), calls=%async_computation.8 | async-start | bytes 34603008 | tf_op jit(solution)/shard_map/all_gather | solution.py:1109
  15.7 1112.1 %reduce-scatter.8.cloned.1.call-start = ((), (), s32[]{:S(2)}) async-start(), calls=%async_computation.9 | async-start | bytes 37748736 | tf_op jit(solution)/shard_map/reduce_scatter | solution.py:1061
  16.5 130.9 %copy-start.55 = (f32[512]{0:T(512)}, f32[512]{0:T(512)S(1)}, u32[]{:S(2)}) copy-start(f32[512]{0:T(512)S(1)} %dynamic_slice.48) | copy-start | bytes 6148
  17.3 130.1 %copy-start.57 = (f32[512]{0:T(512)}, f32[512]{0:T(512)S(1)}, u32[]{:S(2)}) copy-start(f32[512]{0:T(512)S(1)} %dynamic_slice.47) | copy-start | bytes 6148
  18.2 104.0 %copy-start.59 = (f32[256]{0:T(256)}, f32[256]{0:T(256)S(1)}, u32[]{:S(2)}) copy-start(f32[256]{0:T(256)S(1)} %get-tuple-element.441) | copy-start | bytes 3076
  147.4 4.7 copy-start.50
  147.4 4.7 copy-start.52
  202.3 136.9 %copy-start.2 = (bf16[1024,4,128]{2,0,1:T(8,128)(2,1)}, bf16[1024,4,128]{2,0,1:T(8,128)(2,1)S(1)}, u32[]{:S(2)}) copy-start(bf16[1024,4,128]{2,0,1:T(8,128)(2,1)S(1)} %get-tuple-element.779) | copy-start | bytes 3145732
  202.3 136.9 %copy-start.6 = (bf16[1024,4,128]{2,0,1:T(8,128)(2,1)}, bf16[1024,4,128]{2,0,1:T(8,128)(2,1)S(1)}, u32[]{:S(2)}) copy-start(bf16[1024,4,128]{2,0,1:T(8,128)(2,1)S(1)} %get-tuple-element.780) | copy-start | bytes 3145732
  202.3 136.9 %copy-start.8 = (bf16[1024,4,128]{2,0,1:T(8,128)(2,1)}, bf16[1024,4,128]{2,0,1:T(8,128)(2,1)S(1)}, u32[]{:S(2)}) copy-start(bf16[1024,4,128]{2,0,1:T(8,128)(2,1)S(1)} %get-tuple-element.781) | copy-start | bytes 3145732
  202.3 136.9 %copy-start.35 = (s32[3,1024]{1,0:T(4,128)}, s32[3,1024]{1,0:T(4,128)S(1)}, u32[]{:S(2)}) copy-start(s32[3,1024]{1,0:T(4,128)S(1)} %get-tuple-element.804) | copy-start | bytes 36868
  202.3 136.9 %copy-start.42 = (s32[1024]{0:T(1024)}, s32[1024]{0:T(1024)S(1)}, u32[]{:S(2)}) copy-start(s32[1024]{0:T(1024)S(1)} %get-tuple-element.807) | copy-start | bytes 12292
  202.3 136.9 %copy-start.45 = (f32[2,4,512]{2,1,0:T(4,128)}, f32[2,4,512]{2,1,0:T(4,128)S(1)}, u32[]{:S(2)}) copy-start(f32[2,4,512]{2,1,0:T(4,128)S(1)} %get-tuple-element.713) | copy-start | bytes 49156
  202.3 136.9 %copy-start.66 = (s32[2]{0:T(128)}, s32[2]{0:T(128)S(1)}, u32[]{:S(2)}) copy-start(s32[2]{0:T(128)S(1)} %get-tuple-element.817) | copy-start | bytes 28
  340.2 190.8 %copy-start = (s32[32,8,256]{2,1,0:T(8,128)}, s32[32,8,256]{2,1,0:T(8,128)S(1)}, u32[]{:S(2)}) copy-start(s32[32,8,256]{2,1,0:T(8,128)S(1)} %dynamic-slice_convert_fusion.slots_ref) | copy-start | bytes 786436
  897.0 3.9 copy-start.37
  897.0 3.9 copy-start.49
  897.0 275.5 %reduce-scatter.20.cloned.1.call-start = ((), (), s32[]{:S(2)}) async-start(), calls=%async_computation.15 | async-start | bytes 2359296 | tf_op jit(solution)/shard_map/reduce_scatter | solution.py:1344
  897.9 6.9 copy-start.29
  900.9 3.9 copy-start.63
  1007.4 6.6 copy-start.3
  1007.4 6.6 copy-start.36
  1007.4 6.6 copy-start.43
  1007.4 6.6 copy-start.46
  1007.4 6.6 copy-start.67
  1024.3 7.9 copy-start.4
  1024.3 7.8 slice-start
  1024.3 7.8 slice-start.1
  1035.9 4.1 copy-start.5
  1035.9 4.1 copy-start.19
  1035.9 4.1 copy-start.31
  1040.0 5.5 copy-start.1
  1040.0 5.7 copy-start.17
  1058.5 7.8 copy-start.4
  1058.5 7.8 slice-start
  1058.5 7.8 slice-start.1
  1070.0 3.9 copy-start.5
  1070.0 3.9 copy-start.19
  1070.0 3.9 copy-start.31
  1074.0 5.5 copy-start.1
  1074.0 5.5 copy-start.17
  1084.0 5.2 slice-start.2
  1084.0 5.9 slice-start.3
  1084.0 5.9 copy-start.51
  1084.0 5.9 copy-start.53
  1084.0 5.8 copy-start.56
  1084.0 5.8 copy-start.58
  1089.9 11.1 copy-start.40
  1107.2 109.7 %reduce-scatter.14.cloned.1.call-start = ((), (), s32[]{:S(2)}) async-start(), calls=%async_computation.12 | async-start | bytes 2359296 | tf_op jit(solution)/shard_map/reduce_scatter | solution.py:1326
  1107.9 6.5 copy-start.33
  1140.5 121.2 %reduce-scatter.16.cloned.1.call-start = ((), (), s32[]{:S(2)}) async-start(), calls=%async_computation.13 | async-start | bytes 2359296 | tf_op jit(solution)/shard_map/reduce_scatter | solution.py:1332
  1141.0 165.2 %reduce-scatter.18.cloned.1.call-start = ((), (), s32[]{:S(2)}) async-start(), calls=%async_computation.14 | async-start | bytes 2359296 | tf_op jit(solution)/shard_map/reduce_scatter | solution.py:1338
  1141.8 243.6 %reduce-scatter.12.cloned.1.call-start = ((), (), s32[]{:S(2)}) async-start(), calls=%async_computation.11 | async-start | bytes 5242880 | tf_op jit(solution)/shard_map/reduce_scatter | solution.py:1050
  1153.8 311.2 %reduce-scatter.10.cloned.1.call-start = ((), (), s32[]{:S(2)}) async-start(), calls=%async_computation.10 | async-start | bytes 5242880 | tf_op jit(solution)/shard_map/reduce_scatter | solution.py:1065
  1154.5 445.5 %all-reduce.5.cloned.1.call-start = ((), (), s32[]{:S(2)}) async-start(), calls=%async_computation.16 | async-start | bytes 1048576 | tf_op jit(solution)/shard_map/psum | solution.py:1355
  1157.9 227.5 %copy-start.12 = (bf16[256,2048]{1,0:T(8,128)(2,1)S(1)}, bf16[256,2048]{1,0:T(8,128)(2,1)}, u32[]{:S(2)}) copy-start(bf16[256,2048]{1,0:T(8,128)(2,1)} %residual_ref.1) | copy-start | bytes 3145732
  1157.9 227.5 %copy-start.48 = (f32[2048]{0:T(1024)S(1)}, f32[2048]{0:T(1024)}, u32[]{:S(2)}) copy-start(f32[2048]{0:T(1024)} %param.25) | copy-start | bytes 24580
  1157.9 227.5 %copy-start.60 = (f32[256]{0:T(256)S(1)}, f32[256]{0:T(256)}, u32[]{:S(2)}) copy-start(f32[256]{0:T(256)} %copy-done.59) | copy-start | bytes 3076
  1174.3 213.1 %copy-start.65 = (f32[256]{0:T(256)S(1)}, f32[256]{0:T(256)}, u32[]{:S(2)}) copy-start(f32[256]{0:T(256)} %get-tuple-element.440) | copy-start | bytes 3076
  1387.4 77.7 %copy-start.10 = (f32[256,2048]{1,0:T(8,128)S(1)}, f32[256,2048]{1,0:T(8,128)}, u32[]{:S(2)}) copy-start(f32[256,2048]{1,0:T(8,128)} %get-tuple-element.179) | copy-start | bytes 6291460
  1391.2 76.3 %copy-start.54 = (f32[2048]{0:T(1024)S(1)}, f32[2048]{0:T(1024)}, u32[]{:S(2)}) copy-start(f32[2048]{0:T(1024)} %get-tuple-element.332) | copy-start | bytes 24580
  (30 other events, 61.8 us)
Sparse Core Ops, SparseCore 0:
  15.0 57.8 all-gather.2
  75.9 253.8 all-gather.4
  897.1 230.6 reduce-scatter.7
  1131.3 41.1 reduce-scatter.19
  1175.6 41.2 reduce-scatter.13
  1220.4 41.2 reduce-scatter.15
  1265.0 41.2 reduce-scatter.17
  1308.6 76.7 reduce-scatter.11
  1387.7 77.2 reduce-scatter.9
  1471.6 128.4 all-reduce.4

commit v4 on v3

--- a/solution.py
+++ b/solution.py
@@ -841,34 +841,6 @@
     )(hidden, w_query, w_key, w_value, w_out)
 
 
-def line_gather_kernel(line, own_ref, out_ref, local_sem, send_sem, recv_sem):
-    greet(line)
-    gather = LineGather(own_ref, out_ref, send_sem, recv_sem, line)
-    local = pltpu.make_async_copy(own_ref, gather.view(gather.spot[3]), local_sem)
-    gather.begin()
-    local.start()
-    for step in range(line - 1):
-        gather.advance(step)
-    gather.finish()
-    local.wait()
-
-
-def line_gather(own, collective_id):
-    line = 4
-    any_ref = pl.BlockSpec(memory_space=pl.ANY)
-    dma = pltpu.SemaphoreType.DMA
-    return pl.pallas_call(
-        functools.partial(line_gather_kernel, line),
-        out_shape=jax.ShapeDtypeStruct((line * own.shape[0], own.shape[1]), own.dtype),
-        in_specs=[any_ref],
-        out_specs=any_ref,
-        scratch_shapes=[dma(()), dma((2, line)), dma((2, line))],
-        compiler_params=pltpu.CompilerParams(collective_id=collective_id, has_side_effects=True),
-        cost_estimate=pl.CostEstimate(flops=0, bytes_accessed=150 << 20, transcendentals=0),
-        name="line_gather",
-    )(own)
-
-
 class LineReduce:
     def __init__(self, part, up, down, send_sem, recv_sem, line):
         self.part, self.up, self.down = part, up, down
@@ -983,6 +955,295 @@
         cost_estimate=pl.CostEstimate(flops=0, bytes_accessed=150 << 20, transcendentals=0),
         name="mixed_out",
     )(mixed, w_out, residual, gain.reshape(1, width), router_turned)
+
+
+class Butterfly:
+    def __init__(self, data, total, from_core, from_x, from_y, from_z, sums, send_sem, recv_sem):
+        self.data, self.total, self.sums = data, total, sums
+        self.boxes = {"core": from_core, "x": from_x, "y": from_y}
+        self.from_z, self.send_sem, self.recv_sem = from_z, send_sem, recv_sem
+        y, x, core, z = self.spot = place()
+        self.width = data.shape[1]
+        self.near = {"core": (y, x, 1 - core, z), "x": (y, 1 - x, core, z), "y": (1 - y, x, core, z)}
+        half, quarter, eighth = self.width // 2, self.width // 4, self.width // 8
+        first = core * half
+        self.kept = {"core": (first, half), "x": (first + x * quarter, quarter)}
+        self.kept["y"] = (first + x * quarter + y * eighth, eighth)
+        self.away = {
+            "core": ((1 - core) * half, half),
+            "x": (first + (1 - x) * quarter, quarter),
+            "y": (first + x * quarter + (1 - y) * eighth, eighth),
+        }
+
+    def part(self, span):
+        return pl.ds(pl.multiple_of(span[0], span[1]), span[1])
+
+    def fold_copy(self, axis):
+        lane = ("core", "x", "y").index(axis)
+        return remote(
+            self.data.at[:, self.part(self.away[axis])], self.boxes[axis], self.send_sem.at[lane],
+            self.recv_sem.at[lane], self.near[axis],
+        )
+
+    def fold(self, axis):
+        copy = self.fold_copy(axis)
+        copy.start()
+        copy.wait()
+        self.data[:, self.part(self.kept[axis])] += self.boxes[axis][...]
+
+    def line_step(self, step):
+        y, x, core, z = self.spot
+        other = (z + 1 - 2 * (z % 2)) if step == 0 else (z + 2) % 4
+        piece = self.part(self.kept["y"])
+        source = self.data.at[:, piece] if step == 0 else self.sums
+        copy = remote(
+            source, self.from_z.at[step], self.send_sem.at[3 + step], self.recv_sem.at[3 + step], (y, x, core, other)
+        )
+        copy.start()
+        copy.wait()
+        if step == 0:
+            self.sums[...] = self.data[:, piece] + self.from_z[0]
+        else:
+            self.total[:, piece] = self.sums[...] + self.from_z[1]
+
+    def unfold(self, axis):
+        lane = 5 + ("core", "x", "y").index(axis)
+        mine = self.total.at[:, self.part(self.kept[axis])]
+        copy = remote(mine, mine, self.send_sem.at[lane], self.recv_sem.at[lane], self.near[axis])
+        copy.start()
+        copy.wait_send()
+        landed(self.total.at[:, self.part(self.away[axis])], self.recv_sem.at[lane])
+
+    def scratch(rows, width):
+        low = jnp.float32
+        return [
+            pltpu.VMEM((rows, width // 2), low),
+            pltpu.VMEM((rows, width // 4), low),
+            pltpu.VMEM((rows, width // 8), low),
+            pltpu.VMEM((2, rows, width // 8), low),
+            pltpu.VMEM((rows, width // 8), low),
+            pltpu.SemaphoreType.DMA((8,)),
+            pltpu.SemaphoreType.DMA((8,)),
+        ]
+
+
+def greet_far(line):
+    y, x, core, z = place()
+    barrier = pltpu.get_barrier_semaphore()
+    for near in ((y, x, 1 - core, z), (y, 1 - x, core, z), (1 - y, x, core, z)):
+        pl.semaphore_signal(barrier, inc=1, device_id=peer(*near), device_id_type=MESH)
+    for step in range(1, line):
+        pl.semaphore_signal(barrier, inc=1, device_id=peer(y, x, core, (z + step) % line), device_id_type=MESH)
+    pl.semaphore_wait(barrier, 3 + line - 1)
+
+
+def back_gather_kernel(line, own_ref, sums_ref, out_ref, total_ref, data, local_sem, send_sem, recv_sem, *fly):
+    greet_far(line)
+    gather = LineGather(own_ref, out_ref, send_sem, recv_sem, line)
+    local = pltpu.make_async_copy(own_ref, gather.view(gather.spot[3]), local_sem)
+    gather.begin()
+    local.start()
+    data[...] = sums_ref[...]
+    butterfly = Butterfly(data, total_ref, *fly)
+    for axis in ("core", "x", "y"):
+        butterfly.fold(axis)
+    gather.advance(0)
+    butterfly.line_step(0)
+    gather.advance(1)
+    butterfly.line_step(1)
+    for axis in ("y", "x", "core"):
+        butterfly.unfold(axis)
+    gather.advance(2)
+    gather.finish()
+    local.wait()
+
+
+def back_gather(own, sums, collective_id):
+    line = 4
+    any_ref = pl.BlockSpec(memory_space=pl.ANY)
+    vmem = pl.BlockSpec(memory_space=pltpu.VMEM)
+    dma = pltpu.SemaphoreType.DMA
+    return pl.pallas_call(
+        functools.partial(back_gather_kernel, line),
+        out_shape=(
+            jax.ShapeDtypeStruct((line * own.shape[0], own.shape[1]), own.dtype),
+            jax.ShapeDtypeStruct(sums.shape, jnp.float32),
+        ),
+        in_specs=[any_ref, vmem],
+        out_specs=[any_ref, vmem],
+        scratch_shapes=[
+            pltpu.VMEM(sums.shape, jnp.float32), dma(()), dma((2, line)), dma((2, line)),
+            *Butterfly.scratch(*sums.shape),
+        ],
+        compiler_params=pltpu.CompilerParams(collective_id=collective_id, has_side_effects=True),
+        cost_estimate=pl.CostEstimate(flops=0, bytes_accessed=150 << 20, transcendentals=0),
+        name="back_gather",
+    )(own, sums)
+
+
+def last_kernel(line, joined_ref, weight_ref, hidden_ref, mixed_ref, attn_ref, residual_ref, gain_ref, x_grad_ref, gains_ref,
+                input_ref, wq_ref, wk_ref, wv_ref, wo_ref, total_ref,
+                part, up, down, stage, near, far_x, far_y, from_x, from_y, data,
+                line_send, line_recv, stage_sem, near_sem, send_sem, recv_sem, *fly):
+    y, x, core, z = place()
+    rows, width = input_ref.shape
+    columns = joined_ref.shape[1]
+    half = rows // 2
+    low = jnp.bfloat16
+    greet_far(line)
+    reduce = LineReduce(part, up, down, line_send, line_recv, line)
+
+    def term(i, carry):
+        goal = reduce.order(i)
+        first = pl.multiple_of(goal * rows, rows)
+        for column in range(0, width, 512):
+            piece = slice(column, column + 512)
+            value = across(joined_ref[pl.ds(first, rows), :], weight_ref[piece, :])
+
+            @pl.when(goal == z)
+            def _():
+                input_ref[:, piece] = value
+
+            part[goal, :, piece] = value.astype(low)
+        reduce.lead(goal)
+        return carry
+
+    lax.fori_loop(0, line, term, 0)
+    near_x, near_y, sibling = (y, 1 - x, core, z), (1 - y, x, core, z), (y, x, 1 - core, z)
+
+    def terms(j, own, store):
+        dy, dx = (j + 1) % 2, 1 - j // 2
+        group = (y + dy) % 2 * 4 + (x + dx) % 2 * 2 + (core if own else 1 - core)
+        span = pl.ds(pl.multiple_of(group * rows, rows), rows)
+        turned_rows = hidden_ref[:, span]
+        for column in range(0, columns, 512):
+            piece = slice(column, column + 512)
+            store(piece, turned(turned_rows, joined_ref[:, piece]))
+        value = turned(mixed_ref[...], attn_ref[:, span])
+        store(slice(columns, columns + rows), value[:rows])
+        store(slice(columns + rows, columns + 2 * rows), value[rows:])
+
+    def to_sibling(j):
+        return remote(stage.at[j], near.at[j], stage_sem.at[j], near_sem.at[j], sibling)
+
+    def away(j, carry):
+        def store(piece, value):
+            stage[j, :, piece] = value.astype(low)
+
+        terms(j, False, store)
+        to_sibling(j).start()
+        return carry
+
+    def own(j, carry):
+        to_sibling(j).wait_recv()
+
+        def store(piece, value):
+            near[j, :, piece] = (value + near[j, :, piece].astype(jnp.float32)).astype(low)
+
+        terms(j, True, store)
+        return carry
+
+    lax.fori_loop(0, 4, away, 0)
+    lax.fori_loop(0, 4, own, 0)
+
+    def line_rows(h):
+        return pl.ds(h * half, half)
+
+    def cross(kind):
+        column, h, target, where = {
+            "far_x": (0, 0, far_x, near_x),
+            "far_y": (0, 1, far_y, near_y),
+            "x0": (1, 0, from_x.at[line_rows(0)], near_x),
+            "x1": (1, 1, from_x.at[line_rows(1)], near_x),
+            "y0": (2, 0, from_y.at[line_rows(0)], near_y),
+            "y1": (2, 1, from_y.at[line_rows(1)], near_y),
+        }[kind]
+        lane = kinds.index(kind)
+        return remote(near.at[column, line_rows(h)], target, send_sem.at[lane], recv_sem.at[lane], where)
+
+    kinds = ("far_x", "far_y", "x0", "y1", "x1", "y0")
+    for kind in kinds[:4]:
+        cross(kind).start()
+
+    def add(column, h, source):
+        near[column, line_rows(h), :] = (
+            near[column, line_rows(h), :].astype(jnp.float32) + source[...].astype(jnp.float32)
+        ).astype(low)
+
+    reduce.advance(1, input_ref)
+    cross("far_y").wait_recv()
+    add(1, 1, far_y)
+    cross("x1").start()
+    cross("far_x").wait_recv()
+    add(2, 0, far_x)
+    cross("y0").start()
+    reduce.advance(2, input_ref)
+    for kind in kinds[2:]:
+        cross(kind).wait_recv()
+    for n, ref in enumerate((wq_ref, wk_ref, wv_ref, wo_ref, wo_ref)):
+        count = columns // 3 if n < 3 else rows
+        first = n * (columns // 3) if n < 3 else columns + (n - 3) * rows
+        piece = slice(first, first + count)
+        total = sum(r[:, piece].astype(jnp.float32) for r in (near.at[3], from_x, from_y))
+        if n < 3:
+            ref[...] = total
+        else:
+            ref[(n - 3) * rows : (n - 2) * rows, :] = total
+    reduce.advance(3, input_ref)
+    grad = input_ref[...]
+    values = residual_ref[...].astype(jnp.float32)
+    scale = lax.rsqrt(jnp.mean(values * values, axis=-1, keepdims=True) + norm_eps)
+    gained = grad * gain_ref[...]
+    inner = jnp.sum(gained * values, axis=-1, keepdims=True)
+    data[...] = gains_ref[...]
+    data[2:3, :] = jnp.sum(grad * values * scale, axis=0, keepdims=True)
+    input_ref[...] = x_grad_ref[...] + scale * gained - values * (scale * scale * scale * inner / width)
+    butterfly = Butterfly(data, total_ref, *fly)
+    for axis in ("core", "x", "y"):
+        butterfly.fold(axis)
+    butterfly.line_step(0)
+    butterfly.line_step(1)
+    for axis in ("y", "x", "core"):
+        butterfly.unfold(axis)
+    reduce.finish()
+    for j in range(4):
+        to_sibling(j).wait_send()
+    for kind in kinds:
+        cross(kind).wait_send()
+
+
+def last_exchange(joined, weight, hidden, mixed, attn, residual, gain, x_grad, gains, collective_id):
+    line = 4
+    rows, width = residual.shape
+    columns = joined.shape[1] // 3
+    low, wide = jnp.bfloat16, jnp.float32
+    vmem = pl.BlockSpec(memory_space=pltpu.VMEM)
+    dma = pltpu.SemaphoreType.DMA
+    block = pltpu.VMEM((line, rows, width), low)
+    one = pltpu.VMEM((rows, width), low)
+    part = pltpu.VMEM((rows // 2, width), low)
+    square = jax.ShapeDtypeStruct((rows, columns), wide)
+    return pl.pallas_call(
+        functools.partial(last_kernel, line),
+        out_shape=(
+            jax.ShapeDtypeStruct((rows, width), wide), square, square, square,
+            jax.ShapeDtypeStruct((2 * rows, rows), wide),
+            jax.ShapeDtypeStruct(gains.shape, wide),
+        ),
+        in_specs=[vmem] * 9,
+        out_specs=[vmem] * 6,
+        scratch_shapes=[
+            block, block, block, pltpu.VMEM((4, rows, width), low), pltpu.VMEM((4, rows, width), low),
+            part, part, one, one, pltpu.VMEM(gains.shape, wide),
+            dma((2, line)), dma((2, line)), dma((4,)), dma((4,)), dma((6,)), dma((6,)),
+            *Butterfly.scratch(*gains.shape),
+        ],
+        compiler_params=pltpu.CompilerParams(
+            collective_id=collective_id, has_side_effects=True, vmem_limit_bytes=62 << 20
+        ),
+        cost_estimate=pl.CostEstimate(flops=0, bytes_accessed=250 << 20, transcendentals=0),
+        name="last_exchange",
+    )(joined, weight, hidden, mixed, attn, residual, gain.reshape(1, width), x_grad, gains)
 
 
 def visible_block(row_paths, key_paths, key_valid, row_first):
@@ -1217,8 +1478,8 @@
         grad_logits, router_float, (((1,), (1,)), ((), ())), precision=lax.Precision.HIGHEST
     )
     grad_router_part = lax.dot_general(
+        grad_logits,
         hidden_two.astype(jnp.float32),
-        grad_logits,
         (((0,), (0,)), ((), ())),
         precision=lax.Precision.HIGHEST,
     )
@@ -1228,13 +1489,14 @@
     )
     grad_x_one = grad_out + grad_norm_two
     grad_attn_low = grad_x_one.astype(jnp.bfloat16)
+    early_sums = jnp.concatenate(
+        (grad_router_part, grad_moe_gain_part[None], jnp.zeros((7, width), jnp.float32)), axis=0
+    )
     if direct:
-        grad_attn_all = line_gather(grad_attn_low, 5)
+        grad_attn_all, early_sums = back_gather(grad_attn_low, early_sums, 5)
     else:
         grad_attn_all = lax.all_gather(grad_attn_low, "tensor", axis=0, tiled=True)
-    grad_out_weight = lax.dot_general(
-        attn_mixed, grad_attn_all, (((0,), (0,)), ((), ())), preferred_element_type=jnp.float32
-    )
+        early_sums = lax.psum(early_sums, everyone)
     grad_mixed = (
         lax.dot_general(
             grad_attn_all,
@@ -1307,44 +1569,6 @@
     ).astype(jnp.bfloat16)
     out_part, grad_joined = lax.optimization_barrier((out_part, grad_joined))
     block_out = (x_one + sum_over_tensor(out_part).astype(jnp.float32)).astype(jnp.bfloat16)
-    grad_joined_weight = lax.dot_general(
-        hidden_all, grad_joined, (((0,), (0,)), ((), ())), preferred_element_type=jnp.float32
-    )
-
-    def back_term(first_row, row_count):
-        return lax.dot_general(
-            grad_joined, joined_weight, (((1,), (1,)), ((), ())), preferred_element_type=jnp.float32
-        )
-
-    grad_hidden = heads_to_rows(back_term, tok_dev)
-    inner_one = jnp.sum(grad_hidden * attn_gain * residual_float, axis=-1, keepdims=True)
-    grad_norm_one, grad_attn_gain_part = rms_grad(
-        residual_float, scale_one, attn_gain, grad_hidden, inner_one, width
-    )
-    grad_input = grad_x_one + grad_norm_one
-    grad_w_query, grad_w_key, grad_w_value, grad_w_out = (
-        lax.psum_scatter(
-            grad_joined_weight[:, :head_cols].astype(jnp.bfloat16),
-            "dp",
-            scatter_dimension=0,
-            tiled=True,
-        ).astype(jnp.float32),
-        lax.psum_scatter(
-            grad_joined_weight[:, head_cols : 2 * head_cols].astype(jnp.bfloat16),
-            "dp",
-            scatter_dimension=0,
-            tiled=True,
-        ).astype(jnp.float32),
-        lax.psum_scatter(
-            grad_joined_weight[:, 2 * head_cols :].astype(jnp.bfloat16),
-            "dp",
-            scatter_dimension=0,
-            tiled=True,
-        ).astype(jnp.float32),
-        lax.psum_scatter(
-            grad_out_weight.astype(jnp.bfloat16), "dp", scatter_dimension=1, tiled=True
-        ).astype(jnp.float32),
-    )
     zero_width = jnp.zeros((full_width,), jnp.float32)
     grad_query_full = lax.dynamic_update_slice_in_dim(
         zero_width, grad_query_gain_dev, tensor_rank * head_cols, 0
@@ -1352,22 +1576,66 @@
     grad_key_full = lax.dynamic_update_slice_in_dim(
         zero_width, grad_key_gain_dev, tensor_rank * head_cols, 0
     )
-    summed = lax.psum(
-        (grad_attn_gain_part, grad_moe_gain_part, grad_query_full, grad_key_full, grad_router_part),
-        ("dp", "tensor"),
-    )
+    if direct:
+        gains = jnp.concatenate(
+            (grad_query_full[None], grad_key_full[None], jnp.zeros((6, width), jnp.float32)), axis=0
+        )
+        grad_input, grad_w_query, grad_w_key, grad_w_value, grad_w_out, gains = last_exchange(
+            grad_joined,
+            joined_weight,
+            hidden_all,
+            attn_mixed,
+            grad_attn_all,
+            residual,
+            attn_gain,
+            grad_x_one,
+            gains,
+            6,
+        )
+    else:
+        grad_joined_weight = lax.dot_general(
+            hidden_all, grad_joined, (((0,), (0,)), ((), ())), preferred_element_type=jnp.float32
+        ).astype(jnp.bfloat16)
+        grad_out_weight = lax.dot_general(
+            attn_mixed, grad_attn_all, (((0,), (0,)), ((), ())), preferred_element_type=jnp.float32
+        ).astype(jnp.bfloat16)
+
+        def back_term(first_row, row_count):
+            return lax.dot_general(
+                grad_joined, joined_weight, (((1,), (1,)), ((), ())), preferred_element_type=jnp.float32
+            )
+
+        grad_hidden = heads_to_rows(back_term, tok_dev)
+        inner_one = jnp.sum(grad_hidden * attn_gain * residual_float, axis=-1, keepdims=True)
+        grad_norm_one, grad_attn_gain_part = rms_grad(
+            residual_float, scale_one, attn_gain, grad_hidden, inner_one, width
+        )
+        grad_input = grad_x_one + grad_norm_one
+        grad_w_query, grad_w_key, grad_w_value = (
+            lax.psum_scatter(
+                grad_joined_weight[:, n * head_cols : (n + 1) * head_cols],
+                "dp",
+                scatter_dimension=0,
+                tiled=True,
+            ).astype(jnp.float32)
+            for n in range(3)
+        )
+        grad_w_out = lax.psum_scatter(
+            grad_out_weight, "dp", scatter_dimension=1, tiled=True
+        ).astype(jnp.float32)
+        gains = lax.psum(jnp.stack((grad_query_full, grad_key_full, grad_attn_gain_part)), everyone)
     return (
         block_out,
         grad_input,
-        summed[0],
+        gains[2],
         grad_w_query,
         grad_w_key,
         grad_w_value,
-        summed[2],
-        summed[3],
+        gains[0],
+        gains[1],
         grad_w_out,
-        summed[1],
-        summed[4],
+        early_sums[experts],
+        early_sums[:experts].T,
         grad_w_gate,
         grad_w_up,
         grad_w_down,

time: 1620 us -> 1320 us (0.81)
  waiting for transfers between devices: 397 us -> 12.9 us
  Pallas kernels: 892 us -> 1060 us
  blocking collectives: 61.9 us -> 19.5 us
  matrix products: 108 us -> 80.3 us
    reduce_scatter x5 -> x0, waiting for transfers between devices: 220 us -> none  [the longest x1 77.4 us: heads_to_rows(): lax.psum_scatter(term(jnp.int32(0), rows * lax.axis_size('tensor')).astyp...]
    pallas_call x1 -> x2, Pallas kernels: 100 us -> 269 us  [the longest x1 164 us: last_exchange(): pl.pallas_call(functools.partial(last_kernel, line), out_shape=(jax.Shape...]
    psum x1 -> x0, waiting for transfers between devices: 90.7 us -> none  [body(): lax.psum((grad_attn_gain_part, grad_moe_gain_part, grad_query_full, grad_...]
    reduce_scatter x1, waiting for transfers between devices: 73.9 us -> 0.01 us  [sum_over_tensor(): return lax.psum_scatter(part, 'tensor', scatter_dimension=0, tiled=True)]
    psum x1 -> x0, blocking collectives: 41.8 us -> none  [body(): lax.psum((grad_attn_gain_part, grad_moe_gain_part, grad_query_full, grad_...]
    dot_general x4 -> x1, matrix products: 29.6 us -> 1.68 us  [body(): lax.dot_general(grad_logits, hidden_two.astype(jnp.float32), (((0,), (0,)...]
  transfers between devices with their start and end apart: 10 -> 4, of which waited for: 8 -> 1; matrix products, arithmetic and copies ran while one was open for 13% -> 13% of each run, Pallas kernels for 21% -> 39%
where the time goes in v4:
time: 1320 us; the launch traced here: 1310 us
  Pallas kernels  1060 us (80%)
  matrix products  80.3 us (6%)
  other arithmetic  70.5 us (5%)
  local copies, waits for them, and re-layouts  41.4 us (3%)
  blocking collectives  19.5 us (1%)
  between operations  15.1 us (1%)
    pallas_call x1, Pallas kernels, reduce_all(): pl.pallas_call(functools.partial(reduce_kernel, line), out_shape=(jax.Sha...  191 us
    pallas_call x1, Pallas kernels, last_exchange(): pl.pallas_call(functools.partial(last_kernel, line), out_shape=(jax.Shape...  164 us
    pallas_call x1, Pallas kernels, gather_all(): pl.pallas_call(functools.partial(gather_kernel, line, count), out_shape=[...  157 us
    pallas_call x1, Pallas kernels, expert_pass(): pl.pallas_call(kernel, grid_spec=pltpu.PrefetchScalarGridSpec(num_scalar_...  141 us
    pallas_call x1, Pallas kernels, mixed_out(): pl.pallas_call(functools.partial(mixed_out_kernel, line), out_shape=(jax....  134 us
    pallas_call x1, Pallas kernels, back_gather(): pl.pallas_call(functools.partial(back_gather_kernel, line), out_shape=(ja...  105 us
    pallas_call x1, Pallas kernels, start_exchange(): pl.pallas_call(functools.partial(start_kernel, line), out_shape=(jax.Shap...  103 us
    pallas_call x1, Pallas kernels, dispatch(): pl.pallas_call(dispatch_kernel, out_shape=(out, jax.ShapeDtypeStruct((exp...  34.4 us
  transfers between devices with their start and end apart: 4, of which 1 were waited for; matrix products, arithmetic and copies ran while one was open for 13% of the time, Pallas kernels for 39%

profile of v4, /device:TPU:0, one launch (start us, length us, event | category | flops | bytes accessed | tf_op | source)
XLA Modules:
  0.0 1314.6 jit_solution(4865549216161181946)
XLA Ops:
  9.1 5.2 convert_reduce_fusion.1
  17.6 1.3 fusion.44.hidden_ref
  18.9 103.0 %start_exchange.1 = (bf16[1024,2048]{1,0:T(8,128)(2,1)}, bf16[2048,1536]{1,0:T(8,128)(2,1)}, bf16[512,2048]{1,0:T(8,128)(2,1)}) custom-call(bf16[256,2048]{1,0:T(8,128)(2,1)} %fusion.44.hidden_ref, bf16[256,512]{1,0:T(8,128)(2,1)} %wq_ref.1, bf16[256,512]{1,0:T(8,128)(2,1)} %wk_ref.1, bf16[256,512]{1,0:T(8,128)(2,1)} %wv_ref.1, bf16[512,256]{1,0:T(8,128)(2,1)} %wo_ref.1), custom_call_target="tpu_custom_call" | custom-call | bytes 157286400 | tf_op jit(solution)/shard_map/start_exchange/pallas_call | solution.py:828
  121.9 10.0 fusion.67
  132.0 2.6 copy-done.7
  134.9 11.0 all-reduce.1
  146.5 4.7 multiply_multiply_fusion
  151.2 1.9 reshape.552
  153.2 9.3 while.37
  156.5 1.3 convert_reduce_fusion.3
  161.1 1.3 convert_reduce_fusion.3
  162.5 2.9 reshape.551
  165.4 1.9 multiply_cosine_fusion
  167.4 1.2 fusion.64
  172.8 1.7 copy_bitcast_fusion.1
  174.5 26.9 %while.38 = (s32[]{:T(128)}, bf16[2,512,4,128]{3,2,1,0:T(4,128)(2,1)}, f32[2,4,512]{2,1,0:T(4,128)S(1)}, s32[3,1024]{1,0:T(4,128)S(1)}, s32[2]{0:T(128)S(1)}, /*...) while((s32[]{:T(128)}, ...), condition=%wide.region_11.12_spmd, body=%wide.region_8.0_spmd.sunk | while | flops 1104412160 | bytes 39952676 | solution.py:1429
  178.1 1.2 fusion.102
  179.3 1.8 fusion.103
  181.2 2.4 fusion.104
  183.6 3.1 fusion.105
  192.6 1.9 fusion.103
  194.5 2.4 fusion.104
  196.9 3.1 fusion.105
  201.5 3.2 copy.152
  204.7 134.2 %mixed_out.1 = (f32[256,2048]{1,0:T(8,128)}, bf16[256,2048]{1,0:T(8,128)(2,1)}, f32[64,256]{1,0:T(8,128)}) custom-call(bf16[1024,512]{1,0:T(8,128)(2,1)} %bitcast.204, bf16[512,2048]{1,0:T(8,128)(2,1)} %get-tuple-element.186.w_ref, bf16[256,2048]{1,0:T(8,128)(2,1)} %residual_ref.3, f32[1,2048]{1,0:T(1,128)} %bitcast.221, bf16[64,2048]{1,0:T(8,128)(2,1)} %bitcast.210), custom_call_target="tpu_custom_call" | custom-call | bytes 157286400 | tf_op jit(solution)/shard_map/mixed_out/pallas_call | solution.py:942
  340.0 33.2 %pick.1.c_ref = bf16[8,1280,2048]{2,1,0:T(8,128)(2,1)} custom-call(s32[32,8,256]{2,1,0:T(8,128)S(1)} %dynamic-slice_convert_fusion.slots_ref, bf16[8192,2048]{1,0:T(8,128)(2,1)} %all-gather.5.cloned.1.call-done.rows_ref), custom_call_target="tpu_custom_call" | custom-call | flops 10737418240 | bytes 75497472 | tf_op jit(solution)/shard_map/pick/pallas_call | solution.py:90
  373.2 156.6 %gather_all.1 = (bf16[8192,2048]{1,0:T(8,128)(2,1)}, f32[2048,256]{1,0:T(8,128)}) custom-call(bf16[256,2048]{1,0:T(8,128)(2,1)} %get-tuple-element.189.refs_0_, f32[64,256]{1,0:T(8,128)} %get-tuple-element.190.refs_1_), custom_call_target="tpu_custom_call" | custom-call | tf_op jit(solution)/shard_map/gather_all/pallas_call | solution.py:405
  530.9 34.4 %dispatch.1 = (bf16[8,1280,2048]{2,1,0:T(8,128)(2,1)}, f32[8,1280,128]{2,1,0:T(8,128)}) custom-call(s32[32,8,256]{2,1,0:T(8,128)S(1)} %dynamic-slice_convert_fusion.slots_ref, f32[32,8,256]{2,1,0:T(8,128)S(1)} %constant_dynamic-slice_fusion.3.gates_ref, bf16[8192,2048]{1,0:T(8,128)(2,1)} %get-tuple-element.192.rows_ref), custom_call_target="tpu_custom_call" | custom-call | flops 10737418240 | bytes 75497472 | tf_op jit(solution)/shard_map/dispatch/pallas_call | solution.py:93
  565.3 140.7 %experts.1 = (bf16[32,8,48,2048]{3,2,1,0:T(8,128)(2,1)}, bf16[32,8,48,2176]{3,2,1,0:T(8,128)(2,1)}, f32[8,2048,256]{2,1,0:T(8,128)}, f32[8,2048,256]{2,1,0:T(8,128)}, f32[8,256,2048]{2,1,0:T(8,128)}) custom-call(s32[1]{0:T(128)} %bitcast.18.first_ref, bf16[8,1280,2048]{2,1,0:T(8,128)(2,1)} %get-tuple-element.193.x_ref, bf16[8,1280,2048]{2,1,0:T(8,128)(2,1)} %pick.1.c_ref, ...), custom_call_target="tpu_custom_call" | custom-call | flops 96636764160 | bytes 243269632 | tf_op jit(solution)/shard_map/experts/pallas_call | solution.py:174
  706.0 190.9 %reduce_all.1 = (f32[256,2176]{1,0:T(8,128)}, bf16[8192,2048]{1,0:T(8,128)(2,1)}) custom-call(s32[32,8,256]{2,1,0:T(8,128)} %copy-done, bf16[32,8,48,2176]{3,2,1,0:T(8,128)(2,1)} %get-tuple-element.196.grads_ref, bf16[32,8,48,2048]{3,2,1,0:T(8,128)(2,1)} %get-tuple-element.197.outs_ref), custom_call_target="tpu_custom_call" | custom-call | flops 26575110144 | bytes 103809024 | tf_op jit(solution)/shard_map/reduce_all/pallas_call | solution.py:642
  897.9 2.0 multiply_reduce_fusion.3
  900.9 1.7 fusion.62
  902.7 3.3 multiply_reduce_fusion.1
  906.9 2.4 fusion.63
  909.3 104.7 %back_gather.1 = (bf16[1024,2048]{1,0:T(8,128)(2,1)}, f32[72,2048]{1,0:T(8,128)}) custom-call(bf16[256,2048]{1,0:T(8,128)(2,1)} %get-tuple-element.406.own_ref, f32[72,2048]{1,0:T(8,128)} %maximum_maximum_fusion.sums_ref), custom_call_target="tpu_custom_call" | custom-call | bytes 157286400 | tf_op jit(solution)/shard_map/back_gather/pallas_call | solution.py:1066
  1014.1 6.5 convolution_convert_fusion
  1020.7 68.8 %while.39 = (s32[]{:T(128)}, f32[1024,4,128]{0,2,1:T(8,128)S(1)}, f32[1024,4,128]{0,2,1:T(8,128)}, f32[2,512,4,128]{3,1,0,2:T(8,128)}, s32[2]{0:T(128)S(1)}, /*i...) while((s32[]{:T(128)}, f32[1024,4,128]{0,2,1:T(8,128)S(1)}, ...), condition=%wide.region_21.22_spmd.clone, body=%wide.region_19.21_spmd.clone.sunk | while | flops 2723937792 | bytes 163676752 | solution.py:1548
  1023.4 5.7 fusion.115
  1031.1 7.9 multiply_reduce_fusion.7
  1039.1 3.7 multiply_convert_fusion.2
  1042.8 3.9 bitcast_add_fusion.4
  1046.8 5.5 bitcast_add_fusion.5
  1052.6 1.3 fusion.117
  1053.9 1.3 copy-done.16
  1057.7 5.6 fusion.115
  1065.4 7.7 multiply_reduce_fusion.7
  1073.1 3.7 multiply_convert_fusion.2
  1076.9 3.8 bitcast_add_fusion.4
  1080.7 6.1 bitcast_add_fusion.5
  1086.9 1.3 fusion.117
  1088.2 1.3 copy-done.16
  1089.5 1.7 convert.32
  1091.2 1.3 copy.109
  1092.6 2.0 copy.103
  1094.7 5.1 multiply_add_fusion.1
  1100.3 2.3 fusion.56
  1102.6 8.6 all-reduce
  1111.3 5.6 fusion.52
  1116.9 1.8 pad_maximum_fusion.joined_ref
  1118.7 12.1 reduce-scatter.3.cloned.1.call-done
  1134.1 164.1 %last_exchange.1 = (f32[256,2048]{1,0:T(8,128)}, f32[256,512]{1,0:T(8,128)}, f32[256,512]{1,0:T(8,128)}, f32[256,512]{1,0:T(8,128)}, f32[512,256]{1,0:T(8,128)}, /*index=5*/f32[8,2048]{1,0:T(8,128)}) custom-call(bf16[1024,1536]{1,0:T(8,128)(2,1)} %pad_maximum_fusion.joined_ref, bf16[2048,1536]{1,0:T(8,128)(2,1)} %get-tuple-element.183.weight_ref, ...), custom_call_target="tpu_custom_call" | custom-call | bytes 262144000 | tf_op jit(solution)/shard_map/last_exchange/pallas_call | solution.py:1226
  1298.2 1.6 fusion.66
  1299.8 3.3 add_convert_fusion
  1303.1 1.3 copy.193
  (246 shorter events, 37.1 us)
Async XLA Ops:
  7.2 10.1 copy-start.14
  7.2 10.4 copy-start.50
  7.2 331.8 %all-gather.3.cloned.1.call-start = ((), (), s32[]{:S(2)}) async-start(), calls=%async_computation.2 | async-start | bytes 1081344 | tf_op jit(solution)/shard_map/all_gather | solution.py:1367
  14.9 325.1 %all-gather.5.cloned.1.call-start = ((), (), s32[]{:S(2)}) async-start(), calls=%async_computation.3 | async-start | bytes 34603008 | tf_op jit(solution)/shard_map/all_gather | solution.py:1370
  15.7 1115.2 %reduce-scatter.3.cloned.1.call-start = ((), (), s32[]{:S(2)}) async-start(), calls=%async_computation.4 | async-start | bytes 37748736 | tf_op jit(solution)/shard_map/reduce_scatter | solution.py:1322
  16.5 130.0 %copy-start.51 = (f32[512]{0:T(512)}, f32[512]{0:T(512)S(1)}, u32[]{:S(2)}) copy-start(f32[512]{0:T(512)S(1)} %dynamic_slice.48) | copy-start | bytes 6148
  17.3 129.2 %copy-start.53 = (f32[512]{0:T(512)}, f32[512]{0:T(512)S(1)}, u32[]{:S(2)}) copy-start(f32[512]{0:T(512)S(1)} %dynamic_slice.47) | copy-start | bytes 6148
  131.9 2.6 copy-start.7
  146.5 4.7 copy-start.46
  146.5 4.7 copy-start.48
  167.3 3.2 copy-start.18
  167.3 3.2 copy-start.20
  183.5 3.2 copy-start.32
  196.9 3.2 copy-start.32
  201.5 137.5 %copy-start.2 = (bf16[1024,4,128]{2,0,1:T(8,128)(2,1)}, bf16[1024,4,128]{2,0,1:T(8,128)(2,1)S(1)}, u32[]{:S(2)}) copy-start(bf16[1024,4,128]{2,0,1:T(8,128)(2,1)S(1)} %get-tuple-element.795) | copy-start | bytes 3145732
  201.5 137.5 %copy-start.6 = (bf16[1024,4,128]{2,0,1:T(8,128)(2,1)}, bf16[1024,4,128]{2,0,1:T(8,128)(2,1)S(1)}, u32[]{:S(2)}) copy-start(bf16[1024,4,128]{2,0,1:T(8,128)(2,1)S(1)} %get-tuple-element.796) | copy-start | bytes 3145732
  201.5 137.5 %copy-start.8 = (bf16[1024,4,128]{2,0,1:T(8,128)(2,1)}, bf16[1024,4,128]{2,0,1:T(8,128)(2,1)S(1)}, u32[]{:S(2)}) copy-start(bf16[1024,4,128]{2,0,1:T(8,128)(2,1)S(1)} %get-tuple-element.797) | copy-start | bytes 3145732
  201.5 137.5 %copy-start.29 = (s32[3,1024]{1,0:T(4,128)}, s32[3,1024]{1,0:T(4,128)S(1)}, u32[]{:S(2)}) copy-start(s32[3,1024]{1,0:T(4,128)S(1)} %get-tuple-element.807) | copy-start | bytes 36868
  201.5 137.5 %copy-start.35 = (s32[1024]{0:T(1024)}, s32[1024]{0:T(1024)S(1)}, u32[]{:S(2)}) copy-start(s32[1024]{0:T(1024)S(1)} %get-tuple-element.810) | copy-start | bytes 12292
  201.5 137.5 %copy-start.43 = (f32[2,4,512]{2,1,0:T(4,128)}, f32[2,4,512]{2,1,0:T(4,128)S(1)}, u32[]{:S(2)}) copy-start(f32[2,4,512]{2,1,0:T(4,128)S(1)} %get-tuple-element.721) | copy-start | bytes 49156
  201.5 137.5 %copy-start.57 = (s32[2]{0:T(128)}, s32[2]{0:T(128)S(1)}, u32[]{:S(2)}) copy-start(s32[2]{0:T(128)S(1)} %get-tuple-element.815) | copy-start | bytes 28
  340.0 190.9 %copy-start = (s32[32,8,256]{2,1,0:T(8,128)}, s32[32,8,256]{2,1,0:T(8,128)S(1)}, u32[]{:S(2)}) copy-start(s32[32,8,256]{2,1,0:T(8,128)S(1)} %dynamic-slice_convert_fusion.slots_ref) | copy-start | bytes 786436
  896.9 4.0 copy-start.22
  896.9 402.8 %reduce-scatter.5.cloned.1.call-start = ((), (), s32[]{:S(2)}) async-start(), calls=%async_computation.5 | async-start | bytes 5242880 | tf_op jit(solution)/shard_map/reduce_scatter | solution.py:1326
  897.9 4.7 copy-start.9
  897.9 4.7 copy-start.31
  897.9 4.7 copy-start.45
  902.7 4.3 copy-start.24
  1014.0 6.6 copy-start.3
  1014.0 6.6 copy-start.30
  1014.1 6.6 copy-start.36
  1014.1 6.6 copy-start.44
  1014.1 6.6 copy-start.58
  1031.1 8.0 copy-start.4
  1031.1 8.0 slice-start
  1031.1 8.0 slice-start.1
  1042.8 4.0 copy-start.5
  1042.8 4.0 copy-start.17
  1042.8 4.0 copy-start.25
  1046.8 5.5 copy-start.1
  1046.8 5.8 copy-start.15
  1065.3 7.8 copy-start.4
  1065.3 7.8 slice-start
  1065.3 7.7 slice-start.1
  1076.9 3.8 copy-start.5
  1076.9 3.8 copy-start.17
  1076.9 3.8 copy-start.25
  1080.7 6.2 copy-start.1
  1080.7 6.2 copy-start.15
  1094.6 5.2 slice-start.2
  1094.6 5.6 slice-start.3
  1094.6 5.6 copy-start.47
  1094.7 5.6 copy-start.49
  1094.7 5.6 copy-start.52
  1094.7 5.6 copy-start.54
  1099.8 2.8 copy-start.11
  1099.8 2.8 copy-start.12
  1099.8 2.8 copy-start.13
  1100.2 11.0 copy-start.55
  1100.3 11.0 copy-start.56
  1111.2 5.6 copy-start.23
  1299.8 3.3 copy-start.27
  1303.1 3.0 copy-start.38
  1304.4 2.4 copy-start.37
  (15 other events, 23.0 us)
Sparse Core Ops, SparseCore 0:
  15.0 57.9 all-gather.2
  75.9 254.0 all-gather.4
  897.1 233.7 reduce-scatter.2
  1133.1 133.7 reduce-scatter.4

commit v5 on v4

--- a/solution.py
+++ b/solution.py
@@ -278,143 +278,244 @@
     pl.semaphore_wait(barrier, 3 + (z + line - 1) // line + (2 * line - 2 - z) // line)
 
 
-def gather_kernel(line, count, *refs):
-    owns, outs = refs[:count], refs[count : 2 * count]
-    local_sem, send_sem, recv_sem = refs[2 * count :]
+def either(first, second, take):
+    return first * (1 - take) + second * take
+
+
+def remote(source, target, send_sem, recv_sem, where):
+    return pltpu.make_async_remote_copy(
+        src_ref=source, dst_ref=target, send_sem=send_sem, recv_sem=recv_sem,
+        device_id=peer(*where), device_id_type=MESH,
+    )
+
+
+def landed(target, sem):
+    pltpu.make_async_copy(target, target, sem).wait()
+
+
+def slot_order(y, x, core, z):
+    return ((y * 2 + x) * 4 + z) * 2 + core
+
+
+def near_first(z, i):
+    side = z // 2
+    low = either(z, 3 - z, side)
+    first, second = (4 - i) // 4, (5 - i) // 4 - (4 - i) // 4
+    return either(i + low * (first - second), 3 - i - low * (first - second), side)
+
+
+def gather_dispatch_kernel(line, rows, slots_ref, hidden_ref, gates_ref, cots_ref,
+                           rows_out, gates_out, x_out, c_out, gate_out,
+                           in_c, in_x, in_gate, stage_c, stage_x, stage_gate,
+                           local_sem, send_sem, recv_sem, load_sem, store_sem):
     y, x, core, z = place()
+    tokens, width = hidden_ref.shape
+    experts = slots_ref.shape[1]
+    first_expert = (y * 4 + x * 2 + core) * experts
+    owns, outs = (hidden_ref, gates_ref), (rows_out, gates_out)
+    near_x, near_y, sibling = (y, 1 - x, core, z), (1 - y, x, core, z), (y, x, 1 - core, z)
+    last = 24
     greet(line)
-    waits = []
-    sent = [0]
-
-    def send(cond, n, block, source_own, target):
-        rows = owns[n].shape[0]
-        part = pl.ds(block * rows, rows)
-        copy = pltpu.make_async_remote_copy(
-            src_ref=owns[n] if source_own else outs[n].at[part],
-            dst_ref=outs[n].at[part],
-            send_sem=send_sem.at[sent[0]],
-            recv_sem=recv_sem.at[n, block],
-            device_id=peer(*target),
-            device_id_type=MESH,
-        )
-        sent[0] += 1
-        waits.append((cond, copy))
-        if cond is None:
-            copy.start()
-        else:
-            pl.when(cond)(copy.start)
-
-    def arrive(n, block):
-        rows = owns[n].shape[0]
-        part = pl.ds(block * rows, rows)
-        pltpu.make_async_copy(outs[n].at[part], outs[n].at[part], recv_sem.at[n, block]).wait()
-
-    def both(a, b):
-        return b if a is None else a & b
-
-    sibling, near_x, near_y = (y, x, 1 - core, z), (y, 1 - x, core, z), (1 - y, x, core, z)
+
+    def span(n, block):
+        count = owns[n].shape[0]
+        return outs[n].at[pl.ds(block * count, count)]
+
+    def spot(m):
+        q = m % 4
+        i = m // 4 - (q + 1) // 2
+        live = (i >= 0) & (i < line)
+        held = i * live.astype(jnp.int32)
+        yy, xx = (y + q // 2) % 2, (x + q % 2) % 2
+        return q, held, live, yy, xx, near_first(z, held)
+
+    def sends(m):
+        q, i, live, yy, xx, zz = spot(m)
+        block = block_of(yy, xx, core, zz)
+        own = live & (q == 0)
+        table = (
+            (own & (zz <= z) & (z < line - 1), (y, x, core, z + 1)),
+            (own & (zz >= z) & (z > 0), (y, x, core, z - 1)),
+            (own | (live & (q == 2) & (zz % 2 == 1)), near_x),
+            (own | (live & (q == 1) & (zz % 2 == 0)), near_y),
+            (live, sibling),
+        )
+        for lane, (wanted, where) in enumerate(table):
+            for n in range(2):
+                part = span(n, block)
+                yield wanted, remote(part, part, send_sem.at[n, lane, m], recv_sem.at[n, block], where)
+
+    def load_c(chip):
+        yy, xx, zz = chip // 8, chip // 4 % 2, chip % 4
+        for c in range(2):
+            b = block_of(yy, xx, c, zz)
+            yield pltpu.make_async_copy(
+                cots_ref.at[pl.ds(b * tokens, tokens)], in_c.at[pl.ds(c * tokens, tokens)], load_sem.at[0, c]
+            )
+
+    def load_x(yy, xx, zz):
+        for c in range(2):
+            b = block_of(yy, xx, c, zz)
+            yield pltpu.make_async_copy(
+                rows_out.at[pl.ds(b * tokens, tokens)], in_x.at[pl.ds(c * tokens, tokens)], load_sem.at[1, c]
+            )
+            yield pltpu.make_async_copy(
+                gates_out.at[pl.ds(b * gates_ref.shape[0] + first_expert, experts)], in_gate.at[c], load_sem.at[2, c]
+            )
+
+    def store(stage, target, lane, chip):
+        return pltpu.make_async_copy(stage, target.at[:, pl.ds(chip * 2 * rows, 2 * rows)], store_sem.at[lane])
+
+    def pick(source, target, yy, xx, zz, gated):
+        picks = []
+        for c in range(2):
+            slots = slots_ref[block_of(yy, xx, c, zz)]
+            pieces = []
+            for e in range(experts):
+                hit = slot_hits(slots, e, rows)
+                pieces.append(hit.astype(jnp.float32))
+                if gated:
+                    gate = jnp.sum(jnp.where(hit, in_gate[c, e : e + 1, :], 0.0), axis=1, keepdims=True)
+                    stage_gate[e, c * rows : (c + 1) * rows, :] = jnp.broadcast_to(gate, (rows, 128))
+            picks.append(jnp.concatenate(pieces, axis=0).astype(jnp.bfloat16))
+        step = min(512, width)
+        for first in range(0, width, step):
+            parts = [
+                jnp.dot(
+                    picks[c], source[c * tokens : (c + 1) * tokens, first : first + step],
+                    preferred_element_type=jnp.float32,
+                )
+                for c in range(2)
+            ]
+            for e in range(experts):
+                target[e, :, first : first + step] = jnp.concatenate(
+                    [part[e * rows : (e + 1) * rows] for part in parts], axis=0
+                ).astype(jnp.bfloat16)
+
     mine = block_of(y, x, core, z)
-    locals_ = []
-    for n in range(count):
-        rows = owns[n].shape[0]
-        own_copy = pltpu.make_async_copy(owns[n], outs[n].at[pl.ds(mine * rows, rows)], local_sem.at[n])
-        own_copy.start()
-        locals_.append(own_copy)
-
-    def own_column(n, step, sign):
-        zz = z + sign * step
-        valid = None if step == 0 else (zz >= 0) & (zz < line)
-        block = block_of(y, x, core, zz)
-
-        def fetch():
-            if step:
-                arrive(n, block)
-
-        if step:
-            pl.when(valid)(fetch)
-        if step == 0:
-            send(z > 0, n, block, True, (y, x, core, z - 1))
-            send(z < line - 1, n, block, True, (y, x, core, z + 1))
-        elif sign < 0:
-            send(both(valid, z < line - 1), n, block, False, (y, x, core, z + 1))
-        else:
-            send(both(valid, z > 0), n, block, False, (y, x, core, z - 1))
-        send(valid, n, block, step == 0, near_x)
-        send(valid, n, block, step == 0, near_y)
-        send(valid, n, block, step == 0, sibling)
-
-    def next_column(n, step, sign, along_x):
-        zz = z + sign * step
-        valid = None if step == 0 else (zz >= 0) & (zz < line)
-        yy, xx = (y, 1 - x) if along_x else (1 - y, x)
-        block = block_of(yy, xx, core, zz)
-        if step:
-            pl.when(valid)(lambda: arrive(n, block))
-        else:
-            arrive(n, block)
-        if step % 2 == (0 if along_x else 1):
-            send(valid, n, block, False, near_y if along_x else near_x)
-        send(valid, n, block, False, sibling)
-
-    def far_column(n, step, sign):
-        zz = z + sign * step
-        valid = None if step == 0 else (zz >= 0) & (zz < line)
-        block = block_of(1 - y, 1 - x, core, zz)
-        if step:
-            pl.when(valid)(lambda: arrive(n, block))
-        else:
-            arrive(n, block)
-        send(valid, n, block, False, sibling)
-
-    def signs(step):
-        return (1,) if step == 0 else (-1, 1)
-
-    for n in range(count):
-        own_column(n, 0, 1)
-    for step in range(line + 1):
-        for n in range(count):
-            if step + 1 < line:
-                for sign in signs(step + 1):
-                    own_column(n, step + 1, sign)
-            if step < line:
-                for sign in signs(step):
-                    next_column(n, step, sign, True)
-                    next_column(n, step, sign, False)
-            if step:
-                for sign in signs(step - 1):
-                    far_column(n, step - 1, sign)
-    for yy in range(2):
-        for xx in range(2):
-            for zz in range(line):
-                for n in range(count):
-                    arrive(n, block_of(yy, xx, 1 - core, zz))
-    for cond, copy in waits:
-        if cond is None:
-            copy.wait_send()
-        else:
-            pl.when(cond)(copy.wait_send)
-    for copy in locals_:
+    local = [pltpu.make_async_copy(owns[n], span(n, mine), local_sem.at[n]) for n in range(2)]
+    for copy in local:
+        copy.start()
+    for copy in load_c(0):
+        copy.start()
+    for copy in local:
         copy.wait()
-
-
-def gather_all(arrays, collective_id):
-    count = len(arrays)
+    chips = 4 * line
+    lag = 2
+
+    def work(m, carry):
+        q, i, live, yy, xx, zz = spot(m)
+
+        @pl.when((m < last) & live & (q + i > 0))
+        def _():
+            for n in range(2):
+                landed(span(n, block_of(yy, xx, core, zz)), recv_sem.at[n, block_of(yy, xx, core, zz)])
+
+        for wanted, copy in sends(m):
+            pl.when((m < last) & wanted)(copy.start)
+
+        @pl.when(m < chips)
+        def _():
+            for copy in load_c(m):
+                copy.wait()
+
+            @pl.when(m > 0)
+            def _():
+                store(stage_c, c_out, 0, m - 1).wait()
+
+            pick(in_c, stage_c, m // 8, m // 4 % 2, m % 4, False)
+            store(stage_c, c_out, 0, m).start()
+
+            @pl.when(m + 1 < chips)
+            def _():
+                for copy in load_c(m + 1):
+                    copy.start()
+
+        back = m - lag
+        q = (back + 8) % 4
+        i = (back + 8) // 4 - 2 - (q + 1) // 2
+        live = (i >= 0) & (i < line)
+        held = i * live.astype(jnp.int32)
+        yy, xx = (y + q // 2) % 2, (x + q % 2) % 2
+        zz = near_first(z, held)
+
+        @pl.when(live)
+        def _():
+            block = block_of(yy, xx, 1 - core, zz)
+            for n in range(2):
+                landed(span(n, block), recv_sem.at[n, block])
+            for copy in load_x(yy, xx, zz):
+                copy.start()
+            chip = (yy * 2 + xx) * 4 + zz
+
+            @pl.when(q + held > 0)
+            def _():
+                store(stage_x, x_out, 1, chip).wait()
+                store(stage_gate, gate_out, 2, chip).wait()
+
+            for copy in load_x(yy, xx, zz):
+                copy.wait()
+            pick(in_x, stage_x, yy, xx, zz, True)
+            store(stage_x, x_out, 1, chip).start()
+            store(stage_gate, gate_out, 2, chip).start()
+
+        return carry
+
+    lax.fori_loop(0, last + lag, work, 0)
+    store(stage_c, c_out, 0, chips - 1).wait()
+    store(stage_x, x_out, 1, 0).wait()
+    store(stage_gate, gate_out, 2, 0).wait()
+
+    def finish(m, carry):
+        for wanted, copy in sends(m):
+            pl.when(wanted)(copy.wait_send)
+        return carry
+
+    lax.fori_loop(0, last, finish, 0)
+
+
+def gather_dispatch(slots, hidden, gates, cots_all, rows, collective_id):
+    line = 4
+    blocks, experts, tokens = slots.shape
+    width = hidden.shape[1]
+    pair = 2 * rows
+    low, wide = jnp.bfloat16, jnp.float32
     any_ref = pl.BlockSpec(memory_space=pl.ANY)
-    line = lax.axis_size("tensor")
-    devices = 8 * line
+    vmem = pl.BlockSpec(memory_space=pltpu.VMEM)
+    dma = pltpu.SemaphoreType.DMA
+    slot_shape = jax.ShapeDtypeStruct((experts, blocks * rows, width), low)
     return pl.pallas_call(
-        functools.partial(gather_kernel, line, count),
-        out_shape=[jax.ShapeDtypeStruct((devices * a.shape[0],) + a.shape[1:], a.dtype) for a in arrays],
-        in_specs=[any_ref] * count,
-        out_specs=[any_ref] * count,
+        functools.partial(gather_dispatch_kernel, line, rows),
+        out_shape=(
+            jax.ShapeDtypeStruct((blocks * tokens, width), low),
+            jax.ShapeDtypeStruct((blocks * gates.shape[0], tokens), wide),
+            slot_shape,
+            slot_shape,
+            jax.ShapeDtypeStruct((experts, blocks * rows, 128), wide),
+        ),
+        in_specs=[vmem, any_ref, any_ref, any_ref],
+        out_specs=[any_ref] * 5,
         scratch_shapes=[
-            pltpu.SemaphoreType.DMA((count,)),
-            pltpu.SemaphoreType.DMA((count * 80,)),
-            pltpu.SemaphoreType.DMA((count, devices)),
+            pltpu.VMEM((2 * tokens, width), low),
+            pltpu.VMEM((2 * tokens, width), low),
+            pltpu.VMEM((2, experts, tokens), wide),
+            pltpu.VMEM((experts, pair, width), low),
+            pltpu.VMEM((experts, pair, width), low),
+            pltpu.VMEM((experts, pair, 128), wide),
+            dma((2,)),
+            dma((2, 5, 24)),
+            dma((2, blocks)),
+            dma((3, 2)),
+            dma((3,)),
         ],
-        compiler_params=pltpu.CompilerParams(collective_id=collective_id, has_side_effects=True),
-        name="gather_all",
-    )(*arrays)
+        compiler_params=pltpu.CompilerParams(
+            collective_id=collective_id, has_side_effects=True, vmem_limit_bytes=40 << 20
+        ),
+        cost_estimate=pl.CostEstimate(
+            flops=4 * blocks * experts * rows * tokens * width, bytes_accessed=200 << 20, transcendentals=0
+        ),
+        name="gather_dispatch",
+    )(slots, hidden, gates, cots_all)[2:]
 
 
 def reduce_kernel(line, slots_ref, grads_ref, outs_ref, sum_ref, part_ref,
@@ -431,23 +532,23 @@
         early = 1 - r // 2
         return (line - 1) * (r % 2) * early + (r - 1) * (1 - early)
 
-    def block_at(q):
+    def spot_at(q):
         r, j = q // 8, q % 8
         column = j % 4
         dy, dx = (column + 1) % 2, 1 - column // 2
         own = j // 4
         target_core = core * own + (1 - core) * (1 - own)
-        return block_of((y + dy) % 2, (x + dx) % 2, target_core, goal(r))
+        return (y + dy) % 2, (x + dx) % 2, target_core, goal(r)
 
     def load(q):
-        b = block_at(q)
+        b = slot_order(*spot_at(q))
         return (
             pltpu.make_async_copy(grads_ref.at[b], grad_in.at[q % 2], in_sem.at[0, q % 2]),
             pltpu.make_async_copy(outs_ref.at[b], out_in.at[q % 2], in_sem.at[1, q % 2]),
         )
 
     def to_part(q):
-        b = block_at(q)
+        b = block_of(*spot_at(q))
         return pltpu.make_async_copy(out_stage.at[q % 2], part_ref.at[pl.ds(b * tokens, tokens)], part_sem.at[q % 2])
 
     def to_sibling(r, j):
@@ -485,7 +586,7 @@
 
     def term(q, source, target_width, store):
         picks = jnp.concatenate(
-            [slot_hits(slots_ref[block_at(q)], e, room).astype(jnp.float32) for e in range(experts)], axis=0
+            [slot_hits(slots_ref[block_of(*spot_at(q))], e, room).astype(jnp.float32) for e in range(experts)], axis=0
         ).astype(jnp.bfloat16)
         for first in range(0, target_width, 512):
             part = slice(first, min(first + 512, target_width))
@@ -681,21 +782,6 @@
     )(slots, grads, outs)
 
 
-def either(first, second, take):
-    return first * (1 - take) + second * take
-
-
-def remote(source, target, send_sem, recv_sem, where):
-    return pltpu.make_async_remote_copy(
-        src_ref=source, dst_ref=target, send_sem=send_sem, recv_sem=recv_sem,
-        device_id=peer(*where), device_id_type=MESH,
-    )
-
-
-def landed(target, sem):
-    pltpu.make_async_copy(target, target, sem).wait()
-
-
 class LineGather:
     def __init__(self, own, out, send_sem, recv_sem, line):
         self.own, self.out, self.send_sem, self.recv_sem, self.line = own, out, send_sem, recv_sem, line
@@ -1368,7 +1454,7 @@
     slots = lax.dynamic_slice_in_dim(slots_all, first_expert, local_experts, 1).astype(jnp.int32)
     blocks = slots.shape[0]
     cots_all = lax.all_gather(cotangent, everyone, axis=0, tiled=True)
-    c_slots = dispatch(slots, None, cots_all, slot_rows)
+    c_slots = None if direct else dispatch(slots, None, cots_all, slot_rows)
     head_cols = w_query.shape[1]
     local_heads = head_cols // HD
     residual_float = residual.astype(jnp.float32)
@@ -1442,16 +1528,14 @@
         logits = jnp.dot(hidden_two, router, preferred_element_type=jnp.float32)
         probs = jax.nn.softmax(logits, axis=-1)
         gates_own = probs.T
-    hidden_two, c_slots = lax.optimization_barrier((hidden_two, c_slots))
     scale_two = lax.rsqrt(jnp.mean(x_one * x_one, axis=-1, keepdims=True) + norm_eps)
     if direct:
-        rows_all, gates_all = gather_all([hidden_two, gates_own], 1)
-        gates_all = gates_all.reshape(-1, experts, tok_dev)
+        x_slots, c_slots, gate_slots = gather_dispatch(slots, hidden_two, gates_own, cots_all, slot_rows, 1)
     else:
         gates_all = lax.all_gather(gates_own, everyone, axis=0)
         rows_all = lax.all_gather(hidden_two, everyone, axis=0, tiled=True)
-    gates = lax.dynamic_slice_in_dim(gates_all, first_expert, local_experts, 1)
-    x_slots, gate_slots = dispatch(slots, gates, rows_all, slot_rows)
+        gates = lax.dynamic_slice_in_dim(gates_all, first_expert, local_experts, 1)
+        x_slots, gate_slots = dispatch(slots, gates, rows_all, slot_rows)
     outs, grads, grad_w_gate, grad_w_up, grad_w_down = expert_pass(
         first_expert.reshape(1),
         x_slots,

time: 1320 us -> 1280 us (0.970)
  Pallas kernels: 1060 us -> 1020 us
    pallas_call x3 -> x1, Pallas kernels: 224 us -> 177 us  [gather_dispatch(): pl.pallas_call(functools.partial(gather_dispatch_kernel, line, rows), out...]
  transfers between devices with their start and end apart: 4 -> 4, of which waited for: 1 -> 1; matrix products, arithmetic and copies ran while one was open for 13% -> 13% of each run, Pallas kernels for 39% -> 40%
where the time goes in v5:
time: 1280 us
  Pallas kernels  1020 us (80%)
  matrix products  80.1 us (6%)
  other arithmetic  70.6 us (6%)
  local copies, waits for them, and re-layouts  45.1 us (4%)
  blocking collectives  20.3 us (2%)
  between operations  15.1 us (1%)
  waiting for transfers between devices  13.1 us (1%)
    pallas_call x1, Pallas kernels, reduce_all(): pl.pallas_call(functools.partial(reduce_kernel, line), out_shape=(jax.Sha...  196 us
    pallas_call x1, Pallas kernels, gather_dispatch(): pl.pallas_call(functools.partial(gather_dispatch_kernel, line, rows), out...  177 us
    pallas_call x1, Pallas kernels, last_exchange(): pl.pallas_call(functools.partial(last_kernel, line), out_shape=(jax.Shape...  164 us
    pallas_call x1, Pallas kernels, expert_pass(): pl.pallas_call(kernel, grid_spec=pltpu.PrefetchScalarGridSpec(num_scalar_...  141 us
    pallas_call x1, Pallas kernels, mixed_out(): pl.pallas_call(functools.partial(mixed_out_kernel, line), out_shape=(jax....  134 us
    pallas_call x1, Pallas kernels, back_gather(): pl.pallas_call(functools.partial(back_gather_kernel, line), out_shape=(ja...  104 us
    pallas_call x1, Pallas kernels, start_exchange(): pl.pallas_call(functools.partial(start_kernel, line), out_shape=(jax.Shap...  103 us
  transfers between devices with their start and end apart: 4, of which 1 were waited for; matrix products, arithmetic and copies ran while one was open for 13% of the time, Pallas kernels for 40%

profile of v5, /device:TPU:0, one launch (start us, length us, event | category | flops | bytes accessed | tf_op | source)
XLA Modules:
  0.0 1275.6 jit_solution(794441238793314525)
XLA Ops:
  9.1 5.2 convert_reduce_fusion.1
  17.6 1.3 fusion.44.hidden_ref
  18.9 103.0 %start_exchange.1 = (bf16[1024,2048]{1,0:T(8,128)(2,1)}, bf16[2048,1536]{1,0:T(8,128)(2,1)}, bf16[512,2048]{1,0:T(8,128)(2,1)}) custom-call(bf16[256,2048]{1,0:T(8,128)(2,1)} %fusion.44.hidden_ref, bf16[256,512]{1,0:T(8,128)(2,1)} %wq_ref.1, bf16[256,512]{1,0:T(8,128)(2,1)} %wk_ref.1, bf16[256,512]{1,0:T(8,128)(2,1)} %wv_ref.1, bf16[512,256]{1,0:T(8,128)(2,1)} %wo_ref.1), custom_call_target="tpu_custom_call" | custom-call | bytes 157286400 | tf_op jit(solution)/shard_map/start_exchange/pallas_call | solution.py:914
  121.9 10.0 fusion.67
  131.9 2.6 copy-done.12
  134.9 11.0 all-reduce.1
  146.5 4.7 multiply_multiply_fusion
  151.2 1.9 reshape.549
  153.1 9.3 while.37
  156.4 1.3 convert_reduce_fusion.3
  161.1 1.3 convert_reduce_fusion.3
  162.5 2.9 reshape.548
  165.4 1.9 multiply_cosine_fusion
  167.4 1.2 fusion.64
  172.8 1.7 copy_bitcast_fusion.1
  174.5 26.9 %while.38 = (s32[]{:T(128)}, bf16[2,512,4,128]{3,2,1,0:T(4,128)(2,1)}, f32[2,4,512]{2,1,0:T(4,128)S(1)}, s32[3,1024]{1,0:T(4,128)S(1)}, s32[2]{0:T(128)S(1)}, /*...) while((s32[]{:T(128)}, ...), condition=%wide.region_11.12_spmd, body=%wide.region_8.0_spmd.sunk | while | flops 1104412160 | bytes 39952676 | solution.py:1515
  179.3 1.8 fusion.103
  181.1 2.4 fusion.104
  183.5 3.1 fusion.105
  191.4 1.2 fusion.102
  192.6 1.9 fusion.103
  194.5 2.4 fusion.104
  196.9 3.1 fusion.105
  201.5 3.2 copy.152
  204.7 134.3 %mixed_out.1 = (f32[256,2048]{1,0:T(8,128)}, bf16[256,2048]{1,0:T(8,128)(2,1)}, f32[64,256]{1,0:T(8,128)}) custom-call(bf16[1024,512]{1,0:T(8,128)(2,1)} %bitcast.203, bf16[512,2048]{1,0:T(8,128)(2,1)} %get-tuple-element.183.w_ref, bf16[256,2048]{1,0:T(8,128)(2,1)} %residual_ref.3, f32[1,2048]{1,0:T(1,128)} %bitcast.220, bf16[64,2048]{1,0:T(8,128)(2,1)} %bitcast.209), custom_call_target="tpu_custom_call" | custom-call | bytes 157286400 | tf_op jit(solution)/shard_map/mixed_out/pallas_call | solution.py:1028
  340.1 1.3 copy-done.1
  342.2 176.5 %gather_dispatch.1 = (bf16[8192,2048]{1,0:T(8,128)(2,1)}, f32[2048,256]{1,0:T(8,128)}, bf16[8,1280,2048]{2,1,0:T(8,128)(2,1)}, bf16[8,1280,2048]{2,1,0:T(8,128)(2,1)}, f32[8,1280,128]{2,1,0:T(8,128)S(1)}) custom-call(s32[32,8,256]{2,1,0:T(8,128)S(1)} %dynamic-slice_convert_fusion.slots_ref, bf16[256,2048]{1,0:T(8,128)(2,1)S(1)} %copy-done.1, ...), custom_call_target="tpu_custom_call" | custom-call | flops 21474836480 | bytes 209715200 | tf_op jit(solution)/shard_map/gather_dispatch/pallas_call | solution.py:487
  518.8 2.3 copy-done.5
  521.1 140.7 %experts.1 = (bf16[32,8,48,2048]{3,2,1,0:T(8,128)(2,1)}, bf16[32,8,48,2176]{3,2,1,0:T(8,128)(2,1)}, f32[8,2048,256]{2,1,0:T(8,128)}, f32[8,2048,256]{2,1,0:T(8,128)}, f32[8,256,2048]{2,1,0:T(8,128)}) custom-call(s32[1]{0:T(128)} %bitcast.18.first_ref, bf16[8,1280,2048]{2,1,0:T(8,128)(2,1)} %get-tuple-element.187.x_ref, ...), custom_call_target="tpu_custom_call" | custom-call | flops 96636764160 | bytes 243269632 | tf_op jit(solution)/shard_map/experts/pallas_call | solution.py:174
  661.8 195.7 %reduce_all.1 = (f32[256,2176]{1,0:T(8,128)}, bf16[8192,2048]{1,0:T(8,128)(2,1)}) custom-call(s32[32,8,256]{2,1,0:T(8,128)} %copy-done, bf16[32,8,48,2176]{3,2,1,0:T(8,128)(2,1)} %get-tuple-element.190.grads_ref, bf16[32,8,48,2048]{3,2,1,0:T(8,128)(2,1)} %get-tuple-element.191.outs_ref), custom_call_target="tpu_custom_call" | custom-call | flops 26575110144 | bytes 103809024 | tf_op jit(solution)/shard_map/reduce_all/pallas_call | solution.py:743
  858.5 2.0 multiply_reduce_fusion.3
  861.5 1.7 fusion.62
  863.2 3.3 multiply_reduce_fusion.1
  867.5 2.4 fusion.63
  869.8 104.1 %back_gather.1 = (bf16[1024,2048]{1,0:T(8,128)(2,1)}, f32[72,2048]{1,0:T(8,128)}) custom-call(bf16[256,2048]{1,0:T(8,128)(2,1)} %get-tuple-element.400.own_ref, f32[72,2048]{1,0:T(8,128)} %maximum_maximum_fusion.sums_ref), custom_call_target="tpu_custom_call" | custom-call | bytes 157286400 | tf_op jit(solution)/shard_map/back_gather/pallas_call | solution.py:1152
  974.0 6.4 convolution_convert_fusion
  980.5 68.6 %while.39 = (s32[]{:T(128)}, f32[1024,4,128]{0,2,1:T(8,128)S(1)}, f32[1024,4,128]{0,2,1:T(8,128)}, f32[2,512,4,128]{3,1,0,2:T(8,128)}, s32[2]{0:T(128)S(1)}, /*i...) while((s32[]{:T(128)}, f32[1024,4,128]{0,2,1:T(8,128)S(1)}, ...), condition=%wide.region_21.22_spmd.clone, body=%wide.region_19.21_spmd.clone.sunk | while | flops 2723937792 | bytes 163676752 | solution.py:1632
  983.2 5.6 fusion.115
  990.8 7.8 multiply_reduce_fusion.7
  998.7 3.7 multiply_convert_fusion.2
  1002.4 4.0 bitcast_add_fusion.4
  1006.4 5.7 bitcast_add_fusion.5
  1012.2 1.3 fusion.117
  1013.5 1.3 copy-done.21
  1017.4 5.6 fusion.115
  1025.0 7.8 multiply_reduce_fusion.7
  1032.8 3.7 multiply_convert_fusion.2
  1036.5 3.9 bitcast_add_fusion.4
  1040.5 5.8 bitcast_add_fusion.5
  1046.5 1.3 fusion.117
  1047.8 1.3 copy-done.21
  1049.1 2.0 convert.32
  1051.1 1.3 copy.109
  1052.4 2.0 copy.103
  1054.5 5.1 multiply_add_fusion.1
  1060.4 2.3 fusion.56
  1062.7 9.3 all-reduce
  1072.1 5.6 fusion.52
  1077.7 1.8 pad_maximum_fusion.joined_ref
  1079.5 12.3 reduce-scatter.3.cloned.1.call-done
  1095.1 164.1 %last_exchange.1 = (f32[256,2048]{1,0:T(8,128)}, f32[256,512]{1,0:T(8,128)}, f32[256,512]{1,0:T(8,128)}, f32[256,512]{1,0:T(8,128)}, f32[512,256]{1,0:T(8,128)}, /*index=5*/f32[8,2048]{1,0:T(8,128)}) custom-call(bf16[1024,1536]{1,0:T(8,128)(2,1)} %pad_maximum_fusion.joined_ref, bf16[2048,1536]{1,0:T(8,128)(2,1)} %get-tuple-element.180.weight_ref, ...), custom_call_target="tpu_custom_call" | custom-call | bytes 262144000 | tf_op jit(solution)/shard_map/last_exchange/pallas_call | solution.py:1312
  1259.2 1.6 fusion.66
  1260.8 3.3 add_convert_fusion
  1264.1 1.3 copy.193
  (249 shorter events, 37.2 us)
Async XLA Ops:
  7.2 10.1 copy-start.19
  7.2 10.4 copy-start.53
  7.2 331.9 %all-gather.3.cloned.1.call-start = ((), (), s32[]{:S(2)}) async-start(), calls=%async_computation.2 | async-start | bytes 1081344 | tf_op jit(solution)/shard_map/all_gather | solution.py:1453
  14.9 325.1 %all-gather.5.cloned.1.call-start = ((), (), s32[]{:S(2)}) async-start(), calls=%async_computation.3 | async-start | bytes 34603008 | tf_op jit(solution)/shard_map/all_gather | solution.py:1456
  15.7 1076.2 %reduce-scatter.3.cloned.1.call-start = ((), (), s32[]{:S(2)}) async-start(), calls=%async_computation.4 | async-start | bytes 37748736 | tf_op jit(solution)/shard_map/reduce_scatter | solution.py:1408
  16.5 130.0 %copy-start.54 = (f32[512]{0:T(512)}, f32[512]{0:T(512)S(1)}, u32[]{:S(2)}) copy-start(f32[512]{0:T(512)S(1)} %dynamic_slice.45) | copy-start | bytes 6148
  17.3 129.2 %copy-start.56 = (f32[512]{0:T(512)}, f32[512]{0:T(512)S(1)}, u32[]{:S(2)}) copy-start(f32[512]{0:T(512)S(1)} %dynamic_slice.44) | copy-start | bytes 6148
  131.9 2.6 copy-start.12
  146.5 4.7 copy-start.49
  146.5 4.7 copy-start.51
  167.3 3.2 copy-start.23
  167.3 3.2 copy-start.25
  183.5 3.2 copy-start.36
  196.9 3.2 copy-start.36
  201.5 137.5 %copy-start.7 = (bf16[1024,4,128]{2,0,1:T(8,128)(2,1)}, bf16[1024,4,128]{2,0,1:T(8,128)(2,1)S(1)}, u32[]{:S(2)}) copy-start(bf16[1024,4,128]{2,0,1:T(8,128)(2,1)S(1)} %get-tuple-element.789) | copy-start | bytes 3145732
  201.5 137.5 %copy-start.11 = (bf16[1024,4,128]{2,0,1:T(8,128)(2,1)}, bf16[1024,4,128]{2,0,1:T(8,128)(2,1)S(1)}, u32[]{:S(2)}) copy-start(bf16[1024,4,128]{2,0,1:T(8,128)(2,1)S(1)} %get-tuple-element.790) | copy-start | bytes 3145732
  201.5 137.5 %copy-start.13 = (bf16[1024,4,128]{2,0,1:T(8,128)(2,1)}, bf16[1024,4,128]{2,0,1:T(8,128)(2,1)S(1)}, u32[]{:S(2)}) copy-start(bf16[1024,4,128]{2,0,1:T(8,128)(2,1)S(1)} %get-tuple-element.791) | copy-start | bytes 3145732
  201.5 137.6 %copy-start.33 = (s32[3,1024]{1,0:T(4,128)}, s32[3,1024]{1,0:T(4,128)S(1)}, u32[]{:S(2)}) copy-start(s32[3,1024]{1,0:T(4,128)S(1)} %get-tuple-element.800) | copy-start | bytes 36868
  201.5 137.6 %copy-start.39 = (s32[1024]{0:T(1024)}, s32[1024]{0:T(1024)S(1)}, u32[]{:S(2)}) copy-start(s32[1024]{0:T(1024)S(1)} %get-tuple-element.803) | copy-start | bytes 12292
  201.5 137.6 %copy-start.46 = (f32[2,4,512]{2,1,0:T(4,128)}, f32[2,4,512]{2,1,0:T(4,128)S(1)}, u32[]{:S(2)}) copy-start(f32[2,4,512]{2,1,0:T(4,128)S(1)} %get-tuple-element.715) | copy-start | bytes 49156
  201.5 137.6 %copy-start.60 = (s32[2]{0:T(128)}, s32[2]{0:T(128)S(1)}, u32[]{:S(2)}) copy-start(s32[2]{0:T(128)S(1)} %get-tuple-element.809) | copy-start | bytes 28
  340.0 178.7 %copy-start = (s32[32,8,256]{2,1,0:T(8,128)}, s32[32,8,256]{2,1,0:T(8,128)S(1)}, u32[]{:S(2)}) copy-start(s32[32,8,256]{2,1,0:T(8,128)S(1)} %dynamic-slice_convert_fusion.slots_ref) | copy-start | bytes 786436
  857.5 4.0 copy-start.2
  857.5 403.3 %reduce-scatter.5.cloned.1.call-start = ((), (), s32[]{:S(2)}) async-start(), calls=%async_computation.5 | async-start | bytes 5242880 | tf_op jit(solution)/shard_map/reduce_scatter | solution.py:1412
  858.5 4.7 copy-start.14
  858.5 4.7 copy-start.35
  858.5 4.7 copy-start.48
  863.2 4.3 copy-start.28
  973.9 6.5 copy-start.8
  973.9 6.5 copy-start.34
  973.9 6.5 copy-start.40
  974.0 6.5 copy-start.47
  974.0 6.5 copy-start.61
  990.8 7.9 copy-start.9
  990.8 7.8 slice-start
  990.8 7.8 slice-start.1
  1002.4 4.0 copy-start.10
  1002.4 4.0 copy-start.22
  1002.4 4.0 copy-start.29
  1006.4 5.7 copy-start.6
  1006.4 5.8 copy-start.20
  1025.0 7.8 copy-start.9
  1025.0 7.8 slice-start
  1025.0 7.8 slice-start.1
  1036.5 3.9 copy-start.10
  1036.5 3.9 copy-start.22
  1036.5 3.9 copy-start.29
  1040.5 5.9 copy-start.6
  1040.5 6.0 copy-start.20
  1054.4 5.2 slice-start.2
  1054.5 5.8 slice-start.3
  1054.5 5.8 copy-start.50
  1054.5 5.8 copy-start.52
  1054.5 5.8 copy-start.55
  1054.5 5.8 copy-start.57
  1059.6 3.1 copy-start.16
  1059.6 3.1 copy-start.17
  1059.6 3.1 copy-start.18
  1060.3 11.7 copy-start.58
  1060.3 11.7 copy-start.59
  1072.1 5.7 copy-start.27
  1260.8 3.3 copy-start.31
  1264.1 3.0 copy-start.42
  1265.5 2.4 copy-start.41
  (18 other events, 27.4 us)
Sparse Core Ops, SparseCore 0:
  15.0 57.9 all-gather.2
  75.9 254.1 all-gather.4
  857.6 234.1 reduce-scatter.2
  1094.1 133.7 reduce-scatter.4

commit v6 on v5

--- a/solution.py
+++ b/solution.py
@@ -533,10 +533,10 @@
         return (line - 1) * (r % 2) * early + (r - 1) * (1 - early)
 
     def spot_at(q):
-        r, j = q // 8, q % 8
-        column = j % 4
+        r, p = q // 8, q % 8
+        own = (1 - p % 2) * ((p + 7) // 8) + p // 7
+        column = own * (p // 2 - 1 + p // 7) + (1 - own) * ((p + 1) // 2)
         dy, dx = (column + 1) % 2, 1 - column // 2
-        own = j // 4
         target_core = core * own + (1 - core) * (1 - own)
         return (y + dy) % 2, (x + dx) % 2, target_core, goal(r)
 
@@ -596,8 +596,8 @@
     for copy in load(0):
         copy.start()
 
-    def one(r, j, own):
-        q = r * 8 + own * 4 + j
+    def one(r, p, j, own):
+        q = r * 8 + p
         for copy in load(q):
             copy.wait()
 
@@ -648,10 +648,13 @@
         @pl.when(s < rounds)
         def _():
             r = s
-            lax.fori_loop(0, 4, lambda j, c: (one(r, j, 0), c)[1], 0)
-            lax.fori_loop(0, 4, lambda j, c: (one(r, j, 1), c)[1], 0)
-            for kind in ("far_x", "far_y", "x0", "y1"):
-                cross(kind, r).start()
+            one(r, 0, 0, 0)
+            for j in range(4):
+                if j < 3:
+                    one(r, 2 * j + 1, j + 1, 0)
+                one(r, min(2 * j + 2, 7), j, 1)
+                for kind in (("far_x", "far_y"), ("x0",), ("y1",), ())[j]:
+                    cross(kind, r).start()
             cross("far_y", r).wait_recv()
             add(r * 4 + 1, rows(1), lambda part: far_y[r, :, part])
             cross("x1", r).start()
@@ -1356,26 +1359,147 @@
     return (jnp.cos(angles), jnp.sin(angles))
 
 
-def rotate(values, cosine, sine):
-    half = values.shape[-1] // 2
-    first = values[..., :half]
-    second = values[..., half:]
-    cosine = cosine[:, None, :]
-    sine = sine[:, None, :]
-    return jnp.concatenate(
-        (first * cosine - second * sine, second * cosine + first * sine), axis=-1
-    )
-
-
-def unrotate(grads, cosine, sine):
-    half = grads.shape[-1] // 2
-    first = grads[..., :half]
-    second = grads[..., half:]
-    cosine = cosine[:, None, :]
-    sine = sine[:, None, :]
-    return jnp.concatenate(
-        (first * cosine + second * sine, second * cosine - first * sine), axis=-1
-    )
+def visible_bias(row_first, row_paths, row_places, key_segment, key_valid, key_places):
+    on_path = (key_segment == row_paths[0]) | (key_segment == row_paths[1]) | (key_segment == row_paths[2])
+    seen = (on_path & (key_places <= row_places) & (key_valid == 1)) | (key_places == row_places)
+    return jnp.where(seen, 0.0, masked_score)
+
+
+def attend_kernel(step, raw_ref, scale_ref, gain_ref, cos_ref, sin_ref, column_ref, line_ref,
+                  query_ref, key_ref, value_ref, mixed_ref, log_ref, bias, logs):
+    seq, columns = query_ref.shape
+    heads = columns // HD
+
+    def prepare(i, carry):
+        rows = pl.ds(pl.multiple_of(i * step, step), step)
+        cosine, sine = cos_ref[rows, :], sin_ref[rows, :]
+        for n, ref in enumerate((query_ref, key_ref)):
+            scale = scale_ref[rows, n : n + 1]
+            for h in range(heads):
+                span = slice(h * HD, (h + 1) * HD)
+                values = raw_ref[rows, n * columns + h * HD : n * columns + (h + 1) * HD]
+                values = values * scale * gain_ref[n : n + 1, span]
+                turn = pltpu.roll(values, HD // 2, 1)
+                ref[rows, span] = (values * cosine + turn * sine).astype(jnp.bfloat16)
+        value_ref[rows, :] = raw_ref[rows, 2 * columns :].astype(jnp.bfloat16)
+        return carry
+
+    lax.fori_loop(0, seq // step, prepare, 0)
+    for i in range(seq // step):
+        rows = slice(i * step, (i + 1) * step)
+        wide = (i + 1) * step
+        places = lax.broadcasted_iota(jnp.int32, (step, wide), 0) + i * step
+        bias[:, :wide] = visible_bias(
+            i * step,
+            [column_ref[rows, n : n + 1] for n in range(3)],
+            places,
+            line_ref[0:1, :wide],
+            line_ref[3:4, :wide],
+            lax.broadcasted_iota(jnp.int32, (step, wide), 1),
+        )
+
+        def head(h, carry):
+            span = pl.ds(pl.multiple_of(h * HD, HD), HD)
+            scores = across(query_ref[rows, span], key_ref[:wide, span]) * HD ** (-0.5) + bias[:, :wide]
+            top = jnp.max(scores, axis=1, keepdims=True)
+            weights = jnp.exp(scores - top)
+            total = jnp.sum(weights, axis=1, keepdims=True)
+            low = (weights / total).astype(jnp.bfloat16)
+            mixed = jnp.dot(low, value_ref[:wide, span], preferred_element_type=jnp.float32)
+            mixed_ref[rows, span] = mixed.astype(jnp.bfloat16)
+            lanes = lax.broadcasted_iota(jnp.int32, (step, 128), 1)
+            logs[...] = jnp.where(lanes == h, top + jnp.log(total), logs[...])
+            return carry
+
+        logs[...] = jnp.zeros_like(logs)
+        lax.fori_loop(0, heads, head, 0)
+        log_ref[:, rows] = jnp.transpose(logs[...])[: log_ref.shape[0]]
+
+
+def attend(raw, scales, gains, cosine, sine, path_columns, path_lines):
+    seq = raw.shape[0]
+    columns = raw.shape[1] // 3
+    step = min(256, seq)
+    vmem = pl.BlockSpec(memory_space=pltpu.VMEM)
+    low = jax.ShapeDtypeStruct((seq, columns), jnp.bfloat16)
+    return pl.pallas_call(
+        functools.partial(attend_kernel, step),
+        out_shape=(low, low, low, low, jax.ShapeDtypeStruct((8, seq), jnp.float32)),
+        in_specs=[vmem] * 7,
+        out_specs=[vmem] * 5,
+        scratch_shapes=[pltpu.VMEM((step, seq), jnp.float32), pltpu.VMEM((step, 128), jnp.float32)],
+        compiler_params=pltpu.CompilerParams(vmem_limit_bytes=50 << 20),
+        cost_estimate=pl.CostEstimate(
+            flops=4 * seq * seq * columns, bytes_accessed=16 * seq * columns, transcendentals=seq * seq
+        ),
+        name="attend",
+    )(raw, scales, gains, cosine, sine, path_columns, path_lines)
+
+
+def attend_back_kernel(step, grad_ref, w_ref, query_ref, key_ref, value_ref, log_ref, cos_ref, sin_ref,
+                       column_ref, line_ref, dq_ref, dk_ref, dv_ref, bias, mixed):
+    seq, columns = query_ref.shape
+    heads = columns // HD
+    dk_ref[...] = jnp.zeros_like(dk_ref)
+    dv_ref[...] = jnp.zeros_like(dv_ref)
+
+    def unturn(values, rows):
+        return values * cos_ref[rows, :] - pltpu.roll(values, HD // 2, 1) * sin_ref[rows, :]
+
+    for i in range(seq // step):
+        rows = slice(i * step, (i + 1) * step)
+        wide = (i + 1) * step
+        mixed[...] = across(grad_ref[rows, :], w_ref[...]).astype(jnp.bfloat16)
+        places = lax.broadcasted_iota(jnp.int32, (wide, step), 1) + i * step
+        bias[:wide, :] = visible_bias(
+            i * step,
+            [line_ref[n : n + 1, rows] for n in range(3)],
+            places,
+            column_ref[:wide, 0:1],
+            column_ref[:wide, 3:4],
+            lax.broadcasted_iota(jnp.int32, (wide, step), 0),
+        )
+
+        def head(h, carry):
+            span = pl.ds(pl.multiple_of(h * HD, HD), HD)
+            query, key, grad = query_ref[rows, span], key_ref[:wide, span], mixed[:, span]
+            scores = across(key, query) * HD ** (-0.5) + bias[:wide, :]
+            weights = jnp.exp(scores - log_ref[pl.ds(h, 1), rows])
+            grad_weights = across(value_ref[:wide, span], grad)
+            inner = jnp.sum(weights * grad_weights, axis=0, keepdims=True)
+            grad_scores = (weights * (grad_weights - inner)).astype(jnp.bfloat16)
+            dq_ref[rows, span] = unturn(turned(grad_scores, key) * HD ** (-0.5), rows)
+            dk_ref[:wide, span] += jnp.dot(grad_scores, query, preferred_element_type=jnp.float32)
+            dv_ref[:wide, span] += jnp.dot(
+                weights.astype(jnp.bfloat16), grad, preferred_element_type=jnp.float32
+            )
+            return carry
+
+        lax.fori_loop(0, heads, head, 0)
+    for i in range(seq // step):
+        rows = slice(i * step, (i + 1) * step)
+        for h in range(heads):
+            span = slice(h * HD, (h + 1) * HD)
+            dk_ref[rows, span] = unturn(dk_ref[rows, span] * HD ** (-0.5), rows)
+
+
+def attend_back(grads, w_out, query, key, value, logs, cosine, sine, path_columns, path_lines):
+    seq, columns = query.shape
+    step = min(256, seq)
+    vmem = pl.BlockSpec(memory_space=pltpu.VMEM)
+    wide = jax.ShapeDtypeStruct((seq, columns), jnp.float32)
+    return pl.pallas_call(
+        functools.partial(attend_back_kernel, step),
+        out_shape=(wide, wide, wide),
+        in_specs=[vmem] * 10,
+        out_specs=[vmem] * 3,
+        scratch_shapes=[pltpu.VMEM((seq, step), jnp.float32), pltpu.VMEM((step, columns), jnp.bfloat16)],
+        compiler_params=pltpu.CompilerParams(vmem_limit_bytes=56 << 20),
+        cost_estimate=pl.CostEstimate(
+            flops=10 * seq * seq * columns, bytes_accessed=24 * seq * columns, transcendentals=seq * seq
+        ),
+        name="attend_back",
+    )(grads, w_out, query, key, value, logs, cosine, sine, path_columns, path_lines)
 
 
 def rms_apply(values, gain):
@@ -1441,9 +1565,6 @@
     dp_groups = experts // local_experts
     capacity = 9 * tok_dev * top_count // (8 * experts)
     full_width = H * HD
-    block_rows = min(512, seq_len)
-    block_count = seq_len // block_rows
-    score_scale = HD ** (-0.5)
     everyone = ("dp", "tensor")
     direct = dp_groups == 8 and lax.axis_size("tensor") == 4
     first_expert = lax.axis_index("dp") * local_experts
@@ -1456,10 +1577,15 @@
     cots_all = lax.all_gather(cotangent, everyone, axis=0, tiled=True)
     c_slots = None if direct else dispatch(slots, None, cots_all, slot_rows)
     head_cols = w_query.shape[1]
-    local_heads = head_cols // HD
     residual_float = residual.astype(jnp.float32)
     normed_one, scale_one = rms_apply(residual_float, attn_gain)
     hidden = normed_one.astype(jnp.bfloat16)
+    path_lines = jnp.concatenate((segment_path, token_valid[None]), axis=0)
+    path_columns = path_lines.T
+    positions = jnp.sum(visible_block(segment_path, segment_path, token_valid, 0).astype(jnp.int32), axis=1) - 1
+    cosine, sine = rotation(positions, HD)
+    cosine = jnp.concatenate((cosine, cosine), axis=1)
+    sine = jnp.concatenate((-sine, sine), axis=1)
     if direct:
         hidden_all, joined_weight, gathered_out = start_exchange(hidden, w_query, w_key, w_value, w_out, 3)
     else:
@@ -1471,50 +1597,20 @@
     projected = jnp.dot(hidden_all, joined_weight, preferred_element_type=jnp.float32)
     q_raw = projected[:, :head_cols]
     k_raw = projected[:, head_cols : 2 * head_cols]
-    value_low = projected[:, 2 * head_cols :].astype(jnp.bfloat16).reshape(seq_len, local_heads, HD)
     query_sq, key_sq = tensor_sums((jnp.sum(q_raw * q_raw, axis=1), jnp.sum(k_raw * k_raw, axis=1)))
     query_scale = lax.rsqrt(query_sq / full_width + norm_eps)[:, None]
     key_scale = lax.rsqrt(key_sq / full_width + norm_eps)[:, None]
     query_gain_dev = lax.dynamic_slice_in_dim(query_gain, tensor_rank * head_cols, head_cols)
     key_gain_dev = lax.dynamic_slice_in_dim(key_gain, tensor_rank * head_cols, head_cols)
-    block_starts = lax.iota(jnp.int32, block_count) * block_rows
-
-    def block_mask(row_first):
-        row_paths = lax.dynamic_slice_in_dim(segment_path, row_first, block_rows, 1)
-        return visible_block(row_paths, segment_path, token_valid, row_first)
-
-    def count_seen(row_first):
-        return jnp.sum(block_mask(row_first).astype(jnp.int32), axis=1)
-
-    positions = lax.map(count_seen, block_starts).reshape(seq_len) - 1
-    cosine, sine = rotation(positions, HD)
-    query_low = rotate(
-        (q_raw * query_scale * query_gain_dev).reshape(seq_len, local_heads, HD), cosine, sine
-    ).astype(jnp.bfloat16)
-    key_low = rotate(
-        (k_raw * key_scale * key_gain_dev).reshape(seq_len, local_heads, HD), cosine, sine
-    ).astype(jnp.bfloat16)
-
-    def attend(row_first):
-        visible = block_mask(row_first)
-        query_block = lax.dynamic_slice_in_dim(query_low, row_first, block_rows, 0)
-        scores = (
-            jnp.einsum("qhd,khd->hqk", query_block, key_low, preferred_element_type=jnp.float32)
-            * score_scale
-        )
-        scores = jnp.where(visible[None], scores, masked_score)
-        top_score = jnp.max(scores, axis=-1, keepdims=True)
-        exp_scores = jnp.exp(scores - top_score)
-        total = jnp.sum(exp_scores, axis=-1, keepdims=True)
-        weights_low = (exp_scores / total).astype(jnp.bfloat16)
-        mixed_block = jnp.einsum(
-            "hqk,khd->qhd", weights_low, value_low, preferred_element_type=jnp.float32
-        )
-        return (mixed_block.astype(jnp.bfloat16), (top_score + jnp.log(total))[..., 0])
-
-    mixed_blocks, log_totals = lax.map(attend, block_starts)
-    attn_mixed = mixed_blocks.reshape(seq_len, head_cols)
-
+    query_low, key_low, value_low, attn_mixed, log_totals = attend(
+        projected,
+        jnp.concatenate((query_scale, key_scale), axis=1),
+        jnp.stack((query_gain_dev, key_gain_dev)),
+        cosine,
+        sine,
+        path_columns,
+        path_lines,
+    )
     if direct:
         x_one, hidden_two, gates_own = mixed_out(attn_mixed, gathered_out, residual, moe_gain, router.T, 4)
         probs = gates_own.T
@@ -1581,61 +1677,18 @@
     else:
         grad_attn_all = lax.all_gather(grad_attn_low, "tensor", axis=0, tiled=True)
         early_sums = lax.psum(early_sums, everyone)
-    grad_mixed = (
-        lax.dot_general(
-            grad_attn_all,
-            gathered_out,
-            (((1,), (1,)), ((), ())),
-            preferred_element_type=jnp.float32,
-        )
-        .astype(jnp.bfloat16)
-        .reshape(seq_len, local_heads, HD)
-    )
-
-    def attend_back(carry, pieces):
-        grad_key_sum, grad_value_sum = carry
-        row_first, log_total = pieces
-        visible = block_mask(row_first)
-        query_block = lax.dynamic_slice_in_dim(query_low, row_first, block_rows, 0)
-        grad_block = lax.dynamic_slice_in_dim(grad_mixed, row_first, block_rows, 0)
-        scores = (
-            jnp.einsum("qhd,khd->hqk", query_block, key_low, preferred_element_type=jnp.float32)
-            * score_scale
-        )
-        scores = jnp.where(visible[None], scores, masked_score)
-        weights = jnp.exp(scores - log_total[..., None])
-        grad_weights = jnp.einsum(
-            "qhd,khd->hqk", grad_block, value_low, preferred_element_type=jnp.float32
-        )
-        inner = jnp.sum(weights * grad_weights, axis=-1, keepdims=True)
-        grad_scores = (weights * (grad_weights - inner)).astype(jnp.bfloat16)
-        grad_query_block = (
-            jnp.einsum("hqk,khd->qhd", grad_scores, key_low, preferred_element_type=jnp.float32)
-            * score_scale
-        )
-        grad_key_sum = (
-            grad_key_sum
-            + jnp.einsum(
-                "hqk,qhd->khd", grad_scores, query_block, preferred_element_type=jnp.float32
-            )
-            * score_scale
-        )
-        grad_value_sum = grad_value_sum + jnp.einsum(
-            "hqk,qhd->khd",
-            weights.astype(jnp.bfloat16),
-            grad_block,
-            preferred_element_type=jnp.float32,
-        )
-        return ((grad_key_sum, grad_value_sum), grad_query_block)
-
-    zero_heads = jnp.zeros((seq_len, local_heads, HD), jnp.float32)
-    (grad_key_all, grad_value_all), grad_query_blocks = lax.scan(
-        attend_back, (zero_heads, zero_heads), (block_starts, log_totals)
-    )
-    grad_q_norm = unrotate(
-        grad_query_blocks.reshape(seq_len, local_heads, HD), cosine, sine
-    ).reshape(seq_len, head_cols)
-    grad_k_norm = unrotate(grad_key_all, cosine, sine).reshape(seq_len, head_cols)
+    grad_q_norm, grad_k_norm, grad_value_all = attend_back(
+        grad_attn_all,
+        gathered_out,
+        query_low,
+        key_low,
+        value_low,
+        log_totals,
+        cosine,
+        sine,
+        path_columns,
+        path_lines,
+    )
     query_inner, key_inner = tensor_sums(
         (
             jnp.sum(grad_q_norm * query_gain_dev * q_raw, axis=1),
@@ -1649,10 +1702,8 @@
         k_raw, key_scale, key_gain_dev, grad_k_norm, key_inner[:, None], full_width
     )
     grad_joined = jnp.concatenate(
-        (grad_q_raw, grad_k_raw, grad_value_all.reshape(seq_len, head_cols)), axis=1
+        (grad_q_raw, grad_k_raw, grad_value_all), axis=1
     ).astype(jnp.bfloat16)
-    out_part, grad_joined = lax.optimization_barrier((out_part, grad_joined))
-    block_out = (x_one + sum_over_tensor(out_part).astype(jnp.float32)).astype(jnp.bfloat16)
     zero_width = jnp.zeros((full_width,), jnp.float32)
     grad_query_full = lax.dynamic_update_slice_in_dim(
         zero_width, grad_query_gain_dev, tensor_rank * head_cols, 0
@@ -1708,6 +1759,8 @@
             grad_out_weight, "dp", scatter_dimension=1, tiled=True
         ).astype(jnp.float32)
         gains = lax.psum(jnp.stack((grad_query_full, grad_key_full, grad_attn_gain_part)), everyone)
+    out_part, grad_input = lax.optimization_barrier((out_part, grad_input))
+    block_out = (x_one + sum_over_tensor(out_part).astype(jnp.float32)).astype(jnp.bfloat16)
     return (
         block_out,
         grad_input,

time: 1280 us -> 1230 us (0.961)
  waiting for transfers between devices: 13.1 us -> 90.3 us
  matrix products: 80.1 us -> 15 us
  other arithmetic: 70.6 us -> 35 us
  local copies, waits for them, and re-layouts: 45.1 us -> 21.5 us
    reduce_scatter x1, waiting for transfers between devices: 0.01 us -> 71.2 us  [sum_over_tensor(): return lax.psum_scatter(part, 'tensor', scatter_dimension=0, tiled=True)]
    dot_general x15 -> x0, matrix products: 65.1 us -> none  [the longest x2 15.6 us: attend_back(): jnp.einsum('qhd,khd->hqk', grad_block, value_low, preferred_element_type=...]
    pallas_call x0 -> x2, Pallas kernels: none -> 43.9 us  [the longest x1 25.2 us: attend_back(): pl.pallas_call(functools.partial(attend_back_kernel, step), out_shape=(wi...]
    pallas_call x1, Pallas kernels: 164 us -> 123 us  [last_exchange(): pl.pallas_call(functools.partial(last_kernel, line), out_shape=(jax.Shape...]
    all_gather x1, waiting for transfers between devices: 0.02 us -> 18.3 us  [body(): cots_all = lax.all_gather(cotangent, everyone, axis=0, tiled=True)]
  transfers between devices with their start and end apart: 4 -> 4, of which waited for: 1 -> 2; matrix products, arithmetic and copies ran while one was open for 13% -> 4% of each run, Pallas kernels for 40% -> 42%
where the time goes in v6:
time: 1230 us; the launch traced here: 1220 us
  Pallas kernels  1020 us (83%)
  waiting for transfers between devices  90.3 us (7%)
  other arithmetic  35 us (3%)
  local copies, waits for them, and re-layouts  21.5 us (2%)
  blocking collectives  20.7 us (2%)
  matrix products  15 us (1%)
  between operations  14.8 us (1%)
    pallas_call x1, Pallas kernels, reduce_all(): pl.pallas_call(functools.partial(reduce_kernel, line), out_shape=(jax.Sha...  184 us
    pallas_call x1, Pallas kernels, gather_dispatch(): pl.pallas_call(functools.partial(gather_dispatch_kernel, line, rows), out...  182 us
    pallas_call x1, Pallas kernels, mixed_out(): pl.pallas_call(functools.partial(mixed_out_kernel, line), out_shape=(jax....  143 us
    pallas_call x1, Pallas kernels, expert_pass(): pl.pallas_call(kernel, grid_spec=pltpu.PrefetchScalarGridSpec(num_scalar_...  141 us
    pallas_call x1, Pallas kernels, last_exchange(): pl.pallas_call(functools.partial(last_kernel, line), out_shape=(jax.Shape...  123 us
    pallas_call x1, Pallas kernels, back_gather(): pl.pallas_call(functools.partial(back_gather_kernel, line), out_shape=(ja...  105 us
    pallas_call x1, Pallas kernels, start_exchange(): pl.pallas_call(functools.partial(start_kernel, line), out_shape=(jax.Shap...  102 us
    reduce_scatter x1, waiting for transfers between devices, sum_over_tensor(): return lax.psum_scatter(part, 'tensor', scatter_dimension=0, tiled=True)  71.2 us
  transfers between devices with their start and end apart: 4, of which 2 were waited for; matrix products, arithmetic and copies ran while one was open for 4% of the time, Pallas kernels for 42%

profile of v6, /device:TPU:0, one launch (start us, length us, event | category | flops | bytes accessed | tf_op | source)
XLA Modules:
  0.0 1221.6 jit_solution(15341688729971664045)
XLA Ops:
  7.3 0.8 dynamic-slice_compare_fusion
  8.1 1.0 select_reduce_fusion
  9.1 5.2 convert_reduce_fusion
  14.3 0.6 fusion.9
  15.0 0.7 all-gather.5.cloned.1.call-update
  15.7 0.3 fusion.3
  16.0 1.3 fusion.5.hidden_ref
  17.3 102.3 %start_exchange.1 = (bf16[1024,2048]{1,0:T(8,128)(2,1)}, bf16[2048,1536]{1,0:T(8,128)(2,1)}, bf16[512,2048]{1,0:T(8,128)(2,1)}) custom-call(bf16[256,2048]{1,0:T(8,128)(2,1)} %fusion.5.hidden_ref, bf16[256,512]{1,0:T(8,128)(2,1)} %wq_ref.1, bf16[256,512]{1,0:T(8,128)(2,1)} %wk_ref.1, bf16[256,512]{1,0:T(8,128)(2,1)} %wv_ref.1, bf16[512,256]{1,0:T(8,128)(2,1)} %wo_ref.1), custom_call_target="tpu_custom_call" | custom-call | bytes 157286400 | tf_op jit(solution)/shard_map/start_exchange/pallas_call | solution.py:917
  119.6 10.0 fusion.15.raw_ref
  129.6 2.6 copy-done.12
  132.3 0.3 multiply_reduce_fusion.8
  132.6 11.1 all-reduce.1
  143.7 0.6 multiply_multiply_fusion
  144.3 0.6 copy-done.27
  144.9 0.2 copy.50.scale_ref
  145.1 0.8 dynamic_slice.13
  145.9 0.8 dynamic_slice.12
  146.7 0.2 copy.51.column_ref
  147.0 2.8 convert_reduce_fusion.1
  149.9 1.9 fusion.7
  151.8 0.3 pad_maximum_fusion.1
  152.2 18.7 %attend.1 = (bf16[1024,512]{1,0:T(8,128)(2,1)S(1)}, bf16[1024,512]{1,0:T(8,128)(2,1)}, bf16[1024,512]{1,0:T(8,128)(2,1)}, bf16[1024,512]{1,0:T(8,128)(2,1)}, f32[8,1024]{1,0:T(8,128)S(1)}) custom-call(f32[1024,1536]{1,0:T(8,128)} %copy-done.12, f32[1024,2]{1,0:T(8,128)S(1)} %copy.50.scale_ref, f32[2,512]{1,0:T(2,128)S(1)} %pad_maximum_fusion.4.gain_ref, ...), custom_call_target="tpu_custom_call" | custom-call | flops 2147483648 | bytes 8388608 | tf_op jit(solution)/shard_map/attend/pallas_call | solution.py:1425
  170.9 1.0 copy-done.9
  171.9 0.6 copy-done.10
  172.5 142.8 %mixed_out.1 = (f32[256,2048]{1,0:T(8,128)}, bf16[256,2048]{1,0:T(8,128)(2,1)}, f32[64,256]{1,0:T(8,128)}) custom-call(bf16[1024,512]{1,0:T(8,128)(2,1)} %get-tuple-element.50.mixed_ref, bf16[512,2048]{1,0:T(8,128)(2,1)} %get-tuple-element.51.w_ref, bf16[256,2048]{1,0:T(8,128)(2,1)} %residual_ref.3, f32[1,2048]{1,0:T(1,128)} %bitcast.54, ...), custom_call_target="tpu_custom_call" | custom-call | bytes 157286400 | tf_op jit(solution)/shard_map/mixed_out/pallas_call | solution.py:1031
  315.3 0.9 dynamic-slice_convert_fusion.slots_ref
  316.3 18.3 %all-gather.5.cloned.1.call-done.cots_ref = bf16[8192,2048]{1,0:T(8,128)(2,1)} async-done(((bf16[256,2048]{1,0:T(8,128)(2,1)}), bf16[8192,2048]{1,0:T(8,128)(2,1)}) %all-gather.5.cloned.1.call-update) | async-done | bytes 33554448 | tf_op jit(solution)/shard_map/all_gather | solution.py:1577
  334.6 1.2 copy-done.4
  335.8 0.8 copy-done.7
  336.6 182.0 %gather_dispatch.1 = (bf16[8192,2048]{1,0:T(8,128)(2,1)}, f32[2048,256]{1,0:T(8,128)}, bf16[8,1280,2048]{2,1,0:T(8,128)(2,1)}, bf16[8,1280,2048]{2,1,0:T(8,128)(2,1)}, f32[8,1280,128]{2,1,0:T(8,128)S(1)}) custom-call(s32[32,8,256]{2,1,0:T(8,128)S(1)} %dynamic-slice_convert_fusion.slots_ref, bf16[256,2048]{1,0:T(8,128)(2,1)S(1)} %copy-done.4, ...), custom_call_target="tpu_custom_call" | custom-call | flops 21474836480 | bytes 209715200 | tf_op jit(solution)/shard_map/gather_dispatch/pallas_call | solution.py:487
  518.6 2.3 copy-done.11
  520.9 140.7 %experts.1 = (bf16[32,8,48,2048]{3,2,1,0:T(8,128)(2,1)}, bf16[32,8,48,2176]{3,2,1,0:T(8,128)(2,1)}, f32[8,2048,256]{2,1,0:T(8,128)}, f32[8,2048,256]{2,1,0:T(8,128)}, f32[8,256,2048]{2,1,0:T(8,128)}) custom-call(s32[1]{0:T(128)} %bitcast.13.first_ref, bf16[8,1280,2048]{2,1,0:T(8,128)(2,1)} %get-tuple-element.55.x_ref, ...), custom_call_target="tpu_custom_call" | custom-call | flops 96636764160 | bytes 243269632 | tf_op jit(solution)/shard_map/experts/pallas_call | solution.py:174
  661.7 184.1 %reduce_all.1 = (f32[256,2176]{1,0:T(8,128)}, bf16[8192,2048]{1,0:T(8,128)(2,1)}) custom-call(s32[32,8,256]{2,1,0:T(8,128)} %copy-done.3, bf16[32,8,48,2176]{3,2,1,0:T(8,128)(2,1)} %get-tuple-element.58.grads_ref, bf16[32,8,48,2048]{3,2,1,0:T(8,128)(2,1)} %get-tuple-element.59.outs_ref), custom_call_target="tpu_custom_call" | custom-call | flops 26575110144 | bytes 103809024 | tf_op jit(solution)/shard_map/reduce_all/pallas_call | solution.py:746
  845.8 0.3 reduce-scatter.5.cloned.1.call-start
  846.0 0.5 copy-done.8
  846.6 0.1 copy.52
  846.8 0.5 copy-done.13
  847.4 0.2 multiply_reduce_fusion.6
  847.6 1.0 fusion.8
  848.6 1.7 fusion.11
  850.3 3.3 multiply_reduce_fusion.4
  853.6 0.9 maximum_maximum_fusion.sums_ref
  854.5 2.4 fusion.12
  856.9 104.7 %back_gather.1 = (bf16[1024,2048]{1,0:T(8,128)(2,1)}, f32[72,2048]{1,0:T(8,128)}) custom-call(bf16[256,2048]{1,0:T(8,128)(2,1)} %get-tuple-element.96.own_ref, f32[72,2048]{1,0:T(8,128)} %maximum_maximum_fusion.sums_ref), custom_call_target="tpu_custom_call" | custom-call | bytes 157286400 | tf_op jit(solution)/shard_map/back_gather/pallas_call | solution.py:1155
  961.6 25.2 %attend_back.1 = (f32[1024,512]{1,0:T(8,128)}, f32[1024,512]{1,0:T(8,128)}, f32[1024,512]{1,0:T(8,128)}) custom-call(bf16[1024,2048]{1,0:T(8,128)(2,1)} %get-tuple-element.62.grad_ref.attn_ref, bf16[512,2048]{1,0:T(8,128)(2,1)} %get-tuple-element.51.w_ref, bf16[1024,512]{1,0:T(8,128)(2,1)} %copy-done.9, bf16[1024,512]{1,0:T(8,128)(2,1)} %get-tuple-element.64.key_ref, ...), custom_call_target="tpu_custom_call" | custom-call | flops 5368709120 | bytes 12582912 | tf_op jit(solution)/shard_map/attend_back/pallas_call | solution.py:1491
  986.8 2.0 convert.11
  988.8 0.4 copy-done.16
  989.3 2.8 multiply_reduce_fusion.1
  992.1 9.7 all-reduce
  1001.8 4.3 subtract_convert_fusion.1
  1006.1 1.8 pad_maximum_fusion.joined_ref
  1007.9 0.7 maximum_maximum_fusion.1.gains_ref
  1008.6 123.5 %last_exchange.1 = (f32[256,2048]{1,0:T(8,128)}, f32[256,512]{1,0:T(8,128)}, f32[256,512]{1,0:T(8,128)}, f32[256,512]{1,0:T(8,128)}, f32[512,256]{1,0:T(8,128)}, /*index=5*/f32[8,2048]{1,0:T(8,128)}) custom-call(bf16[1024,1536]{1,0:T(8,128)(2,1)} %pad_maximum_fusion.joined_ref, bf16[2048,1536]{1,0:T(8,128)(2,1)} %get-tuple-element.49.weight_ref, ...), custom_call_target="tpu_custom_call" | custom-call | bytes 262144000 | tf_op jit(solution)/shard_map/last_exchange/pallas_call | solution.py:1315
  1132.2 1.0 copy-done.24
  1133.2 0.6 slice.47
  1133.8 1.6 fusion.13
  1135.4 0.8 slice_bitcast_fusion
  1136.2 71.2 %reduce-scatter.5.cloned.1.call-done = bf16[256,2048]{1,0:T(8,128)(2,1)} async-done(((bf16[1024,2048]{1,0:T(8,128)(2,1)}), bf16[256,2048]{1,0:T(8,128)(2,1)}) %reduce-scatter.5.cloned.1.call-update) | async-done | bytes 1048592 | tf_op jit(solution)/shard_map/reduce_scatter | solution.py:1536
  1207.4 2.6 add_convert_fusion
  1210.1 1.3 copy.61
  1211.5 0.8 copy.62
  1212.3 0.8 copy.63
  1213.0 0.8 copy.64
  1213.8 0.8 copy.65
  (98 shorter events, 0.7 us)
Async XLA Ops:
  7.2 8.5 copy-start.15
  7.2 8.8 copy-start.32
  7.2 308.1 %all-gather.3.cloned.1.call-start = ((), (), s32[]{:S(2)}) async-start(), calls=%async_computation.2 | async-start | bytes 1081344 | tf_op jit(solution)/shard_map/all_gather | solution.py:1574
  14.9 319.7 %all-gather.5.cloned.1.call-start = ((), (), s32[]{:S(2)}) async-start(), calls=%async_computation.3 | async-start | bytes 34603008 | tf_op jit(solution)/shard_map/all_gather | solution.py:1577
  15.7 1116.5 %reduce-scatter.3.cloned.1.call-start = ((), (), s32[]{:S(2)}) async-start(), calls=%async_computation.4 | async-start | bytes 37748736 | tf_op jit(solution)/shard_map/reduce_scatter | solution.py:1532
  129.6 2.6 copy-start.12
  132.3 14.4 %copy-start.25 = (s32[3,1024]{1,0:T(4,128)S(1)}, s32[3,1024]{1,0:T(4,128)}, u32[]{:S(2)}) copy-start(s32[3,1024]{1,0:T(4,128)} %param.31) | copy-start | bytes 36868
  132.3 14.4 %copy-start.31 = (s32[1024]{0:T(1024)S(1)}, s32[1024]{0:T(1024)}, u32[]{:S(2)}) copy-start(s32[1024]{0:T(1024)} %param.32) | copy-start | bytes 12292
  144.3 0.6 copy-start.27
  144.3 0.6 copy-start.29
  145.9 6.2 copy-start.33
  146.7 5.5 copy-start.35
  146.9 5.2 copy-start.2
  147.0 5.2 copy-start.6
  152.1 18.8 %copy-start = (f32[1024,128]{1,0:T(8,128)}, f32[1024,128]{1,0:T(8,128)S(1)}, u32[]{:S(2)}) copy-start(f32[1024,128]{1,0:T(8,128)S(1)} %get-tuple-element.118.cos_ref) | copy-start | bytes 1572868
  152.2 18.8 %copy-start.1 = (f32[1024,128]{1,0:T(8,128)}, f32[1024,128]{1,0:T(8,128)S(1)}, u32[]{:S(2)}) copy-start(f32[1024,128]{1,0:T(8,128)S(1)} %get-tuple-element.119.sin_ref) | copy-start | bytes 1572868
  170.9 1.0 copy-start.9
  171.9 0.6 copy-start.10
  316.3 202.3 %copy-start.3 = (s32[32,8,256]{2,1,0:T(8,128)}, s32[32,8,256]{2,1,0:T(8,128)S(1)}, u32[]{:S(2)}) copy-start(s32[32,8,256]{2,1,0:T(8,128)S(1)} %dynamic-slice_convert_fusion.slots_ref) | copy-start | bytes 786436
  334.6 1.2 copy-start.4
  335.8 0.8 copy-start.7
  518.6 2.3 copy-start.11
  845.7 0.8 copy-start.8
  845.7 1.6 copy-start.13
  845.8 2.8 copy-start.5
  845.8 361.7 %reduce-scatter.5.cloned.1.call-start = ((), (), s32[]{:S(2)}) async-start(), calls=%async_computation.5 | async-start | bytes 5242880 | tf_op jit(solution)/shard_map/reduce_scatter | solution.py:1536
  847.3 3.0 copy-start.19
  847.3 3.0 copy-start.26
  850.3 4.2 copy-start.17
  961.6 27.2 %slice-start = ((s8[6291456]{0:T(1024)(128)(4,1)}), s8[4194304]{0:T(1024)(128)(4,1)S(1)}, s32[]{:S(2)}) async-start(s8[6291456]{0:T(1024)(128)(4,1)} %bitcast.49), calls=%async_computation.6 | async-start | bytes 8388608
  961.6 27.2 %slice-start.1 = ((s8[6291456]{0:T(1024)(128)(4,1)}), s8[2097152]{0:T(1024)(128)(4,1)S(1)}, s32[]{:S(2)}) async-start(s8[6291456]{0:T(1024)(128)(4,1)} %bitcast.49), calls=%async_computation.7 | async-start | bytes 4194304
  986.8 2.4 copy-start.16
  986.8 2.4 copy-start.28
  986.8 2.4 copy-start.30
  986.8 2.4 copy-start.34
  986.8 2.4 copy-start.36
  989.2 12.6 %copy-start.37 = (f32[1024]{0:T(1024)S(1)}, f32[1024]{0:T(1024)}, u32[]{:S(2)}) copy-start(f32[1024]{0:T(1024)} %get-tuple-element.111) | copy-start | bytes 12292
  989.2 12.6 %copy-start.38 = (f32[1024]{0:T(1024)S(1)}, f32[1024]{0:T(1024)}, u32[]{:S(2)}) copy-start(f32[1024]{0:T(1024)} %get-tuple-element.117) | copy-start | bytes 12292
  1132.1 1.1 copy-start.24
  1132.1 75.3 %copy-start.14 = (f32[256,2048]{1,0:T(8,128)S(1)}, f32[256,2048]{1,0:T(8,128)}, u32[]{:S(2)}) copy-start(f32[256,2048]{1,0:T(8,128)} %get-tuple-element.52) | copy-start | bytes 6291460
  1207.4 2.6 copy-start.18
  1210.1 1.4 copy-start.23
  1210.1 2.2 copy-start.22
  1211.5 1.6 copy-start.21
  1211.5 2.4 copy-start.20
Sparse Core Ops, SparseCore 0:
  15.0 57.8 all-gather.2
  75.9 258.6 all-gather.4
  845.9 268.1 reduce-scatter.2
  1132.3 75.0 reduce-scatter.4

commit v7 on v6

--- a/solution.py
+++ b/solution.py
@@ -109,7 +109,7 @@
 
 
 def expert_kernel(rows, first_ref, x_ref, c_ref, gate_ref, wg_ref, wu_ref, wd_ref,
-                  o_ref, dx_ref, dwg_ref, dwu_ref, dwd_ref):
+                  o_ref, dx_ref, pre_ref, gated_ref):
     expert = pl.program_id(0)
     tile, width = x_ref.shape[1:]
     units = wg_ref.shape[2]
@@ -148,16 +148,50 @@
     lanes = lax.broadcasted_iota(jnp.int32, (tile, 128), 1)
     dx_ref[:, 0, :, width:] = spread(jnp.where(lanes == first_ref[0] + expert, grad_gate, 0.0))
 
-    @pl.when(pl.program_id(1) == 0)
-    def _():
-        for ref in (dwg_ref, dwu_ref, dwd_ref):
-            ref[...] = jnp.zeros_like(ref)
-
+    pre_ref[0, :, :units] = grad_gate_pre
+    pre_ref[0, :, units:] = grad_up_pre
+    gated_ref[0] = gated
+
+
+def weight_terms(x_ref, c_ref, pre_ref, gated_ref, gate_ref, up_ref, down_ref):
+    units = gated_ref.shape[1]
+    width = x_ref.shape[1]
+    step = min(512, width)
     for first in range(0, width, step):
         part = slice(first, first + step)
-        dwg_ref[0, part, :] += turned(x_ref[0, :, part], grad_gate_pre)
-        dwu_ref[0, part, :] += turned(x_ref[0, :, part], grad_up_pre)
-        dwd_ref[0, :, part] += turned(gated, c_ref[0, :, part])
+        both = turned(x_ref[:, part], pre_ref[...])
+        gate_ref[part, :] = both[:, :units]
+        up_ref[part, :] = both[:, units:]
+        down_ref[:, part] = turned(gated_ref[...], c_ref[:, part])
+
+
+def weight_kernel(x_ref, c_ref, pre_ref, gated_ref, gate_ref, up_ref, down_ref):
+    weight_terms(*(r.at[0] for r in (x_ref, c_ref, pre_ref, gated_ref, gate_ref, up_ref, down_ref)))
+
+
+def weight_grads(x_slots, c_slots, pre, gated):
+    experts, total, width = x_slots.shape
+    units = gated.shape[2]
+    step = min(512, width)
+    part = pl.BlockSpec((1, total, step), lambda e, j: (e, 0, j))
+    tall = pl.BlockSpec((1, step, units), lambda e, j: (e, j, 0))
+    return pl.pallas_call(
+        weight_kernel,
+        grid=(experts, width // step),
+        out_shape=(
+            jax.ShapeDtypeStruct((experts, width, units), jnp.float32),
+            jax.ShapeDtypeStruct((experts, width, units), jnp.float32),
+            jax.ShapeDtypeStruct((experts, units, width), jnp.float32),
+        ),
+        in_specs=[
+            part, part,
+            pl.BlockSpec((1, total, 2 * units), lambda e, j: (e, 0, 0)),
+            pl.BlockSpec((1, total, units), lambda e, j: (e, 0, 0)),
+        ],
+        out_specs=[tall, tall, pl.BlockSpec((1, units, step), lambda e, j: (e, 0, j))],
+        compiler_params=pltpu.CompilerParams(vmem_limit_bytes=50 << 20),
+        name="weight_grads",
+    )(x_slots, c_slots, pre, gated)
 
 
 def expert_pass(first_expert, x_slots, c_slots, gate_slots, w_gate, w_up, w_down, blocks, room):
@@ -180,20 +214,20 @@
             out_specs=[
                 pl.BlockSpec((group, 1, room, width), lambda e, r, _: (r, e, 0, 0)),
                 pl.BlockSpec((group, 1, room, width + extra), lambda e, r, _: (r, e, 0, 0)),
-                tall, tall, wide,
+                pl.BlockSpec((1, tile, 2 * units), lambda e, r, _: (e, r, 0)),
+                pl.BlockSpec((1, tile, units), lambda e, r, _: (e, r, 0)),
             ],
         ),
         out_shape=(
             jax.ShapeDtypeStruct((blocks, experts, room, width), jnp.bfloat16),
             jax.ShapeDtypeStruct((blocks, experts, room, width + extra), jnp.bfloat16),
-            jax.ShapeDtypeStruct(w_gate.shape, jnp.float32),
-            jax.ShapeDtypeStruct(w_up.shape, jnp.float32),
-            jax.ShapeDtypeStruct(w_down.shape, jnp.float32),
+            jax.ShapeDtypeStruct((experts, total, 2 * units), jnp.bfloat16),
+            jax.ShapeDtypeStruct((experts, total, units), jnp.bfloat16),
         ),
         compiler_params=pltpu.CompilerParams(vmem_limit_bytes=60 << 20),
         cost_estimate=pl.CostEstimate(
-            flops=18 * experts * total * width * units,
-            bytes_accessed=8 * experts * total * width + 18 * experts * width * units,
+            flops=12 * experts * total * width * units,
+            bytes_accessed=8 * experts * total * width + 6 * experts * width * units,
             transcendentals=experts * total * units,
         ),
         name="experts",
@@ -414,23 +448,6 @@
         for wanted, copy in sends(m):
             pl.when((m < last) & wanted)(copy.start)
 
-        @pl.when(m < chips)
-        def _():
-            for copy in load_c(m):
-                copy.wait()
-
-            @pl.when(m > 0)
-            def _():
-                store(stage_c, c_out, 0, m - 1).wait()
-
-            pick(in_c, stage_c, m // 8, m // 4 % 2, m % 4, False)
-            store(stage_c, c_out, 0, m).start()
-
-            @pl.when(m + 1 < chips)
-            def _():
-                for copy in load_c(m + 1):
-                    copy.start()
-
         back = m - lag
         q = (back + 8) % 4
         i = (back + 8) // 4 - 2 - (q + 1) // 2
@@ -438,6 +455,7 @@
         held = i * live.astype(jnp.int32)
         yy, xx = (y + q // 2) % 2, (x + q % 2) % 2
         zz = near_first(z, held)
+        chip = (yy * 2 + xx) * 4 + zz
 
         @pl.when(live)
         def _():
@@ -446,8 +464,26 @@
                 landed(span(n, block), recv_sem.at[n, block])
             for copy in load_x(yy, xx, zz):
                 copy.start()
-            chip = (yy * 2 + xx) * 4 + zz
-
+
+        @pl.when(m < chips)
+        def _():
+            for copy in load_c(m):
+                copy.wait()
+
+            @pl.when(m > 0)
+            def _():
+                store(stage_c, c_out, 0, m - 1).wait()
+
+            pick(in_c, stage_c, m // 8, m // 4 % 2, m % 4, False)
+            store(stage_c, c_out, 0, m).start()
+
+            @pl.when(m + 1 < chips)
+            def _():
+                for copy in load_c(m + 1):
+                    copy.start()
+
+        @pl.when(live)
+        def _():
             @pl.when(q + held > 0)
             def _():
                 store(stage_x, x_out, 1, chip).wait()
@@ -833,8 +869,8 @@
                 pl.when(self.sends(sign, step))(self.copy(sign, step).wait_send)
 
 
-def start_kernel(line, hidden_ref, wq_ref, wk_ref, wv_ref, wo_ref, hidden_out, joined_out, wo_out,
-                 local_sem, line_send, line_recv, plane_send, plane_recv):
+def start_kernel(line, hidden_ref, wq_ref, wk_ref, wv_ref, wo_ref, slots_ref, hidden_out, joined_out, wo_out, slots_out,
+                 local_sem, line_send, line_recv, plane_send, plane_recv, slot_send, slot_recv, slot_line_send, slot_line_recv):
     y, x, core, z = place()
     owns = (wq_ref, wk_ref, wv_ref, wo_ref)
     near_x, near_y, sibling = (y, 1 - x, core, z), (1 - y, x, core, z), (y, x, 1 - core, z)
@@ -870,10 +906,39 @@
             return joined_out.at[pl.ds(group * rows, rows), pl.ds(n * columns, columns)]
         return wo_out.at[pl.ds(0, rows), pl.ds(pl.multiple_of(group * columns, columns), columns)]
 
-    greet(line)
+    barrier = pltpu.get_barrier_semaphore()
+    shifts = [(dy, dx, dc) for dy in range(2) for dx in range(2) for dc in range(2) if dy + dx + dc]
+    plane = [((y + dy) % 2, (x + dx) % 2, (core + dc) % 2, z) for dy, dx, dc in shifts]
+    for other_spot in plane:
+        pl.semaphore_signal(barrier, inc=1, device_id=peer(*other_spot), device_id_type=MESH)
+    for step in (-1, 1):
+
+        @pl.when((z + step >= 0) & (z + step < line))
+        def _():
+            pl.semaphore_signal(barrier, inc=1, device_id=peer(y, x, core, z + step), device_id_type=MESH)
+
+    pl.semaphore_wait(barrier, 7 + (z + line - 1) // line + (2 * line - 2 - z) // line)
+    experts = slots_out.shape[1]
+    group = peer(y, x, core, z)[0]
+    slot_copies = []
+    for n, other_spot in enumerate(plane):
+        their_group = peer(*other_spot)[0]
+        slot_copies.append(
+            remote(
+                slots_ref.at[pl.ds(their_group * experts, experts)], slots_out.at[z * 8 + group],
+                slot_send.at[n], slot_recv.at[group], other_spot,
+            )
+        )
+    own_slots = pltpu.make_async_copy(
+        slots_ref.at[pl.ds(group * experts, experts)], slots_out.at[z * 8 + group], local_sem.at[5]
+    )
+    own_slots.start()
+    slot_line = LineGather(slots_out.at[pl.ds(z * 8, 8)], slots_out, slot_line_send, slot_line_recv, line)
     hidden = LineGather(hidden_ref, hidden_out, line_send, line_recv, line)
     locals_ = [pltpu.make_async_copy(hidden_ref, hidden.view(z), local_sem.at[4])]
     locals_ += [pltpu.make_async_copy(owns[n], view(n, y, x), local_sem.at[n]) for n in range(4)]
+    for slot_copy in slot_copies:
+        slot_copy.start()
     hidden.begin()
     for n in range(4):
         for kind in ("x", "y", "s"):
@@ -887,12 +952,19 @@
         landed(view(n, 1 - y, x), plane_recv.at[1, n])
         copy("fx", n).start()
         copy("sy", n).start()
+    own_slots.wait()
+    for other_spot in plane:
+        their_group = peer(*other_spot)[0]
+        landed(slots_out.at[z * 8 + their_group], slot_recv.at[their_group])
+    slot_line.begin()
     hidden.advance(0)
+    slot_line.advance(0)
     for n in range(4):
         landed(view(n, 1 - y, 1 - x, 0), plane_recv.at[3, n])
         landed(view(n, 1 - y, 1 - x, 1), plane_recv.at[4, n])
         copy("sf", n).start()
     for step in range(1, line - 1):
+        slot_line.advance(step)
         hidden.advance(step)
     for n in range(4):
         landed(other(n, y, x), plane_recv.at[2, n])
@@ -900,6 +972,9 @@
         landed(other(n, 1 - y, x), plane_recv.at[6, n])
         landed(other(n, 1 - y, 1 - x), plane_recv.at[7, n])
     hidden.finish()
+    slot_line.finish()
+    for slot_copy in slot_copies:
+        slot_copy.wait_send()
     for n in range(4):
         for kind in kinds:
             copy(kind, n).wait_send()
@@ -907,7 +982,7 @@
         local.wait()
 
 
-def start_exchange(hidden, w_query, w_key, w_value, w_out, collective_id):
+def start_exchange(hidden, w_query, w_key, w_value, w_out, slots, collective_id):
     line = 4
     any_ref = pl.BlockSpec(memory_space=pl.ANY)
     dma = pltpu.SemaphoreType.DMA
@@ -920,14 +995,18 @@
             jax.ShapeDtypeStruct((line * rows, width), low),
             jax.ShapeDtypeStruct((8 * part, 3 * columns), low),
             jax.ShapeDtypeStruct((w_out.shape[0], 8 * w_out.shape[1]), low),
-        ),
-        in_specs=[any_ref] * 5,
-        out_specs=[any_ref] * 3,
-        scratch_shapes=[dma((5,)), dma((2, line)), dma((2, line)), dma((8, 4)), dma((8, 4))],
+            jax.ShapeDtypeStruct((line * 8, slots.shape[0] // 8, slots.shape[1]), slots.dtype),
+        ),
+        in_specs=[any_ref] * 6,
+        out_specs=[any_ref] * 4,
+        scratch_shapes=[
+            dma((6,)), dma((2, line)), dma((2, line)), dma((8, 4)), dma((8, 4)),
+            dma((7,)), dma((8,)), dma((2, line)), dma((2, line)),
+        ],
         compiler_params=pltpu.CompilerParams(collective_id=collective_id, has_side_effects=True),
         cost_estimate=pl.CostEstimate(flops=0, bytes_accessed=150 << 20, transcendentals=0),
         name="start_exchange",
-    )(hidden, w_query, w_key, w_value, w_out)
+    )(hidden, w_query, w_key, w_value, w_out, slots)
 
 
 class LineReduce:
@@ -1126,7 +1205,13 @@
     pl.semaphore_wait(barrier, 3 + line - 1)
 
 
-def back_gather_kernel(line, own_ref, sums_ref, out_ref, total_ref, data, local_sem, send_sem, recv_sem, *fly):
+def back_gather_kernel(line, own_ref, sums_ref, x_ref, c_ref, pre_ref, gated_ref,
+                       out_ref, total_ref, gate_ref, up_ref, down_ref,
+                       data, x_in, c_in, pre_in, gated_in, gate_out, up_out, down_out,
+                       local_sem, send_sem, recv_sem, load_sem, store_sem, *fly):
+    experts = x_ref.shape[0]
+    half = x_in.shape[2]
+    steps = 2 * experts
     greet_far(line)
     gather = LineGather(own_ref, out_ref, send_sem, recv_sem, line)
     local = pltpu.make_async_copy(own_ref, gather.view(gather.spot[3]), local_sem)
@@ -1134,21 +1219,80 @@
     local.start()
     data[...] = sums_ref[...]
     butterfly = Butterfly(data, total_ref, *fly)
-    for axis in ("core", "x", "y"):
-        butterfly.fold(axis)
-    gather.advance(0)
-    butterfly.line_step(0)
-    gather.advance(1)
-    butterfly.line_step(1)
-    for axis in ("y", "x", "core"):
-        butterfly.unfold(axis)
+
+    def loads(t):
+        e, slot = t // 2, t % 2
+        columns = pl.ds(pl.multiple_of(t % 2 * half, half), half)
+        return (
+            pltpu.make_async_copy(x_ref.at[e, :, columns], x_in.at[slot], load_sem.at[0, slot]),
+            pltpu.make_async_copy(c_ref.at[e, :, columns], c_in.at[slot], load_sem.at[1, slot]),
+            pltpu.make_async_copy(pre_ref.at[e], pre_in.at[slot], load_sem.at[2, slot]),
+            pltpu.make_async_copy(gated_ref.at[e], gated_in.at[slot], load_sem.at[3, slot]),
+        )
+
+    def stores(t):
+        e, slot = t // 2, t % 2
+        columns = pl.ds(pl.multiple_of(t % 2 * half, half), half)
+        return (
+            pltpu.make_async_copy(gate_out.at[slot], gate_ref.at[e, columns], store_sem.at[0, slot]),
+            pltpu.make_async_copy(up_out.at[slot], up_ref.at[e, columns], store_sem.at[1, slot]),
+            pltpu.make_async_copy(down_out.at[slot], down_ref.at[e, :, columns], store_sem.at[2, slot]),
+        )
+
+    for copy in loads(0):
+        copy.start()
+    events = {
+        1: lambda: butterfly.fold("core"),
+        2: lambda: butterfly.fold("x"),
+        4: lambda: butterfly.fold("y"),
+        5: lambda: gather.advance(0),
+        6: lambda: butterfly.line_step(0),
+        9: lambda: gather.advance(1),
+        10: lambda: butterfly.line_step(1),
+        12: lambda: butterfly.unfold("y"),
+        13: lambda: butterfly.unfold("x"),
+        14: lambda: butterfly.unfold("core"),
+    }
+
+    def work(t, carry):
+        for when, event in events.items():
+            pl.when(t == when)(event)
+        for copy in loads(t):
+            copy.wait()
+
+        @pl.when(t + 1 < steps)
+        def _():
+            for copy in loads(t + 1):
+                copy.start()
+
+        @pl.when(t >= 2)
+        def _():
+            for copy in stores(t - 2):
+                copy.wait()
+
+        slot = t % 2
+        weight_terms(
+            *(r.at[slot] for r in (x_in, c_in, pre_in, gated_in, gate_out, up_out, down_out))
+        )
+        for copy in stores(t):
+            copy.start()
+        return carry
+
+    lax.fori_loop(0, steps, work, 0)
     gather.advance(2)
+    for t in (steps - 2, steps - 1):
+        for copy in stores(t):
+            copy.wait()
     gather.finish()
     local.wait()
 
 
-def back_gather(own, sums, collective_id):
+def back_gather(own, sums, x_slots, c_slots, pre, gated, collective_id):
     line = 4
+    experts, total, width = x_slots.shape
+    units = gated.shape[2]
+    half = width // 2
+    low, wide = jnp.bfloat16, jnp.float32
     any_ref = pl.BlockSpec(memory_space=pl.ANY)
     vmem = pl.BlockSpec(memory_space=pltpu.VMEM)
     dma = pltpu.SemaphoreType.DMA
@@ -1156,18 +1300,33 @@
         functools.partial(back_gather_kernel, line),
         out_shape=(
             jax.ShapeDtypeStruct((line * own.shape[0], own.shape[1]), own.dtype),
-            jax.ShapeDtypeStruct(sums.shape, jnp.float32),
-        ),
-        in_specs=[any_ref, vmem],
-        out_specs=[any_ref, vmem],
+            jax.ShapeDtypeStruct(sums.shape, wide),
+            jax.ShapeDtypeStruct((experts, width, units), wide),
+            jax.ShapeDtypeStruct((experts, width, units), wide),
+            jax.ShapeDtypeStruct((experts, units, width), wide),
+        ),
+        in_specs=[any_ref, vmem] + [any_ref] * 4,
+        out_specs=[any_ref, vmem] + [any_ref] * 3,
         scratch_shapes=[
-            pltpu.VMEM(sums.shape, jnp.float32), dma(()), dma((2, line)), dma((2, line)),
+            pltpu.VMEM(sums.shape, wide),
+            pltpu.VMEM((2, total, half), low),
+            pltpu.VMEM((2, total, half), low),
+            pltpu.VMEM((2, total, 2 * units), low),
+            pltpu.VMEM((2, total, units), low),
+            pltpu.VMEM((2, half, units), wide),
+            pltpu.VMEM((2, half, units), wide),
+            pltpu.VMEM((2, units, half), wide),
+            dma(()), dma((2, line)), dma((2, line)), dma((4, 2)), dma((3, 2)),
             *Butterfly.scratch(*sums.shape),
         ],
-        compiler_params=pltpu.CompilerParams(collective_id=collective_id, has_side_effects=True),
-        cost_estimate=pl.CostEstimate(flops=0, bytes_accessed=150 << 20, transcendentals=0),
+        compiler_params=pltpu.CompilerParams(
+            collective_id=collective_id, has_side_effects=True, vmem_limit_bytes=50 << 20
+        ),
+        cost_estimate=pl.CostEstimate(
+            flops=6 * experts * total * width * units, bytes_accessed=180 << 20, transcendentals=0
+        ),
         name="back_gather",
-    )(own, sums)
+    )(own, sums, x_slots, c_slots, pre, gated)
 
 
 def last_kernel(line, joined_ref, weight_ref, hidden_ref, mixed_ref, attn_ref, residual_ref, gain_ref, x_grad_ref, gains_ref,
@@ -1571,11 +1730,7 @@
     slot_rows = padded(capacity, 8)
     valid_dev = lax.dynamic_slice_in_dim(token_valid, tensor_rank * tok_dev, tok_dev)
     slots_own = slot_table(routes, route_order, valid_dev, experts, capacity)
-    slots_all = lax.all_gather(slots_own.astype(jnp.bfloat16), everyone, axis=0)
-    slots = lax.dynamic_slice_in_dim(slots_all, first_expert, local_experts, 1).astype(jnp.int32)
-    blocks = slots.shape[0]
     cots_all = lax.all_gather(cotangent, everyone, axis=0, tiled=True)
-    c_slots = None if direct else dispatch(slots, None, cots_all, slot_rows)
     head_cols = w_query.shape[1]
     residual_float = residual.astype(jnp.float32)
     normed_one, scale_one = rms_apply(residual_float, attn_gain)
@@ -1587,14 +1742,20 @@
     cosine = jnp.concatenate((cosine, cosine), axis=1)
     sine = jnp.concatenate((-sine, sine), axis=1)
     if direct:
-        hidden_all, joined_weight, gathered_out = start_exchange(hidden, w_query, w_key, w_value, w_out, 3)
+        hidden_all, joined_weight, gathered_out, slots = start_exchange(
+            hidden, w_query, w_key, w_value, w_out, slots_own, 3
+        )
+        slots = jnp.swapaxes(slots.reshape(4, 8, local_experts, tok_dev), 0, 1).reshape(32, local_experts, tok_dev)
     else:
         hidden_all = lax.all_gather(hidden, "tensor", axis=0, tiled=True)
         joined_weight = jnp.concatenate(
             [lax.all_gather(w, "dp", axis=0, tiled=True) for w in (w_query, w_key, w_value)], axis=1
         )
         gathered_out = lax.all_gather(w_out, "dp", axis=1, tiled=True)
+        slots_all = lax.all_gather(slots_own.astype(jnp.bfloat16), everyone, axis=0)
+        slots = lax.dynamic_slice_in_dim(slots_all, first_expert, local_experts, 1).astype(jnp.int32)
     projected = jnp.dot(hidden_all, joined_weight, preferred_element_type=jnp.float32)
+    blocks = slots.shape[0]
     q_raw = projected[:, :head_cols]
     k_raw = projected[:, head_cols : 2 * head_cols]
     query_sq, key_sq = tensor_sums((jnp.sum(q_raw * q_raw, axis=1), jnp.sum(k_raw * k_raw, axis=1)))
@@ -1632,7 +1793,8 @@
         rows_all = lax.all_gather(hidden_two, everyone, axis=0, tiled=True)
         gates = lax.dynamic_slice_in_dim(gates_all, first_expert, local_experts, 1)
         x_slots, gate_slots = dispatch(slots, gates, rows_all, slot_rows)
-    outs, grads, grad_w_gate, grad_w_up, grad_w_down = expert_pass(
+        c_slots = dispatch(slots, None, cots_all, slot_rows)
+    outs, grads, pre, gated = expert_pass(
         first_expert.reshape(1),
         x_slots,
         c_slots,
@@ -1673,10 +1835,13 @@
         (grad_router_part, grad_moe_gain_part[None], jnp.zeros((7, width), jnp.float32)), axis=0
     )
     if direct:
-        grad_attn_all, early_sums = back_gather(grad_attn_low, early_sums, 5)
+        grad_attn_all, early_sums, grad_w_gate, grad_w_up, grad_w_down = back_gather(
+            grad_attn_low, early_sums, x_slots, c_slots, pre, gated, 5
+        )
     else:
         grad_attn_all = lax.all_gather(grad_attn_low, "tensor", axis=0, tiled=True)
         early_sums = lax.psum(early_sums, everyone)
+        grad_w_gate, grad_w_up, grad_w_down = weight_grads(x_slots, c_slots, pre, gated)
     grad_q_norm, grad_k_norm, grad_value_all = attend_back(
         grad_attn_all,
         gathered_out,

time: 1230 us -> 1230 us (level)
  local copies, waits for them, and re-layouts: 21.5 us -> 53.2 us
  waiting for transfers between devices: 90.3 us -> 73.9 us
    pallas_call x1, Pallas kernels: 102 us -> 195 us  [start_exchange(): pl.pallas_call(functools.partial(start_kernel, line), out_shape=(jax.Shap...]
    pallas_call x1, Pallas kernels: 143 us -> 78.1 us  [mixed_out(): pl.pallas_call(functools.partial(mixed_out_kernel, line), out_shape=(jax....]
    pallas_call x1, Pallas kernels: 141 us -> 98.2 us  [expert_pass(): pl.pallas_call(kernel, grid_spec=pltpu.PrefetchScalarGridSpec(num_scalar_...]
    unnamed x87 -> x104, local copies, waits for them, and re-layouts: 16.3 us -> 47.9 us
    pallas_call x1, Pallas kernels: 105 us -> 136 us  [back_gather(): pl.pallas_call(functools.partial(back_gather_kernel, line), out_shape=(ja...]
    pallas_call x1, Pallas kernels: 123 us -> 105 us  [last_exchange(): pl.pallas_call(functools.partial(last_kernel, line), out_shape=(jax.Shape...]
    all_gather x1, waiting for transfers between devices: 18.3 us -> 0.02 us  [body(): cots_all = lax.all_gather(cotangent, everyone, axis=0, tiled=True)]
  transfers between devices with their start and end apart: 4 -> 3, of which waited for: 2 -> 1; matrix products, arithmetic and copies ran while one was open for 4% -> 4% of each run, Pallas kernels for 42% -> 46%
where the time goes in v7:
time: 1230 us; the launch traced here: 1220 us
  Pallas kernels  1010 us (82%)
  waiting for transfers between devices  73.9 us (6%)
  local copies, waits for them, and re-layouts  53.2 us (4%)
  other arithmetic  34.3 us (3%)
  blocking collectives  20 us (2%)
  matrix products  15.1 us (1%)
  between operations  14.6 us (1%)
    pallas_call x1, Pallas kernels, start_exchange(): pl.pallas_call(functools.partial(start_kernel, line), out_shape=(jax.Shap...  195 us
    pallas_call x1, Pallas kernels, reduce_all(): pl.pallas_call(functools.partial(reduce_kernel, line), out_shape=(jax.Sha...  184 us
    pallas_call x1, Pallas kernels, gather_dispatch(): pl.pallas_call(functools.partial(gather_dispatch_kernel, line, rows), out...  172 us
    pallas_call x1, Pallas kernels, back_gather(): pl.pallas_call(functools.partial(back_gather_kernel, line), out_shape=(ja...  136 us
    pallas_call x1, Pallas kernels, last_exchange(): pl.pallas_call(functools.partial(last_kernel, line), out_shape=(jax.Shape...  105 us
    pallas_call x1, Pallas kernels, expert_pass(): pl.pallas_call(kernel, grid_spec=pltpu.PrefetchScalarGridSpec(num_scalar_...  98.2 us
    pallas_call x1, Pallas kernels, mixed_out(): pl.pallas_call(functools.partial(mixed_out_kernel, line), out_shape=(jax....  78.1 us
    reduce_scatter x1, waiting for transfers between devices, sum_over_tensor(): return lax.psum_scatter(part, 'tensor', scatter_dimension=0, tiled=True)  73.1 us
  transfers between devices with their start and end apart: 3, of which 1 were waited for; matrix products, arithmetic and copies ran while one was open for 4% of the time, Pallas kernels for 46%

profile of v7, /device:TPU:0, one launch (start us, length us, event | category | flops | bytes accessed | tf_op | source)
XLA Modules:
  0.0 1224.0 jit_solution(9945082342452135428)
XLA Ops:
  7.2 0.7 all-gather.2.cloned.1.call-update
  8.0 0.8 dynamic-slice_compare_fusion
  8.8 1.0 select_reduce_fusion
  9.8 1.5 fusion.3
  11.3 5.2 convert_reduce_fusion
  16.4 0.6 and_select_fusion.slots_ref
  17.1 1.3 fusion.5.hidden_ref
  18.4 194.6 %start_exchange.1 = (bf16[1024,2048]{1,0:T(8,128)(2,1)}, bf16[2048,1536]{1,0:T(8,128)(2,1)}, bf16[512,2048]{1,0:T(8,128)(2,1)}, s32[32,8,256]{2,1,0:T(8,128)}) custom-call(bf16[256,2048]{1,0:T(8,128)(2,1)} %fusion.5.hidden_ref, bf16[256,512]{1,0:T(8,128)(2,1)} %wq_ref.1, bf16[256,512]{1,0:T(8,128)(2,1)} %wk_ref.1, bf16[256,512]{1,0:T(8,128)(2,1)} %wv_ref.1, ...), custom_call_target="tpu_custom_call" | custom-call | bytes 157286400 | tf_op jit(solution)/shard_map/start_exchange/pallas_call | solution.py:992
  213.0 10.2 fusion.13.raw_ref
  223.2 2.7 copy-done.12
  225.9 0.3 multiply_reduce_fusion.8
  226.2 9.6 all-reduce.1
  235.8 0.6 multiply_multiply_fusion
  236.4 0.6 copy-done.26
  237.0 0.2 copy.53.scale_ref
  237.3 0.8 dynamic_slice.11
  238.0 0.8 dynamic_slice.10
  238.8 0.2 copy.54.column_ref
  239.2 2.8 convert_reduce_fusion.1
  242.0 1.9 fusion.7
  243.9 0.3 pad_maximum_fusion.1
  244.3 19.2 %attend.1 = (bf16[1024,512]{1,0:T(8,128)(2,1)S(1)}, bf16[1024,512]{1,0:T(8,128)(2,1)}, bf16[1024,512]{1,0:T(8,128)(2,1)}, bf16[1024,512]{1,0:T(8,128)(2,1)}, f32[8,1024]{1,0:T(8,128)S(1)}) custom-call(f32[1024,1536]{1,0:T(8,128)} %copy-done.12, f32[1024,2]{1,0:T(8,128)S(1)} %copy.53.scale_ref, f32[2,512]{1,0:T(2,128)S(1)} %pad_maximum_fusion.4.gain_ref, ...), custom_call_target="tpu_custom_call" | custom-call | flops 2147483648 | bytes 8388608 | tf_op jit(solution)/shard_map/attend/pallas_call | solution.py:1584
  263.5 1.0 copy-done.9
  264.5 78.1 %mixed_out.1 = (f32[256,2048]{1,0:T(8,128)}, bf16[256,2048]{1,0:T(8,128)(2,1)}, f32[64,256]{1,0:T(8,128)}) custom-call(bf16[1024,512]{1,0:T(8,128)(2,1)} %get-tuple-element.53.mixed_ref, bf16[512,2048]{1,0:T(8,128)(2,1)} %get-tuple-element.54.w_ref, bf16[256,2048]{1,0:T(8,128)(2,1)} %residual_ref.3, f32[1,2048]{1,0:T(1,128)} %bitcast.54, ...), custom_call_target="tpu_custom_call" | custom-call | bytes 157286400 | tf_op jit(solution)/shard_map/mixed_out/pallas_call | solution.py:1110
  342.7 1.2 copy-done.4
  343.9 0.8 copy-done.7
  344.7 172.0 %gather_dispatch.1 = (bf16[8192,2048]{1,0:T(8,128)(2,1)}, f32[2048,256]{1,0:T(8,128)}, bf16[8,1280,2048]{2,1,0:T(8,128)(2,1)}, bf16[8,1280,2048]{2,1,0:T(8,128)(2,1)}, f32[8,1280,128]{2,1,0:T(8,128)S(1)}) custom-call(s32[32,8,256]{2,1,0:T(8,128)S(1)} %bitcast.42, bf16[256,2048]{1,0:T(8,128)(2,1)S(1)} %copy-done.4, f32[64,256]{1,0:T(8,128)S(1)} %copy-done.7, ...), custom_call_target="tpu_custom_call" | custom-call | flops 21474836480 | bytes 209715200 | tf_op jit(solution)/shard_map/gather_dispatch/pallas_call | solution.py:523
  516.7 2.3 copy-done.11
  519.1 98.2 %experts.1 = (bf16[32,8,48,2048]{3,2,1,0:T(8,128)(2,1)}, bf16[32,8,48,2176]{3,2,1,0:T(8,128)(2,1)}, bf16[8,1280,512]{2,1,0:T(8,128)(2,1)}, bf16[8,1280,256]{2,1,0:T(8,128)(2,1)}) custom-call(s32[1]{0:T(128)} %bitcast.14.first_ref, bf16[8,1280,2048]{2,1,0:T(8,128)(2,1)} %get-tuple-element.59.x_ref, bf16[8,1280,2048]{2,1,0:T(8,128)(2,1)} %get-tuple-element.60.c_ref, ...), custom_call_target="tpu_custom_call" | custom-call | flops 64424509440 | bytes 192937984 | tf_op jit(solution)/shard_map/experts/pallas_call | solution.py:208
  617.3 184.4 %reduce_all.1 = (f32[256,2176]{1,0:T(8,128)}, bf16[8192,2048]{1,0:T(8,128)(2,1)}) custom-call(s32[32,8,256]{2,1,0:T(8,128)} %bitcast.43, bf16[32,8,48,2176]{3,2,1,0:T(8,128)(2,1)} %get-tuple-element.62.grads_ref, bf16[32,8,48,2048]{3,2,1,0:T(8,128)(2,1)} %get-tuple-element.63.outs_ref), custom_call_target="tpu_custom_call" | custom-call | flops 26575110144 | bytes 103809024 | tf_op jit(solution)/shard_map/reduce_all/pallas_call | solution.py:782
  802.0 0.6 copy-done.8
  802.8 0.5 copy-done.13
  803.6 1.0 fusion.8
  804.6 1.7 fusion.9
  806.3 3.3 multiply_reduce_fusion.4
  809.7 2.0 fusion.10
  811.8 136.2 %back_gather.1 = (bf16[1024,2048]{1,0:T(8,128)(2,1)}, f32[72,2048]{1,0:T(8,128)S(1)}, f32[8,2048,256]{2,1,0:T(8,128)}, f32[8,2048,256]{2,1,0:T(8,128)}, f32[8,256,2048]{2,1,0:T(8,128)}) custom-call(bf16[256,2048]{1,0:T(8,128)(2,1)S(1)} %get-tuple-element.102.own_ref, f32[72,2048]{1,0:T(8,128)S(1)} %maximum_maximum_fusion.sums_ref, ...), custom_call_target="tpu_custom_call" | custom-call | flops 32212254720 | bytes 188743680 | tf_op jit(solution)/shard_map/back_gather/pallas_call | solution.py:1299
  948.0 25.1 %attend_back.1 = (f32[1024,512]{1,0:T(8,128)}, f32[1024,512]{1,0:T(8,128)}, f32[1024,512]{1,0:T(8,128)}) custom-call(bf16[1024,2048]{1,0:T(8,128)(2,1)} %get-tuple-element.68.grad_ref.attn_ref, bf16[512,2048]{1,0:T(8,128)(2,1)} %get-tuple-element.54.w_ref, bf16[1024,512]{1,0:T(8,128)(2,1)} %copy-done.9, bf16[1024,512]{1,0:T(8,128)(2,1)} %get-tuple-element.70.key_ref, ...), custom_call_target="tpu_custom_call" | custom-call | flops 5368709120 | bytes 12582912 | tf_op jit(solution)/shard_map/attend_back/pallas_call | solution.py:1650
  973.2 1.9 convert.11
  975.1 0.3 copy-done.15
  975.5 2.7 multiply_reduce_fusion.1
  978.2 10.4 all-reduce
  988.7 4.2 subtract_convert_fusion.1
  992.9 1.8 pad_maximum_fusion.joined_ref
  994.7 0.7 maximum_maximum_fusion.1.gains_ref
  995.4 104.8 %last_exchange.1 = (f32[256,2048]{1,0:T(8,128)}, f32[256,512]{1,0:T(8,128)}, f32[256,512]{1,0:T(8,128)}, f32[256,512]{1,0:T(8,128)}, f32[512,256]{1,0:T(8,128)}, /*index=5*/f32[8,2048]{1,0:T(8,128)}) custom-call(bf16[1024,1536]{1,0:T(8,128)(2,1)} %pad_maximum_fusion.joined_ref, bf16[2048,1536]{1,0:T(8,128)(2,1)} %get-tuple-element.52.weight_ref, ...), custom_call_target="tpu_custom_call" | custom-call | bytes 262144000 | tf_op jit(solution)/shard_map/last_exchange/pallas_call | solution.py:1474
  1100.3 0.6 slice.47
  1100.9 1.6 fusion.11
  1102.5 0.8 slice_bitcast_fusion
  1103.3 73.1 %reduce-scatter.5.cloned.1.call-done = bf16[256,2048]{1,0:T(8,128)(2,1)} async-done(((bf16[1024,2048]{1,0:T(8,128)(2,1)}), bf16[256,2048]{1,0:T(8,128)(2,1)}) %reduce-scatter.5.cloned.1.call-update) | async-done | bytes 1048592 | tf_op jit(solution)/shard_map/reduce_scatter | solution.py:1695
  1176.4 3.2 add_convert_fusion
  1179.6 1.3 copy.68
  1180.9 0.8 copy.69
  1181.7 0.8 copy.70
  1182.5 0.6 copy-done.20
  1183.1 0.8 copy.71
  1183.9 0.8 copy.72
  1184.7 13.2 %copy.73 = f32[8,2048,256]{2,1,0:T(8,128)} copy(f32[8,2048,256]{2,1,0:T(8,128)} %get-tuple-element.151) | data formatting | bytes 33554432
  1198.0 0.6 slice-done.8
  1198.6 1.5 slice-done.9
  1200.0 8.5 copy.74
  1208.5 1.4 slice-done.4
  1209.9 1.2 slice-done.5
  1211.1 6.2 copy.75
  (114 shorter events, 1.3 us)
Async XLA Ops:
  7.2 9.9 copy-start.14
  7.2 9.9 copy-start.31
  7.2 335.4 %all-gather.2.cloned.1.call-start = ((), (), s32[]{:S(2)}) async-start(), calls=%async_computation.2 | async-start | bytes 34603008 | tf_op jit(solution)/shard_map/all_gather | solution.py:1733
  7.9 1092.3 %reduce-scatter.3.cloned.1.call-start = ((), (), s32[]{:S(2)}) async-start(), calls=%async_computation.3 | async-start | bytes 37748736 | tf_op jit(solution)/shard_map/reduce_scatter | solution.py:1691
  223.2 2.7 copy-start.12
  225.9 12.9 %copy-start.24 = (s32[3,1024]{1,0:T(4,128)S(1)}, s32[3,1024]{1,0:T(4,128)}, u32[]{:S(2)}) copy-start(s32[3,1024]{1,0:T(4,128)} %param.31) | copy-start | bytes 36868
  225.9 12.9 %copy-start.30 = (s32[1024]{0:T(1024)S(1)}, s32[1024]{0:T(1024)}, u32[]{:S(2)}) copy-start(s32[1024]{0:T(1024)} %param.32) | copy-start | bytes 12292
  225.9 13.2 %copy-start.23 = (s32[32,8,256]{2,1,0:T(8,128)S(1)}, s32[32,8,256]{2,1,0:T(8,128)}, u32[]{:S(2)}) copy-start(s32[32,8,256]{2,1,0:T(8,128)} %get-tuple-element.56) | copy-start | bytes 786436
  236.4 0.6 copy-start.26
  236.4 0.6 copy-start.28
  238.0 6.2 copy-start.32
  238.8 5.5 copy-start.34
  239.1 5.3 copy-start.2
  239.1 103.6 %copy-start.3 = (s32[4,8,8,256]{3,2,0,1:T(8,128)}, s32[4,8,8,256]{3,2,0,1:T(8,128)S(1)}, u32[]{:S(2)}) copy-start(s32[4,8,8,256]{3,2,0,1:T(8,128)S(1)} %copy.55) | copy-start | bytes 786436
  239.2 5.2 copy-start.6
  244.3 19.2 %copy-start = (f32[1024,128]{1,0:T(8,128)}, f32[1024,128]{1,0:T(8,128)S(1)}, u32[]{:S(2)}) copy-start(f32[1024,128]{1,0:T(8,128)S(1)} %get-tuple-element.124.cos_ref) | copy-start | bytes 1572868
  244.3 19.2 %copy-start.1 = (f32[1024,128]{1,0:T(8,128)}, f32[1024,128]{1,0:T(8,128)S(1)}, u32[]{:S(2)}) copy-start(f32[1024,128]{1,0:T(8,128)S(1)} %get-tuple-element.125.sin_ref) | copy-start | bytes 1572868
  263.5 1.0 copy-start.9
  264.5 78.1 %copy-start.10 = (f32[8,1024]{1,0:T(8,128)}, f32[8,1024]{1,0:T(8,128)S(1)}, u32[]{:S(2)}) copy-start(f32[8,1024]{1,0:T(8,128)S(1)} %get-tuple-element.72.log_ref) | copy-start | bytes 98308
  342.7 1.2 copy-start.4
  343.9 0.8 copy-start.7
  516.7 2.4 copy-start.11
  801.7 0.8 copy-start.8
  801.7 1.6 copy-start.13
  801.8 2.8 copy-start.5
  801.8 374.6 %reduce-scatter.5.cloned.1.call-start = ((), (), s32[]{:S(2)}) async-start(), calls=%async_computation.4 | async-start | bytes 5242880 | tf_op jit(solution)/shard_map/reduce_scatter | solution.py:1695
  803.3 3.0 copy-start.18
  803.4 3.0 copy-start.25
  806.3 3.4 copy-start.16
  948.0 27.1 %slice-start = ((s8[6291456]{0:T(1024)(128)(4,1)}), s8[4194304]{0:T(1024)(128)(4,1)S(1)}, s32[]{:S(2)}) async-start(s8[6291456]{0:T(1024)(128)(4,1)} %bitcast.44), calls=%async_computation.5 | async-start | bytes 8388608
  948.0 27.1 %slice-start.1 = ((s8[6291456]{0:T(1024)(128)(4,1)}), s8[2097152]{0:T(1024)(128)(4,1)S(1)}, s32[]{:S(2)}) async-start(s8[6291456]{0:T(1024)(128)(4,1)} %bitcast.44), calls=%async_computation.6 | async-start | bytes 4194304
  973.2 2.3 copy-start.15
  973.2 2.3 copy-start.27
  973.2 2.3 copy-start.29
  973.2 2.3 copy-start.33
  973.2 2.3 copy-start.35
  975.5 13.2 %copy-start.36 = (f32[1024]{0:T(1024)S(1)}, f32[1024]{0:T(1024)}, u32[]{:S(2)}) copy-start(f32[1024]{0:T(1024)} %get-tuple-element.117) | copy-start | bytes 12292
  975.5 13.2 %copy-start.37 = (f32[1024]{0:T(1024)S(1)}, f32[1024]{0:T(1024)}, u32[]{:S(2)}) copy-start(f32[1024]{0:T(1024)} %get-tuple-element.123) | copy-start | bytes 12292
  1103.3 76.3 %copy-start.17 = (f32[256,2048]{1,0:T(8,128)S(1)}, f32[256,2048]{1,0:T(8,128)}, u32[]{:S(2)}) copy-start(f32[256,2048]{1,0:T(8,128)} %get-tuple-element.141) | copy-start | bytes 6291460
  1176.4 4.5 copy-start.22
  1179.6 2.1 copy-start.21
  1179.6 18.4 %slice-start.6 = ((s8[16777216]{0:T(1024)(128)(4,1)}), s8[4194304]{0:T(1024)(128)(4,1)S(1)}, s32[]{:S(2)}) async-start(s8[16777216]{0:T(1024)(128)(4,1)} %bitcast.49), calls=%async_computation.11 | async-start | bytes 8388608
  1180.9 2.2 copy-start.20
  1180.9 3.0 copy-start.19
  1184.7 13.2 %slice-start.7 = ((s8[16777216]{0:T(1024)(128)(4,1)}), s8[4194304]{0:T(1024)(128)(4,1)S(1)}, s32[]{:S(2)}) async-start(s8[16777216]{0:T(1024)(128)(4,1)} %bitcast.49), calls=%async_computation.12 | async-start | bytes 8388608
  1184.7 13.8 %slice-start.8 = ((s8[16777216]{0:T(1024)(128)(4,1)}), s8[4194304]{0:T(1024)(128)(4,1)S(1)}, s32[]{:S(2)}) async-start(s8[16777216]{0:T(1024)(128)(4,1)} %bitcast.49), calls=%async_computation.13 | async-start | bytes 8388608
  1184.7 15.3 %slice-start.9 = ((s8[16777216]{0:T(1024)(128)(4,1)}), s8[4194304]{0:T(1024)(128)(4,1)S(1)}, s32[]{:S(2)}) async-start(s8[16777216]{0:T(1024)(128)(4,1)} %bitcast.49), calls=%async_computation.14 | async-start | bytes 8388608
  1184.7 23.8 %slice-start.2 = ((s8[16777216]{0:T(1024)(128)(4,1)}), s8[4194304]{0:T(1024)(128)(4,1)S(1)}, s32[]{:S(2)}) async-start(s8[16777216]{0:T(1024)(128)(4,1)} %bitcast.47), calls=%async_computation.7 | async-start | bytes 8388608
  1184.7 23.8 %slice-start.3 = ((s8[16777216]{0:T(1024)(128)(4,1)}), s8[4194304]{0:T(1024)(128)(4,1)S(1)}, s32[]{:S(2)}) async-start(s8[16777216]{0:T(1024)(128)(4,1)} %bitcast.47), calls=%async_computation.8 | async-start | bytes 8388608
  1200.0 9.9 slice-start.4
  1200.0 11.1 slice-start.5
Sparse Core Ops, SparseCore 0:
  11.0 248.3 all-gather.1
  801.9 241.7 reduce-scatter.2
  1100.4 75.9 reduce-scatter.4

commit v8 on v7

--- a/solution.py
+++ b/solution.py
@@ -190,6 +190,11 @@
         ],
         out_specs=[tall, tall, pl.BlockSpec((1, units, step), lambda e, j: (e, 0, j))],
         compiler_params=pltpu.CompilerParams(vmem_limit_bytes=50 << 20),
+        cost_estimate=pl.CostEstimate(
+            flops=6 * experts * total * width * units,
+            bytes_accessed=4 * experts * total * width + 12 * experts * width * units,
+            transcendentals=0,
+        ),
         name="weight_grads",
     )(x_slots, c_slots, pre, gated)
 
@@ -1205,13 +1210,7 @@
     pl.semaphore_wait(barrier, 3 + line - 1)
 
 
-def back_gather_kernel(line, own_ref, sums_ref, x_ref, c_ref, pre_ref, gated_ref,
-                       out_ref, total_ref, gate_ref, up_ref, down_ref,
-                       data, x_in, c_in, pre_in, gated_in, gate_out, up_out, down_out,
-                       local_sem, send_sem, recv_sem, load_sem, store_sem, *fly):
-    experts = x_ref.shape[0]
-    half = x_in.shape[2]
-    steps = 2 * experts
+def back_gather_kernel(line, own_ref, sums_ref, out_ref, total_ref, data, local_sem, send_sem, recv_sem, *fly):
     greet_far(line)
     gather = LineGather(own_ref, out_ref, send_sem, recv_sem, line)
     local = pltpu.make_async_copy(own_ref, gather.view(gather.spot[3]), local_sem)
@@ -1219,80 +1218,21 @@
     local.start()
     data[...] = sums_ref[...]
     butterfly = Butterfly(data, total_ref, *fly)
-
-    def loads(t):
-        e, slot = t // 2, t % 2
-        columns = pl.ds(pl.multiple_of(t % 2 * half, half), half)
-        return (
-            pltpu.make_async_copy(x_ref.at[e, :, columns], x_in.at[slot], load_sem.at[0, slot]),
-            pltpu.make_async_copy(c_ref.at[e, :, columns], c_in.at[slot], load_sem.at[1, slot]),
-            pltpu.make_async_copy(pre_ref.at[e], pre_in.at[slot], load_sem.at[2, slot]),
-            pltpu.make_async_copy(gated_ref.at[e], gated_in.at[slot], load_sem.at[3, slot]),
-        )
-
-    def stores(t):
-        e, slot = t // 2, t % 2
-        columns = pl.ds(pl.multiple_of(t % 2 * half, half), half)
-        return (
-            pltpu.make_async_copy(gate_out.at[slot], gate_ref.at[e, columns], store_sem.at[0, slot]),
-            pltpu.make_async_copy(up_out.at[slot], up_ref.at[e, columns], store_sem.at[1, slot]),
-            pltpu.make_async_copy(down_out.at[slot], down_ref.at[e, :, columns], store_sem.at[2, slot]),
-        )
-
-    for copy in loads(0):
-        copy.start()
-    events = {
-        1: lambda: butterfly.fold("core"),
-        2: lambda: butterfly.fold("x"),
-        4: lambda: butterfly.fold("y"),
-        5: lambda: gather.advance(0),
-        6: lambda: butterfly.line_step(0),
-        9: lambda: gather.advance(1),
-        10: lambda: butterfly.line_step(1),
-        12: lambda: butterfly.unfold("y"),
-        13: lambda: butterfly.unfold("x"),
-        14: lambda: butterfly.unfold("core"),
-    }
-
-    def work(t, carry):
-        for when, event in events.items():
-            pl.when(t == when)(event)
-        for copy in loads(t):
-            copy.wait()
-
-        @pl.when(t + 1 < steps)
-        def _():
-            for copy in loads(t + 1):
-                copy.start()
-
-        @pl.when(t >= 2)
-        def _():
-            for copy in stores(t - 2):
-                copy.wait()
-
-        slot = t % 2
-        weight_terms(
-            *(r.at[slot] for r in (x_in, c_in, pre_in, gated_in, gate_out, up_out, down_out))
-        )
-        for copy in stores(t):
-            copy.start()
-        return carry
-
-    lax.fori_loop(0, steps, work, 0)
+    for axis in ("core", "x", "y"):
+        butterfly.fold(axis)
+    gather.advance(0)
+    butterfly.line_step(0)
+    gather.advance(1)
+    butterfly.line_step(1)
+    for axis in ("y", "x", "core"):
+        butterfly.unfold(axis)
     gather.advance(2)
-    for t in (steps - 2, steps - 1):
-        for copy in stores(t):
-            copy.wait()
     gather.finish()
     local.wait()
 
 
-def back_gather(own, sums, x_slots, c_slots, pre, gated, collective_id):
+def back_gather(own, sums, collective_id):
     line = 4
-    experts, total, width = x_slots.shape
-    units = gated.shape[2]
-    half = width // 2
-    low, wide = jnp.bfloat16, jnp.float32
     any_ref = pl.BlockSpec(memory_space=pl.ANY)
     vmem = pl.BlockSpec(memory_space=pltpu.VMEM)
     dma = pltpu.SemaphoreType.DMA
@@ -1300,33 +1240,18 @@
         functools.partial(back_gather_kernel, line),
         out_shape=(
             jax.ShapeDtypeStruct((line * own.shape[0], own.shape[1]), own.dtype),
-            jax.ShapeDtypeStruct(sums.shape, wide),
-            jax.ShapeDtypeStruct((experts, width, units), wide),
-            jax.ShapeDtypeStruct((experts, width, units), wide),
-            jax.ShapeDtypeStruct((experts, units, width), wide),
-        ),
-        in_specs=[any_ref, vmem] + [any_ref] * 4,
-        out_specs=[any_ref, vmem] + [any_ref] * 3,
+            jax.ShapeDtypeStruct(sums.shape, jnp.float32),
+        ),
+        in_specs=[any_ref, vmem],
+        out_specs=[any_ref, vmem],
         scratch_shapes=[
-            pltpu.VMEM(sums.shape, wide),
-            pltpu.VMEM((2, total, half), low),
-            pltpu.VMEM((2, total, half), low),
-            pltpu.VMEM((2, total, 2 * units), low),
-            pltpu.VMEM((2, total, units), low),
-            pltpu.VMEM((2, half, units), wide),
-            pltpu.VMEM((2, half, units), wide),
-            pltpu.VMEM((2, units, half), wide),
-            dma(()), dma((2, line)), dma((2, line)), dma((4, 2)), dma((3, 2)),
+            pltpu.VMEM(sums.shape, jnp.float32), dma(()), dma((2, line)), dma((2, line)),
             *Butterfly.scratch(*sums.shape),
         ],
-        compiler_params=pltpu.CompilerParams(
-            collective_id=collective_id, has_side_effects=True, vmem_limit_bytes=50 << 20
-        ),
-        cost_estimate=pl.CostEstimate(
-            flops=6 * experts * total * width * units, bytes_accessed=180 << 20, transcendentals=0
-        ),
+        compiler_params=pltpu.CompilerParams(collective_id=collective_id, has_side_effects=True),
+        cost_estimate=pl.CostEstimate(flops=0, bytes_accessed=150 << 20, transcendentals=0),
         name="back_gather",
-    )(own, sums, x_slots, c_slots, pre, gated)
+    )(own, sums)
 
 
 def last_kernel(line, joined_ref, weight_ref, hidden_ref, mixed_ref, attn_ref, residual_ref, gain_ref, x_grad_ref, gains_ref,
@@ -1835,13 +1760,10 @@
         (grad_router_part, grad_moe_gain_part[None], jnp.zeros((7, width), jnp.float32)), axis=0
     )
     if direct:
-        grad_attn_all, early_sums, grad_w_gate, grad_w_up, grad_w_down = back_gather(
-            grad_attn_low, early_sums, x_slots, c_slots, pre, gated, 5
-        )
+        grad_attn_all, early_sums = back_gather(grad_attn_low, early_sums, 5)
     else:
         grad_attn_all = lax.all_gather(grad_attn_low, "tensor", axis=0, tiled=True)
         early_sums = lax.psum(early_sums, everyone)
-        grad_w_gate, grad_w_up, grad_w_down = weight_grads(x_slots, c_slots, pre, gated)
     grad_q_norm, grad_k_norm, grad_value_all = attend_back(
         grad_attn_all,
         gathered_out,
@@ -1924,8 +1846,12 @@
             grad_out_weight, "dp", scatter_dimension=1, tiled=True
         ).astype(jnp.float32)
         gains = lax.psum(jnp.stack((grad_query_full, grad_key_full, grad_attn_gain_part)), everyone)
-    out_part, grad_input = lax.optimization_barrier((out_part, grad_input))
-    block_out = (x_one + sum_over_tensor(out_part).astype(jnp.float32)).astype(jnp.bfloat16)
+    out_part, pre, grad_input = lax.optimization_barrier((out_part, pre, grad_input))
+    grad_w_gate, grad_w_up, grad_w_down = weight_grads(x_slots, c_slots, pre, gated)
+    moe_out, grad_w_gate, grad_w_up, grad_w_down = lax.optimization_barrier(
+        (sum_over_tensor(out_part), grad_w_gate, grad_w_up, grad_w_down)
+    )
+    block_out = (x_one + moe_out.astype(jnp.float32)).astype(jnp.bfloat16)
     return (
         block_out,
         grad_input,

time: 1230 us -> 1180 us (0.959)
  waiting for transfers between devices: 73.9 us -> 7.26 us
  Pallas kernels: 1010 us -> 1070 us
  local copies, waits for them, and re-layouts: 53.2 us -> 20.5 us
    reduce_scatter x1, waiting for transfers between devices: 73.1 us -> 6.5 us  [sum_over_tensor(): return lax.psum_scatter(part, 'tensor', scatter_dimension=0, tiled=True)]
    pallas_call x0 -> x1, Pallas kernels: none -> 65.2 us  [weight_grads(): pl.pallas_call(weight_kernel, grid=(experts, width // step), out_shape=(j...]
    unnamed x104 -> x69, local copies, waits for them, and re-layouts: 47.9 us -> 15.2 us
    pallas_call x1, Pallas kernels: 136 us -> 106 us  [back_gather(): pl.pallas_call(functools.partial(back_gather_kernel, line), out_shape=(ja...]
    pallas_call x1, Pallas kernels: 105 us -> 122 us  [last_exchange(): pl.pallas_call(functools.partial(last_kernel, line), out_shape=(jax.Shape...]
  transfers between devices with their start and end apart: 3 -> 3, of which waited for: 1 -> 1; matrix products, arithmetic and copies ran while one was open for 4% -> 4% of each run, Pallas kernels for 46% -> 52%
where the time goes in v8:
time: 1180 us
  Pallas kernels  1070 us (91%)
  other arithmetic  34.4 us (3%)
  local copies, waits for them, and re-layouts  20.5 us (2%)
  blocking collectives  18.7 us (2%)
  matrix products  15.1 us (1%)
  between operations  14.5 us (1%)
    pallas_call x1, Pallas kernels, start_exchange(): pl.pallas_call(functools.partial(start_kernel, line), out_shape=(jax.Shap...  195 us
    pallas_call x1, Pallas kernels, reduce_all(): pl.pallas_call(functools.partial(reduce_kernel, line), out_shape=(jax.Sha...  184 us
    pallas_call x1, Pallas kernels, gather_dispatch(): pl.pallas_call(functools.partial(gather_dispatch_kernel, line, rows), out...  173 us
    pallas_call x1, Pallas kernels, last_exchange(): pl.pallas_call(functools.partial(last_kernel, line), out_shape=(jax.Shape...  122 us
    pallas_call x1, Pallas kernels, back_gather(): pl.pallas_call(functools.partial(back_gather_kernel, line), out_shape=(ja...  106 us
    pallas_call x1, Pallas kernels, expert_pass(): pl.pallas_call(kernel, grid_spec=pltpu.PrefetchScalarGridSpec(num_scalar_...  98.3 us
    pallas_call x1, Pallas kernels, mixed_out(): pl.pallas_call(functools.partial(mixed_out_kernel, line), out_shape=(jax....  78.5 us
    pallas_call x1, Pallas kernels, weight_grads(): pl.pallas_call(weight_kernel, grid=(experts, width // step), out_shape=(j...  65.2 us
  transfers between devices with their start and end apart: 3, of which 1 were waited for; matrix products, arithmetic and copies ran while one was open for 4% of the time, Pallas kernels for 52%

profile of v8, /device:TPU:0, one launch (start us, length us, event | category | flops | bytes accessed | tf_op | source)
XLA Modules:
  0.0 1176.8 jit_solution(6255969433420428282)
XLA Ops:
  7.2 0.7 all-gather.2.cloned.1.call-update
  7.9 0.0 reduce-scatter.3.cloned.1.call-start
  8.0 0.8 dynamic-slice_compare_fusion
  8.8 1.0 select_reduce_fusion
  9.8 1.5 fusion.3
  11.3 5.2 convert_reduce_fusion
  16.4 0.6 and_select_fusion.slots_ref
  17.1 1.3 fusion.5.hidden_ref
  18.4 194.6 %start_exchange.1 = (bf16[1024,2048]{1,0:T(8,128)(2,1)}, bf16[2048,1536]{1,0:T(8,128)(2,1)}, bf16[512,2048]{1,0:T(8,128)(2,1)}, s32[32,8,256]{2,1,0:T(8,128)}) custom-call(bf16[256,2048]{1,0:T(8,128)(2,1)} %fusion.5.hidden_ref, bf16[256,512]{1,0:T(8,128)(2,1)} %wq_ref.1, bf16[256,512]{1,0:T(8,128)(2,1)} %wk_ref.1, bf16[256,512]{1,0:T(8,128)(2,1)} %wv_ref.1, ...), custom_call_target="tpu_custom_call" | custom-call | bytes 157286400 | tf_op jit(solution)/shard_map/start_exchange/pallas_call | solution.py:997
  213.0 10.2 fusion.13.raw_ref
  223.2 2.7 copy-done.12
  225.9 0.3 multiply_reduce_fusion.8
  226.2 9.6 all-reduce.1
  235.9 0.2 copy.53.scale_ref
  236.1 0.8 dynamic_slice.11
  236.9 0.8 dynamic_slice.10
  237.6 0.2 copy.54.column_ref
  238.0 2.8 convert_reduce_fusion.1
  240.9 1.9 fusion.7
  242.8 0.3 pad_maximum_fusion.1
  243.1 19.3 %attend.1 = (bf16[1024,512]{1,0:T(8,128)(2,1)S(1)}, bf16[1024,512]{1,0:T(8,128)(2,1)}, bf16[1024,512]{1,0:T(8,128)(2,1)}, bf16[1024,512]{1,0:T(8,128)(2,1)}, f32[8,1024]{1,0:T(8,128)S(1)}) custom-call(f32[1024,1536]{1,0:T(8,128)} %copy-done.12, f32[1024,2]{1,0:T(8,128)S(1)} %copy.53.scale_ref, f32[2,512]{1,0:T(2,128)S(1)} %pad_maximum_fusion.4.gain_ref, ...), custom_call_target="tpu_custom_call" | custom-call | flops 2147483648 | bytes 8388608 | tf_op jit(solution)/shard_map/attend/pallas_call | solution.py:1509
  262.4 1.0 copy-done.9
  263.4 78.5 %mixed_out.1 = (f32[256,2048]{1,0:T(8,128)}, bf16[256,2048]{1,0:T(8,128)(2,1)}, f32[64,256]{1,0:T(8,128)}) custom-call(bf16[1024,512]{1,0:T(8,128)(2,1)} %get-tuple-element.58.mixed_ref, bf16[512,2048]{1,0:T(8,128)(2,1)} %get-tuple-element.59.w_ref, bf16[256,2048]{1,0:T(8,128)(2,1)} %residual_ref.3, f32[1,2048]{1,0:T(1,128)} %bitcast.50, ...), custom_call_target="tpu_custom_call" | custom-call | bytes 157286400 | tf_op jit(solution)/shard_map/mixed_out/pallas_call | solution.py:1115
  342.0 1.2 copy-done.4
  343.2 0.8 copy-done.7
  344.0 172.9 %gather_dispatch.1 = (bf16[8192,2048]{1,0:T(8,128)(2,1)}, f32[2048,256]{1,0:T(8,128)}, bf16[8,1280,2048]{2,1,0:T(8,128)(2,1)}, bf16[8,1280,2048]{2,1,0:T(8,128)(2,1)}, f32[8,1280,128]{2,1,0:T(8,128)S(1)}) custom-call(s32[32,8,256]{2,1,0:T(8,128)S(1)} %bitcast.42, bf16[256,2048]{1,0:T(8,128)(2,1)S(1)} %copy-done.4, f32[64,256]{1,0:T(8,128)S(1)} %copy-done.7, ...), custom_call_target="tpu_custom_call" | custom-call | flops 21474836480 | bytes 209715200 | tf_op jit(solution)/shard_map/gather_dispatch/pallas_call | solution.py:528
  517.0 2.3 copy-done.11
  519.3 98.3 %experts.1 = (bf16[32,8,48,2048]{3,2,1,0:T(8,128)(2,1)}, bf16[32,8,48,2176]{3,2,1,0:T(8,128)(2,1)}, bf16[8,1280,512]{2,1,0:T(8,128)(2,1)}, bf16[8,1280,256]{2,1,0:T(8,128)(2,1)}) custom-call(s32[1]{0:T(128)} %bitcast.14.first_ref, bf16[8,1280,2048]{2,1,0:T(8,128)(2,1)} %get-tuple-element.64.x_ref, bf16[8,1280,2048]{2,1,0:T(8,128)(2,1)} %get-tuple-element.65.c_ref, ...), custom_call_target="tpu_custom_call" | custom-call | flops 64424509440 | bytes 192937984 | tf_op jit(solution)/shard_map/experts/pallas_call | solution.py:213
  617.6 184.5 %reduce_all.1 = (f32[256,2176]{1,0:T(8,128)}, bf16[8192,2048]{1,0:T(8,128)(2,1)}) custom-call(s32[32,8,256]{2,1,0:T(8,128)} %bitcast.43, bf16[32,8,48,2176]{3,2,1,0:T(8,128)(2,1)} %get-tuple-element.67.grads_ref, bf16[32,8,48,2048]{3,2,1,0:T(8,128)(2,1)} %get-tuple-element.68.outs_ref), custom_call_target="tpu_custom_call" | custom-call | flops 26575110144 | bytes 103809024 | tf_op jit(solution)/shard_map/reduce_all/pallas_call | solution.py:787
  802.1 0.2 reduce-scatter.5.cloned.1.call-start
  802.3 0.6 copy-done.8
  802.9 0.1 copy.56
  803.0 0.1 pad.8.clone
  803.1 0.1 pad.2.clone
  803.2 0.5 copy-done.13
  803.7 0.2 multiply_reduce_fusion.6
  803.9 1.0 fusion.8
  805.0 1.7 fusion.9
  806.7 3.3 multiply_reduce_fusion.4
  809.9 0.9 maximum_maximum_fusion.sums_ref
  810.9 2.4 fusion.10
  813.2 105.6 %back_gather.1 = (bf16[1024,2048]{1,0:T(8,128)(2,1)}, f32[72,2048]{1,0:T(8,128)}) custom-call(bf16[256,2048]{1,0:T(8,128)(2,1)} %get-tuple-element.112.own_ref, f32[72,2048]{1,0:T(8,128)} %maximum_maximum_fusion.sums_ref), custom_call_target="tpu_custom_call" | custom-call | bytes 157286400 | tf_op jit(solution)/shard_map/back_gather/pallas_call | solution.py:1239
  918.9 25.0 %attend_back.1 = (f32[1024,512]{1,0:T(8,128)}, f32[1024,512]{1,0:T(8,128)}, f32[1024,512]{1,0:T(8,128)}) custom-call(bf16[1024,2048]{1,0:T(8,128)(2,1)} %get-tuple-element.72.grad_ref.attn_ref, bf16[512,2048]{1,0:T(8,128)(2,1)} %get-tuple-element.59.w_ref, bf16[1024,512]{1,0:T(8,128)(2,1)} %copy-done.9, bf16[1024,512]{1,0:T(8,128)(2,1)} %get-tuple-element.74.key_ref, ...), custom_call_target="tpu_custom_call" | custom-call | flops 5368709120 | bytes 12582912 | tf_op jit(solution)/shard_map/attend_back/pallas_call | solution.py:1575
  943.9 1.9 convert.11
  945.8 0.3 copy-done.16
  946.1 2.7 multiply_reduce_fusion.1
  948.9 9.1 all-reduce
  958.0 4.3 subtract_convert_fusion.1
  962.3 1.8 pad_maximum_fusion.joined_ref
  964.1 0.7 maximum_maximum_fusion.1.gains_ref
  964.8 122.3 %last_exchange.1 = (f32[256,2048]{1,0:T(8,128)}, f32[256,512]{1,0:T(8,128)}, f32[256,512]{1,0:T(8,128)}, f32[256,512]{1,0:T(8,128)}, f32[512,256]{1,0:T(8,128)}, /*index=5*/f32[8,2048]{1,0:T(8,128)}) custom-call(bf16[1024,1536]{1,0:T(8,128)(2,1)} %pad_maximum_fusion.joined_ref, bf16[2048,1536]{1,0:T(8,128)(2,1)} %get-tuple-element.57.weight_ref, ...), custom_call_target="tpu_custom_call" | custom-call | bytes 262144000 | tf_op jit(solution)/shard_map/last_exchange/pallas_call | solution.py:1399
  1087.2 1.0 copy-done.24
  1088.2 0.6 slice.47
  1088.8 1.6 fusion.11
  1090.4 0.8 slice_bitcast_fusion
  1091.2 65.2 %weight_grads.1 = (f32[8,2048,256]{2,1,0:T(8,128)}, f32[8,2048,256]{2,1,0:T(8,128)}, f32[8,256,2048]{2,1,0:T(8,128)}) custom-call(bf16[8,1280,2048]{2,1,0:T(8,128)(2,1)} %get-tuple-element.64.x_ref, bf16[8,1280,2048]{2,1,0:T(8,128)(2,1)} %get-tuple-element.65.c_ref, bf16[8,1280,512]{2,1,0:T(8,128)(2,1)} %get-tuple-element.82.pre_ref, ...), custom_call_target="tpu_custom_call" | custom-call | flops 32212254720 | bytes 134217728 | tf_op jit(solution)/shard_map/weight_grads/pallas_call | solution.py:178
  1156.4 6.5 reduce-scatter.5.cloned.1.call-done
  1162.9 2.6 add_convert_fusion
  1165.5 1.3 copy.65
  1166.9 0.1 copy-done.23
  1166.9 0.8 copy.66
  1167.7 0.8 copy.67
  1168.5 0.8 copy.68
  1169.3 0.8 copy.69
  (78 shorter events, 0.4 us)
Async XLA Ops:
  7.2 9.9 copy-start.15
  7.2 9.9 copy-start.29
  7.2 334.7 %all-gather.2.cloned.1.call-start = ((), (), s32[]{:S(2)}) async-start(), calls=%async_computation.2 | async-start | bytes 34603008 | tf_op jit(solution)/shard_map/all_gather | solution.py:1658
  7.9 1079.2 %reduce-scatter.3.cloned.1.call-start = ((), (), s32[]{:S(2)}) async-start(), calls=%async_computation.3 | async-start | bytes 37748736 | tf_op jit(solution)/shard_map/reduce_scatter | solution.py:1616
  223.2 2.7 copy-start.12
  225.9 11.8 copy-start.26
  225.9 11.8 copy-start.28
  225.9 12.0 %copy-start.25 = (s32[32,8,256]{2,1,0:T(8,128)S(1)}, s32[32,8,256]{2,1,0:T(8,128)}, u32[]{:S(2)}) copy-start(s32[32,8,256]{2,1,0:T(8,128)} %get-tuple-element.61) | copy-start | bytes 786436
  237.9 5.3 copy-start.2
  237.9 104.0 %copy-start.3 = (s32[4,8,8,256]{3,2,0,1:T(8,128)}, s32[4,8,8,256]{3,2,0,1:T(8,128)S(1)}, u32[]{:S(2)}) copy-start(s32[4,8,8,256]{3,2,0,1:T(8,128)S(1)} %copy.55) | copy-start | bytes 786436
  238.0 5.2 copy-start.6
  243.1 19.3 %copy-start = (f32[1024,128]{1,0:T(8,128)}, f32[1024,128]{1,0:T(8,128)S(1)}, u32[]{:S(2)}) copy-start(f32[1024,128]{1,0:T(8,128)S(1)} %get-tuple-element.134.cos_ref) | copy-start | bytes 1572868
  243.1 19.3 %copy-start.1 = (f32[1024,128]{1,0:T(8,128)}, f32[1024,128]{1,0:T(8,128)S(1)}, u32[]{:S(2)}) copy-start(f32[1024,128]{1,0:T(8,128)S(1)} %get-tuple-element.135.sin_ref) | copy-start | bytes 1572868
  262.4 1.0 copy-start.9
  263.4 78.5 %copy-start.10 = (f32[8,1024]{1,0:T(8,128)}, f32[8,1024]{1,0:T(8,128)S(1)}, u32[]{:S(2)}) copy-start(f32[8,1024]{1,0:T(8,128)S(1)} %get-tuple-element.76.log_ref) | copy-start | bytes 98308
  342.0 1.2 copy-start.4
  343.2 0.8 copy-start.7
  516.9 2.4 copy-start.11
  802.1 0.8 copy-start.8
  802.1 1.6 copy-start.13
  802.1 2.8 copy-start.5
  802.1 360.8 %reduce-scatter.5.cloned.1.call-start = ((), (), s32[]{:S(2)}) async-start(), calls=%async_computation.4 | async-start | bytes 5242880 | tf_op jit(solution)/shard_map/reduce_scatter | solution.py:1620
  803.7 3.0 copy-start.19
  803.7 3.0 copy-start.27
  806.7 4.2 copy-start.17
  918.9 26.9 %slice-start = ((s8[6291456]{0:T(1024)(128)(4,1)}), s8[4194304]{0:T(1024)(128)(4,1)S(1)}, s32[]{:S(2)}) async-start(s8[6291456]{0:T(1024)(128)(4,1)} %bitcast.44), calls=%async_computation.5 | async-start | bytes 8388608
  918.9 26.9 %slice-start.1 = ((s8[6291456]{0:T(1024)(128)(4,1)}), s8[2097152]{0:T(1024)(128)(4,1)S(1)}, s32[]{:S(2)}) async-start(s8[6291456]{0:T(1024)(128)(4,1)} %bitcast.44), calls=%async_computation.6 | async-start | bytes 4194304
  943.9 2.2 copy-start.16
  1087.1 1.1 copy-start.24
  1091.2 71.7 %copy-start.14 = (f32[256,2048]{1,0:T(8,128)S(1)}, f32[256,2048]{1,0:T(8,128)}, u32[]{:S(2)}) copy-start(f32[256,2048]{1,0:T(8,128)} %get-tuple-element.60) | copy-start | bytes 6291460
  1162.9 2.6 copy-start.18
  1165.5 1.4 copy-start.23
  1165.5 2.2 copy-start.22
  1166.9 1.6 copy-start.21
  1166.9 2.4 copy-start.20
Sparse Core Ops, SparseCore 0:
  11.0 248.3 all-gather.1
  802.2 267.8 reduce-scatter.2
  1087.3 75.5 reduce-scatter.4

commit v9 on v8

--- a/solution.py
+++ b/solution.py
@@ -874,8 +874,9 @@
                 pl.when(self.sends(sign, step))(self.copy(sign, step).wait_send)
 
 
-def start_kernel(line, hidden_ref, wq_ref, wk_ref, wv_ref, wo_ref, slots_ref, hidden_out, joined_out, wo_out, slots_out,
-                 local_sem, line_send, line_recv, plane_send, plane_recv, slot_send, slot_recv, slot_line_send, slot_line_recv):
+def start_kernel(line, hidden_ref, wq_ref, wk_ref, wv_ref, wo_ref, slots_ref, hidden_out, joined_out, wo_out, slots_out, raw_out, scale_out,
+                 weights, rows_in, sums, local_sem, line_send, line_recv, plane_send, plane_recv,
+                 slot_send, slot_recv, slot_line_send, slot_line_recv, sum_send, sum_recv):
     y, x, core, z = place()
     owns = (wq_ref, wk_ref, wv_ref, wo_ref)
     near_x, near_y, sibling = (y, 1 - x, core, z), (1 - y, x, core, z), (y, x, 1 - core, z)
@@ -916,13 +917,9 @@
     plane = [((y + dy) % 2, (x + dx) % 2, (core + dc) % 2, z) for dy, dx, dc in shifts]
     for other_spot in plane:
         pl.semaphore_signal(barrier, inc=1, device_id=peer(*other_spot), device_id_type=MESH)
-    for step in (-1, 1):
-
-        @pl.when((z + step >= 0) & (z + step < line))
-        def _():
-            pl.semaphore_signal(barrier, inc=1, device_id=peer(y, x, core, z + step), device_id_type=MESH)
-
-    pl.semaphore_wait(barrier, 7 + (z + line - 1) // line + (2 * line - 2 - z) // line)
+    for step in range(1, line):
+        pl.semaphore_signal(barrier, inc=1, device_id=peer(y, x, core, (z + step) % line), device_id_type=MESH)
+    pl.semaphore_wait(barrier, 7 + line - 1)
     experts = slots_out.shape[1]
     group = peer(y, x, core, z)[0]
     slot_copies = []
@@ -968,14 +965,65 @@
         landed(view(n, 1 - y, 1 - x, 0), plane_recv.at[3, n])
         landed(view(n, 1 - y, 1 - x, 1), plane_recv.at[4, n])
         copy("sf", n).start()
-    for step in range(1, line - 1):
-        slot_line.advance(step)
-        hidden.advance(step)
     for n in range(4):
         landed(other(n, y, x), plane_recv.at[2, n])
         landed(other(n, y, 1 - x), plane_recv.at[5, n])
         landed(other(n, 1 - y, x), plane_recv.at[6, n])
         landed(other(n, 1 - y, 1 - x), plane_recv.at[7, n])
+    for local in locals_:
+        local.wait()
+    columns = wq_ref.shape[1]
+    rows = hidden_ref.shape[0]
+    fetch = pltpu.make_async_copy(joined_out, weights, local_sem.at[0])
+    fetch.start()
+    fetch.wait()
+
+    def project(block):
+        rows_copy = pltpu.make_async_copy(hidden.view(block), rows_in, local_sem.at[1])
+        rows_copy.start()
+        rows_copy.wait()
+        span = pl.ds(pl.multiple_of(block * rows, rows), rows)
+        lanes = lax.broadcasted_iota(jnp.int32, (rows, 128), 1)
+        tile = jnp.zeros((rows, 128), jnp.float32)
+        for n in range(3):
+            part = slice(n * columns, (n + 1) * columns)
+            value = jnp.dot(rows_in[...], weights[:, part], preferred_element_type=jnp.float32)
+            raw_out[span, part] = value
+            if n < 2:
+                tile = jnp.where(lanes == n, jnp.sum(value * value, axis=1, keepdims=True), tile)
+        sums[z, :, span] = jnp.transpose(tile)[:8]
+
+    project(z)
+    for step in range(line - 1):
+        if step:
+            slot_line.advance(step)
+            hidden.advance(step)
+        for sign in (1, -1):
+            block = z - sign * (step + 1)
+
+            @pl.when((block >= 0) & (block < line))
+            def _():
+                project(block)
+
+    sum_copies = [
+        remote(sums.at[z], sums.at[z], sum_send.at[step - 1], sum_recv.at[z], (y, x, core, (z + step) % line))
+        for step in range(1, line)
+    ]
+    for sum_copy in sum_copies:
+        sum_copy.start()
+    for step in range(1, line):
+        other_z = (z + step) % line
+        landed(sums.at[other_z], sum_recv.at[other_z])
+    total = sums[0]
+    for other_z in range(1, line):
+        total = total + sums[other_z]
+    scale = lax.rsqrt(total / (line * columns) + norm_eps)
+    for block in range(line):
+        piece = scale[:, block * rows : (block + 1) * rows]
+        tall = jnp.concatenate((piece, jnp.zeros((120, rows), jnp.float32)), axis=0)
+        scale_out[block * rows : (block + 1) * rows, :] = jnp.transpose(tall)
+    for sum_copy in sum_copies:
+        sum_copy.wait_send()
     hidden.finish()
     slot_line.finish()
     for slot_copy in slot_copies:
@@ -983,8 +1031,6 @@
     for n in range(4):
         for kind in kinds:
             copy(kind, n).wait_send()
-    for local in locals_:
-        local.wait()
 
 
 def start_exchange(hidden, w_query, w_key, w_value, w_out, slots, collective_id):
@@ -1001,14 +1047,21 @@
             jax.ShapeDtypeStruct((8 * part, 3 * columns), low),
             jax.ShapeDtypeStruct((w_out.shape[0], 8 * w_out.shape[1]), low),
             jax.ShapeDtypeStruct((line * 8, slots.shape[0] // 8, slots.shape[1]), slots.dtype),
+            jax.ShapeDtypeStruct((line * rows, 3 * columns), jnp.float32),
+            jax.ShapeDtypeStruct((line * rows, 128), jnp.float32),
         ),
         in_specs=[any_ref] * 6,
-        out_specs=[any_ref] * 4,
+        out_specs=[any_ref] * 4 + [pl.BlockSpec(memory_space=pltpu.VMEM)] * 2,
         scratch_shapes=[
+            pltpu.VMEM((8 * part, 3 * columns), low),
+            pltpu.VMEM((rows, width), low),
+            pltpu.VMEM((line, 8, line * rows), jnp.float32),
             dma((6,)), dma((2, line)), dma((2, line)), dma((8, 4)), dma((8, 4)),
-            dma((7,)), dma((8,)), dma((2, line)), dma((2, line)),
+            dma((7,)), dma((8,)), dma((2, line)), dma((2, line)), dma((line - 1,)), dma((line,)),
         ],
-        compiler_params=pltpu.CompilerParams(collective_id=collective_id, has_side_effects=True),
+        compiler_params=pltpu.CompilerParams(
+            collective_id=collective_id, has_side_effects=True, vmem_limit_bytes=40 << 20
+        ),
         cost_estimate=pl.CostEstimate(flops=0, bytes_accessed=150 << 20, transcendentals=0),
         name="start_exchange",
     )(hidden, w_query, w_key, w_value, w_out, slots)
@@ -1667,7 +1720,8 @@
     cosine = jnp.concatenate((cosine, cosine), axis=1)
     sine = jnp.concatenate((-sine, sine), axis=1)
     if direct:
-        hidden_all, joined_weight, gathered_out, slots = start_exchange(
+        hidden, cosine, sine, path_columns = lax.optimization_barrier((hidden, cosine, sine, path_columns))
+        hidden_all, joined_weight, gathered_out, slots, projected, scales = start_exchange(
             hidden, w_query, w_key, w_value, w_out, slots_own, 3
         )
         slots = jnp.swapaxes(slots.reshape(4, 8, local_experts, tok_dev), 0, 1).reshape(32, local_experts, tok_dev)
@@ -1679,18 +1733,19 @@
         gathered_out = lax.all_gather(w_out, "dp", axis=1, tiled=True)
         slots_all = lax.all_gather(slots_own.astype(jnp.bfloat16), everyone, axis=0)
         slots = lax.dynamic_slice_in_dim(slots_all, first_expert, local_experts, 1).astype(jnp.int32)
-    projected = jnp.dot(hidden_all, joined_weight, preferred_element_type=jnp.float32)
+    if not direct:
+        projected = jnp.dot(hidden_all, joined_weight, preferred_element_type=jnp.float32)
+        squares = [jnp.sum(projected[:, n * head_cols : (n + 1) * head_cols] ** 2, axis=1) for n in range(2)]
+        scales = lax.rsqrt(jnp.stack(tensor_sums(squares), axis=1) / full_width + norm_eps)
     blocks = slots.shape[0]
     q_raw = projected[:, :head_cols]
     k_raw = projected[:, head_cols : 2 * head_cols]
-    query_sq, key_sq = tensor_sums((jnp.sum(q_raw * q_raw, axis=1), jnp.sum(k_raw * k_raw, axis=1)))
-    query_scale = lax.rsqrt(query_sq / full_width + norm_eps)[:, None]
-    key_scale = lax.rsqrt(key_sq / full_width + norm_eps)[:, None]
+    query_scale, key_scale = scales[:, 0:1], scales[:, 1:2]
     query_gain_dev = lax.dynamic_slice_in_dim(query_gain, tensor_rank * head_cols, head_cols)
     key_gain_dev = lax.dynamic_slice_in_dim(key_gain, tensor_rank * head_cols, head_cols)
     query_low, key_low, value_low, attn_mixed, log_totals = attend(
         projected,
-        jnp.concatenate((query_scale, key_scale), axis=1),
+        scales,
         jnp.stack((query_gain_dev, key_gain_dev)),
         cosine,
         sine,

time: 1180 us -> 1200 us (1.017)
  Pallas kernels: 1070 us -> 1090 us
    pallas_call x1, Pallas kernels: 173 us -> 187 us  [gather_dispatch(): pl.pallas_call(functools.partial(gather_dispatch_kernel, line, rows), out...]
where the time goes in v9:
time: 1200 us; the launch traced here: 1190 us
  Pallas kernels  1090 us (91%)
  other arithmetic  33.9 us (3%)
  local copies, waits for them, and re-layouts  25.6 us (2%)
  between operations  14.8 us (1%)
    pallas_call x1, Pallas kernels, start_exchange(): pl.pallas_call(functools.partial(start_kernel, line), out_shape=(jax.Shap...  206 us
    pallas_call x1, Pallas kernels, gather_dispatch(): pl.pallas_call(functools.partial(gather_dispatch_kernel, line, rows), out...  187 us
    pallas_call x1, Pallas kernels, reduce_all(): pl.pallas_call(functools.partial(reduce_kernel, line), out_shape=(jax.Sha...  187 us
    pallas_call x1, Pallas kernels, last_exchange(): pl.pallas_call(functools.partial(last_kernel, line), out_shape=(jax.Shape...  122 us
    pallas_call x1, Pallas kernels, back_gather(): pl.pallas_call(functools.partial(back_gather_kernel, line), out_shape=(ja...  106 us
    pallas_call x1, Pallas kernels, expert_pass(): pl.pallas_call(kernel, grid_spec=pltpu.PrefetchScalarGridSpec(num_scalar_...  98.3 us
    pallas_call x1, Pallas kernels, mixed_out(): pl.pallas_call(functools.partial(mixed_out_kernel, line), out_shape=(jax....  77.7 us
    pallas_call x1, Pallas kernels, weight_grads(): pl.pallas_call(weight_kernel, grid=(experts, width // step), out_shape=(j...  65.3 us
  transfers between devices with their start and end apart: 3, of which 1 were waited for; matrix products, arithmetic and copies ran while one was open for 4% of the time, Pallas kernels for 52%

profile of v9, /device:TPU:0, one launch (start us, length us, event | category | flops | bytes accessed | tf_op | source)
XLA Modules:
  0.0 1188.4 jit_solution(14209308322969896147)
XLA Ops:
  7.2 0.7 all-gather.2.cloned.1.call-update
  8.0 0.8 dynamic_slice.10
  8.7 0.8 dynamic_slice.11
  9.5 0.7 fusion.17
  10.3 0.7 broadcast_compare_fusion
  10.9 0.8 fusion.14
  11.8 2.8 convert_reduce_fusion.1
  14.6 1.9 fusion.9
  16.6 0.3 pad_maximum_fusion.1
  17.0 0.3 fusion.3
  17.3 0.3 fusion.5.hidden_ref
  17.6 1.0 copy.44.column_ref
  18.7 0.1 dynamic-slice_compare_fusion
  18.7 0.3 select_reduce_fusion
  19.0 5.2 convert_reduce_fusion
  24.2 0.9 copy-done.10
  25.2 0.9 copy-done.11
  26.1 205.8 %start_exchange.1 = (bf16[1024,2048]{1,0:T(8,128)(2,1)S(1)}, bf16[2048,1536]{1,0:T(8,128)(2,1)}, bf16[512,2048]{1,0:T(8,128)(2,1)S(1)}, s32[32,8,256]{2,1,0:T(8,...) custom-call(bf16[256,2048]{1,0:T(8,128)(2,1)S(1)} %fusion.5.hidden_ref, bf16[256,512]{1,0:T(8,128)(2,1)S(1)} %copy-done.8, ...), custom_call_target="tpu_custom_call" | custom-call | bytes 157286400 | tf_op jit(solution)/shard_map/start_exchange/pallas_call | solution.py:1043
  231.9 2.0 copy-done
  233.9 1.3 copy-done.1
  235.4 1.1 copy-done.4
  236.4 18.2 %attend.1 = (bf16[1024,512]{1,0:T(8,128)(2,1)S(1)}, bf16[1024,512]{1,0:T(8,128)(2,1)}, bf16[1024,512]{1,0:T(8,128)(2,1)}, bf16[1024,512]{1,0:T(8,128)(2,1)}, f32[8,1024]{1,0:T(8,128)S(1)}) custom-call(f32[1024,1536]{1,0:T(8,128)} %get-tuple-element.63.raw_ref, f32[1024,128]{1,0:T(8,128)S(1)} %get-tuple-element.64.scale_ref, ...), custom_call_target="tpu_custom_call" | custom-call | flops 2147483648 | bytes 8388608 | tf_op jit(solution)/shard_map/attend/pallas_call | solution.py:1562
  254.7 1.0 copy-done.15
  255.7 0.6 copy-done.16
  256.3 77.7 %mixed_out.1 = (f32[256,2048]{1,0:T(8,128)}, bf16[256,2048]{1,0:T(8,128)(2,1)}, f32[64,256]{1,0:T(8,128)}) custom-call(bf16[1024,512]{1,0:T(8,128)(2,1)} %get-tuple-element.68.mixed_ref, bf16[512,2048]{1,0:T(8,128)(2,1)} %copy-done.1, bf16[256,2048]{1,0:T(8,128)(2,1)} %residual_ref.3, f32[1,2048]{1,0:T(1,128)} %bitcast.46, bf16[64,2048]{1,0:T(8,128)(2,1)} %bitcast.45), custom_call_target="tpu_custom_call" | custom-call | bytes 157286400 | tf_op jit(solution)/shard_map/mixed_out/pallas_call | solution.py:1168
  334.0 1.2 copy-done.6
  335.3 0.8 copy-done.13
  336.1 187.3 %gather_dispatch.1 = (bf16[8192,2048]{1,0:T(8,128)(2,1)}, f32[2048,256]{1,0:T(8,128)}, bf16[8,1280,2048]{2,1,0:T(8,128)(2,1)}, bf16[8,1280,2048]{2,1,0:T(8,128)(2,1)}, f32[8,1280,128]{2,1,0:T(8,128)S(1)}) custom-call(s32[32,8,256]{2,1,0:T(8,128)S(1)} %bitcast.38, bf16[256,2048]{1,0:T(8,128)(2,1)S(1)} %copy-done.6, f32[64,256]{1,0:T(8,128)S(1)} %copy-done.13, ...), custom_call_target="tpu_custom_call" | custom-call | flops 21474836480 | bytes 209715200 | tf_op jit(solution)/shard_map/gather_dispatch/pallas_call | solution.py:528
  523.4 2.3 copy-done.17
  525.7 98.3 %experts.1 = (bf16[32,8,48,2048]{3,2,1,0:T(8,128)(2,1)}, bf16[32,8,48,2176]{3,2,1,0:T(8,128)(2,1)}, bf16[8,1280,512]{2,1,0:T(8,128)(2,1)}, bf16[8,1280,256]{2,1,0:T(8,128)(2,1)}) custom-call(s32[1]{0:T(128)} %bitcast.12.first_ref, bf16[8,1280,2048]{2,1,0:T(8,128)(2,1)} %get-tuple-element.74.x_ref, bf16[8,1280,2048]{2,1,0:T(8,128)(2,1)} %get-tuple-element.75.c_ref, ...), custom_call_target="tpu_custom_call" | custom-call | flops 64424509440 | bytes 192937984 | tf_op jit(solution)/shard_map/experts/pallas_call | solution.py:213
  624.0 187.2 %reduce_all.1 = (f32[256,2176]{1,0:T(8,128)}, bf16[8192,2048]{1,0:T(8,128)(2,1)}) custom-call(s32[32,8,256]{2,1,0:T(8,128)} %bitcast.39, bf16[32,8,48,2176]{3,2,1,0:T(8,128)(2,1)} %get-tuple-element.77.grads_ref, bf16[32,8,48,2048]{3,2,1,0:T(8,128)(2,1)} %get-tuple-element.78.outs_ref), custom_call_target="tpu_custom_call" | custom-call | flops 26575110144 | bytes 103809024 | tf_op jit(solution)/shard_map/reduce_all/pallas_call | solution.py:787
  811.3 0.3 reduce-scatter.5.cloned.1.call-start
  811.5 0.5 copy-done.14
  812.1 0.1 copy.46
  812.2 0.1 pad.2.clone
  812.3 0.8 slice_reduce_fusion.1
  813.1 2.0 multiply_reduce_fusion.6
  815.1 1.0 fusion.10
  816.1 1.7 fusion.11
  817.9 3.3 multiply_reduce_fusion.4
  821.1 1.0 maximum_maximum_fusion.sums_ref
  822.1 2.4 fusion.12
  824.5 106.0 %back_gather.1 = (bf16[1024,2048]{1,0:T(8,128)(2,1)}, f32[72,2048]{1,0:T(8,128)}) custom-call(bf16[256,2048]{1,0:T(8,128)(2,1)} %get-tuple-element.124.own_ref, f32[72,2048]{1,0:T(8,128)} %maximum_maximum_fusion.sums_ref), custom_call_target="tpu_custom_call" | custom-call | bytes 157286400 | tf_op jit(solution)/shard_map/back_gather/pallas_call | solution.py:1292
  930.5 25.0 %attend_back.1 = (f32[1024,512]{1,0:T(8,128)}, f32[1024,512]{1,0:T(8,128)}, f32[1024,512]{1,0:T(8,128)}) custom-call(bf16[1024,2048]{1,0:T(8,128)(2,1)} %get-tuple-element.82.grad_ref.attn_ref, bf16[512,2048]{1,0:T(8,128)(2,1)} %copy-done.1, bf16[1024,512]{1,0:T(8,128)(2,1)} %copy-done.15, bf16[1024,512]{1,0:T(8,128)(2,1)} %get-tuple-element.84.key_ref, ...), custom_call_target="tpu_custom_call" | custom-call | flops 5368709120 | bytes 12582912 | tf_op jit(solution)/shard_map/attend_back/pallas_call | solution.py:1628
  955.6 1.9 convert.11
  957.5 0.3 copy-done.21
  957.8 2.8 multiply_reduce_fusion.1
  960.6 8.8 all-reduce
  969.4 4.3 subtract_convert_fusion.1
  973.7 1.8 pad_maximum_fusion.joined_ref
  975.5 0.7 maximum_maximum_fusion.1.gains_ref
  976.2 121.8 %last_exchange.1 = (f32[256,2048]{1,0:T(8,128)}, f32[256,512]{1,0:T(8,128)}, f32[256,512]{1,0:T(8,128)}, f32[256,512]{1,0:T(8,128)}, f32[512,256]{1,0:T(8,128)}, /*index=5*/f32[8,2048]{1,0:T(8,128)}) custom-call(bf16[1024,1536]{1,0:T(8,128)(2,1)} %pad_maximum_fusion.joined_ref, bf16[2048,1536]{1,0:T(8,128)(2,1)} %get-tuple-element.90.weight_ref, ...), custom_call_target="tpu_custom_call" | custom-call | bytes 262144000 | tf_op jit(solution)/shard_map/last_exchange/pallas_call | solution.py:1452
  1098.1 1.0 copy-done.29
  1099.2 0.6 slice.55
  1099.8 1.6 fusion.13
  1101.3 0.8 slice_bitcast_fusion
  1102.2 65.3 %weight_grads.1 = (f32[8,2048,256]{2,1,0:T(8,128)}, f32[8,2048,256]{2,1,0:T(8,128)}, f32[8,256,2048]{2,1,0:T(8,128)}) custom-call(bf16[8,1280,2048]{2,1,0:T(8,128)(2,1)} %get-tuple-element.74.x_ref, bf16[8,1280,2048]{2,1,0:T(8,128)(2,1)} %get-tuple-element.75.c_ref, bf16[8,1280,512]{2,1,0:T(8,128)(2,1)} %get-tuple-element.94.pre_ref, ...), custom_call_target="tpu_custom_call" | custom-call | flops 32212254720 | bytes 134217728 | tf_op jit(solution)/shard_map/weight_grads/pallas_call | solution.py:178
  1167.4 6.8 reduce-scatter.5.cloned.1.call-done
  1174.2 2.6 add_convert_fusion
  1176.8 1.3 copy.55
  1178.2 0.8 copy.56
  1179.0 0.8 copy.57
  1179.8 0.8 copy.58
  1180.6 0.8 copy.59
  (85 shorter events, 0.6 us)
Async XLA Ops:
  7.2 326.8 %all-gather.2.cloned.1.call-start = ((), (), s32[]{:S(2)}) async-start(), calls=%async_computation.2 | async-start | bytes 34603008 | tf_op jit(solution)/shard_map/all_gather | solution.py:1711
  7.9 1090.2 %reduce-scatter.3.cloned.1.call-start = ((), (), s32[]{:S(2)}) async-start(), calls=%async_computation.3 | async-start | bytes 37748736 | tf_op jit(solution)/shard_map/reduce_scatter | solution.py:1669
  14.6 2.3 copy-start.20
  16.5 0.7 copy-start.33
  16.9 218.5 %copy-start.2 = (f32[1024,128]{1,0:T(8,128)}, f32[1024,128]{1,0:T(8,128)S(1)}, u32[]{:S(2)}) copy-start(f32[1024,128]{1,0:T(8,128)S(1)} %get-tuple-element.65.cos_ref) | copy-start | bytes 1572868
  16.9 218.5 %copy-start.3 = (f32[1024,128]{1,0:T(8,128)}, f32[1024,128]{1,0:T(8,128)S(1)}, u32[]{:S(2)}) copy-start(f32[1024,128]{1,0:T(8,128)S(1)} %get-tuple-element.66.sin_ref) | copy-start | bytes 1572868
  16.9 1.7 copy-start.32
  16.9 1.8 copy-start.34
  17.0 1.8 copy-start.35
  17.0 7.2 copy-start.8
  17.0 7.2 copy-start.9
  17.6 217.7 %copy-start.30 = (s32[3,1024]{1,0:T(4,128)S(1)}, s32[3,1024]{1,0:T(4,128)}, u32[]{:S(2)}) copy-start(s32[3,1024]{1,0:T(4,128)} %param.31) | copy-start | bytes 36868
  24.2 1.0 copy-start.10
  25.2 0.9 copy-start.11
  231.9 2.0 copy-start
  233.9 1.3 copy-start.1
  235.3 98.7 %copy-start.5 = (s32[4,8,8,256]{3,2,0,1:T(8,128)}, s32[4,8,8,256]{3,2,0,1:T(8,128)S(1)}, u32[]{:S(2)}) copy-start(s32[4,8,8,256]{3,2,0,1:T(8,128)S(1)} %copy.45) | copy-start | bytes 786436
  235.4 19.3 %copy-start.12 = (s32[4,1024]{1,0:T(4,128)}, s32[4,1024]{1,0:T(4,128)S(1)}, u32[]{:S(2)}) copy-start(s32[4,1024]{1,0:T(4,128)S(1)} %pad_add_fusion.line_ref) | copy-start | bytes 49156
  235.4 1.1 copy-start.4
  254.7 1.0 copy-start.15
  255.7 0.6 copy-start.16
  334.0 1.2 copy-start.6
  335.3 0.8 copy-start.13
  523.4 2.4 copy-start.17
  811.2 0.8 copy-start.14
  811.3 4.9 copy-start.7
  811.3 362.9 %reduce-scatter.5.cloned.1.call-start = ((), (), s32[]{:S(2)}) async-start(), calls=%async_computation.4 | async-start | bytes 5242880 | tf_op jit(solution)/shard_map/reduce_scatter | solution.py:1673
  813.1 4.7 copy-start.18
  813.1 4.7 copy-start.24
  813.1 4.7 copy-start.31
  817.8 4.3 copy-start.22
  930.5 26.9 %slice-start = ((s8[6291456]{0:T(1024)(128)(4,1)}), s8[4194304]{0:T(1024)(128)(4,1)S(1)}, s32[]{:S(2)}) async-start(s8[6291456]{0:T(1024)(128)(4,1)} %bitcast.41), calls=%async_computation.5 | async-start | bytes 8388608
  930.5 26.9 %slice-start.1 = ((s8[6291456]{0:T(1024)(128)(4,1)}), s8[2097152]{0:T(1024)(128)(4,1)S(1)}, s32[]{:S(2)}) async-start(s8[6291456]{0:T(1024)(128)(4,1)} %bitcast.41), calls=%async_computation.6 | async-start | bytes 4194304
  955.6 2.2 copy-start.21
  1098.1 1.1 copy-start.29
  1102.2 72.0 %copy-start.19 = (f32[256,2048]{1,0:T(8,128)S(1)}, f32[256,2048]{1,0:T(8,128)}, u32[]{:S(2)}) copy-start(f32[256,2048]{1,0:T(8,128)} %get-tuple-element.70) | copy-start | bytes 6291460
  1174.2 2.6 copy-start.23
  1176.8 1.4 copy-start.28
  1176.8 2.2 copy-start.27
  1178.2 1.6 copy-start.26
  1178.2 2.4 copy-start.25
Sparse Core Ops, SparseCore 0:
  10.9 252.3 all-gather.1
  811.4 267.8 reduce-scatter.2
  1098.2 75.9 reduce-scatter.4

commit v10 on v8

--- a/solution.py
+++ b/solution.py
@@ -343,7 +343,7 @@
     return either(i + low * (first - second), 3 - i - low * (first - second), side)
 
 
-def gather_dispatch_kernel(line, rows, slots_ref, hidden_ref, gates_ref, cots_ref,
+def gather_dispatch_kernel(line, rows, slots_ref, hidden_ref, gates_ref, cots_left, cots_right,
                            rows_out, gates_out, x_out, c_out, gate_out,
                            in_c, in_x, in_gate, stage_c, stage_x, stage_gate,
                            local_sem, send_sem, recv_sem, load_sem, store_sem):
@@ -388,9 +388,13 @@
         yy, xx, zz = chip // 8, chip // 4 % 2, chip % 4
         for c in range(2):
             b = block_of(yy, xx, c, zz)
-            yield pltpu.make_async_copy(
-                cots_ref.at[pl.ds(b * tokens, tokens)], in_c.at[pl.ds(c * tokens, tokens)], load_sem.at[0, c]
-            )
+            half = width // 2
+            for n, source in enumerate((cots_left, cots_right)):
+                yield pltpu.make_async_copy(
+                    source.at[pl.ds(b * tokens, tokens)],
+                    in_c.at[pl.ds(c * tokens, tokens), pl.ds(n * half, half)],
+                    load_sem.at[3 * n, c],
+                )
 
     def load_x(yy, xx, zz):
         for c in range(2):
@@ -515,7 +519,7 @@
     lax.fori_loop(0, last, finish, 0)
 
 
-def gather_dispatch(slots, hidden, gates, cots_all, rows, collective_id):
+def gather_dispatch(slots, hidden, gates, cots, rows, collective_id):
     line = 4
     blocks, experts, tokens = slots.shape
     width = hidden.shape[1]
@@ -534,7 +538,7 @@
             slot_shape,
             jax.ShapeDtypeStruct((experts, blocks * rows, 128), wide),
         ),
-        in_specs=[vmem, any_ref, any_ref, any_ref],
+        in_specs=[vmem, any_ref, any_ref, any_ref, any_ref],
         out_specs=[any_ref] * 5,
         scratch_shapes=[
             pltpu.VMEM((2 * tokens, width), low),
@@ -546,7 +550,7 @@
             dma((2,)),
             dma((2, 5, 24)),
             dma((2, blocks)),
-            dma((3, 2)),
+            dma((4, 2)),
             dma((3,)),
         ],
         compiler_params=pltpu.CompilerParams(
@@ -556,7 +560,7 @@
             flops=4 * blocks * experts * rows * tokens * width, bytes_accessed=200 << 20, transcendentals=0
         ),
         name="gather_dispatch",
-    )(slots, hidden, gates, cots_all)[2:]
+    )(slots, hidden, gates, *cots)[2:]
 
 
 def reduce_kernel(line, slots_ref, grads_ref, outs_ref, sum_ref, part_ref,
@@ -1655,7 +1659,10 @@
     slot_rows = padded(capacity, 8)
     valid_dev = lax.dynamic_slice_in_dim(token_valid, tensor_rank * tok_dev, tok_dev)
     slots_own = slot_table(routes, route_order, valid_dev, experts, capacity)
-    cots_all = lax.all_gather(cotangent, everyone, axis=0, tiled=True)
+    if direct:
+        cots_left = lax.all_gather(cotangent[:, : width // 2], everyone, axis=0, tiled=True)
+    else:
+        cots_all = lax.all_gather(cotangent, everyone, axis=0, tiled=True)
     head_cols = w_query.shape[1]
     residual_float = residual.astype(jnp.float32)
     normed_one, scale_one = rms_apply(residual_float, attn_gain)
@@ -1670,6 +1677,8 @@
         hidden_all, joined_weight, gathered_out, slots = start_exchange(
             hidden, w_query, w_key, w_value, w_out, slots_own, 3
         )
+        right, hidden_all = lax.optimization_barrier((cotangent[:, width // 2 :], hidden_all))
+        cots_right = lax.all_gather(right, everyone, axis=0, tiled=True)
         slots = jnp.swapaxes(slots.reshape(4, 8, local_experts, tok_dev), 0, 1).reshape(32, local_experts, tok_dev)
     else:
         hidden_all = lax.all_gather(hidden, "tensor", axis=0, tiled=True)
@@ -1712,7 +1721,9 @@
         gates_own = probs.T
     scale_two = lax.rsqrt(jnp.mean(x_one * x_one, axis=-1, keepdims=True) + norm_eps)
     if direct:
-        x_slots, c_slots, gate_slots = gather_dispatch(slots, hidden_two, gates_own, cots_all, slot_rows, 1)
+        x_slots, c_slots, gate_slots = gather_dispatch(
+            slots, hidden_two, gates_own, (cots_left, cots_right), slot_rows, 1
+        )
     else:
         gates_all = lax.all_gather(gates_own, everyone, axis=0)
         rows_all = lax.all_gather(hidden_two, everyone, axis=0, tiled=True)

time: 1180 us -> 1190 us (level)
    pallas_call x1, Pallas kernels: 78.5 us -> 119 us  [mixed_out(): pl.pallas_call(functools.partial(mixed_out_kernel, line), out_shape=(jax....]
    pallas_call x1, Pallas kernels: 195 us -> 158 us  [start_exchange(): pl.pallas_call(functools.partial(start_kernel, line), out_shape=(jax.Shap...]
  transfers between devices with their start and end apart: 3 -> 4, of which waited for: 1 -> 1; matrix products, arithmetic and copies ran while one was open for 4% -> 4% of each run, Pallas kernels for 52% -> 52%
where the time goes in v10:
time: 1190 us; the launch traced here: 1180 us
  Pallas kernels  1070 us (90%)
  other arithmetic  31.7 us (3%)
  local copies, waits for them, and re-layouts  22.9 us (2%)
  blocking collectives  20.5 us (2%)
  matrix products  15 us (1%)
  between operations  14.6 us (1%)
    pallas_call x1, Pallas kernels, reduce_all(): pl.pallas_call(functools.partial(reduce_kernel, line), out_shape=(jax.Sha...  184 us
    pallas_call x1, Pallas kernels, gather_dispatch(): pl.pallas_call(functools.partial(gather_dispatch_kernel, line, rows), out...  172 us
    pallas_call x1, Pallas kernels, start_exchange(): pl.pallas_call(functools.partial(start_kernel, line), out_shape=(jax.Shap...  158 us
    pallas_call x1, Pallas kernels, last_exchange(): pl.pallas_call(functools.partial(last_kernel, line), out_shape=(jax.Shape...  122 us
    pallas_call x1, Pallas kernels, mixed_out(): pl.pallas_call(functools.partial(mixed_out_kernel, line), out_shape=(jax....  119 us
    pallas_call x1, Pallas kernels, back_gather(): pl.pallas_call(functools.partial(back_gather_kernel, line), out_shape=(ja...  106 us
    pallas_call x1, Pallas kernels, expert_pass(): pl.pallas_call(kernel, grid_spec=pltpu.PrefetchScalarGridSpec(num_scalar_...  98.3 us
    pallas_call x1, Pallas kernels, weight_grads(): pl.pallas_call(weight_kernel, grid=(experts, width // step), out_shape=(j...  65.2 us
  transfers between devices with their start and end apart: 4, of which 1 were waited for; matrix products, arithmetic and copies ran while one was open for 4% of the time, Pallas kernels for 52%

profile of v10, /device:TPU:0, one launch (start us, length us, event | category | flops | bytes accessed | tf_op | source)
XLA Modules:
  0.0 1179.7 jit_solution(10724315871871211879)
XLA Ops:
  7.3 2.3 fusion.11
  9.6 0.0 all-gather.5.cloned.1.call-start
  9.7 0.1 dynamic-slice_compare_fusion
  9.8 0.3 select_reduce_fusion
  10.1 0.3 fusion.3
  10.4 5.2 convert_reduce_fusion
  15.5 0.6 and_select_fusion.slots_ref
  16.2 1.3 fusion.5.hidden_ref
  17.4 158.3 %start_exchange.1 = (bf16[1024,2048]{1,0:T(8,128)(2,1)}, bf16[2048,1536]{1,0:T(8,128)(2,1)}, bf16[512,2048]{1,0:T(8,128)(2,1)}, s32[32,8,256]{2,1,0:T(8,128)}) custom-call(bf16[256,2048]{1,0:T(8,128)(2,1)} %fusion.5.hidden_ref, bf16[256,512]{1,0:T(8,128)(2,1)} %wq_ref.1, bf16[256,512]{1,0:T(8,128)(2,1)} %wk_ref.1, bf16[256,512]{1,0:T(8,128)(2,1)} %wv_ref.1, ...), custom_call_target="tpu_custom_call" | custom-call | bytes 157286400 | tf_op jit(solution)/shard_map/start_exchange/pallas_call | solution.py:1001
  175.9 10.0 fusion.14.raw_ref
  185.9 2.7 copy-done.12
  188.6 0.3 multiply_reduce_fusion.8
  188.9 11.4 all-reduce.1
  200.4 0.2 copy.53.scale_ref
  200.7 0.8 dynamic_slice.11
  201.4 0.8 dynamic_slice.10
  202.2 0.2 copy.54.column_ref
  202.6 2.8 convert_reduce_fusion.1
  205.4 1.9 fusion.7
  207.3 0.3 pad_maximum_fusion.1
  207.7 18.7 %attend.1 = (bf16[1024,512]{1,0:T(8,128)(2,1)S(1)}, bf16[1024,512]{1,0:T(8,128)(2,1)}, bf16[1024,512]{1,0:T(8,128)(2,1)}, bf16[1024,512]{1,0:T(8,128)(2,1)}, f32[8,1024]{1,0:T(8,128)S(1)}) custom-call(f32[1024,1536]{1,0:T(8,128)} %copy-done.12, f32[1024,2]{1,0:T(8,128)S(1)} %copy.53.scale_ref, f32[2,512]{1,0:T(2,128)S(1)} %pad_maximum_fusion.4.gain_ref, ...), custom_call_target="tpu_custom_call" | custom-call | flops 2147483648 | bytes 8388608 | tf_op jit(solution)/shard_map/attend/pallas_call | solution.py:1513
  226.4 1.0 copy-done.9
  227.4 118.7 %mixed_out.1 = (f32[256,2048]{1,0:T(8,128)}, bf16[256,2048]{1,0:T(8,128)(2,1)}, f32[64,256]{1,0:T(8,128)}) custom-call(bf16[1024,512]{1,0:T(8,128)(2,1)} %get-tuple-element.61.mixed_ref, bf16[512,2048]{1,0:T(8,128)(2,1)} %get-tuple-element.62.w_ref, bf16[256,2048]{1,0:T(8,128)(2,1)} %residual_ref.3, f32[1,2048]{1,0:T(1,128)} %bitcast.50, ...), custom_call_target="tpu_custom_call" | custom-call | bytes 157286400 | tf_op jit(solution)/shard_map/mixed_out/pallas_call | solution.py:1119
  346.2 1.2 copy-done.4
  347.4 0.8 copy-done.7
  348.2 171.6 %gather_dispatch.1 = (bf16[8192,2048]{1,0:T(8,128)(2,1)}, f32[2048,256]{1,0:T(8,128)}, bf16[8,1280,2048]{2,1,0:T(8,128)(2,1)}, bf16[8,1280,2048]{2,1,0:T(8,128)(2,1)}, f32[8,1280,128]{2,1,0:T(8,128)S(1)}) custom-call(s32[32,8,256]{2,1,0:T(8,128)S(1)} %bitcast.42, bf16[256,2048]{1,0:T(8,128)(2,1)S(1)} %copy-done.4, f32[64,256]{1,0:T(8,128)S(1)} %copy-done.7, ...), custom_call_target="tpu_custom_call" | custom-call | flops 21474836480 | bytes 209715200 | tf_op jit(solution)/shard_map/gather_dispatch/pallas_call | solution.py:532
  519.8 2.3 copy-done.11
  522.2 98.3 %experts.1 = (bf16[32,8,48,2048]{3,2,1,0:T(8,128)(2,1)}, bf16[32,8,48,2176]{3,2,1,0:T(8,128)(2,1)}, bf16[8,1280,512]{2,1,0:T(8,128)(2,1)}, bf16[8,1280,256]{2,1,0:T(8,128)(2,1)}) custom-call(s32[1]{0:T(128)} %bitcast.14.first_ref, bf16[8,1280,2048]{2,1,0:T(8,128)(2,1)} %get-tuple-element.68.x_ref, bf16[8,1280,2048]{2,1,0:T(8,128)(2,1)} %get-tuple-element.69.c_ref, ...), custom_call_target="tpu_custom_call" | custom-call | flops 64424509440 | bytes 192937984 | tf_op jit(solution)/shard_map/experts/pallas_call | solution.py:213
  620.5 184.5 %reduce_all.1 = (f32[256,2176]{1,0:T(8,128)}, bf16[8192,2048]{1,0:T(8,128)(2,1)}) custom-call(s32[32,8,256]{2,1,0:T(8,128)} %bitcast.43, bf16[32,8,48,2176]{3,2,1,0:T(8,128)(2,1)} %get-tuple-element.71.grads_ref, bf16[32,8,48,2048]{3,2,1,0:T(8,128)(2,1)} %get-tuple-element.72.outs_ref), custom_call_target="tpu_custom_call" | custom-call | flops 26575110144 | bytes 103809024 | tf_op jit(solution)/shard_map/reduce_all/pallas_call | solution.py:791
  805.0 0.2 reduce-scatter.5.cloned.1.call-start
  805.2 0.6 copy-done.8
  805.8 0.1 copy.56
  805.9 0.1 pad.8.clone
  806.0 0.1 pad.2.clone
  806.0 0.5 copy-done.13
  806.6 0.2 multiply_reduce_fusion.6
  806.8 1.0 fusion.8
  807.8 1.7 fusion.9
  809.5 3.3 multiply_reduce_fusion.4
  812.8 0.9 maximum_maximum_fusion.sums_ref
  813.7 2.4 fusion.10
  816.1 105.6 %back_gather.1 = (bf16[1024,2048]{1,0:T(8,128)(2,1)}, f32[72,2048]{1,0:T(8,128)}) custom-call(bf16[256,2048]{1,0:T(8,128)(2,1)} %get-tuple-element.116.own_ref, f32[72,2048]{1,0:T(8,128)} %maximum_maximum_fusion.sums_ref), custom_call_target="tpu_custom_call" | custom-call | bytes 157286400 | tf_op jit(solution)/shard_map/back_gather/pallas_call | solution.py:1243
  921.8 25.0 %attend_back.1 = (f32[1024,512]{1,0:T(8,128)}, f32[1024,512]{1,0:T(8,128)}, f32[1024,512]{1,0:T(8,128)}) custom-call(bf16[1024,2048]{1,0:T(8,128)(2,1)} %get-tuple-element.76.grad_ref.attn_ref, bf16[512,2048]{1,0:T(8,128)(2,1)} %get-tuple-element.62.w_ref, bf16[1024,512]{1,0:T(8,128)(2,1)} %copy-done.9, bf16[1024,512]{1,0:T(8,128)(2,1)} %get-tuple-element.78.key_ref, ...), custom_call_target="tpu_custom_call" | custom-call | flops 5368709120 | bytes 12582912 | tf_op jit(solution)/shard_map/attend_back/pallas_call | solution.py:1579
  946.8 1.9 convert.11
  948.7 0.3 copy-done.16
  949.0 2.7 multiply_reduce_fusion.1
  951.8 9.1 all-reduce
  960.9 4.3 subtract_convert_fusion.1
  965.2 1.8 pad_maximum_fusion.joined_ref
  967.0 0.7 maximum_maximum_fusion.1.gains_ref
  967.7 122.2 %last_exchange.1 = (f32[256,2048]{1,0:T(8,128)}, f32[256,512]{1,0:T(8,128)}, f32[256,512]{1,0:T(8,128)}, f32[256,512]{1,0:T(8,128)}, f32[512,256]{1,0:T(8,128)}, /*index=5*/f32[8,2048]{1,0:T(8,128)}) custom-call(bf16[1024,1536]{1,0:T(8,128)(2,1)} %pad_maximum_fusion.joined_ref, bf16[2048,1536]{1,0:T(8,128)(2,1)} %get-tuple-element.60.weight_ref, ...), custom_call_target="tpu_custom_call" | custom-call | bytes 262144000 | tf_op jit(solution)/shard_map/last_exchange/pallas_call | solution.py:1403
  1090.0 1.0 copy-done.24
  1091.0 0.6 slice.55
  1091.6 1.6 fusion.12
  1093.2 0.8 slice_bitcast_fusion
  1094.1 65.2 %weight_grads.1 = (f32[8,2048,256]{2,1,0:T(8,128)}, f32[8,2048,256]{2,1,0:T(8,128)}, f32[8,256,2048]{2,1,0:T(8,128)}) custom-call(bf16[8,1280,2048]{2,1,0:T(8,128)(2,1)} %get-tuple-element.68.x_ref, bf16[8,1280,2048]{2,1,0:T(8,128)(2,1)} %get-tuple-element.69.c_ref, bf16[8,1280,512]{2,1,0:T(8,128)(2,1)} %get-tuple-element.86.pre_ref, ...), custom_call_target="tpu_custom_call" | custom-call | flops 32212254720 | bytes 134217728 | tf_op jit(solution)/shard_map/weight_grads/pallas_call | solution.py:178
  1159.3 6.5 reduce-scatter.5.cloned.1.call-done
  1165.8 2.6 add_convert_fusion
  1168.4 1.3 copy.65
  1169.8 0.1 copy-done.23
  1169.8 0.8 copy.66
  1170.6 0.8 copy.67
  1171.4 0.8 copy.68
  1172.2 0.8 copy.69
  (86 shorter events, 0.5 us)
Async XLA Ops:
  7.2 2.5 copy-start.28
  7.2 2.6 copy-start.30
  7.2 2.6 copy-start.31
  7.2 2.8 copy-start.15
  7.2 8.9 copy-start.29
  7.2 338.9 %all-gather.3.cloned.1.call-start = ((), (), s32[]{:S(2)}) async-start(), calls=%async_computation.2 | async-start | bytes 17301504 | tf_op jit(solution)/shard_map/all_gather | solution.py:1663
  9.6 336.5 %all-gather.5.cloned.1.call-start = ((), (), s32[]{:S(2)}) async-start(), calls=%async_computation.3 | async-start | bytes 17301504 | tf_op jit(solution)/shard_map/all_gather | solution.py:1681
  175.8 914.1 %reduce-scatter.3.cloned.1.call-start = ((), (), s32[]{:S(2)}) async-start(), calls=%async_computation.4 | async-start | bytes 37748736 | tf_op jit(solution)/shard_map/reduce_scatter | solution.py:1620
  185.9 2.7 copy-start.12
  188.6 13.6 %copy-start.26 = (s32[3,1024]{1,0:T(4,128)S(1)}, s32[3,1024]{1,0:T(4,128)}, u32[]{:S(2)}) copy-start(s32[3,1024]{1,0:T(4,128)} %param.31) | copy-start | bytes 36868
  188.6 13.9 %copy-start.25 = (s32[32,8,256]{2,1,0:T(8,128)S(1)}, s32[32,8,256]{2,1,0:T(8,128)}, u32[]{:S(2)}) copy-start(s32[32,8,256]{2,1,0:T(8,128)} %get-tuple-element.64) | copy-start | bytes 786436
  202.4 5.3 copy-start.2
  202.5 143.7 %copy-start.3 = (s32[4,8,8,256]{3,2,0,1:T(8,128)}, s32[4,8,8,256]{3,2,0,1:T(8,128)S(1)}, u32[]{:S(2)}) copy-start(s32[4,8,8,256]{3,2,0,1:T(8,128)S(1)} %copy.55) | copy-start | bytes 786436
  202.5 5.2 copy-start.6
  207.7 18.8 %copy-start = (f32[1024,128]{1,0:T(8,128)}, f32[1024,128]{1,0:T(8,128)S(1)}, u32[]{:S(2)}) copy-start(f32[1024,128]{1,0:T(8,128)S(1)} %get-tuple-element.140.cos_ref) | copy-start | bytes 1572868
  207.7 18.7 %copy-start.1 = (f32[1024,128]{1,0:T(8,128)}, f32[1024,128]{1,0:T(8,128)S(1)}, u32[]{:S(2)}) copy-start(f32[1024,128]{1,0:T(8,128)S(1)} %get-tuple-element.141.sin_ref) | copy-start | bytes 1572868
  226.4 1.0 copy-start.9
  227.4 118.7 %copy-start.10 = (f32[8,1024]{1,0:T(8,128)}, f32[8,1024]{1,0:T(8,128)S(1)}, u32[]{:S(2)}) copy-start(f32[8,1024]{1,0:T(8,128)S(1)} %get-tuple-element.80.log_ref) | copy-start | bytes 98308
  346.2 1.2 copy-start.4
  347.4 0.8 copy-start.7
  519.8 2.4 copy-start.11
  804.9 0.8 copy-start.8
  804.9 1.6 copy-start.13
  805.0 2.8 copy-start.5
  805.0 360.8 %reduce-scatter.5.cloned.1.call-start = ((), (), s32[]{:S(2)}) async-start(), calls=%async_computation.5 | async-start | bytes 5242880 | tf_op jit(solution)/shard_map/reduce_scatter | solution.py:1624
  806.6 3.0 copy-start.19
  806.6 3.0 copy-start.27
  809.5 4.2 copy-start.17
  921.8 26.9 %slice-start = ((s8[6291456]{0:T(1024)(128)(4,1)}), s8[4194304]{0:T(1024)(128)(4,1)S(1)}, s32[]{:S(2)}) async-start(s8[6291456]{0:T(1024)(128)(4,1)} %bitcast.44), calls=%async_computation.6 | async-start | bytes 8388608
  921.8 26.9 %slice-start.1 = ((s8[6291456]{0:T(1024)(128)(4,1)}), s8[2097152]{0:T(1024)(128)(4,1)S(1)}, s32[]{:S(2)}) async-start(s8[6291456]{0:T(1024)(128)(4,1)} %bitcast.44), calls=%async_computation.7 | async-start | bytes 4194304
  946.8 2.2 copy-start.16
  1090.0 1.1 copy-start.24
  1094.1 71.7 %copy-start.14 = (f32[256,2048]{1,0:T(8,128)S(1)}, f32[256,2048]{1,0:T(8,128)}, u32[]{:S(2)}) copy-start(f32[256,2048]{1,0:T(8,128)} %get-tuple-element.63) | copy-start | bytes 6291460
  1165.8 2.6 copy-start.18
  1168.4 1.4 copy-start.23
  1168.4 2.2 copy-start.22
  1169.8 1.6 copy-start.21
  1169.8 2.4 copy-start.20
Sparse Core Ops, SparseCore 0:
  11.6 150.3 all-gather.2
  175.9 152.6 all-gather.4
  805.1 267.8 reduce-scatter.2
  1090.1 75.6 reduce-scatter.4

commit v11 on v8

--- a/solution.py
+++ b/solution.py
@@ -617,11 +617,12 @@
             device_id=index, device_id_type=MESH,
         )
 
-    def along(sign, r):
+    def along(sign, r, h):
         target = up if sign > 0 else down
         lane = 0 if sign > 0 else 1
         return pltpu.make_async_remote_copy(
-            src_ref=near.at[r * 4 + 3], dst_ref=target.at[r], send_sem=send_sem.at[6 + lane, r], recv_sem=line_sem.at[lane, r],
+            src_ref=near.at[r * 4 + 3, rows(h)], dst_ref=target.at[r, rows(h)],
+            send_sem=send_sem.at[6 + lane + 2 * h, r], recv_sem=line_sem.at[lane, r, h],
             device_id=peer(y, x, core, z + sign), device_id_type=MESH,
         )
 
@@ -723,19 +724,19 @@
 
             @pl.when(live & (goal(held) > z) & (z == hop))
             def _():
-                if hop:
-                    along(1, held).wait_recv()
-                    for h in range(2):
+                for h in range(2):
+                    if hop:
+                        along(1, held, h).wait_recv()
                         add(held * 4 + 3, rows(h), lambda part: up[held, rows(h), part])
-                along(1, held).start()
+                    along(1, held, h).start()
 
             @pl.when(live & (goal(held) < z) & (line - 1 - z == hop))
             def _():
-                if hop:
-                    along(-1, held).wait_recv()
-                    for h in range(2):
+                for h in range(2):
+                    if hop:
+                        along(-1, held, h).wait_recv()
                         add(held * 4 + 3, rows(h), lambda part: down[held, rows(h), part])
-                along(-1, held).start()
+                    along(-1, held, h).start()
 
         return carry
 
@@ -746,12 +747,14 @@
 
     @pl.when(z > 0)
     def _():
-        along(1, mine).wait_recv()
+        for h in range(2):
+            along(1, mine, h).wait_recv()
         sum_ref[...] += up[mine].astype(jnp.float32)
 
     @pl.when(z < line - 1)
     def _():
-        along(-1, mine).wait_recv()
+        for h in range(2):
+            along(-1, mine, h).wait_recv()
         sum_ref[...] += down[mine].astype(jnp.float32)
 
     def finish(r, carry):
@@ -760,11 +763,13 @@
 
         @pl.when(goal(r) > z)
         def _():
-            along(1, r).wait_send()
+            for h in range(2):
+                along(1, r, h).wait_send()
 
         @pl.when(goal(r) < z)
         def _():
-            along(-1, r).wait_send()
+            for h in range(2):
+                along(-1, r, h).wait_send()
 
         return carry
 
@@ -808,11 +813,11 @@
             dma((2,)),
             dma((4,)),
             dma((line * 4,)),
-            dma((8, line)),
+            dma((10, line)),
             dma((2, line)),
             dma((line, 2)),
             dma((line, 2)),
-            dma((2, line)),
+            dma((2, line, 2)),
         ],
         compiler_params=pltpu.CompilerParams(
             collective_id=collective_id, has_side_effects=True, vmem_limit_bytes=62 << 20

time: 1180 us -> 1170 us (level)
  Pallas kernels: 1070 us -> 1050 us
    pallas_call x1, Pallas kernels: 106 us -> 93.6 us  [back_gather(): pl.pallas_call(functools.partial(back_gather_kernel, line), out_shape=(ja...]
  transfers between devices with their start and end apart: 3 -> 3, of which waited for: 1 -> 1; matrix products, arithmetic and copies ran while one was open for 4% -> 4% of each run, Pallas kernels for 52% -> 51%
where the time goes in v11:
time: 1170 us; the launch traced here: 1160 us
  Pallas kernels  1050 us (90%)
  other arithmetic  34.4 us (3%)
  local copies, waits for them, and re-layouts  20.5 us (2%)
  blocking collectives  18.7 us (2%)
  matrix products  15.1 us (1%)
  between operations  14.5 us (1%)
    pallas_call x1, Pallas kernels, start_exchange(): pl.pallas_call(functools.partial(start_kernel, line), out_shape=(jax.Shap...  195 us
    pallas_call x1, Pallas kernels, reduce_all(): pl.pallas_call(functools.partial(reduce_kernel, line), out_shape=(jax.Sha...  185 us
    pallas_call x1, Pallas kernels, gather_dispatch(): pl.pallas_call(functools.partial(gather_dispatch_kernel, line, rows), out...  173 us
    pallas_call x1, Pallas kernels, last_exchange(): pl.pallas_call(functools.partial(last_kernel, line), out_shape=(jax.Shape...  122 us
    pallas_call x1, Pallas kernels, expert_pass(): pl.pallas_call(kernel, grid_spec=pltpu.PrefetchScalarGridSpec(num_scalar_...  98.3 us
    pallas_call x1, Pallas kernels, back_gather(): pl.pallas_call(functools.partial(back_gather_kernel, line), out_shape=(ja...  93.6 us
    pallas_call x1, Pallas kernels, mixed_out(): pl.pallas_call(functools.partial(mixed_out_kernel, line), out_shape=(jax....  78.5 us
    pallas_call x1, Pallas kernels, weight_grads(): pl.pallas_call(weight_kernel, grid=(experts, width // step), out_shape=(j...  65.2 us
  transfers between devices with their start and end apart: 3, of which 1 were waited for; matrix products, arithmetic and copies ran while one was open for 4% of the time, Pallas kernels for 51%

profile of v11, /device:TPU:0, one launch (start us, length us, event | category | flops | bytes accessed | tf_op | source)
XLA Modules:
  0.0 1165.0 jit_solution(13637180556434286774)
XLA Ops:
  7.2 0.7 all-gather.2.cloned.1.call-update
  7.9 0.0 reduce-scatter.3.cloned.1.call-start
  8.0 0.8 dynamic-slice_compare_fusion
  8.8 1.0 select_reduce_fusion
  9.8 1.5 fusion.3
  11.3 5.2 convert_reduce_fusion
  16.4 0.6 and_select_fusion.slots_ref
  17.1 1.3 fusion.5.hidden_ref
  18.4 194.6 %start_exchange.1 = (bf16[1024,2048]{1,0:T(8,128)(2,1)}, bf16[2048,1536]{1,0:T(8,128)(2,1)}, bf16[512,2048]{1,0:T(8,128)(2,1)}, s32[32,8,256]{2,1,0:T(8,128)}) custom-call(bf16[256,2048]{1,0:T(8,128)(2,1)} %fusion.5.hidden_ref, bf16[256,512]{1,0:T(8,128)(2,1)} %wq_ref.1, bf16[256,512]{1,0:T(8,128)(2,1)} %wk_ref.1, bf16[256,512]{1,0:T(8,128)(2,1)} %wv_ref.1, ...), custom_call_target="tpu_custom_call" | custom-call | bytes 157286400 | tf_op jit(solution)/shard_map/start_exchange/pallas_call | solution.py:1002
  213.0 10.2 fusion.13.raw_ref
  223.2 2.7 copy-done.12
  225.9 0.3 multiply_reduce_fusion.8
  226.2 9.6 all-reduce.1
  235.9 0.2 copy.53.scale_ref
  236.1 0.8 dynamic_slice.11
  236.9 0.8 dynamic_slice.10
  237.6 0.2 copy.54.column_ref
  238.0 2.8 convert_reduce_fusion.1
  240.9 1.9 fusion.7
  242.8 0.3 pad_maximum_fusion.1
  243.1 19.3 %attend.1 = (bf16[1024,512]{1,0:T(8,128)(2,1)S(1)}, bf16[1024,512]{1,0:T(8,128)(2,1)}, bf16[1024,512]{1,0:T(8,128)(2,1)}, bf16[1024,512]{1,0:T(8,128)(2,1)}, f32[8,1024]{1,0:T(8,128)S(1)}) custom-call(f32[1024,1536]{1,0:T(8,128)} %copy-done.12, f32[1024,2]{1,0:T(8,128)S(1)} %copy.53.scale_ref, f32[2,512]{1,0:T(2,128)S(1)} %pad_maximum_fusion.4.gain_ref, ...), custom_call_target="tpu_custom_call" | custom-call | flops 2147483648 | bytes 8388608 | tf_op jit(solution)/shard_map/attend/pallas_call | solution.py:1514
  262.4 1.0 copy-done.9
  263.4 78.5 %mixed_out.1 = (f32[256,2048]{1,0:T(8,128)}, bf16[256,2048]{1,0:T(8,128)(2,1)}, f32[64,256]{1,0:T(8,128)}) custom-call(bf16[1024,512]{1,0:T(8,128)(2,1)} %get-tuple-element.58.mixed_ref, bf16[512,2048]{1,0:T(8,128)(2,1)} %get-tuple-element.59.w_ref, bf16[256,2048]{1,0:T(8,128)(2,1)} %residual_ref.3, f32[1,2048]{1,0:T(1,128)} %bitcast.50, ...), custom_call_target="tpu_custom_call" | custom-call | bytes 157286400 | tf_op jit(solution)/shard_map/mixed_out/pallas_call | solution.py:1120
  342.0 1.2 copy-done.4
  343.2 0.8 copy-done.7
  344.0 172.9 %gather_dispatch.1 = (bf16[8192,2048]{1,0:T(8,128)(2,1)}, f32[2048,256]{1,0:T(8,128)}, bf16[8,1280,2048]{2,1,0:T(8,128)(2,1)}, bf16[8,1280,2048]{2,1,0:T(8,128)(2,1)}, f32[8,1280,128]{2,1,0:T(8,128)S(1)}) custom-call(s32[32,8,256]{2,1,0:T(8,128)S(1)} %bitcast.42, bf16[256,2048]{1,0:T(8,128)(2,1)S(1)} %copy-done.4, f32[64,256]{1,0:T(8,128)S(1)} %copy-done.7, ...), custom_call_target="tpu_custom_call" | custom-call | flops 21474836480 | bytes 209715200 | tf_op jit(solution)/shard_map/gather_dispatch/pallas_call | solution.py:528
  517.0 2.3 copy-done.11
  519.3 98.3 %experts.1 = (bf16[32,8,48,2048]{3,2,1,0:T(8,128)(2,1)}, bf16[32,8,48,2176]{3,2,1,0:T(8,128)(2,1)}, bf16[8,1280,512]{2,1,0:T(8,128)(2,1)}, bf16[8,1280,256]{2,1,0:T(8,128)(2,1)}) custom-call(s32[1]{0:T(128)} %bitcast.14.first_ref, bf16[8,1280,2048]{2,1,0:T(8,128)(2,1)} %get-tuple-element.64.x_ref, bf16[8,1280,2048]{2,1,0:T(8,128)(2,1)} %get-tuple-element.65.c_ref, ...), custom_call_target="tpu_custom_call" | custom-call | flops 64424509440 | bytes 192937984 | tf_op jit(solution)/shard_map/experts/pallas_call | solution.py:213
  617.6 184.6 %reduce_all.1 = (f32[256,2176]{1,0:T(8,128)}, bf16[8192,2048]{1,0:T(8,128)(2,1)}) custom-call(s32[32,8,256]{2,1,0:T(8,128)} %bitcast.43, bf16[32,8,48,2176]{3,2,1,0:T(8,128)(2,1)} %get-tuple-element.67.grads_ref, bf16[32,8,48,2048]{3,2,1,0:T(8,128)(2,1)} %get-tuple-element.68.outs_ref), custom_call_target="tpu_custom_call" | custom-call | flops 26575110144 | bytes 103809024 | tf_op jit(solution)/shard_map/reduce_all/pallas_call | solution.py:792
  802.3 0.2 reduce-scatter.5.cloned.1.call-start
  802.5 0.6 copy-done.8
  803.0 0.1 copy.56
  803.1 0.1 pad.8.clone
  803.2 0.1 pad.2.clone
  803.3 0.5 copy-done.13
  803.8 0.2 multiply_reduce_fusion.6
  804.1 1.0 fusion.8
  805.1 1.7 fusion.9
  806.8 3.3 multiply_reduce_fusion.4
  810.1 0.9 maximum_maximum_fusion.sums_ref
  811.0 2.4 fusion.10
  813.4 93.6 %back_gather.1 = (bf16[1024,2048]{1,0:T(8,128)(2,1)}, f32[72,2048]{1,0:T(8,128)}) custom-call(bf16[256,2048]{1,0:T(8,128)(2,1)} %get-tuple-element.112.own_ref, f32[72,2048]{1,0:T(8,128)} %maximum_maximum_fusion.sums_ref), custom_call_target="tpu_custom_call" | custom-call | bytes 157286400 | tf_op jit(solution)/shard_map/back_gather/pallas_call | solution.py:1244
  907.0 25.0 %attend_back.1 = (f32[1024,512]{1,0:T(8,128)}, f32[1024,512]{1,0:T(8,128)}, f32[1024,512]{1,0:T(8,128)}) custom-call(bf16[1024,2048]{1,0:T(8,128)(2,1)} %get-tuple-element.72.grad_ref.attn_ref, bf16[512,2048]{1,0:T(8,128)(2,1)} %get-tuple-element.59.w_ref, bf16[1024,512]{1,0:T(8,128)(2,1)} %copy-done.9, bf16[1024,512]{1,0:T(8,128)(2,1)} %get-tuple-element.74.key_ref, ...), custom_call_target="tpu_custom_call" | custom-call | flops 5368709120 | bytes 12582912 | tf_op jit(solution)/shard_map/attend_back/pallas_call | solution.py:1580
  932.0 1.9 convert.11
  933.9 0.3 copy-done.16
  934.2 2.7 multiply_reduce_fusion.1
  936.9 9.1 all-reduce
  946.1 4.3 subtract_convert_fusion.1
  950.4 1.8 pad_maximum_fusion.joined_ref
  952.2 0.7 maximum_maximum_fusion.1.gains_ref
  952.9 122.3 %last_exchange.1 = (f32[256,2048]{1,0:T(8,128)}, f32[256,512]{1,0:T(8,128)}, f32[256,512]{1,0:T(8,128)}, f32[256,512]{1,0:T(8,128)}, f32[512,256]{1,0:T(8,128)}, /*index=5*/f32[8,2048]{1,0:T(8,128)}) custom-call(bf16[1024,1536]{1,0:T(8,128)(2,1)} %pad_maximum_fusion.joined_ref, bf16[2048,1536]{1,0:T(8,128)(2,1)} %get-tuple-element.57.weight_ref, ...), custom_call_target="tpu_custom_call" | custom-call | bytes 262144000 | tf_op jit(solution)/shard_map/last_exchange/pallas_call | solution.py:1404
  1075.2 1.0 copy-done.24
  1076.3 0.6 slice.47
  1076.9 1.6 fusion.11
  1078.5 0.8 slice_bitcast_fusion
  1079.3 65.2 %weight_grads.1 = (f32[8,2048,256]{2,1,0:T(8,128)}, f32[8,2048,256]{2,1,0:T(8,128)}, f32[8,256,2048]{2,1,0:T(8,128)}) custom-call(bf16[8,1280,2048]{2,1,0:T(8,128)(2,1)} %get-tuple-element.64.x_ref, bf16[8,1280,2048]{2,1,0:T(8,128)(2,1)} %get-tuple-element.65.c_ref, bf16[8,1280,512]{2,1,0:T(8,128)(2,1)} %get-tuple-element.82.pre_ref, ...), custom_call_target="tpu_custom_call" | custom-call | flops 32212254720 | bytes 134217728 | tf_op jit(solution)/shard_map/weight_grads/pallas_call | solution.py:178
  1144.5 6.5 reduce-scatter.5.cloned.1.call-done
  1151.0 2.6 add_convert_fusion
  1153.7 1.3 copy.65
  1155.0 0.1 copy-done.23
  1155.0 0.8 copy.66
  1155.8 0.8 copy.67
  1156.6 0.8 copy.68
  1157.4 0.8 copy.69
  (78 shorter events, 0.4 us)
Async XLA Ops:
  7.2 9.9 copy-start.15
  7.2 9.9 copy-start.29
  7.2 334.7 %all-gather.2.cloned.1.call-start = ((), (), s32[]{:S(2)}) async-start(), calls=%async_computation.2 | async-start | bytes 34603008 | tf_op jit(solution)/shard_map/all_gather | solution.py:1663
  7.9 1067.3 %reduce-scatter.3.cloned.1.call-start = ((), (), s32[]{:S(2)}) async-start(), calls=%async_computation.3 | async-start | bytes 37748736 | tf_op jit(solution)/shard_map/reduce_scatter | solution.py:1621
  223.2 2.7 copy-start.12
  225.9 11.8 %copy-start.26 = (s32[3,1024]{1,0:T(4,128)S(1)}, s32[3,1024]{1,0:T(4,128)}, u32[]{:S(2)}) copy-start(s32[3,1024]{1,0:T(4,128)} %param.31) | copy-start | bytes 36868
  225.9 11.8 %copy-start.28 = (s32[1024]{0:T(1024)S(1)}, s32[1024]{0:T(1024)}, u32[]{:S(2)}) copy-start(s32[1024]{0:T(1024)} %param.32) | copy-start | bytes 12292
  225.9 12.0 %copy-start.25 = (s32[32,8,256]{2,1,0:T(8,128)S(1)}, s32[32,8,256]{2,1,0:T(8,128)}, u32[]{:S(2)}) copy-start(s32[32,8,256]{2,1,0:T(8,128)} %get-tuple-element.61) | copy-start | bytes 786436
  237.9 5.3 copy-start.2
  237.9 104.0 %copy-start.3 = (s32[4,8,8,256]{3,2,0,1:T(8,128)}, s32[4,8,8,256]{3,2,0,1:T(8,128)S(1)}, u32[]{:S(2)}) copy-start(s32[4,8,8,256]{3,2,0,1:T(8,128)S(1)} %copy.55) | copy-start | bytes 786436
  238.0 5.2 copy-start.6
  243.1 19.3 %copy-start = (f32[1024,128]{1,0:T(8,128)}, f32[1024,128]{1,0:T(8,128)S(1)}, u32[]{:S(2)}) copy-start(f32[1024,128]{1,0:T(8,128)S(1)} %get-tuple-element.134.cos_ref) | copy-start | bytes 1572868
  243.1 19.3 %copy-start.1 = (f32[1024,128]{1,0:T(8,128)}, f32[1024,128]{1,0:T(8,128)S(1)}, u32[]{:S(2)}) copy-start(f32[1024,128]{1,0:T(8,128)S(1)} %get-tuple-element.135.sin_ref) | copy-start | bytes 1572868
  262.4 1.0 copy-start.9
  263.4 78.5 %copy-start.10 = (f32[8,1024]{1,0:T(8,128)}, f32[8,1024]{1,0:T(8,128)S(1)}, u32[]{:S(2)}) copy-start(f32[8,1024]{1,0:T(8,128)S(1)} %get-tuple-element.76.log_ref) | copy-start | bytes 98308
  342.0 1.2 copy-start.4
  343.2 0.8 copy-start.7
  516.9 2.4 copy-start.11
  802.2 0.8 copy-start.8
  802.2 1.6 copy-start.13
  802.2 2.8 copy-start.5
  802.3 348.8 %reduce-scatter.5.cloned.1.call-start = ((), (), s32[]{:S(2)}) async-start(), calls=%async_computation.4 | async-start | bytes 5242880 | tf_op jit(solution)/shard_map/reduce_scatter | solution.py:1625
  803.8 3.0 copy-start.19
  803.8 3.0 copy-start.27
  806.8 4.2 copy-start.17
  906.9 26.9 %slice-start = ((s8[6291456]{0:T(1024)(128)(4,1)}), s8[4194304]{0:T(1024)(128)(4,1)S(1)}, s32[]{:S(2)}) async-start(s8[6291456]{0:T(1024)(128)(4,1)} %bitcast.44), calls=%async_computation.5 | async-start | bytes 8388608
  907.0 26.9 %slice-start.1 = ((s8[6291456]{0:T(1024)(128)(4,1)}), s8[2097152]{0:T(1024)(128)(4,1)S(1)}, s32[]{:S(2)}) async-start(s8[6291456]{0:T(1024)(128)(4,1)} %bitcast.44), calls=%async_computation.6 | async-start | bytes 4194304
  932.0 2.2 copy-start.16
  1075.2 1.1 copy-start.24
  1079.3 71.7 %copy-start.14 = (f32[256,2048]{1,0:T(8,128)S(1)}, f32[256,2048]{1,0:T(8,128)}, u32[]{:S(2)}) copy-start(f32[256,2048]{1,0:T(8,128)} %get-tuple-element.60) | copy-start | bytes 6291460
  1151.0 2.6 copy-start.18
  1153.7 1.4 copy-start.23
  1153.7 2.2 copy-start.22
  1155.0 1.6 copy-start.21
  1155.0 2.4 copy-start.20
Sparse Core Ops, SparseCore 0:
  11.0 248.3 all-gather.1
  802.4 255.7 reduce-scatter.2
  1075.4 75.6 reduce-scatter.4
